TPU v7x, 128 devices: a whole 4x4x4 slice. The times are simulated.
128 devices in a mesh: seq: 8 (over x, core), exp: 16 (over y, z).
Axes of the slice: x: 4, y: 4, z: 4, core: 2. Of those that a mesh axis runs over, the one named last changes fastest.
Arguments:
- xin: bfloat16 [512, 4, 8192], P('seq', None, 'exp'), may hold values from -6 to 6
- zin: bfloat16 [512, 4, 8192], P('seq', None, 'exp'), may hold values from -6 to 6
- conv_weight: float32 [4, 8192], P(None, 'exp'), may hold values from -3 to 3
- conv_bias: float32 [8192], P('exp'), may hold values from -3 to 3
- xproj_weight: bfloat16 [8192, 288], P('exp'), may hold values from -0.0625 to 0.0625
- dtproj_weight: bfloat16 [256, 8192], P(None, 'exp'), may hold values from -0.375 to 0.375
- dt_bias: float32 [8192], P('exp'), may hold values from -5 to -3
- a_log: float32 [16, 8192], P(None, 'exp'), may hold values from -3 to 1
- skip: float32 [8192], P('exp'), may hold values from 0.2 to 1
- out_weight: bfloat16 [8192, 4096], P('exp'), may hold values from -0.0625 to 0.0625
- resid: bfloat16 [512, 4, 4096], P(('seq', 'exp')), may hold values from -6 to 6
- norm_gain: float32 [4096], replicated, may hold values from 0.5 to 1.5
- expert_ids: int32 [512, 4, 2], P(('seq', 'exp')), may hold values from 0 to 7, all different within a row; in each aligned block of 16 rows (0 to 15, 16 to 31, ..., all dimensions but the last counted through in order) at most 8 rows name the same one
- gate_weights: bfloat16 [512, 4, 2], P(('seq', 'exp')), may hold values from 0.19921875 to 1
- w_gate: bfloat16 [16, 4096, 6144], P('exp', None, 'seq'), may hold values from -0.09375 to 0.09375
- w_up: bfloat16 [16, 4096, 6144], P('exp', None, 'seq'), may hold values from -0.09375 to 0.09375
- w_down: bfloat16 [16, 6144, 4096], P('exp', 'seq'), may hold values from -0.0546875 to 0.0546875
Outputs:
- layer_out: bfloat16 [512, 4, 4096], P(('seq', 'exp'))
Inputs may be any that keep to these rules, and one draw needn't show every extreme that they name: `expert_ids`: tokens are ordered by position, then document; in each aligned block of 16 such tokens (the tokens of one device), every expert is named at most 8 times, and in every draw some expert is named exactly 8 times in some block. Each token names 2 different experts.
All inputs are finite; a program needn't handle non-finite values.
Results may differ from a plain program's by a relative error of at most 0.03.
Values may be sent and summed in bfloat16 or wider, within the bound.
No kernel may reach another device: no remote copies, remote signals or barrier semaphores. Data moves between devices by JAX's collectives and lax.ppermute only.
A program may use at most 128 MiB of HBM per device.

v0:
```python
import jax
import jax.numpy as jnp
from jax import lax
from jax.sharding import PartitionSpec as P

D = 4096
STATE = 16
CONV = 4
RANK = 256
EXPERTS = 8
TOPK = 2


def passed_along(value, axis, by):
    count = lax.axis_size(axis)
    pairs = [(i, i + by) for i in range(count) if 0 <= i + by < count]
    return lax.ppermute(value, axis, pairs)


def entering(value, axis, join, neutral):
    place = lax.axis_index(axis)
    gathered = jax.tree.map(
        lambda a, kind: lax.all_gather(a.astype(kind), axis), value, (jnp.bfloat16, jnp.bfloat16)
    )
    state = jax.tree.map(lambda a, e: jnp.zeros_like(a) + jnp.asarray(e, a.dtype), value, neutral)

    def one(step, state):
        return join(
            state,
            jax.tree.map(
                lambda a, own: lax.dynamic_index_in_dim(a, step, 0, False).astype(own.dtype),
                gathered,
                value,
            ),
        )

    return lax.fori_loop(0, place, one, state)


def conv_inputs(window, conv_weight, conv_bias, length):
    running = jnp.zeros(window[:length].shape, jnp.float32) + conv_bias
    for offset in range(CONV):
        running = running + conv_weight[offset] * window[offset : offset + length]
    return running


def make_step(decay_rate):

    def advance(carry_state, series_now):
        step_now, input_now, read_now, value_now = series_now
        factor = jnp.exp(step_now[:, None, :] * decay_rate[None])
        carry_state = (
            factor * carry_state + (step_now * value_now)[:, None, :] * input_now[:, :, None]
        )
        return (carry_state, jnp.sum(read_now[:, :, None] * carry_state, axis=1))

    return advance


def chain(earlier, later):
    return (earlier[0] * later[0], later[0] * earlier[1] + later[1])


def slot_select(route_ids, capacity):
    flat_ids = route_ids.reshape(-1)
    onehot = (flat_ids[:, None] == jnp.arange(EXPERTS, dtype=jnp.int32)[None, :]).astype(jnp.int32)
    before = jnp.sum((jnp.cumsum(onehot, axis=0) - onehot) * onehot, axis=1)
    target = flat_ids * capacity + before
    matches = jnp.arange(EXPERTS * capacity, dtype=jnp.int32)[:, None] == target[None, :]
    return matches.reshape(EXPERTS * capacity, route_ids.shape[0], route_ids.shape[1])


def per_device(
    xin,
    zin,
    conv_weight,
    conv_bias,
    xproj_weight,
    dtproj_weight,
    dt_bias,
    a_log,
    skip,
    out_weight,
    resid,
    norm_gain,
    expert_ids,
    gate_weights,
    w_gate,
    w_up,
    w_down,
):
    section = xin.shape[0]
    edge_rows = passed_along(xin[section - (CONV - 1) :], "seq", 1)
    window = jnp.concatenate([edge_rows, xin], axis=0).astype(jnp.float32)
    inner_act = jax.nn.silu(conv_inputs(window, conv_weight, conv_bias, section)).astype(
        jnp.bfloat16
    )
    inner_f = inner_act.astype(jnp.float32)
    projected = jnp.einsum(
        "pbc,cr->pbr", inner_act, xproj_weight, preferred_element_type=jnp.float32
    )
    projected = lax.psum(projected.astype(jnp.bfloat16), "exp").astype(jnp.float32)
    low_rank = projected[..., :RANK].astype(jnp.bfloat16)
    in_state = projected[..., RANK : RANK + STATE]
    out_state = projected[..., RANK + STATE :]
    step_size = jax.nn.softplus(
        jnp.einsum("pbr,rc->pbc", low_rank, dtproj_weight, preferred_element_type=jnp.float32)
        + dt_bias
    )
    decay_rate = -jnp.exp(a_log)
    advance = make_step(decay_rate)
    series = (step_size, in_state, out_state, inner_f)
    zero_state = jnp.zeros((xin.shape[1], STATE, xin.shape[2]), jnp.float32)
    final_local, local_out = lax.scan(advance, zero_state, series)
    total_decay = jnp.exp(jnp.sum(step_size, axis=0)[:, None, :] * decay_rate[None])
    identity = (jnp.ones_like(total_decay), jnp.zeros_like(final_local))
    incoming = entering((total_decay, final_local), "seq", chain, identity)[1]
    ignored, ssm_out = lax.scan(advance, incoming, series)
    mixed_in = ((ssm_out + skip * inner_f) * jax.nn.silu(zin.astype(jnp.float32))).astype(
        jnp.bfloat16
    )
    row_block = mixed_in
    mamba_rows = lax.psum_scatter(
        jnp.einsum("pbc,cd->pbd", row_block, out_weight, preferred_element_type=jnp.float32).astype(
            jnp.bfloat16
        ),
        "exp",
        scatter_dimension=0,
        tiled=True,
    ).astype(jnp.float32)
    hidden_state = resid.astype(jnp.float32) + mamba_rows
    norm_scale = lax.rsqrt(jnp.mean(hidden_state * hidden_state, axis=-1, keepdims=True) + 1e-05)
    normed = (hidden_state * norm_scale * norm_gain).astype(jnp.bfloat16)
    row_count = resid.shape[0] * resid.shape[1]
    capacity = 2 * TOPK * row_count // EXPERTS
    splits = lax.axis_size("exp") // EXPERTS
    tokens = normed.reshape(row_count, D)
    route_ids = expert_ids.reshape(row_count, TOPK)
    gate_vals = gate_weights.reshape(row_count, TOPK)
    matches = slot_select(route_ids, capacity)
    chosen = jnp.sum(matches.astype(jnp.int32), axis=2).astype(jnp.bfloat16)
    outgoing = (
        jnp.dot(chosen, tokens, preferred_element_type=jnp.float32)
        .astype(jnp.bfloat16)
        .reshape(EXPERTS, capacity, D)
    )
    arrived = lax.all_to_all(
        jnp.tile(outgoing, (splits, 1, 1)), "exp", split_axis=0, concat_axis=0, tiled=True
    )
    everything = lax.all_gather(arrived, "seq", axis=0, tiled=True)
    row_block = everything
    expert_row_block = row_block.reshape(-1, D)
    gate_act = jnp.dot(expert_row_block, w_gate[0], preferred_element_type=jnp.float32)
    up_act = jnp.dot(expert_row_block, w_up[0], preferred_element_type=jnp.float32)
    hidden = (jax.nn.silu(gate_act) * up_act).astype(jnp.bfloat16)
    own_rows = lax.psum_scatter(
        jnp.dot(hidden, w_down[0], preferred_element_type=jnp.float32)
        .reshape(lax.axis_size("seq") * arrived.shape[0], capacity, D)
        .astype(jnp.bfloat16),
        "seq",
        scatter_dimension=0,
        tiled=True,
    ).astype(jnp.float32)
    returned = lax.all_to_all(
        own_rows.astype(jnp.bfloat16), "exp", split_axis=0, concat_axis=0, tiled=True
    ).astype(own_rows.dtype)
    summed = jnp.sum(returned.reshape(splits, EXPERTS * capacity, D), axis=0)
    weights = jnp.sum(matches.astype(jnp.float32) * gate_vals.astype(jnp.float32)[None], axis=2)
    expert_out = jnp.dot(weights.T, summed, precision=lax.Precision.HIGHEST)
    return (hidden_state + expert_out.reshape(hidden_state.shape)).astype(jnp.bfloat16)


def solution(mesh):
    placed = (
        P("seq", None, "exp"),
        P("seq", None, "exp"),
        P(None, "exp"),
        P("exp"),
        P("exp", None),
        P(None, "exp"),
        P("exp"),
        P(None, "exp"),
        P("exp"),
        P("exp", None),
        P(("seq", "exp"), None, None),
        P(),
        P(("seq", "exp"), None, None),
        P(("seq", "exp"), None, None),
        P("exp", None, "seq"),
        P("exp", None, "seq"),
        P("exp", "seq", None),
    )
    return jax.shard_map(
        per_device,
        mesh=mesh,
        in_specs=placed,
        out_specs=P(("seq", "exp"), None, None),
        check_vma=False,
    )
```

profile of v0, /device:TPU:0, one launch (start us, length us, event | category | flops | bytes accessed | tf_op | source)
XLA Modules:
  0.0 484.9 jit_solution(7767882943626385610)
XLA Ops:
  6.6 0.8 slice.38
  7.4 1.3 collective-permute-start
  8.6 0.9 fusion.43
  9.5 1.1 maximum_convert_fusion
  10.7 1.2 fusion.39
  11.8 1.0 convolution_convert_fusion.3
  12.9 88.9 %all-reduce.4.cloned.1.call-done = bf16[64,4,288]{2,0,1:T(8,128)(2,1)} async-done(((bf16[64,4,288]{2,0,1:T(8,128)(2,1)}), bf16[64,4,288]{2,0,1:T(8,128)(2,1)}) %all-reduce.4.cloned.1.call-update) | async-done | bytes 147472 | tf_op jit(solution)/shard_map/psum | solution.py:102
  101.9 1.2 fusion.35
  103.8 1.7 fusion.42
  105.5 10.3 %while.37 = (s32[]{:T(128)}, f32[4,16,512]{2,1,0:T(8,128)S(1)}, f32[64,4,512]{2,1,0:T(4,128)S(1)}, f32[16,512]{1,0:T(8,128)S(1)}, f32[64,4,512]{2,1,0:T(4,128)S(...) while((s32[]{:T(128)}, f32[4,16,512]{2,1,0:T(8,128)S(1)}, f32[64,4,512]{2,1,0:T(4,128)S(1)}, ...), condition=%wide.region_3.4_spmd.clone, body=%wide.region_2.3_spmd.clone.sunk | while | flops 165891 | bytes 353131 | solution.py:114
  115.8 13.4 %all-gather = bf16[32,16,512]{2,1,0:T(8,128)(2,1)S(1)} all-gather(bf16[4,16,512]{2,1,0:T(8,128)(2,1)S(1)} %convert_element_type.103), channel_id=2, replica_groups=mesh['seq'=8,'exp'=16] {'seq'}, dimensions={0}, use_global_device_ids=true | all-gather | bytes 589824 | tf_op jit(solution)/shard_map/all_gather | solution.py:23
  129.3 13.1 %all_gather.13 = bf16[8,4,16,512]{3,2,1,0:T(8,128)(2,1)S(1)} all-gather(bf16[1,4,16,512]{3,2,1,0:T(8,128)(2,1)S(1)} %exponential_convert_fusion), channel_id=1, replica_groups=mesh['seq'=8,'exp'=16] {'seq'}, dimensions={0}, use_global_device_ids=true | all-gather | bytes 589824 | tf_op jit(solution)/shard_map/all_gather | solution.py:23
  142.4 58.7 %while.36 = (s32[]{:T(128)}, f32[4,16,512]{2,1,0:T(8,128)S(1)}, f32[64,4,512]{2,1,0:T(4,128)S(1)}, f32[64,4,512]{2,1,0:T(4,128)S(1)}, f32[16,512]{1,0:T(8,128)S(...) while((s32[]{:T(128)}, f32[4,16,512]{2,1,0:T(8,128)S(1)}, ...), condition=%wide.region_8.9_spmd, body=%wide.region_6.8_spmd.sunk | while | flops 196610 | bytes 378481 | solution.py:118
  142.5 0.7 constant_dynamic-slice_fusion.3
  143.4 0.7 constant_dynamic-slice_fusion.3
  144.3 0.7 constant_dynamic-slice_fusion.3
  145.2 0.7 constant_dynamic-slice_fusion.3
  146.2 0.7 constant_dynamic-slice_fusion.3
  147.1 0.7 constant_dynamic-slice_fusion.3
  148.0 0.7 constant_dynamic-slice_fusion.3
  148.9 0.7 constant_dynamic-slice_fusion.3
  149.8 0.7 constant_dynamic-slice_fusion.3
  150.7 0.7 constant_dynamic-slice_fusion.3
  151.6 0.7 constant_dynamic-slice_fusion.3
  152.6 0.7 constant_dynamic-slice_fusion.3
  153.5 0.7 constant_dynamic-slice_fusion.3
  154.4 0.7 constant_dynamic-slice_fusion.3
  155.3 0.7 constant_dynamic-slice_fusion.3
  156.2 0.7 constant_dynamic-slice_fusion.3
  157.1 0.7 constant_dynamic-slice_fusion.3
  158.0 0.7 constant_dynamic-slice_fusion.3
  159.0 0.7 constant_dynamic-slice_fusion.3
  159.9 0.7 constant_dynamic-slice_fusion.3
  160.8 0.7 constant_dynamic-slice_fusion.3
  179.1 0.8 constant_dynamic-slice_fusion.3
  180.0 0.8 constant_dynamic-slice_fusion.3
  180.9 0.8 constant_dynamic-slice_fusion.3
  181.9 0.8 constant_dynamic-slice_fusion.3
  182.8 0.8 constant_dynamic-slice_fusion.3
  183.7 0.8 constant_dynamic-slice_fusion.3
  184.7 0.8 constant_dynamic-slice_fusion.3
  185.6 0.8 constant_dynamic-slice_fusion.3
  193.9 0.7 constant_dynamic-slice_fusion.3
  194.8 0.7 constant_dynamic-slice_fusion.3
  195.7 0.7 constant_dynamic-slice_fusion.3
  196.6 0.7 constant_dynamic-slice_fusion.3
  197.5 0.7 constant_dynamic-slice_fusion.3
  198.5 0.7 constant_dynamic-slice_fusion.3
  199.4 0.7 constant_dynamic-slice_fusion.3
  200.3 0.7 constant_dynamic-slice_fusion.3
  201.2 1.3 fusion.30
  202.6 4.8 convolution_convert_fusion.1
  209.6 87.6 %all-reduce.6.cloned.1.call-done = bf16[64,4,4096]{2,0,1:T(8,128)(2,1)} async-done(((bf16[64,4,4096]{2,0,1:T(8,128)(2,1)}), bf16[64,4,4096]{2,0,1:T(8,128)(2,1)}) %all-reduce.6.cloned.1.call-update) | async-done | bytes 2097168
  297.2 1.0 constant_dynamic-slice_fusion.1
  299.2 20.6 %all_to_all.10 = bf16[16,8,4096]{2,1,0:T(8,128)(2,1)} all-to-all(bf16[16,8,4096]{2,1,0:T(8,128)(2,1)S(1)} %bitcast.113), channel_id=1, replica_groups=mesh['seq'=8,'exp'=16] {'exp'}, dimensions={0} | all-to-all | bytes 2097152 | tf_op jit(solution)/shard_map/all_to_all | solution.py:147
  320.0 47.4 %all-gather.3.cloned.1.call-done = bf16[128,8,4096]{2,1,0:T(8,128)(2,1)} async-done(((bf16[16,8,4096]{2,1,0:T(8,128)(2,1)}), bf16[128,8,4096]{2,1,0:T(8,128)(2,1)}) %all-gather.3.cloned.1.call-update) | async-done | bytes 8388624 | tf_op jit(solution)/shard_map/all_gather | solution.py:150
  367.5 11.0 %fusion.1 = f32[1024,768]{1,0:T(8,128)S(1)} fusion(bf16[128,8,4096]{2,1,0:T(8,128)(2,1)} %all-gather.3.cloned.1.call-done, bf16[1,4096,768]{2,1,0:T(8,128)(2,1)} %param.38), kind=kOutput, calls=%fused_computation.14 | convolution fusion | flops 6442450944 | bytes 17825792 | tf_op jit(solution)/shard_map/dot_general | solution.py:154
  378.5 9.9 %fusion.16 = bf16[128,8,768]{2,1,0:T(8,128)(2,1)S(1)} fusion(f32[1024,768]{1,0:T(8,128)S(1)} %fusion.1, bf16[1,4096,768]{2,1,0:T(8,128)(2,1)} %param.37, bf16[128,8,4096]{2,1,0:T(8,128)(2,1)S(1)} %copy-done.9), kind=kOutput, calls=%fused_computation.31 | convolution fusion | flops 6447169536 | bytes 19398656 | tf_op jit(solution)/shard_map/dot_general | solution.py:153
  388.5 8.9 %convolution_convert_fusion = bf16[128,8,4096]{2,0,1:T(8,128)(2,1)} fusion(bf16[1,768,4096]{2,1,0:T(8,128)(2,1)S(1)} %bitcast.122, bf16[128,8,768]{2,1,0:T(8,128)(2,1)S(1)} %fusion.16), kind=kOutput, calls=%fused_computation.18 | convolution fusion | flops 6446645248 | bytes 16252928 | tf_op jit(solution)/shard_map/dot_general | solution.py:157
  397.4 52.7 %reduce-scatter.3.cloned.1.call-done = bf16[16,8,4096]{2,0,1:T(8,128)(2,1)} async-done(((bf16[128,8,4096]{2,0,1:T(8,128)(2,1)}), bf16[16,8,4096]{2,0,1:T(8,128)(2,1)}) %reduce-scatter.3.cloned.1.call-update) | async-done | bytes 1048592 | tf_op jit(solution)/shard_map/reduce_scatter | solution.py:156
  450.1 2.8 copy.87
  452.9 7.0 %all-to-all-start.1 = ((bf16[16,8,4096]{2,1,0:T(8,128)(2,1)}), bf16[16,8,4096]{2,1,0:T(8,128)(2,1)S(1)}, u32[]{:S(2)}, u32[]{:S(2)}) async-start(bf16[16,8,4096]{2,1,0:T(8,128)(2,1)} %copy.87), calls=%async_computation.2 | async-start | bytes 2097152 | tf_op jit(solution)/shard_map/all_to_all | solution.py:164
  460.1 16.7 %all-to-all-done.1 = bf16[16,8,4096]{2,1,0:T(8,128)(2,1)S(1)} async-done(((bf16[16,8,4096]{2,1,0:T(8,128)(2,1)}), bf16[16,8,4096]{2,1,0:T(8,128)(2,1)S(1)}, u32[]{:S(2)}, u32[]{:S(2)}) %all-to-all-start.1) | async-done | bytes 1048608 | tf_op jit(solution)/shard_map/all_to_all | solution.py:164
  477.0 1.4 fusion.9
  (672 shorter events, 40.5 us)
Async XLA Ops:
  6.5 5.3 %copy-start = (bf16[512,288]{0,1:T(8,128)(2,1)S(1)}, bf16[512,288]{0,1:T(8,128)(2,1)}, u32[]{:S(2)}) copy-start(bf16[512,288]{0,1:T(8,128)(2,1)} %param.27) | copy-start | bytes 884740
  6.5 6.4 %copy-start.3 = (f32[16,512]{1,0:T(8,128)S(1)}, f32[16,512]{1,0:T(8,128)}, u32[]{:S(2)}) copy-start(f32[16,512]{1,0:T(8,128)} %param.30) | copy-start | bytes 98308
  6.5 95.4 %copy-start.2 = (bf16[256,512]{1,0:T(8,128)(2,1)S(1)}, bf16[256,512]{1,0:T(8,128)(2,1)}, u32[]{:S(2)}) copy-start(bf16[256,512]{1,0:T(8,128)(2,1)} %param.28) | copy-start | bytes 786436
  6.5 95.4 %copy-start.6 = (f32[512]{0:T(512)S(1)}, f32[512]{0:T(512)}, u32[]{:S(2)}) copy-start(f32[512]{0:T(512)} %param.29) | copy-start | bytes 6148
  6.5 95.4 %all-reduce.4.cloned.1.call-start = ((), (), s32[]{:S(2)}) async-start(), calls=%async_computation.3 | async-start | bytes 393216 | tf_op jit(solution)/shard_map/psum | solution.py:102
  7.4 2.2 collective-permute-start
  12.9 284.4 %all-reduce.6.cloned.1.call-start = ((), (), s32[]{:S(2)}) async-start(), calls=%async_computation.6 | async-start | bytes 4194304
  105.4 95.8 %copy-start.7 = (f32[512]{0:T(512)S(1)}, f32[512]{0:T(512)}, u32[]{:S(2)}) copy-start(f32[512]{0:T(512)} %param.31) | copy-start | bytes 6148
  202.5 4.9 %copy-start.5 = (s32[4,4,2]{1,2,0:T(2,128)S(1)}, s32[4,4,2]{1,2,0:T(2,128)}, u32[]{:S(2)}) copy-start(s32[4,4,2]{1,2,0:T(2,128)} %param.35) | copy-start | bytes 388
  202.5 5.7 %copy-start.10 = (u32[128]{0:T(128)S(1)}, u32[128]{0:T(128)}, u32[]{:S(2)}) copy-start(u32[128]{0:T(128)} %constant.77) | copy-start | bytes 1540
  202.5 95.7 %copy-start.1 = (bf16[4,4,4096]{2,1,0:T(4,128)(2,1)S(1)}, bf16[4,4,4096]{2,1,0:T(4,128)(2,1)}, u32[]{:S(2)}) copy-start(bf16[4,4,4096]{2,1,0:T(4,128)(2,1)} %param.33) | copy-start | bytes 393220
  202.6 96.0 %copy-start.4 = (f32[4096]{0:T(1024)S(1)}, f32[4096]{0:T(1024)}, u32[]{:S(2)}) copy-start(f32[4096]{0:T(1024)} %param.34) | copy-start | bytes 49156
  207.4 160.1 %all-gather.3.cloned.1.call-start = ((), (), s32[]{:S(2)}) async-start(), calls=%async_computation.4 | async-start | bytes 9437184 | tf_op jit(solution)/shard_map/all_gather | solution.py:150
  319.8 130.3 %reduce-scatter.3.cloned.1.call-start = ((), (), s32[]{:S(2)}) async-start(), calls=%async_computation.5 | async-start | bytes 9437184 | tf_op jit(solution)/shard_map/reduce_scatter | solution.py:156
  367.5 11.0 %copy-start.9 = (bf16[128,8,4096]{2,1,0:T(8,128)(2,1)S(1)}, bf16[128,8,4096]{2,1,0:T(8,128)(2,1)}, u32[]{:S(2)}) copy-start(bf16[128,8,4096]{2,1,0:T(8,128)(2,1)} %all-gather.3.cloned.1.call-done) | copy-start | bytes 25165828
  367.5 21.0 %slice-start = ((s8[6291456]{0:T(1024)(128)(4,1)}), s8[4194304]{0:T(1024)(128)(4,1)S(1)}, s32[]{:S(2)}) async-start(s8[6291456]{0:T(1024)(128)(4,1)} %bitcast.121), calls=%async_computation.7 | async-start | bytes 8388608
  378.5 10.0 %slice-start.1 = ((s8[6291456]{0:T(1024)(128)(4,1)}), s8[2097152]{0:T(1024)(128)(4,1)S(1)}, s32[]{:S(2)}) async-start(s8[6291456]{0:T(1024)(128)(4,1)} %bitcast.121), calls=%async_computation.8 | async-start | bytes 4194304
  397.4 62.5 %copy-start.8 = (bf16[4,4,2]{1,2,0:T(2,128)(2,1)S(1)}, bf16[4,4,2]{1,2,0:T(2,128)(2,1)}, u32[]{:S(2)}) copy-start(bf16[4,4,2]{1,2,0:T(2,128)(2,1)} %param.36) | copy-start | bytes 196
  452.9 23.9 %all-to-all-start.1 = ((bf16[16,8,4096]{2,1,0:T(8,128)(2,1)}), bf16[16,8,4096]{2,1,0:T(8,128)(2,1)S(1)}, u32[]{:S(2)}, u32[]{:S(2)}) async-start(bf16[16,8,4096]{2,1,0:T(8,128)(2,1)} %copy.87), calls=%async_computation.2 | async-start | bytes 2097152 | tf_op jit(solution)/shard_map/all_to_all | solution.py:164
Sparse Core Ops, SparseCore 0:
  13.0 88.8 all-reduce.3
  207.5 89.6 all-reduce.5
  319.9 47.4 all-gather.2
  397.5 52.5 reduce-scatter.2
where the time goes:
time: 489 us; the launch traced here: 485 us
  waiting for transfers between devices  293 us (60%)
  local copies, waits for them, and re-layouts  58.7 us (12%)
  blocking collectives  47.2 us (10%)
  matrix products  38.5 us (8%)
  other arithmetic  19.1 us (4%)
  between operations  14.1 us (3%)
  starting transfers between devices  8.6 us (2%)
  loops' own time  5.26 us (1%)
    psum x1, waiting for transfers between devices, per_device(): lax.psum(projected.astype(jnp.bfloat16), 'exp').astype(jnp.float32)  88.9 us
    unnamed x5, waiting for transfers between devices  87.7 us
    reduce_scatter x1, waiting for transfers between devices, per_device(): lax.psum_scatter(jnp.dot(hidden, w_down[0], preferred_element_type=jnp.fl...  52.7 us
    all_gather x1, waiting for transfers between devices, per_device(): everything = lax.all_gather(arrived, 'seq', axis=0, tiled=True)  47.4 us
    dynamic_slice x64, local copies, waits for them, and re-layouts, per_device(): final_local, local_out = lax.scan(advance, zero_state, series)  47 us
    all_gather x2, blocking collectives, entering(): lax.all_gather(a.astype(kind), axis)  26.5 us
    all_to_all x1, blocking collectives, per_device(): lax.all_to_all(jnp.tile(outgoing, (splits, 1, 1)), 'exp', split_axis=0, c...  20.6 us
    all_to_all x1, waiting for transfers between devices, per_device(): lax.all_to_all(own_rows.astype(jnp.bfloat16), 'exp', split_axis=0, concat...  16.7 us
  transfers between devices with their start and end apart: 6, of which 5 were waited for; matrix products, arithmetic and copies ran while one was open for 1% of the time, Pallas kernels for 0%

commit v1 on v0

v1 whole, which is shorter than its diff:
```python
import jax
import jax.numpy as jnp
from jax import lax
from jax.sharding import PartitionSpec as P

D = 4096
STATE = 16
CONV = 4
RANK = 256
EXPERTS = 8
TOPK = 2
F32 = jnp.float32
BF16 = jnp.bfloat16


def z_shift(by):
    return [(y * 4 + z, y * 4 + (z + by) % 4) for y in range(4) for z in range(4)]


def y_shift(by):
    return [(y * 4 + z, (y + by) % 4 * 4 + z) for y in range(4) for z in range(4)]


def x_shift(by):
    return [(x * 2 + c, (x + by) % 4 * 2 + c) for x in range(4) for c in range(2)]


CORE = [(x * 2 + c, x * 2 + 1 - c) for x in range(4) for c in range(2)]


def passed_along(value, axis, by):
    count = lax.axis_size(axis)
    pairs = [(i, i + by) for i in range(count) if 0 <= i + by < count]
    return lax.ppermute(value, axis, pairs)


def summed_over_exp(value):
    for shift in (z_shift, y_shift):
        sent = value.astype(BF16)
        parts = [lax.ppermute(sent, "exp", shift(by)) for by in (1, 2, 3)]
        value = sent.astype(F32)
        for part in parts:
            value = value + part.astype(F32)
    return value


def conv_inputs(window, conv_weight, conv_bias, length):
    running = jnp.zeros(window[:length].shape, F32) + conv_bias
    for offset in range(CONV):
        running = running + conv_weight[offset] * window[offset : offset + length]
    return running


def make_step(decay_rate):

    def advance(carry_state, series_now):
        step_now, input_now, read_now, value_now = series_now
        factor = jnp.exp(step_now[:, None, :] * decay_rate[None])
        carry_state = (
            factor * carry_state + (step_now * value_now)[:, None, :] * input_now[:, :, None]
        )
        return (carry_state, jnp.sum(read_now[:, :, None] * carry_state, axis=1))

    return advance


def entering(step_total, final_local, decay_rate):
    place = lax.axis_index("seq")
    high = step_total.astype(BF16)
    low = (step_total - high.astype(F32)).astype(BF16)
    packed = jnp.concatenate([final_local.astype(BF16), high[:, None], low[:, None]], axis=1)
    gathered = lax.all_gather(packed, "seq")
    state = jnp.zeros_like(final_local)
    for section in range(lax.axis_size("seq") - 1):
        total = gathered[section, :, STATE].astype(F32) + gathered[section, :, STATE + 1].astype(F32)
        decay = jnp.exp(total[:, None, :] * decay_rate[None])
        later = decay * state + gathered[section, :, :STATE].astype(F32)
        state = jnp.where(section < place, later, state)
    return state


def slot_select(route_ids, capacity):
    flat_ids = route_ids.reshape(-1)
    onehot = (flat_ids[:, None] == jnp.arange(EXPERTS, dtype=jnp.int32)[None, :]).astype(jnp.int32)
    before = jnp.sum((jnp.cumsum(onehot, axis=0) - onehot) * onehot, axis=1)
    target = flat_ids * capacity + before
    matches = jnp.arange(EXPERTS * capacity, dtype=jnp.int32)[:, None] == target[None, :]
    return matches.reshape(EXPERTS * capacity, route_ids.shape[0], route_ids.shape[1])


def expert_block(rows, w_gate, w_up, w_down):
    gate_act = jnp.dot(rows, w_gate, preferred_element_type=F32)
    up_act = jnp.dot(rows, w_up, preferred_element_type=F32)
    hidden = (jax.nn.silu(gate_act) * up_act).astype(BF16)
    return jnp.dot(hidden, w_down, preferred_element_type=F32).astype(BF16)


def swapped(value):
    return lax.ppermute(value, "seq", CORE)


def experts(own, w_gate, w_up, w_down):
    count = own.shape[0]
    half = count // 2

    def block(rows):
        return expert_block(rows, w_gate, w_up, w_down)

    left = lax.ppermute(own, "seq", x_shift(1))
    right = lax.ppermute(own, "seq", x_shift(-1))
    own_out = block(jnp.concatenate([own, swapped(own)]))
    far = jnp.concatenate(
        [
            lax.ppermute(left[:half], "seq", x_shift(1)),
            lax.ppermute(right[half:], "seq", x_shift(-1)),
        ]
    )
    near_out = block(jnp.concatenate([left, right, swapped(left), swapped(right)]))
    far_out = block(jnp.concatenate([far, swapped(far)]))

    def paired(out):
        mine, other = jnp.split(out, 2)
        return mine.astype(F32) + swapped(other).astype(F32)

    near = paired(near_out).astype(BF16)
    to_left, to_right = near[:count], near[count:]
    from_right = lax.ppermute(to_left, "seq", x_shift(-1))
    from_left = lax.ppermute(to_right, "seq", x_shift(1))
    from_far = lax.ppermute(paired(far_out).astype(BF16), "seq", x_shift(2))
    return (
        paired(own_out)
        + from_left.astype(F32)
        + from_right.astype(F32)
        + from_far.astype(F32)
    )


def per_device(
    xin,
    zin,
    conv_weight,
    conv_bias,
    xproj_weight,
    dtproj_weight,
    dt_bias,
    a_log,
    skip,
    out_weight,
    resid,
    norm_gain,
    expert_ids,
    gate_weights,
    w_gate,
    w_up,
    w_down,
):
    section, docs, channels = xin.shape
    edge_rows = passed_along(xin[section - (CONV - 1) :], "seq", 1)
    window = jnp.concatenate([edge_rows, xin], axis=0).astype(F32)
    inner_act = jax.nn.silu(conv_inputs(window, conv_weight, conv_bias, section)).astype(BF16)
    inner_f = inner_act.astype(F32)
    projected = jnp.dot(
        inner_act.reshape(section * docs, channels), xproj_weight, preferred_element_type=F32
    )
    projected = summed_over_exp(projected).reshape(section, docs, -1)
    low_rank = projected[..., :RANK].astype(BF16)
    in_state = projected[..., RANK : RANK + STATE]
    out_state = projected[..., RANK + STATE :]
    step_size = jax.nn.softplus(
        jnp.einsum("pbr,rc->pbc", low_rank, dtproj_weight, preferred_element_type=F32) + dt_bias
    )
    decay_rate = -jnp.exp(a_log)
    advance = make_step(decay_rate)
    series = (step_size, in_state, out_state, inner_f)
    zero_state = jnp.zeros((docs, STATE, channels), F32)
    final_local, local_out = lax.scan(advance, zero_state, series)
    incoming = entering(jnp.sum(step_size, axis=0), final_local, decay_rate)
    ignored, ssm_out = lax.scan(advance, incoming, series)
    mixed_in = ((ssm_out + skip * inner_f) * jax.nn.silu(zin.astype(F32))).astype(BF16)
    partial_rows = jnp.dot(
        mixed_in.reshape(section * docs, channels), out_weight, preferred_element_type=F32
    ).astype(BF16)
    exchanged = lax.all_to_all(partial_rows, "exp", split_axis=0, concat_axis=0, tiled=True)
    row_count = resid.shape[0] * resid.shape[1]
    mamba_rows = jnp.sum(exchanged.reshape(-1, row_count, D).astype(F32), axis=0)
    hidden_state = resid.reshape(row_count, D).astype(F32) + mamba_rows
    norm_scale = lax.rsqrt(jnp.mean(hidden_state * hidden_state, axis=-1, keepdims=True) + 1e-05)
    tokens = (hidden_state * norm_scale * norm_gain).astype(BF16)
    capacity = 2 * TOPK * row_count // EXPERTS
    splits = lax.axis_size("exp") // EXPERTS
    route_ids = expert_ids.reshape(row_count, TOPK)
    gate_vals = gate_weights.reshape(row_count, TOPK)
    matches = slot_select(route_ids, capacity)
    chosen = jnp.sum(matches.astype(jnp.int32), axis=2).astype(BF16)
    outgoing = jnp.dot(chosen, tokens, preferred_element_type=F32).astype(BF16)
    arrived = lax.all_to_all(
        jnp.tile(outgoing, (splits, 1)), "exp", split_axis=0, concat_axis=0, tiled=True
    )
    own_rows = experts(arrived, w_gate[0], w_up[0], w_down[0])
    returned = lax.all_to_all(
        own_rows.astype(BF16), "exp", split_axis=0, concat_axis=0, tiled=True
    ).astype(F32)
    summed = jnp.sum(returned.reshape(splits, EXPERTS * capacity, D), axis=0)
    weights = jnp.sum(matches.astype(F32) * gate_vals.astype(F32)[None], axis=2)
    expert_out = jnp.dot(weights.T, summed, precision=lax.Precision.HIGHEST)
    return (hidden_state + expert_out).astype(BF16).reshape(resid.shape)


def solution(mesh):
    placed = (
        P("seq", None, "exp"),
        P("seq", None, "exp"),
        P(None, "exp"),
        P("exp"),
        P("exp", None),
        P(None, "exp"),
        P("exp"),
        P(None, "exp"),
        P("exp"),
        P("exp", None),
        P(("seq", "exp"), None, None),
        P(),
        P(("seq", "exp"), None, None),
        P(("seq", "exp"), None, None),
        P("exp", None, "seq"),
        P("exp", None, "seq"),
        P("exp", "seq", None),
    )
    return jax.shard_map(
        per_device,
        mesh=mesh,
        in_specs=placed,
        out_specs=P(("seq", "exp"), None, None),
        check_vma=False,
    )
```

time: 489 us -> 324 us (0.66)
  waiting for transfers between devices: 293 us -> 131 us
  local copies, waits for them, and re-layouts: 58.7 us -> 18.7 us
  starting transfers between devices: 8.6 us -> 42.1 us
  matrix products: 38.5 us -> 60.7 us
  between operations: 14.1 us -> 0.79 us
  blocking collectives: 47.2 us -> 36 us
  other arithmetic: 19.1 us -> 24.5 us
    psum x1 -> x0, waiting for transfers between devices: 88.9 us -> none  [per_device(): lax.psum(projected.astype(jnp.bfloat16), 'exp').astype(jnp.float32)]
    unnamed x5 -> x0, waiting for transfers between devices: 87.7 us -> none
    ppermute x0 -> x20, waiting for transfers between devices: none -> 84 us  [the longest x1 22 us: experts(): from_right = lax.ppermute(to_left, 'seq', x_shift(-1))]
    reduce_scatter x1 -> x0, waiting for transfers between devices: 52.7 us -> none  [per_device(): lax.psum_scatter(jnp.dot(hidden, w_down[0], preferred_element_type=jnp.fl...]
    all_gather x1 -> x0, waiting for transfers between devices: 47.4 us -> none  [per_device(): everything = lax.all_gather(arrived, 'seq', axis=0, tiled=True)]
    dynamic_slice x64 -> x0, local copies, waits for them, and re-layouts: 47 us -> none  [per_device(): final_local, local_out = lax.scan(advance, zero_state, series)]
    ppermute x0 -> x20, starting transfers between devices: none -> 32.7 us  [the longest x7 11.4 us: swapped(): return lax.ppermute(value, 'seq', CORE)]
    all_to_all x1 -> x2, waiting for transfers between devices: 16.7 us -> 46.8 us  [the longest x1 29.7 us: per_device(): lax.all_to_all(partial_rows, 'exp', split_axis=0, concat_axis=0, tiled=True)]
  transfers between devices with their start and end apart: 6 -> 23, of which waited for: 5 -> 12; matrix products, arithmetic and copies ran while one was open for 1% -> 21% of each run, Pallas kernels for 0% -> 0%
where the time goes in v1:
time: 324 us; the launch traced here: 319 us
  waiting for transfers between devices  131 us (40%)
  matrix products  60.7 us (19%)
  starting transfers between devices  42.1 us (13%)
  blocking collectives  36 us (11%)
  other arithmetic  24.5 us (8%)
  local copies, waits for them, and re-layouts  18.7 us (6%)
  loops' own time  5.69 us (2%)
    dot_general x3, matrix products, expert_block(): return jnp.dot(hidden, w_down, preferred_element_type=F32).astype(BF16)  38.5 us
    all_to_all x1, waiting for transfers between devices, per_device(): lax.all_to_all(partial_rows, 'exp', split_axis=0, concat_axis=0, tiled=True)  29.7 us
    all_to_all x1, blocking collectives, per_device(): lax.all_to_all(jnp.tile(outgoing, (splits, 1)), 'exp', split_axis=0, conc...  22.2 us
    ppermute x1, waiting for transfers between devices, experts(): from_right = lax.ppermute(to_left, 'seq', x_shift(-1))  22 us
    ppermute x1, waiting for transfers between devices, experts(): left = lax.ppermute(own, 'seq', x_shift(1))  21 us
    ppermute x1, waiting for transfers between devices, experts(): from_far = lax.ppermute(paired(far_out).astype(BF16), 'seq', x_shift(2))  20.9 us
    ppermute x6, waiting for transfers between devices, summed_over_exp(): parts = [lax.ppermute(sent, 'exp', shift(by)) for by in (1, 2, 3)]  18.2 us
    all_to_all x1, waiting for transfers between devices, per_device(): lax.all_to_all(own_rows.astype(BF16), 'exp', split_axis=0, concat_axis=0,...  17.1 us
  transfers between devices with their start and end apart: 23, of which 12 were waited for; matrix products, arithmetic and copies ran while one was open for 21% of the time, Pallas kernels for 0%

profile of v1, /device:TPU:0, one launch (start us, length us, event | category | flops | bytes accessed | tf_op | source)
XLA Modules:
  0.0 319.4 jit_solution(1654911179708552576)
XLA Ops:
  0.0 0.8 slice.113
  0.8 1.3 collective-permute-start
  2.0 0.9 fusion.85
  2.9 1.2 maximum_convert_fusion
  4.1 1.2 fusion.80
  5.4 0.3 convolution_convert_fusion.2
  5.6 4.6 %collective-permute-start.3 = (bf16[256,288]{0,1:T(8,128)(2,1)S(1)}, bf16[256,288]{0,1:T(8,128)(2,1)S(1)}, u32[]{:S(2)}, u32[]{:S(2)}) collective-permute-start(bf16[256,288]{0,1:T(8,128)(2,1)S(1)} %convolution_convert_fusion.2), channel_id=1, source_target_pairs={{0,3},{1,0},{2,1},{3,2},{4,7},{5,4},{6,5},{7,6},{8,11},{9,8},{10,9... | collective-permute-start | bytes 442376 | tf_op jit(solution)/shard_map/ppermute | solution.py:40
  10.3 1.2 collective-permute-start.1
  11.5 5.4 %collective-permute-done.3 = bf16[256,288]{0,1:T(8,128)(2,1)S(1)} collective-permute-done((bf16[256,288]{0,1:T(8,128)(2,1)S(1)}, bf16[256,288]{0,1:T(8,128)(2,1)S(1)}, u32[]{:S(2)}, u32[]{:S(2)}) %collective-permute-start.3) | collective-permute-done | bytes 147488 | tf_op jit(solution)/shard_map/ppermute | solution.py:40
  16.9 1.2 collective-permute-done.2
  18.2 2.9 collective-permute-done.1
  21.1 3.1 collective-permute-start.6
  24.2 0.6 collective-permute-start.5
  24.8 1.0 collective-permute-start.4
  25.8 5.0 %collective-permute-done.6 = bf16[256,288]{0,1:T(8,128)(2,1)S(1)} collective-permute-done((bf16[256,288]{0,1:T(8,128)(2,1)S(1)}, bf16[256,288]{0,1:T(8,128)(2,1)S(1)}, u32[]{:S(2)}, u32[]{:S(2)}) %collective-permute-start.6) | collective-permute-done | bytes 147488 | tf_op jit(solution)/shard_map/ppermute | solution.py:40
  30.8 1.7 collective-permute-done.5
  32.5 2.0 collective-permute-done.4
  34.9 0.3 fusion.55
  35.2 0.3 fusion.82
  35.7 0.3 copy.54
  36.1 10.3 %while.24 = (s32[]{:T(128)}, f32[4,16,512]{2,1,0:T(8,128)S(1)}, f32[64,4,512]{2,1,0:T(4,128)S(1)}, f32[16,512]{1,0:T(8,128)S(1)}, f32[64,4,512]{2,1,0:T(4,128)S(...) while((s32[]{:T(128)}, f32[4,16,512]{2,1,0:T(8,128)S(1)}, f32[64,4,512]{2,1,0:T(4,128)S(1)}, ...), condition=%wide.region_1.2_spmd.clone, body=%wide.region_0.1_spmd.clone.sunk | while | flops 165891 | bytes 353139 | solution.py:176
  46.4 13.8 %all-gather = bf16[32,18,512]{2,1,0:T(8,128)(2,1)S(1)} all-gather(bf16[4,18,512]{2,1,0:T(8,128)(2,1)S(1)} %pad_maximum_fusion.8), channel_id=2, replica_groups=mesh['seq'=8,'exp'=16] {'seq'}, dimensions={0}, use_global_device_ids=true | all-gather | bytes 663552 | tf_op jit(solution)/shard_map/all_gather | solution.py:72
  60.3 0.2 fusion.56
  60.5 12.6 %while.23 = (s32[]{:T(128)}, f32[4,16,512]{2,1,0:T(8,128)S(1)}, f32[64,4,512]{2,1,0:T(4,128)S(1)}, f32[64,4,512]{2,1,0:T(4,128)S(1)}, f32[16,512]{1,0:T(8,128)S(...) while((s32[]{:T(128)}, f32[4,16,512]{2,1,0:T(8,128)S(1)}, ...), condition=%wide.region_5.6_spmd, body=%wide.region_3.5_spmd.sunk | while | flops 196610 | bytes 378485 | solution.py:178
  73.2 0.4 fusion.43
  73.6 4.8 %convolution_convert_fusion = bf16[256,4096]{1,0:T(8,128)(2,1)} fusion(bf16[256,512]{1,0:T(8,128)(2,1)S(1)} %reshape.252, bf16[512,4096]{1,0:T(8,128)(2,1)} %param.30), kind=kOutput, calls=%fused_computation.31 | convolution fusion | flops 1074790400 | bytes 6553600 | tf_op jit(solution)/shard_map/dot_general | solution.py:180
  78.5 3.8 %all-to-all-start = ((bf16[16,16,4096]{2,1,0:T(8,128)(2,1)}), bf16[16,16,4096]{2,1,0:T(8,128)(2,1)S(1)}, u32[]{:S(2)}, u32[]{:S(2)}) async-start(bf16[16,16,4096]{2,1,0:T(8,128)(2,1)} %bitcast.164), calls=%async_computation | async-start | bytes 4194304 | tf_op jit(solution)/shard_map/all_to_all | solution.py:183
  82.8 0.2 select_reduce_fusion.1
  83.2 29.7 %all-to-all-done = bf16[16,16,4096]{2,1,0:T(8,128)(2,1)S(1)} async-done(((bf16[16,16,4096]{2,1,0:T(8,128)(2,1)}), bf16[16,16,4096]{2,1,0:T(8,128)(2,1)S(1)}, u32[]{:S(2)}, u32[]{:S(2)}) %all-to-all-start) | async-done | bytes 2097184 | tf_op jit(solution)/shard_map/all_to_all | solution.py:183
  113.0 0.3 convert_reduce_fusion
  113.7 0.3 convolution_convert_fusion.1
  114.1 22.2 %all_to_all.30 = bf16[16,8,4096]{2,1,0:T(8,128)(2,1)S(1)} all-to-all(bf16[16,8,4096]{2,1,0:T(8,128)(2,1)S(1)} %bitcast.161), channel_id=1, replica_groups=mesh['seq'=8,'exp'=16] {'exp'}, dimensions={0} | all-to-all | bytes 2097152 | tf_op jit(solution)/shard_map/all_to_all | solution.py:196
  136.3 0.4 collective-permute-start.9
  136.7 2.9 collective-permute-start.10
  139.6 21.0 %collective-permute-done.9 = bf16[128,4096]{1,0:T(8,128)(2,1)S(1)} collective-permute-done((bf16[128,4096]{1,0:T(8,128)(2,1)S(1)}, bf16[128,4096]{1,0:T(8,128)(2,1)S(1)}, u32[]{:S(2)}, u32[]{:S(2)}) %collective-permute-start.9) | collective-permute-done | bytes 1048608 | tf_op jit(solution)/shard_map/ppermute | solution.py:109
  160.8 3.3 %collective-permute-start.17 = (bf16[64,4096]{1,0:T(8,128)(2,1)S(1)}, bf16[64,4096]{1,0:T(8,128)(2,1)S(1)}, u32[]{:S(2)}, u32[]{:S(2)}) collective-permute-start(bf16[64,4096]{1,0:T(8,128)(2,1)S(1)} %slice.180), channel_id=1, source_target_pairs={{0,96},{16,112},{32,0},{48,16},{64,32},{80,48},{96,64},{112,80},{1... | collective-permute-start | bytes 1572872 | tf_op jit(solution)/shard_map/ppermute | solution.py:115
  164.0 0.7 collective-permute-start.12
  164.8 5.9 %fusion.11 = f32[256,768]{1,0:T(8,128)} fusion(bf16[1,4096,768]{2,1,0:T(8,128)(2,1)} %param.36, bf16[128,4096]{1,0:T(8,128)(2,1)S(1)} %collective-permute-done.7, bf16[128,4096]{1,0:T(8,128)(2,1)S(1)} %bitcast.168), kind=kOutput, calls=%fused_computation.22 | convolution fusion | flops 1614807040 | bytes 9175040 | tf_op jit(solution)/shard_map/dot_general | solution.py:93
  170.9 1.9 collective-permute-done.16
  173.0 1.4 copy-done.9
  174.7 2.1 copy-done.7
  176.8 4.6 %fusion.9 = f32[512,768]{1,0:T(8,128)} fusion(bf16[512,4096]{1,0:T(8,128)(2,1)S(1)} %constant_dynamic-update-slice_fusion, bf16[1,4096,768]{2,1,0:T(8,128)(2,1)S(1)} %bitcast.176), kind=kOutput, calls=%fused_computation.20 | convolution fusion | flops 3221225472 | bytes 12058624 | tf_op jit(solution)/shard_map/dot_general | solution.py:93
  181.3 17.0 %fusion.19 = bf16[512,4096]{1,0:T(8,128)(2,1)} fusion(bf16[1,768,4096]{2,1,0:T(8,128)(2,1)} %param.37, f32[512,768]{1,0:T(8,128)} %fusion.9, bf16[512,4096]{1,0:T(8,128)(2,1)} %copy-done.7, bf16[1,4096,768]{2,1,0:T(8,128)(2,1)} %param.35), kind=kOutput, calls=%fused_computation.30 | convolution fusion | flops 6446907392 | bytes 22544384 | tf_op jit(solution)/shard_map/dot_general | solution.py:95
  198.4 3.3 %split.27 = bf16[256,4096]{1,0:T(8,128)(2,1)} slice(bf16[512,4096]{1,0:T(8,128)(2,1)} %fusion.19), slice={[256:512], [0:4096]} | slice | bytes 4194304 | tf_op jit(solution)/shard_map/split | solution.py:122
  201.7 9.9 %collective-permute-start.13 = (bf16[256,4096]{1,0:T(8,128)(2,1)}, bf16[256,4096]{1,0:T(8,128)(2,1)}, u32[]{:S(2)}, u32[]{:S(2)}) collective-permute-start(bf16[256,4096]{1,0:T(8,128)(2,1)} %split.27), channel_id=1, source_target_pairs={{0,16},{16,0},{32,48},{48,32},{64,80},{80,64},{96,112},{112,96},{1... | collective-permute-start | bytes 6291464 | tf_op jit(solution)/shard_map/ppermute | solution.py:99
  211.7 1.4 copy-done.11
  213.1 5.5 %fusion.7 = f32[256,768]{1,0:T(8,128)} fusion(bf16[256,4096]{1,0:T(8,128)(2,1)S(1)} %constant_dynamic-update-slice_fusion.4, bf16[1,4096,768]{2,1,0:T(8,128)(2,1)} %param.36), kind=kOutput, calls=%fused_computation.18 | convolution fusion | flops 1610612736 | bytes 9175040 | tf_op jit(solution)/shard_map/dot_general | solution.py:93
  218.6 10.0 %fusion.25 = bf16[256,4096]{1,0:T(8,128)(2,1)S(1)} fusion(bf16[1,768,4096]{2,1,0:T(8,128)(2,1)} %param.37, f32[256,768]{1,0:T(8,128)} %fusion.7, bf16[256,4096]{1,0:T(8,128)(2,1)} %copy-done.11, bf16[1,4096,768]{2,1,0:T(8,128)(2,1)} %param.35), kind=kOutput, calls=%fused_computation.33 | convolution fusion | flops 3223453696 | bytes 17563648 | tf_op jit(solution)/shard_map/dot_general | solution.py:95
  228.6 1.0 split.29
  229.7 11.5 %fusion.22 = bf16[256,4096]{1,0:T(8,128)(2,1)} fusion(bf16[1,768,4096]{2,1,0:T(8,128)(2,1)} %param.37, f32[256,768]{1,0:T(8,128)} %fusion.11, bf16[1,4096,768]{2,1,0:T(8,128)(2,1)} %param.35, bf16[128,4096]{1,0:T(8,128)(2,1)} %copy-done.18, bf16[128,4096]{1,0:T(8,128)(2,1)} %bitcast.169), kind=kOutput, calls=%fused_computation.32 | convolution fusion | flops 3227648000 | bytes 17563648 | tf_op jit(solution)/shard_map/dot_general | solution.py:95
  241.2 1.4 split.25
  242.6 0.6 collective-permute-start.8
  243.2 1.5 add_convert_fusion.2
  244.7 1.7 collective-permute-start.20
  246.3 2.4 add_convert_fusion
  248.9 1.7 collective-permute-start.15
  250.6 0.8 collective-permute-start.14
  251.4 20.9 %collective-permute-done.20 = bf16[128,4096]{1,0:T(8,128)(2,1)S(1)} collective-permute-done((bf16[128,4096]{1,0:T(8,128)(2,1)S(1)}, bf16[128,4096]{1,0:T(8,128)(2,1)S(1)}, u32[]{:S(2)}, u32[]{:S(2)}) %collective-permute-start.20) | collective-permute-done | bytes 1048608 | tf_op jit(solution)/shard_map/ppermute | solution.py:129
  272.3 22.0 %collective-permute-done.15 = bf16[128,4096]{1,0:T(8,128)(2,1)S(1)} collective-permute-done((bf16[128,4096]{1,0:T(8,128)(2,1)S(1)}, bf16[128,4096]{1,0:T(8,128)(2,1)S(1)}, u32[]{:S(2)}, u32[]{:S(2)}) %collective-permute-start.15) | collective-permute-done | bytes 1048608 | tf_op jit(solution)/shard_map/ppermute | solution.py:127
  294.3 1.8 fusion.29
  296.1 4.3 %all-to-all-start.2 = ((bf16[16,8,4096]{2,1,0:T(8,128)(2,1)}), bf16[16,8,4096]{2,1,0:T(8,128)(2,1)S(1)}, u32[]{:S(2)}, u32[]{:S(2)}) async-start(bf16[16,8,4096]{2,1,0:T(8,128)(2,1)} %fusion.29), calls=%async_computation.2 | async-start | bytes 2097152 | tf_op jit(solution)/shard_map/all_to_all | solution.py:200
  300.6 17.1 %all-to-all-done.2 = bf16[16,8,4096]{2,1,0:T(8,128)(2,1)S(1)} async-done(((bf16[16,8,4096]{2,1,0:T(8,128)(2,1)}), bf16[16,8,4096]{2,1,0:T(8,128)(2,1)S(1)}, u32[]{:S(2)}, u32[]{:S(2)}) %all-to-all-start.2) | async-done | bytes 1048608 | tf_op jit(solution)/shard_map/all_to_all | solution.py:200
  317.9 0.6 fusion.28
  318.5 0.7 reshape.253
  (686 shorter events, 20.7 us)
Async XLA Ops:
  0.0 5.3 %copy-start = (bf16[512,288]{0,1:T(8,128)(2,1)S(1)}, bf16[512,288]{0,1:T(8,128)(2,1)}, u32[]{:S(2)}) copy-start(bf16[512,288]{0,1:T(8,128)(2,1)} %param.25) | copy-start | bytes 884740
  0.0 25.8 %copy-start.12 = (f32[16,512]{1,0:T(8,128)S(1)}, f32[16,512]{1,0:T(8,128)}, u32[]{:S(2)}) copy-start(f32[16,512]{1,0:T(8,128)} %param.28) | copy-start | bytes 98308
  0.8 2.2 collective-permute-start
  2.9 32.0 %copy-start.8 = (bf16[256,512]{1,0:T(8,128)(2,1)S(1)}, bf16[256,512]{1,0:T(8,128)(2,1)}, u32[]{:S(2)}) copy-start(bf16[256,512]{1,0:T(8,128)(2,1)} %param.26) | copy-start | bytes 786436
  2.9 32.0 %copy-start.15 = (f32[512]{0:T(512)S(1)}, f32[512]{0:T(512)}, u32[]{:S(2)}) copy-start(f32[512]{0:T(512)} %param.27) | copy-start | bytes 6148
  5.6 11.3 %collective-permute-start.3 = (bf16[256,288]{0,1:T(8,128)(2,1)S(1)}, bf16[256,288]{0,1:T(8,128)(2,1)S(1)}, u32[]{:S(2)}, u32[]{:S(2)}) collective-permute-start(bf16[256,288]{0,1:T(8,128)(2,1)S(1)} %convolution_convert_fusion.2), channel_id=1, source_target_pairs={{0,3},{1,0},{2,1},{3,2},{4,7},{5,4},{6,5},{7,6},{8,11},{9,8},{10,9... | collective-permute-start | bytes 442376 | tf_op jit(solution)/shard_map/ppermute | solution.py:40
  10.3 7.9 %collective-permute-start.2 = (bf16[256,288]{0,1:T(8,128)(2,1)S(1)}, bf16[256,288]{0,1:T(8,128)(2,1)S(1)}, u32[]{:S(2)}, u32[]{:S(2)}) collective-permute-start(bf16[256,288]{0,1:T(8,128)(2,1)S(1)} %convolution_convert_fusion.2), channel_id=1, source_target_pairs={{0,2},{1,3},{2,0},{3,1},{4,6},{5,7},{6,4},{7,5},{8,10},{9,11},{10,... | collective-permute-start | bytes 442376 | tf_op jit(solution)/shard_map/ppermute | solution.py:40
  10.3 10.8 %collective-permute-start.1 = (bf16[256,288]{0,1:T(8,128)(2,1)S(1)}, bf16[256,288]{0,1:T(8,128)(2,1)S(1)}, u32[]{:S(2)}, u32[]{:S(2)}) collective-permute-start(bf16[256,288]{0,1:T(8,128)(2,1)S(1)} %convolution_convert_fusion.2), channel_id=1, source_target_pairs={{0,1},{1,2},{2,3},{3,0},{4,5},{5,6},{6,7},{7,4},{8,9},{9,10},{10,1... | collective-permute-start | bytes 442376 | tf_op jit(solution)/shard_map/ppermute | solution.py:40
  21.1 9.6 %collective-permute-start.6 = (bf16[256,288]{0,1:T(8,128)(2,1)S(1)}, bf16[256,288]{0,1:T(8,128)(2,1)S(1)}, u32[]{:S(2)}, u32[]{:S(2)}) collective-permute-start(bf16[256,288]{0,1:T(8,128)(2,1)S(1)} %add_convert_fusion.3), channel_id=1, source_target_pairs={{0,12},{1,13},{2,14},{3,15},{4,0},{5,1},{6,2},{7,3},{8,4},{9,5},{1... | collective-permute-start | bytes 442376 | tf_op jit(solution)/shard_map/ppermute | solution.py:40
  24.2 8.3 %collective-permute-start.5 = (bf16[256,288]{0,1:T(8,128)(2,1)S(1)}, bf16[256,288]{0,1:T(8,128)(2,1)S(1)}, u32[]{:S(2)}, u32[]{:S(2)}) collective-permute-start(bf16[256,288]{0,1:T(8,128)(2,1)S(1)} %add_convert_fusion.3), channel_id=1, source_target_pairs={{0,8},{1,9},{2,10},{3,11},{4,12},{5,13},{6,14},{7,15},{8,0},{9,1},... | collective-permute-start | bytes 442376 | tf_op jit(solution)/shard_map/ppermute | solution.py:40
  24.8 9.6 %collective-permute-start.4 = (bf16[256,288]{0,1:T(8,128)(2,1)S(1)}, bf16[256,288]{0,1:T(8,128)(2,1)S(1)}, u32[]{:S(2)}, u32[]{:S(2)}) collective-permute-start(bf16[256,288]{0,1:T(8,128)(2,1)S(1)} %add_convert_fusion.3), channel_id=1, source_target_pairs={{0,4},{1,5},{2,6},{3,7},{4,8},{5,9},{6,10},{7,11},{8,12},{9,13},{1... | collective-permute-start | bytes 442376 | tf_op jit(solution)/shard_map/ppermute | solution.py:40
  35.5 37.6 %copy-start.6 = (bf16[64,4,512]{2,1,0:T(4,128)(2,1)S(1)}, bf16[64,4,512]{2,1,0:T(4,128)(2,1)}, u32[]{:S(2)}) copy-start(bf16[64,4,512]{2,1,0:T(4,128)(2,1)} %param.22) | copy-start | bytes 786436
  35.5 37.6 %copy-start.16 = (f32[512]{0:T(512)S(1)}, f32[512]{0:T(512)}, u32[]{:S(2)}) copy-start(f32[512]{0:T(512)} %param.29) | copy-start | bytes 6148
  78.5 3.9 %copy-start.5 = (bf16[4,4,4096]{2,1,0:T(4,128)(2,1)S(1)}, bf16[4,4,4096]{2,1,0:T(4,128)(2,1)}, u32[]{:S(2)}) copy-start(bf16[4,4,4096]{2,1,0:T(4,128)(2,1)} %param.31) | copy-start | bytes 393220
  78.5 3.9 %copy-start.14 = (s32[4,4,2]{1,2,0:T(2,128)S(1)}, s32[4,4,2]{1,2,0:T(2,128)}, u32[]{:S(2)}) copy-start(s32[4,4,2]{1,2,0:T(2,128)} %param.33) | copy-start | bytes 388
  78.5 35.2 %copy-start.13 = (f32[4096]{0:T(1024)S(1)}, f32[4096]{0:T(1024)}, u32[]{:S(2)}) copy-start(f32[4096]{0:T(1024)} %param.32) | copy-start | bytes 49156
  78.5 34.5 %all-to-all-start = ((bf16[16,16,4096]{2,1,0:T(8,128)(2,1)}), bf16[16,16,4096]{2,1,0:T(8,128)(2,1)S(1)}, u32[]{:S(2)}, u32[]{:S(2)}) async-start(bf16[16,16,4096]{2,1,0:T(8,128)(2,1)} %bitcast.164), calls=%async_computation | async-start | bytes 4194304 | tf_op jit(solution)/shard_map/all_to_all | solution.py:183
  136.3 34.3 %copy-start.4 = (bf16[16,8,4096]{2,1,0:T(8,128)(2,1)}, bf16[16,8,4096]{2,1,0:T(8,128)(2,1)S(1)}, u32[]{:S(2)}) copy-start(bf16[16,8,4096]{2,1,0:T(8,128)(2,1)S(1)} %all_to_all.30) | copy-start | bytes 3145732
  136.3 24.2 %collective-permute-start.9 = (bf16[128,4096]{1,0:T(8,128)(2,1)S(1)}, bf16[128,4096]{1,0:T(8,128)(2,1)S(1)}, u32[]{:S(2)}, u32[]{:S(2)}) collective-permute-start(bf16[128,4096]{1,0:T(8,128)(2,1)S(1)} %bitcast.165), channel_id=1, source_target_pairs={{0,32},{16,48},{32,64},{48,80},{64,96},{80,112},{96,0},{112,16},{1... | collective-permute-start | bytes 3145736 | tf_op jit(solution)/shard_map/ppermute | solution.py:109
  136.7 24.0 %collective-permute-start.10 = (bf16[128,4096]{1,0:T(8,128)(2,1)S(1)}, bf16[128,4096]{1,0:T(8,128)(2,1)S(1)}, u32[]{:S(2)}, u32[]{:S(2)}) collective-permute-start(bf16[128,4096]{1,0:T(8,128)(2,1)S(1)} %bitcast.166), channel_id=1, source_target_pairs={{0,96},{16,112},{32,0},{48,16},{64,32},{80,48},{96,64},{112,80},{1... | collective-permute-start | bytes 3145736 | tf_op jit(solution)/shard_map/ppermute | solution.py:110
  139.6 25.2 %collective-permute-start.7 = (bf16[128,4096]{1,0:T(8,128)(2,1)S(1)}, bf16[128,4096]{1,0:T(8,128)(2,1)S(1)}, u32[]{:S(2)}, u32[]{:S(2)}) collective-permute-start(bf16[128,4096]{1,0:T(8,128)(2,1)S(1)} %bitcast.167), channel_id=1, source_target_pairs={{0,16},{16,0},{32,48},{48,32},{64,80},{80,64},{96,112},{112,96},{1... | collective-permute-start | bytes 3145736 | tf_op jit(solution)/shard_map/ppermute | solution.py:99
  160.6 12.1 %collective-permute-start.16 = (bf16[64,4096]{1,0:T(8,128)(2,1)S(1)}, bf16[64,4096]{1,0:T(8,128)(2,1)S(1)}, u32[]{:S(2)}, u32[]{:S(2)}) collective-permute-start(bf16[64,4096]{1,0:T(8,128)(2,1)S(1)} %slice.179), channel_id=1, source_target_pairs={{0,32},{16,48},{32,64},{48,80},{64,96},{80,112},{96,0},{112,16},{1... | collective-permute-start | bytes 1572872 | tf_op jit(solution)/shard_map/ppermute | solution.py:114
  160.7 16.1 %slice-start = ((s8[6291456]{0:T(1024)(128)(4,1)}), s8[4194304]{0:T(1024)(128)(4,1)S(1)}, s32[]{:S(2)}) async-start(s8[6291456]{0:T(1024)(128)(4,1)} %bitcast.175), calls=%async_computation.3 | async-start | bytes 8388608
  160.8 16.0 %slice-start.1 = ((s8[6291456]{0:T(1024)(128)(4,1)}), s8[2097152]{0:T(1024)(128)(4,1)S(1)}, s32[]{:S(2)}) async-start(s8[6291456]{0:T(1024)(128)(4,1)} %bitcast.175), calls=%async_computation.4 | async-start | bytes 4194304
  160.8 12.0 %collective-permute-start.17 = (bf16[64,4096]{1,0:T(8,128)(2,1)S(1)}, bf16[64,4096]{1,0:T(8,128)(2,1)S(1)}, u32[]{:S(2)}, u32[]{:S(2)}) collective-permute-start(bf16[64,4096]{1,0:T(8,128)(2,1)S(1)} %slice.180), channel_id=1, source_target_pairs={{0,96},{16,112},{32,0},{48,16},{64,32},{80,48},{96,64},{112,80},{1... | collective-permute-start | bytes 1572872 | tf_op jit(solution)/shard_map/ppermute | solution.py:115
  164.0 10.4 %collective-permute-start.11 = (bf16[128,4096]{1,0:T(8,128)(2,1)S(1)}, bf16[128,4096]{1,0:T(8,128)(2,1)S(1)}, u32[]{:S(2)}, u32[]{:S(2)}) collective-permute-start(bf16[128,4096]{1,0:T(8,128)(2,1)S(1)} %collective-permute-done.9), channel_id=1, source_target_pairs={{0,16},{16,0},{32,48},{48,32},{64,80},{80,64},{96,112},{112,96},{1... | collective-permute-start | bytes 3145736 | tf_op jit(solution)/shard_map/ppermute | solution.py:99
  164.0 10.5 %collective-permute-start.12 = (bf16[128,4096]{1,0:T(8,128)(2,1)S(1)}, bf16[128,4096]{1,0:T(8,128)(2,1)S(1)}, u32[]{:S(2)}, u32[]{:S(2)}) collective-permute-start(bf16[128,4096]{1,0:T(8,128)(2,1)S(1)} %collective-permute-done.10), channel_id=1, source_target_pairs={{0,16},{16,0},{32,48},{48,32},{64,80},{80,64},{96,112},{112,96},{1... | collective-permute-start | bytes 3145736 | tf_op jit(solution)/shard_map/ppermute | solution.py:99
  164.8 5.9 %copy-start.18 = (bf16[128,4096]{1,0:T(8,128)(2,1)}, bf16[128,4096]{1,0:T(8,128)(2,1)S(1)}, u32[]{:S(2)}) copy-start(bf16[128,4096]{1,0:T(8,128)(2,1)S(1)} %collective-permute-done.7) | copy-start | bytes 3145732
  172.8 38.8 %collective-permute-start.18 = (bf16[128,4096]{1,0:T(8,128)(2,1)S(1)}, bf16[128,4096]{1,0:T(8,128)(2,1)S(1)}, u32[]{:S(2)}, u32[]{:S(2)}) collective-permute-start(bf16[128,4096]{1,0:T(8,128)(2,1)S(1)} %pad_maximum_fusion.3), channel_id=1, source_target_pairs={{0,16},{16,0},{32,48},{48,32},{64,80},{80,64},{96,112},{112,96},{1... | collective-permute-start | bytes 3145736 | tf_op jit(solution)/shard_map/ppermute | solution.py:99
  173.0 1.4 copy-start.9
  174.7 2.1 copy-start.7
  198.4 13.2 %copy-start.10 = (bf16[256,4096]{1,0:T(8,128)(2,1)S(1)}, bf16[256,4096]{1,0:T(8,128)(2,1)}, u32[]{:S(2)}) copy-start(bf16[256,4096]{1,0:T(8,128)(2,1)} %copy-done.9) | copy-start | bytes 6291460
  201.7 44.7 %collective-permute-start.13 = (bf16[256,4096]{1,0:T(8,128)(2,1)}, bf16[256,4096]{1,0:T(8,128)(2,1)}, u32[]{:S(2)}, u32[]{:S(2)}) collective-permute-start(bf16[256,4096]{1,0:T(8,128)(2,1)} %split.27), channel_id=1, source_target_pairs={{0,16},{16,0},{32,48},{48,32},{64,80},{80,64},{96,112},{112,96},{1... | collective-permute-start | bytes 6291464 | tf_op jit(solution)/shard_map/ppermute | solution.py:99
  211.7 1.4 copy-start.11
  229.7 13.5 %collective-permute-start.19 = (bf16[128,4096]{1,0:T(8,128)(2,1)}, bf16[128,4096]{1,0:T(8,128)(2,1)}, u32[]{:S(2)}, u32[]{:S(2)}) collective-permute-start(bf16[128,4096]{1,0:T(8,128)(2,1)} %split.29), channel_id=1, source_target_pairs={{0,16},{16,0},{32,48},{48,32},{64,80},{80,64},{96,112},{112,96},{1... | collective-permute-start | bytes 3145736 | tf_op jit(solution)/shard_map/ppermute | solution.py:99
  241.2 5.2 %copy-start.2 = (bf16[512,4096]{1,0:T(8,128)(2,1)S(1)}, bf16[512,4096]{1,0:T(8,128)(2,1)}, u32[]{:S(2)}) copy-start(bf16[512,4096]{1,0:T(8,128)(2,1)} %fusion.19) | copy-start | bytes 12582916
  242.6 8.8 %collective-permute-start.8 = (bf16[128,4096]{1,0:T(8,128)(2,1)S(1)}, bf16[128,4096]{1,0:T(8,128)(2,1)S(1)}, u32[]{:S(2)}, u32[]{:S(2)}) collective-permute-start(bf16[128,4096]{1,0:T(8,128)(2,1)S(1)} %split.25), channel_id=1, source_target_pairs={{0,16},{16,0},{32,48},{48,32},{64,80},{80,64},{96,112},{112,96},{1... | collective-permute-start | bytes 3145736 | tf_op jit(solution)/shard_map/ppermute | solution.py:99
  244.7 49.6 %copy-start.3 = (bf16[256,4096]{1,0:T(8,128)(2,1)S(1)}, bf16[256,4096]{1,0:T(8,128)(2,1)}, u32[]{:S(2)}) copy-start(bf16[256,4096]{1,0:T(8,128)(2,1)} %fusion.22) | copy-start | bytes 6291460
  244.7 27.6 %collective-permute-start.20 = (bf16[128,4096]{1,0:T(8,128)(2,1)S(1)}, bf16[128,4096]{1,0:T(8,128)(2,1)S(1)}, u32[]{:S(2)}, u32[]{:S(2)}) collective-permute-start(bf16[128,4096]{1,0:T(8,128)(2,1)S(1)} %add_convert_fusion.2), channel_id=1, source_target_pairs={{0,64},{16,80},{32,96},{48,112},{64,0},{80,16},{96,32},{112,48},{1... | collective-permute-start | bytes 3145736 | tf_op jit(solution)/shard_map/ppermute | solution.py:129
  248.9 45.4 %collective-permute-start.15 = (bf16[128,4096]{1,0:T(8,128)(2,1)S(1)}, bf16[128,4096]{1,0:T(8,128)(2,1)S(1)}, u32[]{:S(2)}, u32[]{:S(2)}) collective-permute-start(bf16[128,4096]{1,0:T(8,128)(2,1)S(1)} %get-tuple-element.195), channel_id=1, source_target_pairs={{0,96},{16,112},{32,0},{48,16},{64,32},{80,48},{96,64},{112,80},{1... | collective-permute-start | bytes 3145736 | tf_op jit(solution)/shard_map/ppermute | solution.py:127
  250.6 49.8 %copy-start.17 = (bf16[4,4,2]{1,2,0:T(2,128)(2,1)S(1)}, bf16[4,4,2]{1,2,0:T(2,128)(2,1)}, u32[]{:S(2)}) copy-start(bf16[4,4,2]{1,2,0:T(2,128)(2,1)} %param.34) | copy-start | bytes 196
  250.6 43.7 %collective-permute-start.14 = (bf16[128,4096]{1,0:T(8,128)(2,1)S(1)}, bf16[128,4096]{1,0:T(8,128)(2,1)S(1)}, u32[]{:S(2)}, u32[]{:S(2)}) collective-permute-start(bf16[128,4096]{1,0:T(8,128)(2,1)S(1)} %get-tuple-element.194), channel_id=1, source_target_pairs={{0,32},{16,48},{32,64},{48,80},{64,96},{80,112},{96,0},{112,16},{1... | collective-permute-start | bytes 3145736 | tf_op jit(solution)/shard_map/ppermute | solution.py:128
  294.3 24.9 %copy-start.1 = (bf16[512,288]{0,1:T(8,128)(2,1)S(1)}, bf16[512,288]{0,1:T(8,128)(2,1)}, u32[]{:S(2)}) copy-start(bf16[512,288]{0,1:T(8,128)(2,1)} %param.25) | copy-start | bytes 884740
  296.1 21.6 %all-to-all-start.2 = ((bf16[16,8,4096]{2,1,0:T(8,128)(2,1)}), bf16[16,8,4096]{2,1,0:T(8,128)(2,1)S(1)}, u32[]{:S(2)}, u32[]{:S(2)}) async-start(bf16[16,8,4096]{2,1,0:T(8,128)(2,1)} %fusion.29), calls=%async_computation.2 | async-start | bytes 2097152 | tf_op jit(solution)/shard_map/all_to_all | solution.py:200

commit v2 on v1

v2 whole, which is shorter than its diff:
```python
import jax
import jax.numpy as jnp
from jax import lax
from jax.experimental import pallas as pl
from jax.experimental.pallas import tpu as pltpu
from jax.sharding import PartitionSpec as P

D = 4096
STATE = 16
CONV = 4
RANK = 256
EXPERTS = 8
TOPK = 2
DOCS = 4
SECTION = 64
TOKENS = DOCS * SECTION
LANES = 128
F32 = jnp.float32
BF16 = jnp.bfloat16


def z_shift(by):
    return [(y * 4 + z, y * 4 + (z + by) % 4) for y in range(4) for z in range(4)]


def y_shift(by):
    return [(y * 4 + z, (y + by) % 4 * 4 + z) for y in range(4) for z in range(4)]


def x_shift(by):
    return [(x * 2 + c, (x + by) % 4 * 2 + c) for x in range(4) for c in range(2)]


CORE = [(x * 2 + c, x * 2 + 1 - c) for x in range(4) for c in range(2)]


def passed_along(value, axis, by):
    count = lax.axis_size(axis)
    pairs = [(i, i + by) for i in range(count) if 0 <= i + by < count]
    return lax.ppermute(value, axis, pairs)


def from_others(value, shift):
    return [lax.ppermute(value, "exp", shift(by)) for by in (1, 2, 3)]


def swapped(value):
    return lax.ppermute(value, "seq", CORE)


def document_major(back):
    row = lax.broadcasted_iota(jnp.int32, (TOKENS, TOKENS), 0)
    column = lax.broadcasted_iota(jnp.int32, (TOKENS, TOKENS), 1)
    if back:
        source = (row & (DOCS - 1)) * SECTION + (row >> 2)
    else:
        source = (row & (SECTION - 1)) * DOCS + (row >> 6)
    return jnp.where(column == source, 1.0, 0.0).astype(BF16)


def mixer_in_kernel(xin, edge, conv_weight, conv_bias, xproj, inner, projected, window):
    window[16 - edge.shape[0] : 16, :] = edge[...].astype(F32)
    window[16 : 16 + TOKENS, :] = xin[...].astype(F32)
    blocks = []
    for low in range(0, TOKENS, 64):
        running = jnp.broadcast_to(conv_bias[...], (64, xin.shape[1]))
        for offset in range(CONV):
            tap = window[pl.ds(low + 16 - DOCS * (CONV - 1 - offset), 64), :]
            running = running + conv_weight[offset : offset + 1, :] * tap
        blocks.append(jax.nn.silu(running).astype(BF16))
    by_position = jnp.concatenate(blocks, axis=0)
    ordered = jnp.dot(document_major(False), by_position, preferred_element_type=F32).astype(BF16)
    inner[...] = ordered
    projected[...] = jnp.dot(ordered, xproj[...], preferred_element_type=F32).astype(BF16)


def spread(pairs, target, first):
    lane = lax.broadcasted_iota(jnp.int32, (STATE, LANES), 1)
    entry = lax.broadcasted_iota(jnp.int32, (STATE, LANES), 0)
    mask = jnp.where((lane == first + entry) | (lane == first + STATE + entry), 1.0, 0.0)
    ones = jnp.ones((LANES, LANES), BF16)

    def one(group, carry):
        rows = pairs[pl.ds(pl.multiple_of(group * 16, 16), 16), :].astype(F32)
        wide = jnp.broadcast_to(rows[:, None, :], (16, STATE, LANES)) * mask[None]
        wide = wide.reshape(16 * STATE, LANES).astype(BF16)
        place = pl.ds(pl.multiple_of(group * 16 * STATE, 16 * STATE), 16 * STATE)
        target[place, :] = jnp.dot(wide, ones, preferred_element_type=F32)
        return carry

    lax.fori_loop(0, TOKENS // 16, one, 0)


def four_times(block):
    return jnp.concatenate([block] * 4, axis=1)


def section_kernel(
    p0, p1, p2, p3, dtproj, dt_bias, a_log, inner, step, pairs, packed, taken, entering
):
    total = (p0[...].astype(F32) + p1[...].astype(F32)) + (
        p2[...].astype(F32) + p3[...].astype(F32)
    )
    low_rank = total[:, :RANK].astype(BF16)
    states = total[:, RANK : RANK + 2 * STATE]
    high = states.astype(BF16)
    low = (states - high.astype(F32)).astype(BF16)
    pairs[...] = jnp.concatenate(
        [
            high[:, :STATE],
            low[:, :STATE],
            high[:, STATE:],
            low[:, STATE:],
            jnp.zeros((TOKENS, LANES - 4 * STATE), BF16),
        ],
        axis=1,
    )
    step[...] = jax.nn.softplus(
        jnp.dot(low_rank, dtproj[...], preferred_element_type=F32) + dt_bias[...]
    )
    taken[...] = step[...] * inner[...].astype(F32)
    spread(pairs, entering, 0)
    rate = -jnp.exp(a_log[...])

    def document(doc, carry):
        def eight(group, state):
            first = pl.multiple_of(doc * SECTION + group * 8, 8)
            steps = step[pl.ds(first, 8), :]
            values = taken[pl.ds(first, 8), :]
            for i in range(8):
                into = entering[pl.ds(pl.multiple_of((first + i) * STATE, STATE), STATE), :]
                factor = jnp.exp(steps[i : i + 1] * rate)
                state = factor * state + values[i : i + 1] * four_times(into)
            return state

        state = lax.fori_loop(0, SECTION // 8, eight, jnp.zeros(rate.shape, F32))
        packed[pl.ds(pl.multiple_of(doc * STATE, STATE), STATE), :] = state.astype(BF16)
        return carry

    lax.fori_loop(0, DOCS, document, 0)
    sums = jnp.concatenate(
        [
            jnp.sum(step[doc * SECTION : (doc + 1) * SECTION, :], axis=0, keepdims=True)
            for doc in range(DOCS)
        ],
        axis=0,
    )
    high = sums.astype(BF16).astype(F32)
    both = jnp.concatenate([high, sums - high], axis=0)
    packed[DOCS * STATE : DOCS * STATE + 2 * DOCS, :] = both.astype(BF16)


def mixer_out_kernel(
    place,
    gathered,
    step,
    pairs,
    inner,
    a_log,
    skip,
    zin,
    out_weight,
    rows,
    totals,
    taken,
    entering,
    leaving,
    scanned,
    weight,
    arrived,
):
    copy = pltpu.make_async_copy(out_weight, weight, arrived)
    copy.start()
    sections = gathered.shape[0]
    for section in range(sections - 1):
        both = gathered[section, DOCS * STATE : DOCS * STATE + 2 * DOCS, :].astype(F32)
        totals[8 * section : 8 * section + DOCS, :] = both[:DOCS] + both[DOCS:]
    taken[...] = step[...] * inner[...].astype(F32)
    spread(pairs, entering, 0)
    spread(pairs, leaving, 2 * STATE)
    rate = -jnp.exp(a_log[...])

    def document(doc, carry):
        state = jnp.zeros(rate.shape, F32)
        for section in range(sections - 1):
            total = totals[pl.ds(8 * section + doc, 1), :]
            final = gathered[section, pl.ds(pl.multiple_of(doc * STATE, STATE), STATE), :]
            later = jnp.exp(total * rate) * state + final.astype(F32)
            state = jnp.where(section < place[0], later, state)

        def eight(group, state):
            first = pl.multiple_of(doc * SECTION + group * 8, 8)
            steps = step[pl.ds(first, 8), :]
            values = taken[pl.ds(first, 8), :]
            sums = []
            for i in range(8):
                where = pl.ds(pl.multiple_of((first + i) * STATE, STATE), STATE)
                factor = jnp.exp(steps[i : i + 1] * rate)
                state = factor * state + values[i : i + 1] * four_times(entering[where, :])
                seen = state * four_times(leaving[where, :])
                sums.append(jnp.sum(seen, axis=0, keepdims=True))
            scanned[pl.ds(first, 8), :] = jnp.concatenate(sums, axis=0)
            return state

        lax.fori_loop(0, SECTION // 8, eight, state)
        return carry

    lax.fori_loop(0, DOCS, document, 0)
    gate = jnp.dot(document_major(False), zin[...], preferred_element_type=F32)
    mixed = (scanned[...] + skip[...] * inner[...].astype(F32)) * jax.nn.silu(gate)
    ordered = jnp.dot(
        document_major(True), mixed.astype(BF16), preferred_element_type=F32
    ).astype(BF16)
    copy.wait()
    for low in range(0, D, 1024):
        rows[:, low : low + 1024] = jnp.dot(
            ordered, weight[:, low : low + 1024], preferred_element_type=F32
        ).astype(BF16)


def whole(space=None):
    return pl.BlockSpec(memory_space=pltpu.VMEM if space is None else space)


def mixer_in(xin, edge, conv_weight, conv_bias, xproj):
    channels = xin.shape[1]
    return pl.pallas_call(
        mixer_in_kernel,
        out_shape=(
            jax.ShapeDtypeStruct((TOKENS, channels), BF16),
            jax.ShapeDtypeStruct((TOKENS, xproj.shape[1]), BF16),
        ),
        in_specs=[whole()] * 5,
        out_specs=(whole(), whole()),
        scratch_shapes=[pltpu.VMEM((16 + TOKENS, channels), F32)],
        compiler_params=pltpu.CompilerParams(vmem_limit_bytes=16 << 20),
        name="mixer_in",
    )(xin, edge, conv_weight, conv_bias, xproj)


def section_scan(parts, dtproj, dt_bias, a_log, inner):
    channels = inner.shape[1]
    return pl.pallas_call(
        section_kernel,
        out_shape=(
            jax.ShapeDtypeStruct((TOKENS, channels), F32),
            jax.ShapeDtypeStruct((TOKENS, LANES), BF16),
            jax.ShapeDtypeStruct((DOCS * (STATE + 2), channels), BF16),
        ),
        in_specs=[whole()] * 8,
        out_specs=(whole(),) * 3,
        scratch_shapes=[
            pltpu.VMEM((TOKENS, channels), F32),
            pltpu.VMEM((TOKENS * STATE, LANES), F32),
        ],
        compiler_params=pltpu.CompilerParams(vmem_limit_bytes=16 << 20),
        name="section_scan",
    )(*parts, dtproj, dt_bias, a_log, inner)


def mixer_out(place, gathered, step, pairs, inner, a_log, skip, zin, out_weight):
    channels = inner.shape[1]
    return pl.pallas_call(
        mixer_out_kernel,
        out_shape=jax.ShapeDtypeStruct((TOKENS, D), BF16),
        in_specs=[whole(pltpu.SMEM)] + [whole()] * 7 + [whole(pl.ANY)],
        out_specs=whole(),
        scratch_shapes=[
            pltpu.VMEM((64, channels), F32),
            pltpu.VMEM((TOKENS, channels), F32),
            pltpu.VMEM((TOKENS * STATE, LANES), F32),
            pltpu.VMEM((TOKENS * STATE, LANES), F32),
            pltpu.VMEM((TOKENS, channels), F32),
            pltpu.VMEM(out_weight.shape, BF16),
            pltpu.SemaphoreType.DMA,
        ],
        compiler_params=pltpu.CompilerParams(vmem_limit_bytes=32 << 20),
        name="mixer_out",
    )(place, gathered, step, pairs, inner, a_log, skip, zin, out_weight)


def expert_kernel(count, *refs):
    inputs, (w_gate, w_up, w_down, mine, other, rows, total) = refs[:count], refs[count:]
    block = pl.program_id(0)
    last = pl.num_programs(0) - 1
    size = rows.shape[0]

    @pl.when(block == 0)
    def _():
        low = 0
        for part in inputs:
            rows[low : low + part.shape[0], :] = part[...]
            low += part.shape[0]

    def tile(index, carry):
        place = pl.ds(pl.multiple_of(index * 256, 256), 256)
        these = rows[place, :]
        gate_act = jnp.dot(these, w_gate[...], preferred_element_type=F32)
        up_act = jnp.dot(these, w_up[...], preferred_element_type=F32)
        hidden = (jax.nn.silu(gate_act) * up_act).astype(BF16)
        for low in range(0, D, 1024):
            term = jnp.dot(hidden, w_down[:, low : low + 1024], preferred_element_type=F32)
            before = jnp.where(block == 0, 0.0, total[place, low : low + 1024])
            total[place, low : low + 1024] = before + term
        return carry

    lax.fori_loop(0, size // 256, tile, 0)

    @pl.when(block == last)
    def _():
        mine[...] = total[: size // 2, :].astype(BF16)
        other[...] = total[size // 2 :, :].astype(BF16)


def expert_block(parts, w_gate, w_up, w_down):
    size = sum(part.shape[0] for part in parts)
    units, width = w_down.shape[1], 256

    def once(shape):
        return pl.BlockSpec(shape, lambda i: (0, 0), pipeline_mode=pl.Buffered(1))

    return pl.pallas_call(
        lambda *refs: expert_kernel(len(parts), *refs),
        out_shape=(jax.ShapeDtypeStruct((size // 2, D), BF16),) * 2,
        grid=(units // width,),
        in_specs=[once(part.shape) for part in parts]
        + [pl.BlockSpec((pl.Squeezed(), D, width), lambda i: (0, 0, i))] * 2
        + [pl.BlockSpec((pl.Squeezed(), width, D), lambda i: (0, i, 0))],
        out_specs=(once((size // 2, D)),) * 2,
        scratch_shapes=[pltpu.VMEM((size, D), BF16), pltpu.VMEM((size, D), F32)],
        compiler_params=pltpu.CompilerParams(
            dimension_semantics=("arbitrary",), vmem_limit_bytes=48 << 20
        ),
        cost_estimate=pl.CostEstimate(
            flops=6 * size * D * units,
            bytes_accessed=6 * D * units + 4 * size * D,
            transcendentals=size * units,
        ),
        name=f"experts_{size}",
    )(*parts, w_gate, w_up, w_down)


def slot_select(route_ids, capacity):
    flat_ids = route_ids.reshape(-1)
    onehot = (flat_ids[:, None] == jnp.arange(EXPERTS, dtype=jnp.int32)[None, :]).astype(jnp.int32)
    before = jnp.sum((jnp.cumsum(onehot, axis=0) - onehot) * onehot, axis=1)
    target = flat_ids * capacity + before
    matches = jnp.arange(EXPERTS * capacity, dtype=jnp.int32)[:, None] == target[None, :]
    return matches.reshape(EXPERTS * capacity, route_ids.shape[0], route_ids.shape[1])


def experts(own, w_gate, w_up, w_down):
    half = own.shape[0] // 2
    count = own.shape[0]

    def paired(mine, other):
        return (mine.astype(F32) + swapped(other).astype(F32)).astype(BF16)

    left = lax.ppermute(own, "seq", x_shift(1))
    right = lax.ppermute(own, "seq", x_shift(-1))
    own_mine, own_other = expert_block([own, swapped(own)], w_gate, w_up, w_down)
    left, right, own_mine, own_other = lax.optimization_barrier((left, right, own_mine, own_other))
    far = [
        lax.ppermute(left[:half], "seq", x_shift(1)),
        lax.ppermute(right[half:], "seq", x_shift(-1)),
    ]
    near_parts = [left, right, swapped(left), swapped(right)]
    near_mine, near_other = expert_block(near_parts, w_gate, w_up, w_down)
    own_sum = paired(own_mine, own_other)
    near = paired(near_mine, near_other)
    far = far + [swapped(part) for part in far]
    near, own_sum, *far = lax.optimization_barrier((near, own_sum, *far))
    from_right = lax.ppermute(near[:count], "seq", x_shift(-1))
    from_left = lax.ppermute(near[count:], "seq", x_shift(1))
    far_mine, far_other = expert_block(far, w_gate, w_up, w_down)
    from_far = lax.ppermute(paired(far_mine, far_other), "seq", x_shift(2))
    return (
        own_sum.astype(F32)
        + from_left.astype(F32)
        + from_right.astype(F32)
        + from_far.astype(F32)
    )


def per_device(
    xin,
    zin,
    conv_weight,
    conv_bias,
    xproj_weight,
    dtproj_weight,
    dt_bias,
    a_log,
    skip,
    out_weight,
    resid,
    norm_gain,
    expert_ids,
    gate_weights,
    w_gate,
    w_up,
    w_down,
):
    channels = xin.shape[2]
    xin = xin.reshape(TOKENS, channels)
    edge = passed_along(xin[TOKENS - (CONV - 1) * DOCS :], "seq", 1)
    inner, projected = mixer_in(xin, edge, conv_weight, conv_bias[None], xproj_weight)
    along_z = [projected] + from_others(projected, z_shift)
    projected = sum(part.astype(F32) for part in along_z).astype(BF16)
    parts = [projected] + from_others(projected, y_shift)
    step, pairs, packed = section_scan(parts, dtproj_weight, dt_bias[None], a_log, inner)
    gathered = lax.all_gather(packed, "seq")
    place = lax.axis_index("seq").reshape(1)
    partial_rows = mixer_out(
        place,
        gathered,
        step,
        pairs,
        inner,
        a_log,
        skip[None],
        zin.reshape(TOKENS, channels),
        out_weight,
    )
    exchanged = lax.all_to_all(partial_rows, "exp", split_axis=0, concat_axis=0, tiled=True)
    row_count = resid.shape[0] * resid.shape[1]
    mamba_rows = jnp.sum(exchanged.reshape(-1, row_count, D).astype(F32), axis=0)
    hidden_state = resid.reshape(row_count, D).astype(F32) + mamba_rows
    norm_scale = lax.rsqrt(jnp.mean(hidden_state * hidden_state, axis=-1, keepdims=True) + 1e-05)
    tokens = (hidden_state * norm_scale * norm_gain).astype(BF16)
    capacity = 2 * TOPK * row_count // EXPERTS
    splits = lax.axis_size("exp") // EXPERTS
    route_ids = expert_ids.reshape(row_count, TOPK)
    gate_vals = gate_weights.reshape(row_count, TOPK)
    matches = slot_select(route_ids, capacity)
    chosen = jnp.sum(matches.astype(jnp.int32), axis=2).astype(BF16)
    outgoing = jnp.dot(chosen, tokens, preferred_element_type=F32).astype(BF16)
    arrived = lax.all_to_all(
        jnp.tile(outgoing, (splits, 1)), "exp", split_axis=0, concat_axis=0, tiled=True
    )
    own_rows = experts(arrived, w_gate, w_up, w_down)
    returned = lax.all_to_all(
        own_rows.astype(BF16), "exp", split_axis=0, concat_axis=0, tiled=True
    ).astype(F32)
    summed = jnp.sum(returned.reshape(splits, EXPERTS * capacity, D), axis=0)
    weights = jnp.sum(matches.astype(F32) * gate_vals.astype(F32)[None], axis=2)
    expert_out = jnp.dot(weights.T, summed, precision=lax.Precision.HIGHEST)
    return (hidden_state + expert_out).astype(BF16).reshape(resid.shape)


def solution(mesh):
    placed = (
        P("seq", None, "exp"),
        P("seq", None, "exp"),
        P(None, "exp"),
        P("exp"),
        P("exp", None),
        P(None, "exp"),
        P("exp"),
        P(None, "exp"),
        P("exp"),
        P("exp", None),
        P(("seq", "exp"), None, None),
        P(),
        P(("seq", "exp"), None, None),
        P(("seq", "exp"), None, None),
        P("exp", None, "seq"),
        P("exp", None, "seq"),
        P("exp", "seq", None),
    )
    return jax.shard_map(
        per_device,
        mesh=mesh,
        in_specs=placed,
        out_specs=P(("seq", "exp"), None, None),
        check_vma=False,
    )
```

time: 324 us -> 280 us (0.86); the launches traced: 319 us -> 280 us
  matrix products: 60.7 us -> 0.95 us
  Pallas kernels: 0 us -> 55.3 us
  other arithmetic: 24.5 us -> 4.18 us
  local copies, waits for them, and re-layouts: 18.7 us -> 8.47 us
  waiting for transfers between devices: 131 us -> 138 us
  loops' own time: 5.69 us -> 0 us
  starting transfers between devices: 42.1 us -> 37.3 us
    dot_general x9 -> x0, matrix products: 59.8 us -> none  [the longest x3 38.5 us: expert_block(): return jnp.dot(hidden, w_down, preferred_element_type=F32).astype(BF16)]
    pallas_call x0 -> x6, Pallas kernels: none -> 55.3 us  [the longest x3 37.7 us: expert_block(): pl.pallas_call(lambda *refs: expert_kernel(len(parts), *refs), out_shape=...]
    ppermute x1, waiting for transfers between devices: 1.89 us -> 11.8 us  [experts(): lax.ppermute(left[:half], 'seq', x_shift(1))]
    ppermute x7 -> x8, starting transfers between devices: 11.4 us -> 1.75 us  [swapped(): return lax.ppermute(value, 'seq', CORE)]
    ppermute x1, waiting for transfers between devices: 21 us -> 13.5 us  [experts(): left = lax.ppermute(own, 'seq', x_shift(1))]
    reduce_sum x65 -> x0, other arithmetic: 7.45 us -> none  [the longest x64 7.11 us: advance(): return (carry_state, jnp.sum(read_now[:, :, None] * carry_state, axis=1))]
    split x3 -> x0, local copies, waits for them, and re-layouts: 5.75 us -> none  [paired(): mine, other = jnp.split(out, 2)]
    another operation x2 -> x0, loops' own time: 5.69 us -> none  [the longest x1 3 us: per_device(): final_local, local_out = lax.scan(advance, zero_state, series)]
  transfers between devices with their start and end apart: 23 -> 24, of which waited for: 12 -> 15; matrix products, arithmetic and copies ran while one was open for 21% -> 2% of each run, Pallas kernels for 0% -> 4%
where the time goes in v2:
time: 280 us
  waiting for transfers between devices  138 us (49%)
  Pallas kernels  55.3 us (20%)
  starting transfers between devices  37.3 us (13%)
  blocking collectives  35 us (12%)
  local copies, waits for them, and re-layouts  8.47 us (3%)
  other arithmetic  4.18 us (1%)
    pallas_call x3, Pallas kernels, expert_block(): pl.pallas_call(lambda *refs: expert_kernel(len(parts), *refs), out_shape=...  37.7 us
    all_to_all x1, waiting for transfers between devices, per_device(): lax.all_to_all(partial_rows, 'exp', split_axis=0, concat_axis=0, tiled=True)  29.8 us
    ppermute x1, waiting for transfers between devices, experts(): from_left = lax.ppermute(near[count:], 'seq', x_shift(1))  21.8 us
    ppermute x1, waiting for transfers between devices, experts(): from_right = lax.ppermute(near[:count], 'seq', x_shift(-1))  21.8 us
    all_to_all x1, blocking collectives, per_device(): lax.all_to_all(jnp.tile(outgoing, (splits, 1)), 'exp', split_axis=0, conc...  21.2 us
    all_to_all x1, waiting for transfers between devices, per_device(): lax.all_to_all(own_rows.astype(BF16), 'exp', split_axis=0, concat_axis=0,...  17.5 us
    ppermute x6, waiting for transfers between devices, from_others(): return [lax.ppermute(value, 'exp', shift(by)) for by in (1, 2, 3)]  16.3 us
    all_gather x1, blocking collectives, per_device(): gathered = lax.all_gather(packed, 'seq')  13.8 us
  transfers between devices with their start and end apart: 24, of which 15 were waited for; matrix products, arithmetic and copies ran while one was open for 2% of the time, Pallas kernels for 4%

profile of v2, /device:TPU:0, one launch (start us, length us, event | category | flops | bytes accessed | tf_op | source)
XLA Modules:
  0.0 280.0 jit_solution(13251799540954012114)
XLA Ops:
  0.0 0.8 slice.18
  0.8 1.3 collective-permute-start
  2.1 1.0 reshape.82.xin
  3.1 1.2 copy.32.xproj
  4.3 0.7 copy-done.3
  5.0 0.7 copy-done.4
  5.7 0.7 mixer_in.1
  6.4 2.5 collective-permute-start.1
  8.9 3.6 %collective-permute-start.2 = (bf16[256,288]{1,0:T(8,128)(2,1)S(1)}, bf16[256,288]{1,0:T(8,128)(2,1)S(1)}, u32[]{:S(2)}, u32[]{:S(2)}) collective-permute-start(bf16[256,288]{1,0:T(8,128)(2,1)S(1)} %get-tuple-element.26), channel_id=1, source_target_pairs={{0,2},{1,3},{2,0},{3,1},{4,6},{5,7},{6,4},{7,5},{8,10},{9,11},{10,... | collective-permute-start | bytes 442376 | tf_op jit(solution)/shard_map/ppermute | solution.py:44
  12.5 1.0 collective-permute-start.3
  13.5 2.2 collective-permute-done.1
  15.7 6.0 %collective-permute-done.2 = bf16[256,288]{1,0:T(8,128)(2,1)S(1)} collective-permute-done((bf16[256,288]{1,0:T(8,128)(2,1)S(1)}, bf16[256,288]{1,0:T(8,128)(2,1)S(1)}, u32[]{:S(2)}, u32[]{:S(2)}) %collective-permute-start.2) | collective-permute-done | bytes 147488 | tf_op jit(solution)/shard_map/ppermute | solution.py:44
  21.7 0.1 add_convert_fusion.4.p0
  21.8 1.6 collective-permute-start.4
  23.5 2.9 %collective-permute-start.5 = (bf16[256,288]{1,0:T(8,128)(2,1)S(1)}, bf16[256,288]{1,0:T(8,128)(2,1)S(1)}, u32[]{:S(2)}, u32[]{:S(2)}) collective-permute-start(bf16[256,288]{1,0:T(8,128)(2,1)S(1)} %add_convert_fusion.4.p0), channel_id=1, source_target_pairs={{0,8},{1,9},{2,10},{3,11},{4,12},{5,13},{6,14},{7,15},{8,0},{9,1},... | collective-permute-start | bytes 442376 | tf_op jit(solution)/shard_map/ppermute | solution.py:44
  26.4 1.3 collective-permute-start.6
  27.8 2.8 collective-permute-done.4.p1
  30.6 5.4 %collective-permute-done.5.p2 = bf16[256,288]{1,0:T(8,128)(2,1)S(1)} collective-permute-done((bf16[256,288]{1,0:T(8,128)(2,1)S(1)}, bf16[256,288]{1,0:T(8,128)(2,1)S(1)}, u32[]{:S(2)}, u32[]{:S(2)}) %collective-permute-start.5) | collective-permute-done | bytes 147488 | tf_op jit(solution)/shard_map/ppermute | solution.py:44
  36.0 4.9 %section_scan.1 = (f32[256,512]{1,0:T(8,128)S(1)}, bf16[256,128]{1,0:T(8,128)(2,1)S(1)}, bf16[72,512]{1,0:T(8,128)(2,1)S(1)}) custom-call(bf16[256,288]{1,0:T(8,128)(2,1)S(1)} %add_convert_fusion.4.p0, bf16[256,288]{1,0:T(8,128)(2,1)S(1)} %collective-permute-done.4.p1, bf16[256,288]{1,0:T(8,128)(2,1)S(1)} %collective-permute-done.5.p2, ...), custom_call_target="tpu_custom_call" | custom-call | tf_op jit(solution)/shard_map/section_scan/pallas_call | solution.py:243
  40.9 13.8 %all-gather = bf16[576,512]{1,0:T(8,128)(2,1)S(1)} all-gather(bf16[72,512]{1,0:T(8,128)(2,1)S(1)} %get-tuple-element.28), channel_id=2, replica_groups=mesh['seq'=8,'exp'=16] {'seq'}, dimensions={0}, use_global_device_ids=true | all-gather | bytes 663552 | tf_op jit(solution)/shard_map/all_gather | solution.py:412
  54.7 2.2 copy-done
  56.9 12.0 %mixer_out.1 = bf16[256,4096]{1,0:T(8,128)(2,1)} custom-call(s32[1]{0:T(128)} %bitcast.place, bf16[8,72,512]{2,1,0:T(8,128)(2,1)S(1)} %bitcast.24, f32[256,512]{1,0:T(8,128)S(1)} %get-tuple-element.29.step, bf16[256,128]{1,0:T(8,128)(2,1)S(1)} %get-tuple-element.30.pairs, bf16[256,512]{1,0:T(8,128)(2,1)S(1)} %get-tuple-element.27.inner, ...), custom_call_target="tpu_custom_call" | custom-call | tf_op jit(solution)/shard_map/mixer_out/pallas_call | solution.py:263
  68.9 6.1 %all-to-all-start = ((bf16[16,16,4096]{2,1,0:T(8,128)(2,1)}), bf16[16,16,4096]{2,1,0:T(8,128)(2,1)S(1)}, u32[]{:S(2)}, u32[]{:S(2)}) async-start(bf16[16,16,4096]{2,1,0:T(8,128)(2,1)} %bitcast.5), calls=%async_computation | async-start | bytes 4194304 | tf_op jit(solution)/shard_map/all_to_all | solution.py:425
  75.1 0.1 copy.34
  75.4 0.2 select_reduce_fusion.1
  76.0 29.8 %all-to-all-done = bf16[16,16,4096]{2,1,0:T(8,128)(2,1)S(1)} async-done(((bf16[16,16,4096]{2,1,0:T(8,128)(2,1)}), bf16[16,16,4096]{2,1,0:T(8,128)(2,1)S(1)}, u32[]{:S(2)}, u32[]{:S(2)}) %all-to-all-start) | async-done | bytes 2097184 | tf_op jit(solution)/shard_map/all_to_all | solution.py:425
  105.8 0.3 convert_reduce_fusion
  106.2 0.2 multiply_reduce_fusion
  106.5 0.3 convolution_convert_fusion
  106.8 0.1 tile.2
  107.0 21.2 %all_to_all.29 = bf16[16,8,4096]{2,1,0:T(8,128)(2,1)S(1)} all-to-all(bf16[16,8,4096]{2,1,0:T(8,128)(2,1)S(1)} %bitcast.29), channel_id=1, replica_groups=mesh['seq'=8,'exp'=16] {'exp'}, dimensions={0} | all-to-all | bytes 2097152 | tf_op jit(solution)/shard_map/all_to_all | solution.py:438
  128.1 0.3 collective-permute-start.7
  128.4 3.0 %collective-permute-start.8 = (bf16[128,4096]{1,0:T(8,128)(2,1)S(1)}, bf16[128,4096]{1,0:T(8,128)(2,1)S(1)}, u32[]{:S(2)}, u32[]{:S(2)}) collective-permute-start(bf16[128,4096]{1,0:T(8,128)(2,1)S(1)} %bitcast.22), channel_id=1, source_target_pairs={{0,96},{16,112},{32,0},{48,16},{64,32},{80,48},{96,64},{112,80},{1... | collective-permute-start | bytes 3145736 | tf_op jit(solution)/shard_map/ppermute | solution.py:360
  131.4 10.1 %experts_256.2 = (bf16[128,4096]{1,0:T(8,128)(2,1)S(1)}, bf16[128,4096]{1,0:T(8,128)(2,1)S(1)}) custom-call(bf16[128,4096]{1,0:T(8,128)(2,1)S(1)} %bitcast.23, bf16[128,4096]{1,0:T(8,128)(2,1)S(1)} %collective-permute-done.9.refs_1_, bf16[1,4096,768]{2,1,0:T(8,128)(2,1)} %refs_4_.5, bf16[1,4096,768]{2,1,0:T(8,128)(2,1)} %refs_5_.3, bf16[1,768,4096]{2,1,0:T(8,128)(2,1)} %refs_6_.3), custom_call_target="tpu_custom_call" | custom-call | flops 4831838208 | bytes 23068672 | tf_op jit(solution)/shard_map/experts_256/pallas_call | solution.py:322
  141.5 13.5 %collective-permute-done.7.refs_0_ = bf16[128,4096]{1,0:T(8,128)(2,1)S(1)} collective-permute-done((bf16[128,4096]{1,0:T(8,128)(2,1)S(1)}, bf16[128,4096]{1,0:T(8,128)(2,1)S(1)}, u32[]{:S(2)}, u32[]{:S(2)}) %collective-permute-start.7) | collective-permute-done | bytes 1048608 | tf_op jit(solution)/shard_map/ppermute | solution.py:359
  154.9 0.5 collective-permute-start.11
  155.4 2.1 collective-permute-done.10.refs_2_
  157.6 1.5 collective-permute-done.11.refs_3_
  159.1 17.5 %experts_512.1 = (bf16[256,4096]{1,0:T(8,128)(2,1)}, bf16[256,4096]{1,0:T(8,128)(2,1)}) custom-call(bf16[128,4096]{1,0:T(8,128)(2,1)S(1)} %collective-permute-done.7.refs_0_, bf16[128,4096]{1,0:T(8,128)(2,1)S(1)} %collective-permute-done.8.refs_1_, bf16[128,4096]{1,0:T(8,128)(2,1)S(1)} %collective-permute-done.10.refs_2_, ...), custom_call_target="tpu_custom_call" | custom-call | flops 9663676416 | bytes 27262976 | tf_op jit(solution)/shard_map/experts_512/pallas_call | solution.py:322
  176.6 0.1 collective-permute-start.12
  176.8 0.4 collective-permute-start.13
  177.3 3.3 %collective-permute-start.15 = (bf16[64,4096]{1,0:T(8,128)(2,1)S(1)}, bf16[64,4096]{1,0:T(8,128)(2,1)S(1)}, u32[]{:S(2)}, u32[]{:S(2)}) collective-permute-start(bf16[64,4096]{1,0:T(8,128)(2,1)S(1)} %slice.21), channel_id=1, source_target_pairs={{0,96},{16,112},{32,0},{48,16},{64,32},{80,48},{96,64},{112,80},{1... | collective-permute-start | bytes 1572872 | tf_op jit(solution)/shard_map/ppermute | solution.py:365
  180.6 11.8 %collective-permute-done.14.refs_0_ = bf16[64,4096]{1,0:T(8,128)(2,1)S(1)} collective-permute-done((bf16[64,4096]{1,0:T(8,128)(2,1)S(1)}, bf16[64,4096]{1,0:T(8,128)(2,1)S(1)}, u32[]{:S(2)}, u32[]{:S(2)}) %collective-permute-start.14) | collective-permute-done | bytes 524320 | tf_op jit(solution)/shard_map/ppermute | solution.py:364
  192.4 0.5 collective-permute-start.17
  193.0 0.2 add_convert_fusion.3
  193.2 0.8 add_convert_fusion
  194.0 0.3 collective-permute-done.16.refs_2_
  194.3 0.7 collective-permute-done.17.refs_3_
  195.1 10.1 %experts_256.3 = (bf16[128,4096]{1,0:T(8,128)(2,1)S(1)}, bf16[128,4096]{1,0:T(8,128)(2,1)S(1)}) custom-call(bf16[64,4096]{1,0:T(8,128)(2,1)S(1)} %collective-permute-done.14.refs_0_, bf16[64,4096]{1,0:T(8,128)(2,1)S(1)} %collective-permute-done.15.refs_1_, bf16[64,4096]{1,0:T(8,128)(2,1)S(1)} %collective-permute-done.16.refs_2_, ...), custom_call_target="tpu_custom_call" | custom-call | flops 4831838208 | bytes 23068672 | tf_op jit(solution)/shard_map/experts_256/pallas_call | solution.py:322
  205.2 0.2 collective-permute-start.20
  205.4 0.2 fusion.6
  205.6 0.6 collective-permute-start.18
  206.2 2.7 collective-permute-start.19
  208.9 0.2 add_convert_fusion.2
  209.2 1.3 collective-permute-start.21
  210.5 21.8 %collective-permute-done.18 = bf16[128,4096]{1,0:T(8,128)(2,1)S(1)} collective-permute-done((bf16[128,4096]{1,0:T(8,128)(2,1)S(1)}, bf16[128,4096]{1,0:T(8,128)(2,1)S(1)}, u32[]{:S(2)}, u32[]{:S(2)}) %collective-permute-start.18) | collective-permute-done | bytes 1048608 | tf_op jit(solution)/shard_map/ppermute | solution.py:374
  232.3 21.8 %collective-permute-done.19 = bf16[128,4096]{1,0:T(8,128)(2,1)S(1)} collective-permute-done((bf16[128,4096]{1,0:T(8,128)(2,1)S(1)}, bf16[128,4096]{1,0:T(8,128)(2,1)S(1)}, u32[]{:S(2)}, u32[]{:S(2)}) %collective-permute-start.19) | collective-permute-done | bytes 1048608 | tf_op jit(solution)/shard_map/ppermute | solution.py:373
  254.1 1.3 collective-permute-done.21
  255.4 1.7 fusion.1
  257.0 3.8 %all-to-all-start.2 = ((bf16[16,8,4096]{2,1,0:T(8,128)(2,1)}), bf16[16,8,4096]{2,1,0:T(8,128)(2,1)S(1)}, u32[]{:S(2)}, u32[]{:S(2)}) async-start(bf16[16,8,4096]{2,1,0:T(8,128)(2,1)} %fusion.1), calls=%async_computation.2 | async-start | bytes 2097152 | tf_op jit(solution)/shard_map/all_to_all | solution.py:442
  261.0 17.5 %all-to-all-done.2 = bf16[16,8,4096]{2,1,0:T(8,128)(2,1)S(1)} async-done(((bf16[16,8,4096]{2,1,0:T(8,128)(2,1)}), bf16[16,8,4096]{2,1,0:T(8,128)(2,1)S(1)}, u32[]{:S(2)}, u32[]{:S(2)}) %all-to-all-start.2) | async-done | bytes 1048608 | tf_op jit(solution)/shard_map/all_to_all | solution.py:442
  278.4 0.2 convert_reduce_fusion.1
  278.6 0.6 fusion
  279.2 0.7 reshape.84
  (58 shorter events, 1.3 us)
Async XLA Ops:
  0.0 27.7 %copy-start.9 = (bf16[64,4,512]{2,1,0:T(4,128)(2,1)S(1)}, bf16[64,4,512]{2,1,0:T(4,128)(2,1)}, u32[]{:S(2)}) copy-start(bf16[64,4,512]{2,1,0:T(4,128)(2,1)} %param.18) | copy-start | bytes 786436
  0.0 36.0 %copy-start.5 = (f32[512]{0:T(512)S(1)}, f32[512]{0:T(512)}, u32[]{:S(2)}) copy-start(f32[512]{0:T(512)} %param.23) | copy-start | bytes 6148
  0.0 36.0 %copy-start.1 = (bf16[256,512]{1,0:T(8,128)(2,1)S(1)}, bf16[256,512]{1,0:T(8,128)(2,1)}, u32[]{:S(2)}) copy-start(bf16[256,512]{1,0:T(8,128)(2,1)} %dtproj.1) | copy-start | bytes 786436
  0.0 36.0 %copy-start.2 = (f32[16,512]{1,0:T(8,128)S(1)}, f32[16,512]{1,0:T(8,128)}, u32[]{:S(2)}) copy-start(f32[16,512]{1,0:T(8,128)} %a_log.3) | copy-start | bytes 98308
  0.8 3.5 %collective-permute-start = (bf16[12,512]{1,0:T(8,128)(2,1)S(1)}, bf16[12,512]{1,0:T(8,128)(2,1)S(1)}, u32[]{:S(2)}, u32[]{:S(2)}) collective-permute-start(bf16[12,512]{1,0:T(8,128)(2,1)S(1)} %slice.19), channel_id=1, source_target_pairs={{0,16},{16,32},{32,48},{48,64},{64,80},{80,96},{96,112},{1,17},{17... | collective-permute-start | bytes 36872 | tf_op jit(solution)/shard_map/ppermute | solution.py:40
  4.3 0.7 copy-start.3
  5.0 0.7 copy-start.4
  5.7 49.0 %copy-start.6 = (f32[512]{0:T(512)S(1)}, f32[512]{0:T(512)}, u32[]{:S(2)}) copy-start(f32[512]{0:T(512)} %param.25) | copy-start | bytes 6148
  6.4 9.3 %collective-permute-start.1 = (bf16[256,288]{1,0:T(8,128)(2,1)S(1)}, bf16[256,288]{1,0:T(8,128)(2,1)S(1)}, u32[]{:S(2)}, u32[]{:S(2)}) collective-permute-start(bf16[256,288]{1,0:T(8,128)(2,1)S(1)} %get-tuple-element.26), channel_id=1, source_target_pairs={{0,1},{1,2},{2,3},{3,0},{4,5},{5,6},{6,7},{7,4},{8,9},{9,10},{10,1... | collective-permute-start | bytes 442376 | tf_op jit(solution)/shard_map/ppermute | solution.py:44
  8.9 12.8 %collective-permute-start.2 = (bf16[256,288]{1,0:T(8,128)(2,1)S(1)}, bf16[256,288]{1,0:T(8,128)(2,1)S(1)}, u32[]{:S(2)}, u32[]{:S(2)}) collective-permute-start(bf16[256,288]{1,0:T(8,128)(2,1)S(1)} %get-tuple-element.26), channel_id=1, source_target_pairs={{0,2},{1,3},{2,0},{3,1},{4,6},{5,7},{6,4},{7,5},{8,10},{9,11},{10,... | collective-permute-start | bytes 442376 | tf_op jit(solution)/shard_map/ppermute | solution.py:44
  12.5 9.2 %collective-permute-start.3 = (bf16[256,288]{1,0:T(8,128)(2,1)S(1)}, bf16[256,288]{1,0:T(8,128)(2,1)S(1)}, u32[]{:S(2)}, u32[]{:S(2)}) collective-permute-start(bf16[256,288]{1,0:T(8,128)(2,1)S(1)} %get-tuple-element.26), channel_id=1, source_target_pairs={{0,3},{1,0},{2,1},{3,2},{4,7},{5,4},{6,5},{7,6},{8,11},{9,8},{10,9... | collective-permute-start | bytes 442376 | tf_op jit(solution)/shard_map/ppermute | solution.py:44
  21.8 8.8 %collective-permute-start.4 = (bf16[256,288]{1,0:T(8,128)(2,1)S(1)}, bf16[256,288]{1,0:T(8,128)(2,1)S(1)}, u32[]{:S(2)}, u32[]{:S(2)}) collective-permute-start(bf16[256,288]{1,0:T(8,128)(2,1)S(1)} %add_convert_fusion.4.p0), channel_id=1, source_target_pairs={{0,4},{1,5},{2,6},{3,7},{4,8},{5,9},{6,10},{7,11},{8,12},{9,13},{1... | collective-permute-start | bytes 442376 | tf_op jit(solution)/shard_map/ppermute | solution.py:44
  23.5 12.5 %collective-permute-start.5 = (bf16[256,288]{1,0:T(8,128)(2,1)S(1)}, bf16[256,288]{1,0:T(8,128)(2,1)S(1)}, u32[]{:S(2)}, u32[]{:S(2)}) collective-permute-start(bf16[256,288]{1,0:T(8,128)(2,1)S(1)} %add_convert_fusion.4.p0), channel_id=1, source_target_pairs={{0,8},{1,9},{2,10},{3,11},{4,12},{5,13},{6,14},{7,15},{8,0},{9,1},... | collective-permute-start | bytes 442376 | tf_op jit(solution)/shard_map/ppermute | solution.py:44
  26.4 9.6 %collective-permute-start.6 = (bf16[256,288]{1,0:T(8,128)(2,1)S(1)}, bf16[256,288]{1,0:T(8,128)(2,1)S(1)}, u32[]{:S(2)}, u32[]{:S(2)}) collective-permute-start(bf16[256,288]{1,0:T(8,128)(2,1)S(1)} %add_convert_fusion.4.p0), channel_id=1, source_target_pairs={{0,12},{1,13},{2,14},{3,15},{4,0},{5,1},{6,2},{7,3},{8,4},{9,5},{1... | collective-permute-start | bytes 442376 | tf_op jit(solution)/shard_map/ppermute | solution.py:44
  54.7 2.2 copy-start
  68.9 6.2 %copy-start.8 = (bf16[4,4,4096]{2,1,0:T(4,128)(2,1)S(1)}, bf16[4,4,4096]{2,1,0:T(4,128)(2,1)}, u32[]{:S(2)}) copy-start(bf16[4,4,4096]{2,1,0:T(4,128)(2,1)} %param.27) | copy-start | bytes 393220
  68.9 6.2 %copy-start.11 = (s32[4,4,2]{1,2,0:T(2,128)S(1)}, s32[4,4,2]{1,2,0:T(2,128)}, u32[]{:S(2)}) copy-start(s32[4,4,2]{1,2,0:T(2,128)} %param.29) | copy-start | bytes 388
  68.9 36.9 %all-to-all-start = ((bf16[16,16,4096]{2,1,0:T(8,128)(2,1)}), bf16[16,16,4096]{2,1,0:T(8,128)(2,1)S(1)}, u32[]{:S(2)}, u32[]{:S(2)}) async-start(bf16[16,16,4096]{2,1,0:T(8,128)(2,1)} %bitcast.5), calls=%async_computation | async-start | bytes 4194304 | tf_op jit(solution)/shard_map/all_to_all | solution.py:425
  75.3 31.2 %copy-start.10 = (f32[4096]{0:T(1024)S(1)}, f32[4096]{0:T(1024)}, u32[]{:S(2)}) copy-start(f32[4096]{0:T(1024)} %param.28) | copy-start | bytes 49156
  128.1 3.2 %collective-permute-start.9 = (bf16[128,4096]{1,0:T(8,128)(2,1)S(1)}, bf16[128,4096]{1,0:T(8,128)(2,1)S(1)}, u32[]{:S(2)}, u32[]{:S(2)}) collective-permute-start(bf16[128,4096]{1,0:T(8,128)(2,1)S(1)} %bitcast.20), channel_id=1, source_target_pairs={{0,16},{16,0},{32,48},{48,32},{64,80},{80,64},{96,112},{112,96},{1... | collective-permute-start | bytes 3145736 | tf_op jit(solution)/shard_map/ppermute | solution.py:48
  128.1 26.8 %collective-permute-start.7 = (bf16[128,4096]{1,0:T(8,128)(2,1)S(1)}, bf16[128,4096]{1,0:T(8,128)(2,1)S(1)}, u32[]{:S(2)}, u32[]{:S(2)}) collective-permute-start(bf16[128,4096]{1,0:T(8,128)(2,1)S(1)} %bitcast.21), channel_id=1, source_target_pairs={{0,32},{16,48},{32,64},{48,80},{64,96},{80,112},{96,0},{112,16},{1... | collective-permute-start | bytes 3145736 | tf_op jit(solution)/shard_map/ppermute | solution.py:359
  128.4 26.5 %collective-permute-start.8 = (bf16[128,4096]{1,0:T(8,128)(2,1)S(1)}, bf16[128,4096]{1,0:T(8,128)(2,1)S(1)}, u32[]{:S(2)}, u32[]{:S(2)}) collective-permute-start(bf16[128,4096]{1,0:T(8,128)(2,1)S(1)} %bitcast.22), channel_id=1, source_target_pairs={{0,96},{16,112},{32,0},{48,16},{64,32},{80,48},{96,64},{112,80},{1... | collective-permute-start | bytes 3145736 | tf_op jit(solution)/shard_map/ppermute | solution.py:360
  154.9 2.7 collective-permute-start.10
  154.9 4.2 %collective-permute-start.11 = (bf16[128,4096]{1,0:T(8,128)(2,1)S(1)}, bf16[128,4096]{1,0:T(8,128)(2,1)S(1)}, u32[]{:S(2)}, u32[]{:S(2)}) collective-permute-start(bf16[128,4096]{1,0:T(8,128)(2,1)S(1)} %collective-permute-done.8.refs_1_), channel_id=1, source_target_pairs={{0,16},{16,0},{32,48},{48,32},{64,80},{80,64},{96,112},{112,96},{1... | collective-permute-start | bytes 3145736 | tf_op jit(solution)/shard_map/ppermute | solution.py:48
  176.6 16.6 %collective-permute-start.12 = (bf16[256,4096]{1,0:T(8,128)(2,1)}, bf16[256,4096]{1,0:T(8,128)(2,1)S(1)}, u32[]{:S(2)}, u32[]{:S(2)}) collective-permute-start(bf16[256,4096]{1,0:T(8,128)(2,1)} %get-tuple-element.36), channel_id=1, source_target_pairs={{0,16},{16,0},{32,48},{48,32},{64,80},{80,64},{96,112},{112,96},{1... | collective-permute-start | bytes 6291464 | tf_op jit(solution)/shard_map/ppermute | solution.py:48
  176.8 16.2 %collective-permute-start.13 = (bf16[128,4096]{1,0:T(8,128)(2,1)S(1)}, bf16[128,4096]{1,0:T(8,128)(2,1)S(1)}, u32[]{:S(2)}, u32[]{:S(2)}) collective-permute-start(bf16[128,4096]{1,0:T(8,128)(2,1)S(1)} %get-tuple-element.38), channel_id=1, source_target_pairs={{0,16},{16,0},{32,48},{48,32},{64,80},{80,64},{96,112},{112,96},{1... | collective-permute-start | bytes 3145736 | tf_op jit(solution)/shard_map/ppermute | solution.py:48
  177.2 16.0 %copy-start.7 = (bf16[256,4096]{1,0:T(8,128)(2,1)S(1)}, bf16[256,4096]{1,0:T(8,128)(2,1)}, u32[]{:S(2)}) copy-start(bf16[256,4096]{1,0:T(8,128)(2,1)} %get-tuple-element.35) | copy-start | bytes 6291460
  177.2 15.2 %collective-permute-start.14 = (bf16[64,4096]{1,0:T(8,128)(2,1)S(1)}, bf16[64,4096]{1,0:T(8,128)(2,1)S(1)}, u32[]{:S(2)}, u32[]{:S(2)}) collective-permute-start(bf16[64,4096]{1,0:T(8,128)(2,1)S(1)} %slice.20), channel_id=1, source_target_pairs={{0,32},{16,48},{32,64},{48,80},{64,96},{80,112},{96,0},{112,16},{1... | collective-permute-start | bytes 1572872 | tf_op jit(solution)/shard_map/ppermute | solution.py:364
  177.3 15.1 %collective-permute-start.15 = (bf16[64,4096]{1,0:T(8,128)(2,1)S(1)}, bf16[64,4096]{1,0:T(8,128)(2,1)S(1)}, u32[]{:S(2)}, u32[]{:S(2)}) collective-permute-start(bf16[64,4096]{1,0:T(8,128)(2,1)S(1)} %slice.21), channel_id=1, source_target_pairs={{0,96},{16,112},{32,0},{48,16},{64,32},{80,48},{96,64},{112,80},{1... | collective-permute-start | bytes 1572872 | tf_op jit(solution)/shard_map/ppermute | solution.py:365
  192.4 1.9 collective-permute-start.16
  192.4 2.7 collective-permute-start.17
  205.2 3.8 %collective-permute-start.20 = (bf16[128,4096]{1,0:T(8,128)(2,1)S(1)}, bf16[128,4096]{1,0:T(8,128)(2,1)S(1)}, u32[]{:S(2)}, u32[]{:S(2)}) collective-permute-start(bf16[128,4096]{1,0:T(8,128)(2,1)S(1)} %get-tuple-element.46), channel_id=1, source_target_pairs={{0,16},{16,0},{32,48},{48,32},{64,80},{80,64},{96,112},{112,96},{1... | collective-permute-start | bytes 3145736 | tf_op jit(solution)/shard_map/ppermute | solution.py:48
  205.6 26.7 %collective-permute-start.18 = (bf16[128,4096]{1,0:T(8,128)(2,1)S(1)}, bf16[128,4096]{1,0:T(8,128)(2,1)S(1)}, u32[]{:S(2)}, u32[]{:S(2)}) collective-permute-start(bf16[128,4096]{1,0:T(8,128)(2,1)S(1)} %get-tuple-element.47), channel_id=1, source_target_pairs={{0,32},{16,48},{32,64},{48,80},{64,96},{80,112},{96,0},{112,16},{1... | collective-permute-start | bytes 3145736 | tf_op jit(solution)/shard_map/ppermute | solution.py:374
  206.2 47.9 %collective-permute-start.19 = (bf16[128,4096]{1,0:T(8,128)(2,1)S(1)}, bf16[128,4096]{1,0:T(8,128)(2,1)S(1)}, u32[]{:S(2)}, u32[]{:S(2)}) collective-permute-start(bf16[128,4096]{1,0:T(8,128)(2,1)S(1)} %get-tuple-element.48), channel_id=1, source_target_pairs={{0,96},{16,112},{32,0},{48,16},{64,32},{80,48},{96,64},{112,80},{1... | collective-permute-start | bytes 3145736 | tf_op jit(solution)/shard_map/ppermute | solution.py:373
  209.2 46.2 %collective-permute-start.21 = (bf16[128,4096]{1,0:T(8,128)(2,1)S(1)}, bf16[128,4096]{1,0:T(8,128)(2,1)S(1)}, u32[]{:S(2)}, u32[]{:S(2)}) collective-permute-start(bf16[128,4096]{1,0:T(8,128)(2,1)S(1)} %add_convert_fusion.2), channel_id=1, source_target_pairs={{0,64},{16,80},{32,96},{48,112},{64,0},{80,16},{96,32},{112,48},{1... | collective-permute-start | bytes 3145736 | tf_op jit(solution)/shard_map/ppermute | solution.py:376
  257.0 3.8 %copy-start.12 = (bf16[4,4,2]{1,2,0:T(2,128)(2,1)S(1)}, bf16[4,4,2]{1,2,0:T(2,128)(2,1)}, u32[]{:S(2)}) copy-start(bf16[4,4,2]{1,2,0:T(2,128)(2,1)} %param.30) | copy-start | bytes 196
  257.0 21.4 %all-to-all-start.2 = ((bf16[16,8,4096]{2,1,0:T(8,128)(2,1)}), bf16[16,8,4096]{2,1,0:T(8,128)(2,1)S(1)}, u32[]{:S(2)}, u32[]{:S(2)}) async-start(bf16[16,8,4096]{2,1,0:T(8,128)(2,1)} %fusion.1), calls=%async_computation.2 | async-start | bytes 2097152 | tf_op jit(solution)/shard_map/all_to_all | solution.py:442

commit v3 on v2

--- a/solution.py
+++ b/solution.py
@@ -349,37 +349,39 @@
     return matches.reshape(EXPERTS * capacity, route_ids.shape[0], route_ids.shape[1])
 
 
+def after(values, *others):
+    held = lax.optimization_barrier((tuple(values), others))
+    return held[0]
+
+
 def experts(own, w_gate, w_up, w_down):
-    half = own.shape[0] // 2
     count = own.shape[0]
+    half = count // 2
 
     def paired(mine, other):
-        return (mine.astype(F32) + swapped(other).astype(F32)).astype(BF16)
+        return mine.astype(F32) + swapped(other).astype(F32)
 
     left = lax.ppermute(own, "seq", x_shift(1))
     right = lax.ppermute(own, "seq", x_shift(-1))
-    own_mine, own_other = expert_block([own, swapped(own)], w_gate, w_up, w_down)
-    left, right, own_mine, own_other = lax.optimization_barrier((left, right, own_mine, own_other))
+    own_out = expert_block([own, swapped(own)], w_gate, w_up, w_down)
+    left, right = after((left, right), own_out)
     far = [
         lax.ppermute(left[:half], "seq", x_shift(1)),
         lax.ppermute(right[half:], "seq", x_shift(-1)),
     ]
     near_parts = [left, right, swapped(left), swapped(right)]
-    near_mine, near_other = expert_block(near_parts, w_gate, w_up, w_down)
-    own_sum = paired(own_mine, own_other)
-    near = paired(near_mine, near_other)
-    far = far + [swapped(part) for part in far]
-    near, own_sum, *far = lax.optimization_barrier((near, own_sum, *far))
-    from_right = lax.ppermute(near[:count], "seq", x_shift(-1))
-    from_left = lax.ppermute(near[count:], "seq", x_shift(1))
-    far_mine, far_other = expert_block(far, w_gate, w_up, w_down)
-    from_far = lax.ppermute(paired(far_mine, far_other), "seq", x_shift(2))
-    return (
-        own_sum.astype(F32)
-        + from_left.astype(F32)
-        + from_right.astype(F32)
-        + from_far.astype(F32)
-    )
+    far_out = expert_block(far + [swapped(part) for part in far], w_gate, w_up, w_down)
+    far_sum = paired(*far_out).astype(BF16)
+    for_right = lax.ppermute(far_sum[:half], "seq", x_shift(1))
+    for_left = lax.ppermute(far_sum[half:], "seq", x_shift(-1))
+    near_out = expert_block(near_parts, w_gate, w_up, w_down)
+    near_out = after(near_out, for_right, for_left)
+    near = paired(*near_out)
+    to_left = near[:count] + jnp.concatenate([jnp.zeros((half, D), F32), for_left.astype(F32)])
+    to_right = near[count:] + jnp.concatenate([for_right.astype(F32), jnp.zeros((half, D), F32)])
+    from_right = lax.ppermute(to_left.astype(BF16), "seq", x_shift(-1))
+    from_left = lax.ppermute(to_right.astype(BF16), "seq", x_shift(1))
+    return paired(*own_out) + from_left.astype(F32) + from_right.astype(F32)
 
 
 def per_device(

time: 280 us -> 267 us (0.954)
  waiting for transfers between devices: 138 us -> 123 us
    ppermute x3 -> x4, waiting for transfers between devices: 44.8 us -> 23.2 us  [the longest x1 23.2 us: experts(): from_left = lax.ppermute(to_right.astype(BF16), 'seq', x_shift(1))]
    ppermute x1, waiting for transfers between devices: 0.01 us -> 12.8 us  [experts(): right = lax.ppermute(own, 'seq', x_shift(-1))]
    ppermute x1, waiting for transfers between devices: 13.5 us -> 2.4 us  [experts(): left = lax.ppermute(own, 'seq', x_shift(1))]
    ppermute x8, waiting for transfers between devices: 4.74 us -> 10.2 us  [swapped(): return lax.ppermute(value, 'seq', CORE)]
    ppermute x3 -> x4, starting transfers between devices: 4.66 us -> 6.6 us  [the longest x1 3.22 us: experts(): for_left = lax.ppermute(far_sum[half:], 'seq', x_shift(-1))]
  transfers between devices with their start and end apart: 24 -> 25, of which waited for: 15 -> 15; matrix products, arithmetic and copies ran while one was open for 2% -> 2% of each run, Pallas kernels for 4% -> 10%
where the time goes in v3:
time: 267 us
  waiting for transfers between devices  123 us (46%)
  Pallas kernels  55.3 us (21%)
  starting transfers between devices  38.1 us (14%)
  blocking collectives  35 us (13%)
  local copies, waits for them, and re-layouts  8.35 us (3%)
  other arithmetic  5.85 us (2%)
    pallas_call x3, Pallas kernels, expert_block(): pl.pallas_call(lambda *refs: expert_kernel(len(parts), *refs), out_shape=...  37.7 us
    all_to_all x1, waiting for transfers between devices, per_device(): lax.all_to_all(partial_rows, 'exp', split_axis=0, concat_axis=0, tiled=True)  29.8 us
    ppermute x1, waiting for transfers between devices, experts(): from_left = lax.ppermute(to_right.astype(BF16), 'seq', x_shift(1))  23.2 us
    all_to_all x1, blocking collectives, per_device(): lax.all_to_all(jnp.tile(outgoing, (splits, 1)), 'exp', split_axis=0, conc...  21.2 us
    all_to_all x1, waiting for transfers between devices, per_device(): lax.all_to_all(own_rows.astype(BF16), 'exp', split_axis=0, concat_axis=0,...  17.1 us
    ppermute x6, waiting for transfers between devices, from_others(): return [lax.ppermute(value, 'exp', shift(by)) for by in (1, 2, 3)]  16.3 us
    all_gather x1, blocking collectives, per_device(): gathered = lax.all_gather(packed, 'seq')  13.8 us
    ppermute x6, starting transfers between devices, from_others(): return [lax.ppermute(value, 'exp', shift(by)) for by in (1, 2, 3)]  13 us
  transfers between devices with their start and end apart: 25, of which 15 were waited for; matrix products, arithmetic and copies ran while one was open for 2% of the time, Pallas kernels for 10%

profile of v3, /device:TPU:0, one launch (start us, length us, event | category | flops | bytes accessed | tf_op | source)
XLA Modules:
  0.0 266.7 jit_solution(10612376056085430547)
XLA Ops:
  0.0 0.8 slice.24
  0.8 1.3 collective-permute-start
  2.1 1.0 reshape.82.xin
  3.1 1.2 copy.32.xproj
  4.3 0.7 copy-done.3
  5.0 0.7 copy-done.4
  5.7 0.7 mixer_in.1
  6.4 2.5 collective-permute-start.1
  8.9 3.6 %collective-permute-start.2 = (bf16[256,288]{1,0:T(8,128)(2,1)S(1)}, bf16[256,288]{1,0:T(8,128)(2,1)S(1)}, u32[]{:S(2)}, u32[]{:S(2)}) collective-permute-start(bf16[256,288]{1,0:T(8,128)(2,1)S(1)} %get-tuple-element.20), channel_id=1, source_target_pairs={{0,2},{1,3},{2,0},{3,1},{4,6},{5,7},{6,4},{7,5},{8,10},{9,11},{10,... | collective-permute-start | bytes 442376 | tf_op jit(solution)/shard_map/ppermute | solution.py:44
  12.5 1.0 collective-permute-start.3
  13.5 2.2 collective-permute-done.1
  15.7 6.0 %collective-permute-done.2 = bf16[256,288]{1,0:T(8,128)(2,1)S(1)} collective-permute-done((bf16[256,288]{1,0:T(8,128)(2,1)S(1)}, bf16[256,288]{1,0:T(8,128)(2,1)S(1)}, u32[]{:S(2)}, u32[]{:S(2)}) %collective-permute-start.2) | collective-permute-done | bytes 147488 | tf_op jit(solution)/shard_map/ppermute | solution.py:44
  21.7 0.1 add_convert_fusion.2.p0
  21.8 1.6 collective-permute-start.4
  23.5 2.9 %collective-permute-start.5 = (bf16[256,288]{1,0:T(8,128)(2,1)S(1)}, bf16[256,288]{1,0:T(8,128)(2,1)S(1)}, u32[]{:S(2)}, u32[]{:S(2)}) collective-permute-start(bf16[256,288]{1,0:T(8,128)(2,1)S(1)} %add_convert_fusion.2.p0), channel_id=1, source_target_pairs={{0,8},{1,9},{2,10},{3,11},{4,12},{5,13},{6,14},{7,15},{8,0},{9,1},... | collective-permute-start | bytes 442376 | tf_op jit(solution)/shard_map/ppermute | solution.py:44
  26.4 1.3 collective-permute-start.6
  27.8 2.8 %collective-permute-done.4.p1 = bf16[256,288]{1,0:T(8,128)(2,1)S(1)} collective-permute-done((bf16[256,288]{1,0:T(8,128)(2,1)S(1)}, bf16[256,288]{1,0:T(8,128)(2,1)S(1)}, u32[]{:S(2)}, u32[]{:S(2)}) %collective-permute-start.4) | collective-permute-done | bytes 147488 | tf_op jit(solution)/shard_map/ppermute | solution.py:44
  30.6 5.4 %collective-permute-done.5.p2 = bf16[256,288]{1,0:T(8,128)(2,1)S(1)} collective-permute-done((bf16[256,288]{1,0:T(8,128)(2,1)S(1)}, bf16[256,288]{1,0:T(8,128)(2,1)S(1)}, u32[]{:S(2)}, u32[]{:S(2)}) %collective-permute-start.5) | collective-permute-done | bytes 147488 | tf_op jit(solution)/shard_map/ppermute | solution.py:44
  36.0 4.9 %section_scan.1 = (f32[256,512]{1,0:T(8,128)S(1)}, bf16[256,128]{1,0:T(8,128)(2,1)S(1)}, bf16[72,512]{1,0:T(8,128)(2,1)S(1)}) custom-call(bf16[256,288]{1,0:T(8,128)(2,1)S(1)} %add_convert_fusion.2.p0, bf16[256,288]{1,0:T(8,128)(2,1)S(1)} %collective-permute-done.4.p1, bf16[256,288]{1,0:T(8,128)(2,1)S(1)} %collective-permute-done.5.p2, ...), custom_call_target="tpu_custom_call" | custom-call | tf_op jit(solution)/shard_map/section_scan/pallas_call | solution.py:243
  40.9 13.8 %all-gather = bf16[576,512]{1,0:T(8,128)(2,1)S(1)} all-gather(bf16[72,512]{1,0:T(8,128)(2,1)S(1)} %get-tuple-element.22), channel_id=2, replica_groups=mesh['seq'=8,'exp'=16] {'seq'}, dimensions={0}, use_global_device_ids=true | all-gather | bytes 663552 | tf_op jit(solution)/shard_map/all_gather | solution.py:414
  54.7 2.2 copy-done
  56.9 12.0 %mixer_out.1 = bf16[256,4096]{1,0:T(8,128)(2,1)} custom-call(s32[1]{0:T(128)} %bitcast.place, bf16[8,72,512]{2,1,0:T(8,128)(2,1)S(1)} %bitcast.24, f32[256,512]{1,0:T(8,128)S(1)} %get-tuple-element.23.step, bf16[256,128]{1,0:T(8,128)(2,1)S(1)} %get-tuple-element.24.pairs, bf16[256,512]{1,0:T(8,128)(2,1)S(1)} %get-tuple-element.21.inner, ...), custom_call_target="tpu_custom_call" | custom-call | tf_op jit(solution)/shard_map/mixer_out/pallas_call | solution.py:263
  68.9 6.1 %all-to-all-start = ((bf16[16,16,4096]{2,1,0:T(8,128)(2,1)}), bf16[16,16,4096]{2,1,0:T(8,128)(2,1)S(1)}, u32[]{:S(2)}, u32[]{:S(2)}) async-start(bf16[16,16,4096]{2,1,0:T(8,128)(2,1)} %bitcast.5), calls=%async_computation | async-start | bytes 4194304 | tf_op jit(solution)/shard_map/all_to_all | solution.py:427
  75.1 0.1 copy.34
  75.2 0.1 eq.30
  75.4 0.2 select_reduce_fusion.1
  76.0 29.8 %all-to-all-done = bf16[16,16,4096]{2,1,0:T(8,128)(2,1)S(1)} async-done(((bf16[16,16,4096]{2,1,0:T(8,128)(2,1)}), bf16[16,16,4096]{2,1,0:T(8,128)(2,1)S(1)}, u32[]{:S(2)}, u32[]{:S(2)}) %all-to-all-start) | async-done | bytes 2097184 | tf_op jit(solution)/shard_map/all_to_all | solution.py:427
  105.8 0.3 convert_reduce_fusion
  106.2 0.2 multiply_reduce_fusion
  106.5 0.3 convolution_convert_fusion
  106.8 0.1 tile.2
  106.9 21.2 %all_to_all.29 = bf16[16,8,4096]{2,1,0:T(8,128)(2,1)S(1)} all-to-all(bf16[16,8,4096]{2,1,0:T(8,128)(2,1)S(1)} %bitcast.29), channel_id=1, replica_groups=mesh['seq'=8,'exp'=16] {'exp'}, dimensions={0} | all-to-all | bytes 2097152 | tf_op jit(solution)/shard_map/all_to_all | solution.py:440
  128.1 1.5 collective-permute-start.10
  129.6 0.6 collective-permute-start.9
  130.2 0.6 collective-permute-done.7.refs_1_
  130.8 10.1 %experts_256.2 = (bf16[128,4096]{1,0:T(8,128)(2,1)S(1)}, bf16[128,4096]{1,0:T(8,128)(2,1)S(1)}) custom-call(bf16[128,4096]{1,0:T(8,128)(2,1)S(1)} %bitcast.23, bf16[128,4096]{1,0:T(8,128)(2,1)S(1)} %collective-permute-done.7.refs_1_, bf16[1,4096,768]{2,1,0:T(8,128)(2,1)} %refs_4_.5, bf16[1,4096,768]{2,1,0:T(8,128)(2,1)} %refs_5_.3, bf16[1,768,4096]{2,1,0:T(8,128)(2,1)} %refs_6_.3), custom_call_target="tpu_custom_call" | custom-call | flops 4831838208 | bytes 23068672 | tf_op jit(solution)/shard_map/experts_256/pallas_call | solution.py:322
  140.9 12.8 %collective-permute-done.10.refs_1_ = bf16[128,4096]{1,0:T(8,128)(2,1)S(1)} collective-permute-done((bf16[128,4096]{1,0:T(8,128)(2,1)S(1)}, bf16[128,4096]{1,0:T(8,128)(2,1)S(1)}, u32[]{:S(2)}, u32[]{:S(2)}) %collective-permute-start.10) | collective-permute-done | bytes 1048608 | tf_op jit(solution)/shard_map/ppermute | solution.py:365
  153.7 2.4 collective-permute-done.9.refs_0_
  156.3 3.3 %collective-permute-start.14 = (bf16[64,4096]{1,0:T(8,128)(2,1)S(1)}, bf16[64,4096]{1,0:T(8,128)(2,1)S(1)}, u32[]{:S(2)}, u32[]{:S(2)}) collective-permute-start(bf16[64,4096]{1,0:T(8,128)(2,1)S(1)} %slice.27), channel_id=1, source_target_pairs={{0,96},{16,112},{32,0},{48,16},{64,32},{80,48},{96,64},{112,80},{1... | collective-permute-start | bytes 1572872 | tf_op jit(solution)/shard_map/ppermute | solution.py:370
  159.6 11.1 %collective-permute-done.13.refs_0_ = bf16[64,4096]{1,0:T(8,128)(2,1)S(1)} collective-permute-done((bf16[64,4096]{1,0:T(8,128)(2,1)S(1)}, bf16[64,4096]{1,0:T(8,128)(2,1)S(1)}, u32[]{:S(2)}, u32[]{:S(2)}) %collective-permute-start.13) | collective-permute-done | bytes 524320 | tf_op jit(solution)/shard_map/ppermute | solution.py:369
  170.7 0.5 collective-permute-start.16
  171.2 1.4 collective-permute-done.15.refs_2_
  172.6 0.7 collective-permute-done.16.refs_3_
  173.3 10.1 %experts_256.3 = (bf16[128,4096]{1,0:T(8,128)(2,1)S(1)}, bf16[128,4096]{1,0:T(8,128)(2,1)S(1)}) custom-call(bf16[64,4096]{1,0:T(8,128)(2,1)S(1)} %collective-permute-done.13.refs_0_, bf16[64,4096]{1,0:T(8,128)(2,1)S(1)} %collective-permute-done.14.refs_1_, bf16[64,4096]{1,0:T(8,128)(2,1)S(1)} %collective-permute-done.15.refs_2_, ...), custom_call_target="tpu_custom_call" | custom-call | flops 4831838208 | bytes 23068672 | tf_op jit(solution)/shard_map/experts_256/pallas_call | solution.py:322
  183.4 0.2 collective-permute-start.17
  183.6 0.4 collective-permute-start.11
  184.0 0.1 collective-permute-start.12
  184.1 2.0 collective-permute-done.17
  186.1 0.2 add_convert_fusion.1
  186.4 0.1 fusion.8
  186.6 3.2 %collective-permute-start.19 = (bf16[64,4096]{1,0:T(8,128)(2,1)S(1)}, bf16[64,4096]{1,0:T(8,128)(2,1)S(1)}, u32[]{:S(2)}, u32[]{:S(2)}) collective-permute-start(bf16[64,4096]{1,0:T(8,128)(2,1)S(1)} %get-tuple-element.37), channel_id=1, source_target_pairs={{0,96},{16,112},{32,0},{48,16},{64,32},{80,48},{96,64},{112,80},{1... | collective-permute-start | bytes 1572872 | tf_op jit(solution)/shard_map/ppermute | solution.py:376
  189.8 17.5 %experts_512.1 = (bf16[256,4096]{1,0:T(8,128)(2,1)}, bf16[256,4096]{1,0:T(8,128)(2,1)}) custom-call(bf16[128,4096]{1,0:T(8,128)(2,1)S(1)} %collective-permute-done.9.refs_0_, bf16[128,4096]{1,0:T(8,128)(2,1)S(1)} %collective-permute-done.10.refs_1_, bf16[128,4096]{1,0:T(8,128)(2,1)S(1)} %collective-permute-done.11.refs_2_, ...), custom_call_target="tpu_custom_call" | custom-call | flops 9663676416 | bytes 27262976 | tf_op jit(solution)/shard_map/experts_512/pallas_call | solution.py:322
  207.4 0.5 collective-permute-start.8
  207.9 5.4 %collective-permute-done.20 = bf16[256,4096]{1,0:T(8,128)(2,1)S(1)} collective-permute-done((bf16[256,4096]{1,0:T(8,128)(2,1)}, bf16[256,4096]{1,0:T(8,128)(2,1)S(1)}, u32[]{:S(2)}, u32[]{:S(2)}) %collective-permute-start.20) | collective-permute-done | bytes 2097184 | tf_op jit(solution)/shard_map/ppermute | solution.py:48
  213.3 2.3 convert_add_fusion
  215.6 0.4 fusion.2
  216.1 3.2 %collective-permute-start.22 = (bf16[128,4096]{1,0:T(8,128)(2,1)S(1)}, bf16[128,4096]{1,0:T(8,128)(2,1)S(1)}, u32[]{:S(2)}, u32[]{:S(2)}) collective-permute-start(bf16[128,4096]{1,0:T(8,128)(2,1)S(1)} %get-tuple-element.36), channel_id=1, source_target_pairs={{0,96},{16,112},{32,0},{48,16},{64,32},{80,48},{96,64},{112,80},{1... | collective-permute-start | bytes 3145736 | tf_op jit(solution)/shard_map/ppermute | solution.py:382
  219.3 23.2 %collective-permute-done.21 = bf16[128,4096]{1,0:T(8,128)(2,1)S(1)} collective-permute-done((bf16[128,4096]{1,0:T(8,128)(2,1)S(1)}, bf16[128,4096]{1,0:T(8,128)(2,1)S(1)}, u32[]{:S(2)}, u32[]{:S(2)}) %collective-permute-start.21) | collective-permute-done | bytes 1048608 | tf_op jit(solution)/shard_map/ppermute | solution.py:383
  242.5 1.7 fusion.3
  244.1 3.8 %all-to-all-start.2 = ((bf16[16,8,4096]{2,1,0:T(8,128)(2,1)}), bf16[16,8,4096]{2,1,0:T(8,128)(2,1)S(1)}, u32[]{:S(2)}, u32[]{:S(2)}) async-start(bf16[16,8,4096]{2,1,0:T(8,128)(2,1)} %fusion.3), calls=%async_computation.2 | async-start | bytes 2097152 | tf_op jit(solution)/shard_map/all_to_all | solution.py:444
  248.1 17.1 %all-to-all-done.2 = bf16[16,8,4096]{2,1,0:T(8,128)(2,1)S(1)} async-done(((bf16[16,8,4096]{2,1,0:T(8,128)(2,1)}), bf16[16,8,4096]{2,1,0:T(8,128)(2,1)S(1)}, u32[]{:S(2)}, u32[]{:S(2)}) %all-to-all-start.2) | async-done | bytes 1048608 | tf_op jit(solution)/shard_map/all_to_all | solution.py:444
  265.2 0.2 convert_reduce_fusion.1
  265.4 0.6 fusion
  266.0 0.7 reshape.84
  (58 shorter events, 1.4 us)
Async XLA Ops:
  0.0 27.7 %copy-start.8 = (bf16[64,4,512]{2,1,0:T(4,128)(2,1)S(1)}, bf16[64,4,512]{2,1,0:T(4,128)(2,1)}, u32[]{:S(2)}) copy-start(bf16[64,4,512]{2,1,0:T(4,128)(2,1)} %param.18) | copy-start | bytes 786436
  0.0 36.0 %copy-start.5 = (f32[512]{0:T(512)S(1)}, f32[512]{0:T(512)}, u32[]{:S(2)}) copy-start(f32[512]{0:T(512)} %param.23) | copy-start | bytes 6148
  0.0 36.0 %copy-start.1 = (bf16[256,512]{1,0:T(8,128)(2,1)S(1)}, bf16[256,512]{1,0:T(8,128)(2,1)}, u32[]{:S(2)}) copy-start(bf16[256,512]{1,0:T(8,128)(2,1)} %dtproj.1) | copy-start | bytes 786436
  0.0 36.0 %copy-start.2 = (f32[16,512]{1,0:T(8,128)S(1)}, f32[16,512]{1,0:T(8,128)}, u32[]{:S(2)}) copy-start(f32[16,512]{1,0:T(8,128)} %a_log.3) | copy-start | bytes 98308
  0.8 3.5 %collective-permute-start = (bf16[12,512]{1,0:T(8,128)(2,1)S(1)}, bf16[12,512]{1,0:T(8,128)(2,1)S(1)}, u32[]{:S(2)}, u32[]{:S(2)}) collective-permute-start(bf16[12,512]{1,0:T(8,128)(2,1)S(1)} %slice.25), channel_id=1, source_target_pairs={{0,16},{16,32},{32,48},{48,64},{64,80},{80,96},{96,112},{1,17},{17... | collective-permute-start | bytes 36872 | tf_op jit(solution)/shard_map/ppermute | solution.py:40
  4.3 0.7 copy-start.3
  5.0 0.7 copy-start.4
  5.7 49.0 %copy-start.6 = (f32[512]{0:T(512)S(1)}, f32[512]{0:T(512)}, u32[]{:S(2)}) copy-start(f32[512]{0:T(512)} %param.25) | copy-start | bytes 6148
  6.4 9.3 %collective-permute-start.1 = (bf16[256,288]{1,0:T(8,128)(2,1)S(1)}, bf16[256,288]{1,0:T(8,128)(2,1)S(1)}, u32[]{:S(2)}, u32[]{:S(2)}) collective-permute-start(bf16[256,288]{1,0:T(8,128)(2,1)S(1)} %get-tuple-element.20), channel_id=1, source_target_pairs={{0,1},{1,2},{2,3},{3,0},{4,5},{5,6},{6,7},{7,4},{8,9},{9,10},{10,1... | collective-permute-start | bytes 442376 | tf_op jit(solution)/shard_map/ppermute | solution.py:44
  8.9 12.8 %collective-permute-start.2 = (bf16[256,288]{1,0:T(8,128)(2,1)S(1)}, bf16[256,288]{1,0:T(8,128)(2,1)S(1)}, u32[]{:S(2)}, u32[]{:S(2)}) collective-permute-start(bf16[256,288]{1,0:T(8,128)(2,1)S(1)} %get-tuple-element.20), channel_id=1, source_target_pairs={{0,2},{1,3},{2,0},{3,1},{4,6},{5,7},{6,4},{7,5},{8,10},{9,11},{10,... | collective-permute-start | bytes 442376 | tf_op jit(solution)/shard_map/ppermute | solution.py:44
  12.5 9.2 %collective-permute-start.3 = (bf16[256,288]{1,0:T(8,128)(2,1)S(1)}, bf16[256,288]{1,0:T(8,128)(2,1)S(1)}, u32[]{:S(2)}, u32[]{:S(2)}) collective-permute-start(bf16[256,288]{1,0:T(8,128)(2,1)S(1)} %get-tuple-element.20), channel_id=1, source_target_pairs={{0,3},{1,0},{2,1},{3,2},{4,7},{5,4},{6,5},{7,6},{8,11},{9,8},{10,9... | collective-permute-start | bytes 442376 | tf_op jit(solution)/shard_map/ppermute | solution.py:44
  21.8 8.8 %collective-permute-start.4 = (bf16[256,288]{1,0:T(8,128)(2,1)S(1)}, bf16[256,288]{1,0:T(8,128)(2,1)S(1)}, u32[]{:S(2)}, u32[]{:S(2)}) collective-permute-start(bf16[256,288]{1,0:T(8,128)(2,1)S(1)} %add_convert_fusion.2.p0), channel_id=1, source_target_pairs={{0,4},{1,5},{2,6},{3,7},{4,8},{5,9},{6,10},{7,11},{8,12},{9,13},{1... | collective-permute-start | bytes 442376 | tf_op jit(solution)/shard_map/ppermute | solution.py:44
  23.5 12.5 %collective-permute-start.5 = (bf16[256,288]{1,0:T(8,128)(2,1)S(1)}, bf16[256,288]{1,0:T(8,128)(2,1)S(1)}, u32[]{:S(2)}, u32[]{:S(2)}) collective-permute-start(bf16[256,288]{1,0:T(8,128)(2,1)S(1)} %add_convert_fusion.2.p0), channel_id=1, source_target_pairs={{0,8},{1,9},{2,10},{3,11},{4,12},{5,13},{6,14},{7,15},{8,0},{9,1},... | collective-permute-start | bytes 442376 | tf_op jit(solution)/shard_map/ppermute | solution.py:44
  26.4 9.6 %collective-permute-start.6 = (bf16[256,288]{1,0:T(8,128)(2,1)S(1)}, bf16[256,288]{1,0:T(8,128)(2,1)S(1)}, u32[]{:S(2)}, u32[]{:S(2)}) collective-permute-start(bf16[256,288]{1,0:T(8,128)(2,1)S(1)} %add_convert_fusion.2.p0), channel_id=1, source_target_pairs={{0,12},{1,13},{2,14},{3,15},{4,0},{5,1},{6,2},{7,3},{8,4},{9,5},{1... | collective-permute-start | bytes 442376 | tf_op jit(solution)/shard_map/ppermute | solution.py:44
  54.7 2.2 copy-start
  68.9 6.2 %copy-start.7 = (bf16[4,4,4096]{2,1,0:T(4,128)(2,1)S(1)}, bf16[4,4,4096]{2,1,0:T(4,128)(2,1)}, u32[]{:S(2)}) copy-start(bf16[4,4,4096]{2,1,0:T(4,128)(2,1)} %param.27) | copy-start | bytes 393220
  68.9 6.2 %copy-start.10 = (s32[4,4,2]{1,2,0:T(2,128)S(1)}, s32[4,4,2]{1,2,0:T(2,128)}, u32[]{:S(2)}) copy-start(s32[4,4,2]{1,2,0:T(2,128)} %param.29) | copy-start | bytes 388
  68.9 36.9 %all-to-all-start = ((bf16[16,16,4096]{2,1,0:T(8,128)(2,1)}), bf16[16,16,4096]{2,1,0:T(8,128)(2,1)S(1)}, u32[]{:S(2)}, u32[]{:S(2)}) async-start(bf16[16,16,4096]{2,1,0:T(8,128)(2,1)} %bitcast.5), calls=%async_computation | async-start | bytes 4194304 | tf_op jit(solution)/shard_map/all_to_all | solution.py:427
  75.3 31.2 %copy-start.9 = (f32[4096]{0:T(1024)S(1)}, f32[4096]{0:T(1024)}, u32[]{:S(2)}) copy-start(f32[4096]{0:T(1024)} %param.28) | copy-start | bytes 49156
  128.1 2.7 collective-permute-start.7
  128.1 25.6 %collective-permute-start.10 = (bf16[128,4096]{1,0:T(8,128)(2,1)S(1)}, bf16[128,4096]{1,0:T(8,128)(2,1)S(1)}, u32[]{:S(2)}, u32[]{:S(2)}) collective-permute-start(bf16[128,4096]{1,0:T(8,128)(2,1)S(1)} %bitcast.21), channel_id=1, source_target_pairs={{0,96},{16,112},{32,0},{48,16},{64,32},{80,48},{96,64},{112,80},{1... | collective-permute-start | bytes 3145736 | tf_op jit(solution)/shard_map/ppermute | solution.py:365
  129.6 26.5 %collective-permute-start.9 = (bf16[128,4096]{1,0:T(8,128)(2,1)S(1)}, bf16[128,4096]{1,0:T(8,128)(2,1)S(1)}, u32[]{:S(2)}, u32[]{:S(2)}) collective-permute-start(bf16[128,4096]{1,0:T(8,128)(2,1)S(1)} %bitcast.22), channel_id=1, source_target_pairs={{0,32},{16,48},{32,64},{48,80},{64,96},{80,112},{96,0},{112,16},{1... | collective-permute-start | bytes 3145736 | tf_op jit(solution)/shard_map/ppermute | solution.py:364
  156.1 14.5 %collective-permute-start.13 = (bf16[64,4096]{1,0:T(8,128)(2,1)S(1)}, bf16[64,4096]{1,0:T(8,128)(2,1)S(1)}, u32[]{:S(2)}, u32[]{:S(2)}) collective-permute-start(bf16[64,4096]{1,0:T(8,128)(2,1)S(1)} %slice.26), channel_id=1, source_target_pairs={{0,32},{16,48},{32,64},{48,80},{64,96},{80,112},{96,0},{112,16},{1... | collective-permute-start | bytes 1572872 | tf_op jit(solution)/shard_map/ppermute | solution.py:369
  156.3 14.4 %collective-permute-start.14 = (bf16[64,4096]{1,0:T(8,128)(2,1)S(1)}, bf16[64,4096]{1,0:T(8,128)(2,1)S(1)}, u32[]{:S(2)}, u32[]{:S(2)}) collective-permute-start(bf16[64,4096]{1,0:T(8,128)(2,1)S(1)} %slice.27), channel_id=1, source_target_pairs={{0,96},{16,112},{32,0},{48,16},{64,32},{80,48},{96,64},{112,80},{1... | collective-permute-start | bytes 1572872 | tf_op jit(solution)/shard_map/ppermute | solution.py:370
  170.7 1.9 collective-permute-start.15
  170.7 2.7 collective-permute-start.16
  183.4 2.7 %collective-permute-start.17 = (bf16[128,4096]{1,0:T(8,128)(2,1)S(1)}, bf16[128,4096]{1,0:T(8,128)(2,1)S(1)}, u32[]{:S(2)}, u32[]{:S(2)}) collective-permute-start(bf16[128,4096]{1,0:T(8,128)(2,1)S(1)} %get-tuple-element.32), channel_id=1, source_target_pairs={{0,16},{16,0},{32,48},{48,32},{64,80},{80,64},{96,112},{112,96},{1... | collective-permute-start | bytes 3145736 | tf_op jit(solution)/shard_map/ppermute | solution.py:48
  183.6 6.2 %collective-permute-start.11 = (bf16[128,4096]{1,0:T(8,128)(2,1)S(1)}, bf16[128,4096]{1,0:T(8,128)(2,1)S(1)}, u32[]{:S(2)}, u32[]{:S(2)}) collective-permute-start(bf16[128,4096]{1,0:T(8,128)(2,1)S(1)} %collective-permute-done.9.refs_0_), channel_id=1, source_target_pairs={{0,16},{16,0},{32,48},{48,32},{64,80},{80,64},{96,112},{112,96},{1... | collective-permute-start | bytes 3145736 | tf_op jit(solution)/shard_map/ppermute | solution.py:48
  184.0 5.8 %collective-permute-start.12 = (bf16[128,4096]{1,0:T(8,128)(2,1)S(1)}, bf16[128,4096]{1,0:T(8,128)(2,1)S(1)}, u32[]{:S(2)}, u32[]{:S(2)}) collective-permute-start(bf16[128,4096]{1,0:T(8,128)(2,1)S(1)} %collective-permute-done.10.refs_1_), channel_id=1, source_target_pairs={{0,16},{16,0},{32,48},{48,32},{64,80},{80,64},{96,112},{112,96},{1... | collective-permute-start | bytes 3145736 | tf_op jit(solution)/shard_map/ppermute | solution.py:48
  186.5 20.8 %collective-permute-start.18 = (bf16[64,4096]{1,0:T(8,128)(2,1)S(1)}, bf16[64,4096]{1,0:T(8,128)(2,1)S(1)}, u32[]{:S(2)}, u32[]{:S(2)}) collective-permute-start(bf16[64,4096]{1,0:T(8,128)(2,1)S(1)} %get-tuple-element.38), channel_id=1, source_target_pairs={{0,32},{16,48},{32,64},{48,80},{64,96},{80,112},{96,0},{112,16},{1... | collective-permute-start | bytes 1572872 | tf_op jit(solution)/shard_map/ppermute | solution.py:375
  186.6 20.8 %collective-permute-start.19 = (bf16[64,4096]{1,0:T(8,128)(2,1)S(1)}, bf16[64,4096]{1,0:T(8,128)(2,1)S(1)}, u32[]{:S(2)}, u32[]{:S(2)}) collective-permute-start(bf16[64,4096]{1,0:T(8,128)(2,1)S(1)} %get-tuple-element.37), channel_id=1, source_target_pairs={{0,96},{16,112},{32,0},{48,16},{64,32},{80,48},{96,64},{112,80},{1... | collective-permute-start | bytes 1572872 | tf_op jit(solution)/shard_map/ppermute | solution.py:376
  207.3 6.0 %collective-permute-start.20 = (bf16[256,4096]{1,0:T(8,128)(2,1)}, bf16[256,4096]{1,0:T(8,128)(2,1)S(1)}, u32[]{:S(2)}, u32[]{:S(2)}) collective-permute-start(bf16[256,4096]{1,0:T(8,128)(2,1)} %get-tuple-element.34), channel_id=1, source_target_pairs={{0,16},{16,0},{32,48},{48,32},{64,80},{80,64},{96,112},{112,96},{1... | collective-permute-start | bytes 6291464 | tf_op jit(solution)/shard_map/ppermute | solution.py:48
  207.4 11.9 %collective-permute-start.8 = (bf16[128,4096]{1,0:T(8,128)(2,1)S(1)}, bf16[128,4096]{1,0:T(8,128)(2,1)S(1)}, u32[]{:S(2)}, u32[]{:S(2)}) collective-permute-start(bf16[128,4096]{1,0:T(8,128)(2,1)S(1)} %get-tuple-element.26), channel_id=1, source_target_pairs={{0,16},{16,0},{32,48},{48,32},{64,80},{80,64},{96,112},{112,96},{1... | collective-permute-start | bytes 3145736 | tf_op jit(solution)/shard_map/ppermute | solution.py:48
  216.0 26.5 %collective-permute-start.21 = (bf16[128,4096]{1,0:T(8,128)(2,1)S(1)}, bf16[128,4096]{1,0:T(8,128)(2,1)S(1)}, u32[]{:S(2)}, u32[]{:S(2)}) collective-permute-start(bf16[128,4096]{1,0:T(8,128)(2,1)S(1)} %get-tuple-element.35), channel_id=1, source_target_pairs={{0,32},{16,48},{32,64},{48,80},{64,96},{80,112},{96,0},{112,16},{1... | collective-permute-start | bytes 3145736 | tf_op jit(solution)/shard_map/ppermute | solution.py:383
  216.1 26.4 %collective-permute-start.22 = (bf16[128,4096]{1,0:T(8,128)(2,1)S(1)}, bf16[128,4096]{1,0:T(8,128)(2,1)S(1)}, u32[]{:S(2)}, u32[]{:S(2)}) collective-permute-start(bf16[128,4096]{1,0:T(8,128)(2,1)S(1)} %get-tuple-element.36), channel_id=1, source_target_pairs={{0,96},{16,112},{32,0},{48,16},{64,32},{80,48},{96,64},{112,80},{1... | collective-permute-start | bytes 3145736 | tf_op jit(solution)/shard_map/ppermute | solution.py:382
  244.1 3.8 %copy-start.11 = (bf16[4,4,2]{1,2,0:T(2,128)(2,1)S(1)}, bf16[4,4,2]{1,2,0:T(2,128)(2,1)}, u32[]{:S(2)}) copy-start(bf16[4,4,2]{1,2,0:T(2,128)(2,1)} %param.30) | copy-start | bytes 196
  244.1 21.1 %all-to-all-start.2 = ((bf16[16,8,4096]{2,1,0:T(8,128)(2,1)}), bf16[16,8,4096]{2,1,0:T(8,128)(2,1)S(1)}, u32[]{:S(2)}, u32[]{:S(2)}) async-start(bf16[16,8,4096]{2,1,0:T(8,128)(2,1)} %fusion.3), calls=%async_computation.2 | async-start | bytes 2097152 | tf_op jit(solution)/shard_map/all_to_all | solution.py:444

commit v4 on v3

--- a/solution.py
+++ b/solution.py
@@ -29,6 +29,10 @@
 
 def x_shift(by):
     return [(x * 2 + c, (x + by) % 4 * 2 + c) for x in range(4) for c in range(2)]
+
+
+def x_onward(by):
+    return [(x * 2 + c, (x + by) * 2 + c) for x in range(4 - by) for c in range(2)]
 
 
 CORE = [(x * 2 + c, x * 2 + 1 - c) for x in range(4) for c in range(2)]
@@ -71,7 +75,9 @@
     by_position = jnp.concatenate(blocks, axis=0)
     ordered = jnp.dot(document_major(False), by_position, preferred_element_type=F32).astype(BF16)
     inner[...] = ordered
-    projected[...] = jnp.dot(ordered, xproj[...], preferred_element_type=F32).astype(BF16)
+    projected[...] = lax.dot_general(
+        xproj[...], ordered, (((1,), (1,)), ((), ())), preferred_element_type=F32
+    ).astype(BF16)
 
 
 def spread(pairs, target, first):
@@ -101,8 +107,8 @@
     total = (p0[...].astype(F32) + p1[...].astype(F32)) + (
         p2[...].astype(F32) + p3[...].astype(F32)
     )
-    low_rank = total[:, :RANK].astype(BF16)
-    states = total[:, RANK : RANK + 2 * STATE]
+    low_rank = total[:RANK].astype(BF16)
+    states = total[RANK : RANK + 2 * STATE].T
     high = states.astype(BF16)
     low = (states - high.astype(F32)).astype(BF16)
     pairs[...] = jnp.concatenate(
@@ -116,7 +122,10 @@
         axis=1,
     )
     step[...] = jax.nn.softplus(
-        jnp.dot(low_rank, dtproj[...], preferred_element_type=F32) + dt_bias[...]
+        lax.dot_general(
+            low_rank, dtproj[...], (((0,), (0,)), ((), ())), preferred_element_type=F32
+        )
+        + dt_bias[...]
     )
     taken[...] = step[...] * inner[...].astype(F32)
     spread(pairs, entering, 0)
@@ -151,30 +160,40 @@
 
 
 def mixer_out_kernel(
-    place,
-    gathered,
-    step,
-    pairs,
-    inner,
-    a_log,
-    skip,
-    zin,
-    out_weight,
-    rows,
-    totals,
-    taken,
-    entering,
-    leaving,
-    scanned,
-    weight,
-    arrived,
+    core,
+    *refs,
 ):
+    earlier, refs = refs[:7], refs[7:]
+    (
+        step,
+        pairs,
+        inner,
+        a_log,
+        skip,
+        zin,
+        out_weight,
+        rows,
+        totals,
+        finals,
+        taken,
+        entering,
+        leaving,
+        scanned,
+        weight,
+        arrived,
+    ) = refs
     copy = pltpu.make_async_copy(out_weight, weight, arrived)
     copy.start()
-    sections = gathered.shape[0]
-    for section in range(sections - 1):
-        both = gathered[section, DOCS * STATE : DOCS * STATE + 2 * DOCS, :].astype(F32)
-        totals[8 * section : 8 * section + DOCS, :] = both[:DOCS] + both[DOCS:]
+    first = core[0] == 0
+    partner = earlier[3][...].astype(F32)
+    order = [jnp.where(first, 0.0, partner)]
+    for by in (1, 2, 3):
+        mine, theirs = earlier[by - 1][...].astype(F32), earlier[3 + by][...].astype(F32)
+        order = [jnp.where(first, mine, theirs), jnp.where(first, theirs, mine)] + order
+    for index, packed in enumerate(order):
+        both = packed[DOCS * STATE :]
+        totals[8 * index : 8 * index + DOCS, :] = both[:DOCS] + both[DOCS:]
+        finals[index] = packed[: DOCS * STATE]
     taken[...] = step[...] * inner[...].astype(F32)
     spread(pairs, entering, 0)
     spread(pairs, leaving, 2 * STATE)
@@ -182,11 +201,10 @@
 
     def document(doc, carry):
         state = jnp.zeros(rate.shape, F32)
-        for section in range(sections - 1):
-            total = totals[pl.ds(8 * section + doc, 1), :]
-            final = gathered[section, pl.ds(pl.multiple_of(doc * STATE, STATE), STATE), :]
-            later = jnp.exp(total * rate) * state + final.astype(F32)
-            state = jnp.where(section < place[0], later, state)
+        for index in range(len(order)):
+            total = totals[pl.ds(8 * index + doc, 1), :]
+            final = finals[index, pl.ds(pl.multiple_of(doc * STATE, STATE), STATE), :]
+            state = jnp.exp(total * rate) * state + final
 
         def eight(group, state):
             first = pl.multiple_of(doc * SECTION + group * 8, 8)
@@ -228,7 +246,7 @@
         mixer_in_kernel,
         out_shape=(
             jax.ShapeDtypeStruct((TOKENS, channels), BF16),
-            jax.ShapeDtypeStruct((TOKENS, xproj.shape[1]), BF16),
+            jax.ShapeDtypeStruct((xproj.shape[0], TOKENS), BF16),
         ),
         in_specs=[whole()] * 5,
         out_specs=(whole(), whole()),
@@ -258,15 +276,16 @@
     )(*parts, dtproj, dt_bias, a_log, inner)
 
 
-def mixer_out(place, gathered, step, pairs, inner, a_log, skip, zin, out_weight):
+def mixer_out(core, earlier, step, pairs, inner, a_log, skip, zin, out_weight):
     channels = inner.shape[1]
     return pl.pallas_call(
         mixer_out_kernel,
         out_shape=jax.ShapeDtypeStruct((TOKENS, D), BF16),
-        in_specs=[whole(pltpu.SMEM)] + [whole()] * 7 + [whole(pl.ANY)],
+        in_specs=[whole(pltpu.SMEM)] + [whole()] * 13 + [whole(pl.ANY)],
         out_specs=whole(),
         scratch_shapes=[
             pltpu.VMEM((64, channels), F32),
+            pltpu.VMEM((7, DOCS * STATE, channels), F32),
             pltpu.VMEM((TOKENS, channels), F32),
             pltpu.VMEM((TOKENS * STATE, LANES), F32),
             pltpu.VMEM((TOKENS * STATE, LANES), F32),
@@ -276,7 +295,7 @@
         ],
         compiler_params=pltpu.CompilerParams(vmem_limit_bytes=32 << 20),
         name="mixer_out",
-    )(place, gathered, step, pairs, inner, a_log, skip, zin, out_weight)
+    )(core, *earlier, step, pairs, inner, a_log, skip, zin, out_weight)
 
 
 def expert_kernel(count, *refs):
@@ -369,16 +388,18 @@
         lax.ppermute(left[:half], "seq", x_shift(1)),
         lax.ppermute(right[half:], "seq", x_shift(-1)),
     ]
-    near_parts = [left, right, swapped(left), swapped(right)]
+    left_out = expert_block([left, swapped(left)], w_gate, w_up, w_down)
+    far = list(after(far, left_out))
     far_out = expert_block(far + [swapped(part) for part in far], w_gate, w_up, w_down)
+    left_out = after(left_out, far_out)
     far_sum = paired(*far_out).astype(BF16)
     for_right = lax.ppermute(far_sum[:half], "seq", x_shift(1))
     for_left = lax.ppermute(far_sum[half:], "seq", x_shift(-1))
-    near_out = expert_block(near_parts, w_gate, w_up, w_down)
-    near_out = after(near_out, for_right, for_left)
-    near = paired(*near_out)
-    to_left = near[:count] + jnp.concatenate([jnp.zeros((half, D), F32), for_left.astype(F32)])
-    to_right = near[count:] + jnp.concatenate([for_right.astype(F32), jnp.zeros((half, D), F32)])
+    right_out = expert_block([right, swapped(right)], w_gate, w_up, w_down)
+    right_out = after(right_out, for_right, for_left)
+    nothing = jnp.zeros((half, D), F32)
+    to_left = paired(*left_out) + jnp.concatenate([nothing, for_left.astype(F32)])
+    to_right = paired(*right_out) + jnp.concatenate([for_right.astype(F32), nothing])
     from_right = lax.ppermute(to_left.astype(BF16), "seq", x_shift(-1))
     from_left = lax.ppermute(to_right.astype(BF16), "seq", x_shift(1))
     return paired(*own_out) + from_left.astype(F32) + from_right.astype(F32)
@@ -406,16 +427,15 @@
     channels = xin.shape[2]
     xin = xin.reshape(TOKENS, channels)
     edge = passed_along(xin[TOKENS - (CONV - 1) * DOCS :], "seq", 1)
-    inner, projected = mixer_in(xin, edge, conv_weight, conv_bias[None], xproj_weight)
+    inner, projected = mixer_in(xin, edge, conv_weight, conv_bias[None], xproj_weight.T)
     along_z = [projected] + from_others(projected, z_shift)
     projected = sum(part.astype(F32) for part in along_z).astype(BF16)
     parts = [projected] + from_others(projected, y_shift)
     step, pairs, packed = section_scan(parts, dtproj_weight, dt_bias[None], a_log, inner)
-    gathered = lax.all_gather(packed, "seq")
-    place = lax.axis_index("seq").reshape(1)
+    columns = [lax.ppermute(packed, "seq", x_onward(by)) for by in (1, 2, 3)]
     partial_rows = mixer_out(
-        place,
-        gathered,
+        (lax.axis_index("seq") % 2).reshape(1),
+        columns + [swapped(packed)] + [swapped(column) for column in columns],
         step,
         pairs,
         inner,

time: 267 us -> 254 us (0.951)
  blocking collectives: 35 us -> 19.5 us
  waiting for transfers between devices: 123 us -> 118 us
  starting transfers between devices: 38.1 us -> 42.1 us
  Pallas kernels: 55.3 us -> 58 us
    ppermute x1, waiting for transfers between devices: 0.01 us -> 21.8 us  [experts(): from_right = lax.ppermute(to_left.astype(BF16), 'seq', x_shift(-1))]
    ppermute x1, waiting for transfers between devices: 23.2 us -> 3.5 us  [experts(): from_left = lax.ppermute(to_right.astype(BF16), 'seq', x_shift(1))]
    all_gather x1 -> x0, blocking collectives: 13.8 us -> none  [per_device(): gathered = lax.all_gather(packed, 'seq')]
    ppermute x1, waiting for transfers between devices: 12.8 us -> 0.08 us  [experts(): right = lax.ppermute(own, 'seq', x_shift(-1))]
    ppermute x1, waiting for transfers between devices: 2.4 us -> 13.7 us  [experts(): left = lax.ppermute(own, 'seq', x_shift(1))]
    ppermute x1, waiting for transfers between devices: 11.1 us -> 2.12 us  [experts(): lax.ppermute(left[:half], 'seq', x_shift(1))]
    ppermute x0 -> x3, starting transfers between devices: none -> 8.14 us  [per_device(): columns = [lax.ppermute(packed, 'seq', x_onward(by)) for by in (1, 2, 3)]]
    ppermute x1, waiting for transfers between devices: 0.01 us -> 3.41 us  [experts(): for_right = lax.ppermute(far_sum[:half], 'seq', x_shift(1))]
  transfers between devices with their start and end apart: 25 -> 33, of which waited for: 15 -> 23; matrix products, arithmetic and copies ran while one was open for 2% -> 1% of each run, Pallas kernels for 10% -> 12%
where the time goes in v4:
time: 254 us; the launch traced here: 253 us
  waiting for transfers between devices  118 us (46%)
  Pallas kernels  58 us (23%)
  starting transfers between devices  42.1 us (17%)
  blocking collectives  19.5 us (8%)
  local copies, waits for them, and re-layouts  10.5 us (4%)
  other arithmetic  3.8 us (1%)
    pallas_call x4, Pallas kernels, expert_block(): pl.pallas_call(lambda *refs: expert_kernel(len(parts), *refs), out_shape=...  40.3 us
    all_to_all x1, waiting for transfers between devices, per_device(): lax.all_to_all(partial_rows, 'exp', split_axis=0, concat_axis=0, tiled=True)  30.3 us
    ppermute x1, waiting for transfers between devices, experts(): from_right = lax.ppermute(to_left.astype(BF16), 'seq', x_shift(-1))  21.8 us
    all_to_all x1, blocking collectives, per_device(): lax.all_to_all(jnp.tile(outgoing, (splits, 1)), 'exp', split_axis=0, conc...  19.5 us
    all_to_all x1, waiting for transfers between devices, per_device(): lax.all_to_all(own_rows.astype(BF16), 'exp', split_axis=0, concat_axis=0,...  17.1 us
    ppermute x6, waiting for transfers between devices, from_others(): return [lax.ppermute(value, 'exp', shift(by)) for by in (1, 2, 3)]  15.2 us
    ppermute x1, waiting for transfers between devices, experts(): left = lax.ppermute(own, 'seq', x_shift(1))  13.7 us
    pallas_call x1, Pallas kernels, mixer_out(): pl.pallas_call(mixer_out_kernel, out_shape=jax.ShapeDtypeStruct((TOKENS,...  12 us
  transfers between devices with their start and end apart: 33, of which 23 were waited for; matrix products, arithmetic and copies ran while one was open for 1% of the time, Pallas kernels for 12%

profile of v4, /device:TPU:0, one launch (start us, length us, event | category | flops | bytes accessed | tf_op | source)
XLA Modules:
  0.0 253.1 jit_solution(9412429996169012725)
XLA Ops:
  0.0 0.8 slice.18
  0.8 1.3 collective-permute-start
  2.1 1.0 reshape.82.xin
  3.1 1.0 copy-done.1
  4.1 0.7 copy-done.5
  4.8 0.7 copy-done.6
  5.4 0.7 mixer_in.1
  6.2 4.6 %collective-permute-start.3 = (bf16[288,256]{1,0:T(8,128)(2,1)S(1)}, bf16[288,256]{1,0:T(8,128)(2,1)S(1)}, u32[]{:S(2)}, u32[]{:S(2)}) collective-permute-start(bf16[288,256]{1,0:T(8,128)(2,1)S(1)} %get-tuple-element.26), channel_id=1, source_target_pairs={{0,3},{1,0},{2,1},{3,2},{4,7},{5,4},{6,5},{7,6},{8,11},{9,8},{10,9... | collective-permute-start | bytes 442376 | tf_op jit(solution)/shard_map/ppermute | solution.py:48
  10.9 1.3 collective-permute-start.1
  12.1 5.4 %collective-permute-done.3 = bf16[288,256]{1,0:T(8,128)(2,1)S(1)} collective-permute-done((bf16[288,256]{1,0:T(8,128)(2,1)S(1)}, bf16[288,256]{1,0:T(8,128)(2,1)S(1)}, u32[]{:S(2)}, u32[]{:S(2)}) %collective-permute-start.3) | collective-permute-done | bytes 147488 | tf_op jit(solution)/shard_map/ppermute | solution.py:48
  17.5 1.2 collective-permute-done.2
  18.7 2.9 %collective-permute-done.1 = bf16[288,256]{1,0:T(8,128)(2,1)S(1)} collective-permute-done((bf16[288,256]{1,0:T(8,128)(2,1)S(1)}, bf16[288,256]{1,0:T(8,128)(2,1)S(1)}, u32[]{:S(2)}, u32[]{:S(2)}) %collective-permute-start.1) | collective-permute-done | bytes 147488 | tf_op jit(solution)/shard_map/ppermute | solution.py:48
  21.7 1.6 collective-permute-start.4
  23.4 2.9 %collective-permute-start.5 = (bf16[288,256]{1,0:T(8,128)(2,1)S(1)}, bf16[288,256]{1,0:T(8,128)(2,1)S(1)}, u32[]{:S(2)}, u32[]{:S(2)}) collective-permute-start(bf16[288,256]{1,0:T(8,128)(2,1)S(1)} %add_convert_fusion.4.p0), channel_id=1, source_target_pairs={{0,8},{1,9},{2,10},{3,11},{4,12},{5,13},{6,14},{7,15},{8,0},{9,1},... | collective-permute-start | bytes 442376 | tf_op jit(solution)/shard_map/ppermute | solution.py:48
  26.3 1.3 collective-permute-start.6
  27.6 1.3 collective-permute-done.4.p1
  29.0 4.3 %collective-permute-done.5.p2 = bf16[288,256]{1,0:T(8,128)(2,1)S(1)} collective-permute-done((bf16[288,256]{1,0:T(8,128)(2,1)S(1)}, bf16[288,256]{1,0:T(8,128)(2,1)S(1)}, u32[]{:S(2)}, u32[]{:S(2)}) %collective-permute-start.5) | collective-permute-done | bytes 147488 | tf_op jit(solution)/shard_map/ppermute | solution.py:48
  33.3 0.9 copy-done.2
  34.2 0.8 copy-done.3
  35.0 0.7 copy-done.7
  35.7 5.0 %section_scan.1 = (f32[256,512]{1,0:T(8,128)S(1)}, bf16[256,128]{1,0:T(8,128)(2,1)S(1)}, bf16[72,512]{1,0:T(8,128)(2,1)S(1)}) custom-call(bf16[288,256]{1,0:T(8,128)(2,1)S(1)} %add_convert_fusion.4.p0, bf16[288,256]{1,0:T(8,128)(2,1)S(1)} %collective-permute-done.4.p1, bf16[288,256]{1,0:T(8,128)(2,1)S(1)} %collective-permute-done.5.p2, ...), custom_call_target="tpu_custom_call" | custom-call | tf_op jit(solution)/shard_map/section_scan/pallas_call | solution.py:261
  40.6 3.8 %collective-permute-start.7 = (bf16[72,512]{1,0:T(8,128)(2,1)S(1)}, bf16[72,512]{1,0:T(8,128)(2,1)S(1)}, u32[]{:S(2)}, u32[]{:S(2)}) collective-permute-start(bf16[72,512]{1,0:T(8,128)(2,1)S(1)} %get-tuple-element.28), channel_id=1, source_target_pairs={{0,32},{16,48},{32,64},{48,80},{64,96},{80,112},{1,33},{17,49},{33... | collective-permute-start | bytes 221192 | tf_op jit(solution)/shard_map/ppermute | solution.py:435
  44.4 3.1 %collective-permute-start.8 = (bf16[72,512]{1,0:T(8,128)(2,1)S(1)}, bf16[72,512]{1,0:T(8,128)(2,1)S(1)}, u32[]{:S(2)}, u32[]{:S(2)}) collective-permute-start(bf16[72,512]{1,0:T(8,128)(2,1)S(1)} %get-tuple-element.28), channel_id=1, source_target_pairs={{0,64},{16,80},{32,96},{48,112},{1,65},{17,81},{33,97},{49,113},{2... | collective-permute-start | bytes 221192 | tf_op jit(solution)/shard_map/ppermute | solution.py:435
  47.5 1.3 collective-permute-start.9
  48.9 0.5 collective-permute-start.11
  49.5 1.3 collective-permute-done.9.refs_2_
  50.9 1.2 collective-permute-done.13.refs_6_
  52.0 2.2 copy-done
  54.2 12.0 %mixer_out.1 = bf16[256,4096]{1,0:T(8,128)(2,1)} custom-call(s32[1]{0:T(128)} %bitcast.core, bf16[72,512]{1,0:T(8,128)(2,1)S(1)} %collective-permute-done.7.refs_0_, bf16[72,512]{1,0:T(8,128)(2,1)S(1)} %collective-permute-done.8.refs_1_, bf16[72,512]{1,0:T(8,128)(2,1)S(1)} %collective-permute-done.9.refs_2_, ...), custom_call_target="tpu_custom_call" | custom-call | tf_op jit(solution)/shard_map/mixer_out/pallas_call | solution.py:281
  66.3 4.1 %all-to-all-start = ((bf16[16,16,4096]{2,1,0:T(8,128)(2,1)}), bf16[16,16,4096]{2,1,0:T(8,128)(2,1)S(1)}, u32[]{:S(2)}, u32[]{:S(2)}) async-start(bf16[16,16,4096]{2,1,0:T(8,128)(2,1)} %bitcast.5), calls=%async_computation | async-start | bytes 4194304 | tf_op jit(solution)/shard_map/all_to_all | solution.py:447
  71.3 30.3 %all-to-all-done = bf16[16,16,4096]{2,1,0:T(8,128)(2,1)S(1)} async-done(((bf16[16,16,4096]{2,1,0:T(8,128)(2,1)}), bf16[16,16,4096]{2,1,0:T(8,128)(2,1)S(1)}, u32[]{:S(2)}, u32[]{:S(2)}) %all-to-all-start) | async-done | bytes 2097184 | tf_op jit(solution)/shard_map/all_to_all | solution.py:447
  102.3 0.3 convolution_convert_fusion
  102.7 19.5 %all_to_all.29 = bf16[16,8,4096]{2,1,0:T(8,128)(2,1)S(1)} all-to-all(bf16[16,8,4096]{2,1,0:T(8,128)(2,1)S(1)} %bitcast.29), channel_id=1, replica_groups=mesh['seq'=8,'exp'=16] {'exp'}, dimensions={0} | all-to-all | bytes 2097152 | tf_op jit(solution)/shard_map/all_to_all | solution.py:460
  122.2 3.6 %collective-permute-start.17 = (bf16[128,4096]{1,0:T(8,128)(2,1)S(1)}, bf16[128,4096]{1,0:T(8,128)(2,1)S(1)}, u32[]{:S(2)}, u32[]{:S(2)}) collective-permute-start(bf16[128,4096]{1,0:T(8,128)(2,1)S(1)} %bitcast.22), channel_id=1, source_target_pairs={{0,96},{16,112},{32,0},{48,16},{64,32},{80,48},{96,64},{112,80},{1... | collective-permute-start | bytes 3145736 | tf_op jit(solution)/shard_map/ppermute | solution.py:384
  125.8 10.1 %experts_256.4 = (bf16[128,4096]{1,0:T(8,128)(2,1)S(1)}, bf16[128,4096]{1,0:T(8,128)(2,1)S(1)}) custom-call(bf16[128,4096]{1,0:T(8,128)(2,1)S(1)} %bitcast.23, bf16[128,4096]{1,0:T(8,128)(2,1)S(1)} %collective-permute-done.14.refs_1_, bf16[1,4096,768]{2,1,0:T(8,128)(2,1)} %refs_4_.7, bf16[1,4096,768]{2,1,0:T(8,128)(2,1)} %refs_5_.1, ...), custom_call_target="tpu_custom_call" | custom-call | flops 4831838208 | bytes 23068672 | tf_op jit(solution)/shard_map/experts_256/pallas_call | solution.py:341
  135.9 13.7 %collective-permute-done.16.refs_0_ = bf16[128,4096]{1,0:T(8,128)(2,1)S(1)} collective-permute-done((bf16[128,4096]{1,0:T(8,128)(2,1)S(1)}, bf16[128,4096]{1,0:T(8,128)(2,1)S(1)}, u32[]{:S(2)}, u32[]{:S(2)}) %collective-permute-start.16) | collective-permute-done | bytes 1048608 | tf_op jit(solution)/shard_map/ppermute | solution.py:383
  149.8 2.0 collective-permute-start.19
  151.8 1.6 collective-permute-start.20
  153.4 10.1 %experts_256.6 = (bf16[128,4096]{1,0:T(8,128)(2,1)S(1)}, bf16[128,4096]{1,0:T(8,128)(2,1)S(1)}) custom-call(bf16[128,4096]{1,0:T(8,128)(2,1)S(1)} %collective-permute-done.16.refs_0_, bf16[128,4096]{1,0:T(8,128)(2,1)S(1)} %collective-permute-done.21.refs_1_, bf16[1,4096,768]{2,1,0:T(8,128)(2,1)} %refs_4_.7, bf16[1,4096,768]{2,1,0:T(8,128)(2,1)} %refs_5_.1, ...), custom_call_target="tpu_custom_call" | custom-call | flops 4831838208 | bytes 23068672 | tf_op jit(solution)/shard_map/experts_256/pallas_call | solution.py:341
  163.5 2.1 collective-permute-done.19.refs_0_
  165.6 0.4 collective-permute-done.20.refs_1_
  165.9 0.5 collective-permute-start.23
  166.5 1.4 collective-permute-done.22.refs_2_
  167.9 0.7 collective-permute-done.23.refs_3_
  168.6 10.1 %experts_256.7 = (bf16[128,4096]{1,0:T(8,128)(2,1)S(1)}, bf16[128,4096]{1,0:T(8,128)(2,1)S(1)}) custom-call(bf16[64,4096]{1,0:T(8,128)(2,1)S(1)} %collective-permute-done.19.refs_0_, bf16[64,4096]{1,0:T(8,128)(2,1)S(1)} %collective-permute-done.20.refs_1_, bf16[64,4096]{1,0:T(8,128)(2,1)S(1)} %collective-permute-done.22.refs_2_, ...), custom_call_target="tpu_custom_call" | custom-call | flops 4831838208 | bytes 23068672 | tf_op jit(solution)/shard_map/experts_256/pallas_call | solution.py:341
  178.9 0.4 collective-permute-start.18
  179.4 2.0 collective-permute-done.24
  181.8 2.8 %collective-permute-start.26 = (bf16[64,4096]{1,0:T(8,128)(2,1)S(1)}, bf16[64,4096]{1,0:T(8,128)(2,1)S(1)}, u32[]{:S(2)}, u32[]{:S(2)}) collective-permute-start(bf16[64,4096]{1,0:T(8,128)(2,1)S(1)} %get-tuple-element.48), channel_id=1, source_target_pairs={{0,96},{16,112},{32,0},{48,16},{64,32},{80,48},{96,64},{112,80},{1... | collective-permute-start | bytes 1572872 | tf_op jit(solution)/shard_map/ppermute | solution.py:397
  184.6 10.1 %experts_256.5 = (bf16[128,4096]{1,0:T(8,128)(2,1)S(1)}, bf16[128,4096]{1,0:T(8,128)(2,1)S(1)}) custom-call(bf16[128,4096]{1,0:T(8,128)(2,1)S(1)} %collective-permute-done.17.refs_0_, bf16[128,4096]{1,0:T(8,128)(2,1)S(1)} %collective-permute-done.18.refs_1_, bf16[1,4096,768]{2,1,0:T(8,128)(2,1)} %refs_4_.7, bf16[1,4096,768]{2,1,0:T(8,128)(2,1)} %refs_5_.1, ...), custom_call_target="tpu_custom_call" | custom-call | flops 4831838208 | bytes 23068672 | tf_op jit(solution)/shard_map/experts_256/pallas_call | solution.py:341
  194.6 1.4 collective-permute-done.26
  196.0 3.4 %collective-permute-done.25 = bf16[64,4096]{1,0:T(8,128)(2,1)S(1)} collective-permute-done((bf16[64,4096]{1,0:T(8,128)(2,1)S(1)}, bf16[64,4096]{1,0:T(8,128)(2,1)S(1)}, u32[]{:S(2)}, u32[]{:S(2)}) %collective-permute-start.25) | collective-permute-done | bytes 524320 | tf_op jit(solution)/shard_map/ppermute | solution.py:396
  199.4 0.5 collective-permute-start.15
  200.3 0.4 collective-permute-start.30
  200.7 1.5 collective-permute-done.27
  202.1 0.3 add_convert_fusion.2
  202.5 0.4 collective-permute-start.28
  202.8 0.8 collective-permute-done.15
  203.6 21.8 %collective-permute-done.30 = bf16[128,4096]{1,0:T(8,128)(2,1)S(1)} collective-permute-done((bf16[128,4096]{1,0:T(8,128)(2,1)S(1)}, bf16[128,4096]{1,0:T(8,128)(2,1)S(1)}, u32[]{:S(2)}, u32[]{:S(2)}) %collective-permute-start.30) | collective-permute-done | bytes 1048608 | tf_op jit(solution)/shard_map/ppermute | solution.py:403
  225.4 3.5 %collective-permute-done.28 = bf16[128,4096]{1,0:T(8,128)(2,1)S(1)} collective-permute-done((bf16[128,4096]{1,0:T(8,128)(2,1)S(1)}, bf16[128,4096]{1,0:T(8,128)(2,1)S(1)}, u32[]{:S(2)}, u32[]{:S(2)}) %collective-permute-start.28) | collective-permute-done | bytes 1048608 | tf_op jit(solution)/shard_map/ppermute | solution.py:404
  228.9 1.6 fusion.1
  230.6 3.8 %all-to-all-start.2 = ((bf16[16,8,4096]{2,1,0:T(8,128)(2,1)}), bf16[16,8,4096]{2,1,0:T(8,128)(2,1)S(1)}, u32[]{:S(2)}, u32[]{:S(2)}) async-start(bf16[16,8,4096]{2,1,0:T(8,128)(2,1)} %fusion.1), calls=%async_computation.2 | async-start | bytes 2097152 | tf_op jit(solution)/shard_map/all_to_all | solution.py:464
  234.6 17.1 %all-to-all-done.2 = bf16[16,8,4096]{2,1,0:T(8,128)(2,1)S(1)} async-done(((bf16[16,8,4096]{2,1,0:T(8,128)(2,1)}), bf16[16,8,4096]{2,1,0:T(8,128)(2,1)S(1)}, u32[]{:S(2)}, u32[]{:S(2)}) %all-to-all-start.2) | async-done | bytes 1048608 | tf_op jit(solution)/shard_map/all_to_all | solution.py:464
  251.8 0.6 fusion
  252.4 0.7 reshape.84
  (77 shorter events, 3.6 us)
Async XLA Ops:
  0.0 52.0 %copy-start.4 = (f32[16,512]{1,0:T(8,128)S(1)}, f32[16,512]{1,0:T(8,128)}, u32[]{:S(2)}) copy-start(f32[16,512]{1,0:T(8,128)} %refs_10_.1) | copy-start | bytes 98308
  0.0 50.8 %copy-start.10 = (bf16[64,4,512]{2,1,0:T(4,128)(2,1)S(1)}, bf16[64,4,512]{2,1,0:T(4,128)(2,1)}, u32[]{:S(2)}) copy-start(bf16[64,4,512]{2,1,0:T(4,128)(2,1)} %param.18) | copy-start | bytes 786436
  0.0 52.0 %copy-start.8 = (f32[512]{0:T(512)S(1)}, f32[512]{0:T(512)}, u32[]{:S(2)}) copy-start(f32[512]{0:T(512)} %param.25) | copy-start | bytes 6148
  0.8 2.3 collective-permute-start
  3.1 1.0 copy-start.1
  4.1 0.7 copy-start.5
  4.8 0.7 copy-start.6
  6.2 11.3 %collective-permute-start.3 = (bf16[288,256]{1,0:T(8,128)(2,1)S(1)}, bf16[288,256]{1,0:T(8,128)(2,1)S(1)}, u32[]{:S(2)}, u32[]{:S(2)}) collective-permute-start(bf16[288,256]{1,0:T(8,128)(2,1)S(1)} %get-tuple-element.26), channel_id=1, source_target_pairs={{0,3},{1,0},{2,1},{3,2},{4,7},{5,4},{6,5},{7,6},{8,11},{9,8},{10,9... | collective-permute-start | bytes 442376 | tf_op jit(solution)/shard_map/ppermute | solution.py:48
  10.8 7.9 %collective-permute-start.2 = (bf16[288,256]{1,0:T(8,128)(2,1)S(1)}, bf16[288,256]{1,0:T(8,128)(2,1)S(1)}, u32[]{:S(2)}, u32[]{:S(2)}) collective-permute-start(bf16[288,256]{1,0:T(8,128)(2,1)S(1)} %get-tuple-element.26), channel_id=1, source_target_pairs={{0,2},{1,3},{2,0},{3,1},{4,6},{5,7},{6,4},{7,5},{8,10},{9,11},{10,... | collective-permute-start | bytes 442376 | tf_op jit(solution)/shard_map/ppermute | solution.py:48
  10.9 10.8 %collective-permute-start.1 = (bf16[288,256]{1,0:T(8,128)(2,1)S(1)}, bf16[288,256]{1,0:T(8,128)(2,1)S(1)}, u32[]{:S(2)}, u32[]{:S(2)}) collective-permute-start(bf16[288,256]{1,0:T(8,128)(2,1)S(1)} %get-tuple-element.26), channel_id=1, source_target_pairs={{0,1},{1,2},{2,3},{3,0},{4,5},{5,6},{6,7},{7,4},{8,9},{9,10},{10,1... | collective-permute-start | bytes 442376 | tf_op jit(solution)/shard_map/ppermute | solution.py:48
  21.7 7.2 %collective-permute-start.4 = (bf16[288,256]{1,0:T(8,128)(2,1)S(1)}, bf16[288,256]{1,0:T(8,128)(2,1)S(1)}, u32[]{:S(2)}, u32[]{:S(2)}) collective-permute-start(bf16[288,256]{1,0:T(8,128)(2,1)S(1)} %add_convert_fusion.4.p0), channel_id=1, source_target_pairs={{0,4},{1,5},{2,6},{3,7},{4,8},{5,9},{6,10},{7,11},{8,12},{9,13},{1... | collective-permute-start | bytes 442376 | tf_op jit(solution)/shard_map/ppermute | solution.py:48
  23.4 9.9 %collective-permute-start.5 = (bf16[288,256]{1,0:T(8,128)(2,1)S(1)}, bf16[288,256]{1,0:T(8,128)(2,1)S(1)}, u32[]{:S(2)}, u32[]{:S(2)}) collective-permute-start(bf16[288,256]{1,0:T(8,128)(2,1)S(1)} %add_convert_fusion.4.p0), channel_id=1, source_target_pairs={{0,8},{1,9},{2,10},{3,11},{4,12},{5,13},{6,14},{7,15},{8,0},{9,1},... | collective-permute-start | bytes 442376 | tf_op jit(solution)/shard_map/ppermute | solution.py:48
  26.3 7.0 %collective-permute-start.6 = (bf16[288,256]{1,0:T(8,128)(2,1)S(1)}, bf16[288,256]{1,0:T(8,128)(2,1)S(1)}, u32[]{:S(2)}, u32[]{:S(2)}) collective-permute-start(bf16[288,256]{1,0:T(8,128)(2,1)S(1)} %add_convert_fusion.4.p0), channel_id=1, source_target_pairs={{0,12},{1,13},{2,14},{3,15},{4,0},{5,1},{6,2},{7,3},{8,4},{9,5},{1... | collective-permute-start | bytes 442376 | tf_op jit(solution)/shard_map/ppermute | solution.py:48
  33.3 1.0 copy-start.2
  34.2 0.8 copy-start.3
  35.0 0.7 copy-start.7
  40.6 8.3 %collective-permute-start.7 = (bf16[72,512]{1,0:T(8,128)(2,1)S(1)}, bf16[72,512]{1,0:T(8,128)(2,1)S(1)}, u32[]{:S(2)}, u32[]{:S(2)}) collective-permute-start(bf16[72,512]{1,0:T(8,128)(2,1)S(1)} %get-tuple-element.28), channel_id=1, source_target_pairs={{0,32},{16,48},{32,64},{48,80},{64,96},{80,112},{1,33},{17,49},{33... | collective-permute-start | bytes 221192 | tf_op jit(solution)/shard_map/ppermute | solution.py:435
  44.4 5.0 %collective-permute-start.8 = (bf16[72,512]{1,0:T(8,128)(2,1)S(1)}, bf16[72,512]{1,0:T(8,128)(2,1)S(1)}, u32[]{:S(2)}, u32[]{:S(2)}) collective-permute-start(bf16[72,512]{1,0:T(8,128)(2,1)S(1)} %get-tuple-element.28), channel_id=1, source_target_pairs={{0,64},{16,80},{32,96},{48,112},{1,65},{17,81},{33,97},{49,113},{2... | collective-permute-start | bytes 221192 | tf_op jit(solution)/shard_map/ppermute | solution.py:435
  47.5 3.3 %collective-permute-start.9 = (bf16[72,512]{1,0:T(8,128)(2,1)S(1)}, bf16[72,512]{1,0:T(8,128)(2,1)S(1)}, u32[]{:S(2)}, u32[]{:S(2)}) collective-permute-start(bf16[72,512]{1,0:T(8,128)(2,1)S(1)} %get-tuple-element.28), channel_id=1, source_target_pairs={{0,96},{16,112},{1,97},{17,113},{2,98},{18,114},{3,99},{19,115},{4... | collective-permute-start | bytes 221192 | tf_op jit(solution)/shard_map/ppermute | solution.py:435
  48.8 2.0 collective-permute-start.10
  48.9 2.0 collective-permute-start.11
  49.5 1.4 collective-permute-start.12
  50.8 1.3 collective-permute-start.13
  52.0 2.2 copy-start
  66.3 4.1 %copy-start.9 = (bf16[4,4,4096]{2,1,0:T(4,128)(2,1)S(1)}, bf16[4,4,4096]{2,1,0:T(4,128)(2,1)}, u32[]{:S(2)}) copy-start(bf16[4,4,4096]{2,1,0:T(4,128)(2,1)} %param.27) | copy-start | bytes 393220
  66.3 4.2 %copy-start.12 = (s32[4,4,2]{1,2,0:T(2,128)S(1)}, s32[4,4,2]{1,2,0:T(2,128)}, u32[]{:S(2)}) copy-start(s32[4,4,2]{1,2,0:T(2,128)} %param.29) | copy-start | bytes 388
  66.3 35.3 %all-to-all-start = ((bf16[16,16,4096]{2,1,0:T(8,128)(2,1)}), bf16[16,16,4096]{2,1,0:T(8,128)(2,1)S(1)}, u32[]{:S(2)}, u32[]{:S(2)}) async-start(bf16[16,16,4096]{2,1,0:T(8,128)(2,1)} %bitcast.5), calls=%async_computation | async-start | bytes 4194304 | tf_op jit(solution)/shard_map/all_to_all | solution.py:447
  70.5 31.7 %copy-start.11 = (f32[4096]{0:T(1024)S(1)}, f32[4096]{0:T(1024)}, u32[]{:S(2)}) copy-start(f32[4096]{0:T(1024)} %param.28) | copy-start | bytes 49156
  122.2 3.6 %collective-permute-start.14 = (bf16[128,4096]{1,0:T(8,128)(2,1)S(1)}, bf16[128,4096]{1,0:T(8,128)(2,1)S(1)}, u32[]{:S(2)}, u32[]{:S(2)}) collective-permute-start(bf16[128,4096]{1,0:T(8,128)(2,1)S(1)} %bitcast.20), channel_id=1, source_target_pairs={{0,16},{16,0},{32,48},{48,32},{64,80},{80,64},{96,112},{112,96},{1... | collective-permute-start | bytes 3145736 | tf_op jit(solution)/shard_map/ppermute | solution.py:52
  122.2 27.4 %collective-permute-start.16 = (bf16[128,4096]{1,0:T(8,128)(2,1)S(1)}, bf16[128,4096]{1,0:T(8,128)(2,1)S(1)}, u32[]{:S(2)}, u32[]{:S(2)}) collective-permute-start(bf16[128,4096]{1,0:T(8,128)(2,1)S(1)} %bitcast.21), channel_id=1, source_target_pairs={{0,32},{16,48},{32,64},{48,80},{64,96},{80,112},{96,0},{112,16},{1... | collective-permute-start | bytes 3145736 | tf_op jit(solution)/shard_map/ppermute | solution.py:383
  122.2 27.5 %collective-permute-start.17 = (bf16[128,4096]{1,0:T(8,128)(2,1)S(1)}, bf16[128,4096]{1,0:T(8,128)(2,1)S(1)}, u32[]{:S(2)}, u32[]{:S(2)}) collective-permute-start(bf16[128,4096]{1,0:T(8,128)(2,1)S(1)} %bitcast.22), channel_id=1, source_target_pairs={{0,96},{16,112},{32,0},{48,16},{64,32},{80,48},{96,64},{112,80},{1... | collective-permute-start | bytes 3145736 | tf_op jit(solution)/shard_map/ppermute | solution.py:384
  149.7 3.6 %collective-permute-start.21 = (bf16[128,4096]{1,0:T(8,128)(2,1)S(1)}, bf16[128,4096]{1,0:T(8,128)(2,1)S(1)}, u32[]{:S(2)}, u32[]{:S(2)}) collective-permute-start(bf16[128,4096]{1,0:T(8,128)(2,1)S(1)} %collective-permute-done.16.refs_0_), channel_id=1, source_target_pairs={{0,16},{16,0},{32,48},{48,32},{64,80},{80,64},{96,112},{112,96},{1... | collective-permute-start | bytes 3145736 | tf_op jit(solution)/shard_map/ppermute | solution.py:52
  149.8 15.8 %collective-permute-start.19 = (bf16[64,4096]{1,0:T(8,128)(2,1)S(1)}, bf16[64,4096]{1,0:T(8,128)(2,1)S(1)}, u32[]{:S(2)}, u32[]{:S(2)}) collective-permute-start(bf16[64,4096]{1,0:T(8,128)(2,1)S(1)} %slice.20), channel_id=1, source_target_pairs={{0,32},{16,48},{32,64},{48,80},{64,96},{80,112},{96,0},{112,16},{1... | collective-permute-start | bytes 1572872 | tf_op jit(solution)/shard_map/ppermute | solution.py:388
  151.8 14.1 %collective-permute-start.20 = (bf16[64,4096]{1,0:T(8,128)(2,1)S(1)}, bf16[64,4096]{1,0:T(8,128)(2,1)S(1)}, u32[]{:S(2)}, u32[]{:S(2)}) collective-permute-start(bf16[64,4096]{1,0:T(8,128)(2,1)S(1)} %slice.21), channel_id=1, source_target_pairs={{0,96},{16,112},{32,0},{48,16},{64,32},{80,48},{96,64},{112,80},{1... | collective-permute-start | bytes 1572872 | tf_op jit(solution)/shard_map/ppermute | solution.py:389
  165.9 1.9 collective-permute-start.22
  165.9 2.7 %collective-permute-start.23 = (bf16[64,4096]{1,0:T(8,128)(2,1)S(1)}, bf16[64,4096]{1,0:T(8,128)(2,1)S(1)}, u32[]{:S(2)}, u32[]{:S(2)}) collective-permute-start(bf16[64,4096]{1,0:T(8,128)(2,1)S(1)} %collective-permute-done.20.refs_1_), channel_id=1, source_target_pairs={{0,16},{16,0},{32,48},{48,32},{64,80},{80,64},{96,112},{112,96},{1... | collective-permute-start | bytes 1572872 | tf_op jit(solution)/shard_map/ppermute | solution.py:52
  178.7 2.7 %collective-permute-start.24 = (bf16[128,4096]{1,0:T(8,128)(2,1)S(1)}, bf16[128,4096]{1,0:T(8,128)(2,1)S(1)}, u32[]{:S(2)}, u32[]{:S(2)}) collective-permute-start(bf16[128,4096]{1,0:T(8,128)(2,1)S(1)} %get-tuple-element.42), channel_id=1, source_target_pairs={{0,16},{16,0},{32,48},{48,32},{64,80},{80,64},{96,112},{112,96},{1... | collective-permute-start | bytes 3145736 | tf_op jit(solution)/shard_map/ppermute | solution.py:52
  178.9 5.7 %collective-permute-start.18 = (bf16[128,4096]{1,0:T(8,128)(2,1)S(1)}, bf16[128,4096]{1,0:T(8,128)(2,1)S(1)}, u32[]{:S(2)}, u32[]{:S(2)}) collective-permute-start(bf16[128,4096]{1,0:T(8,128)(2,1)S(1)} %collective-permute-done.17.refs_0_), channel_id=1, source_target_pairs={{0,16},{16,0},{32,48},{48,32},{64,80},{80,64},{96,112},{112,96},{1... | collective-permute-start | bytes 3145736 | tf_op jit(solution)/shard_map/ppermute | solution.py:52
  179.3 20.7 %collective-permute-start.29 = (bf16[128,4096]{1,0:T(8,128)(2,1)S(1)}, bf16[128,4096]{1,0:T(8,128)(2,1)S(1)}, u32[]{:S(2)}, u32[]{:S(2)}) collective-permute-start(bf16[128,4096]{1,0:T(8,128)(2,1)S(1)} %get-tuple-element.46), channel_id=1, source_target_pairs={{0,16},{16,0},{32,48},{48,32},{64,80},{80,64},{96,112},{112,96},{1... | collective-permute-start | bytes 3145736 | tf_op jit(solution)/shard_map/ppermute | solution.py:52
  181.8 14.3 %collective-permute-start.26 = (bf16[64,4096]{1,0:T(8,128)(2,1)S(1)}, bf16[64,4096]{1,0:T(8,128)(2,1)S(1)}, u32[]{:S(2)}, u32[]{:S(2)}) collective-permute-start(bf16[64,4096]{1,0:T(8,128)(2,1)S(1)} %get-tuple-element.48), channel_id=1, source_target_pairs={{0,96},{16,112},{32,0},{48,16},{64,32},{80,48},{96,64},{112,80},{1... | collective-permute-start | bytes 1572872 | tf_op jit(solution)/shard_map/ppermute | solution.py:397
  184.5 14.9 %collective-permute-start.25 = (bf16[64,4096]{1,0:T(8,128)(2,1)S(1)}, bf16[64,4096]{1,0:T(8,128)(2,1)S(1)}, u32[]{:S(2)}, u32[]{:S(2)}) collective-permute-start(bf16[64,4096]{1,0:T(8,128)(2,1)S(1)} %get-tuple-element.47), channel_id=1, source_target_pairs={{0,32},{16,48},{32,64},{48,80},{64,96},{80,112},{96,0},{112,16},{1... | collective-permute-start | bytes 1572872 | tf_op jit(solution)/shard_map/ppermute | solution.py:396
  199.4 2.7 %collective-permute-start.27 = (bf16[128,4096]{1,0:T(8,128)(2,1)S(1)}, bf16[128,4096]{1,0:T(8,128)(2,1)S(1)}, u32[]{:S(2)}, u32[]{:S(2)}) collective-permute-start(bf16[128,4096]{1,0:T(8,128)(2,1)S(1)} %get-tuple-element.44), channel_id=1, source_target_pairs={{0,16},{16,0},{32,48},{48,32},{64,80},{80,64},{96,112},{112,96},{1... | collective-permute-start | bytes 3145736 | tf_op jit(solution)/shard_map/ppermute | solution.py:52
  199.4 4.2 %collective-permute-start.15 = (bf16[128,4096]{1,0:T(8,128)(2,1)S(1)}, bf16[128,4096]{1,0:T(8,128)(2,1)S(1)}, u32[]{:S(2)}, u32[]{:S(2)}) collective-permute-start(bf16[128,4096]{1,0:T(8,128)(2,1)S(1)} %get-tuple-element.32), channel_id=1, source_target_pairs={{0,16},{16,0},{32,48},{48,32},{64,80},{80,64},{96,112},{112,96},{1... | collective-permute-start | bytes 3145736 | tf_op jit(solution)/shard_map/ppermute | solution.py:52
  200.3 25.1 %collective-permute-start.30 = (bf16[128,4096]{1,0:T(8,128)(2,1)S(1)}, bf16[128,4096]{1,0:T(8,128)(2,1)S(1)}, u32[]{:S(2)}, u32[]{:S(2)}) collective-permute-start(bf16[128,4096]{1,0:T(8,128)(2,1)S(1)} %add_convert_fusion.1), channel_id=1, source_target_pairs={{0,96},{16,112},{32,0},{48,16},{64,32},{80,48},{96,64},{112,80},{1... | collective-permute-start | bytes 3145736 | tf_op jit(solution)/shard_map/ppermute | solution.py:403
  202.5 26.5 %collective-permute-start.28 = (bf16[128,4096]{1,0:T(8,128)(2,1)S(1)}, bf16[128,4096]{1,0:T(8,128)(2,1)S(1)}, u32[]{:S(2)}, u32[]{:S(2)}) collective-permute-start(bf16[128,4096]{1,0:T(8,128)(2,1)S(1)} %add_convert_fusion.2), channel_id=1, source_target_pairs={{0,32},{16,48},{32,64},{48,80},{64,96},{80,112},{96,0},{112,16},{1... | collective-permute-start | bytes 3145736 | tf_op jit(solution)/shard_map/ppermute | solution.py:404
  230.6 3.8 %copy-start.13 = (bf16[4,4,2]{1,2,0:T(2,128)(2,1)S(1)}, bf16[4,4,2]{1,2,0:T(2,128)(2,1)}, u32[]{:S(2)}) copy-start(bf16[4,4,2]{1,2,0:T(2,128)(2,1)} %param.30) | copy-start | bytes 196
  230.6 21.1 %all-to-all-start.2 = ((bf16[16,8,4096]{2,1,0:T(8,128)(2,1)}), bf16[16,8,4096]{2,1,0:T(8,128)(2,1)S(1)}, u32[]{:S(2)}, u32[]{:S(2)}) async-start(bf16[16,8,4096]{2,1,0:T(8,128)(2,1)} %fusion.1), calls=%async_computation.2 | async-start | bytes 2097152 | tf_op jit(solution)/shard_map/all_to_all | solution.py:464

commit v5 on v4

--- a/solution.py
+++ b/solution.py
@@ -62,9 +62,24 @@
     return jnp.where(column == source, 1.0, 0.0).astype(BF16)
 
 
-def mixer_in_kernel(xin, edge, conv_weight, conv_bias, xproj, inner, projected, window):
+def fetched(sources, targets, arrived):
+    copies = [
+        pltpu.make_async_copy(source, target, arrived.at[index])
+        for index, (source, target) in enumerate(zip(sources, targets))
+    ]
+    for copy in copies:
+        copy.start()
+    return copies
+
+
+def mixer_in_kernel(xin, edge, *refs):
+    sources, (inner, projected, window, *targets, arrived) = refs[:3], refs[3:]
+    copies = fetched(sources, targets, arrived)
+    conv_weight, conv_bias, xproj = targets
     window[16 - edge.shape[0] : 16, :] = edge[...].astype(F32)
     window[16 : 16 + TOKENS, :] = xin[...].astype(F32)
+    copies[0].wait()
+    copies[1].wait()
     blocks = []
     for low in range(0, TOKENS, 64):
         running = jnp.broadcast_to(conv_bias[...], (64, xin.shape[1]))
@@ -75,52 +90,34 @@
     by_position = jnp.concatenate(blocks, axis=0)
     ordered = jnp.dot(document_major(False), by_position, preferred_element_type=F32).astype(BF16)
     inner[...] = ordered
+    copies[2].wait()
     projected[...] = lax.dot_general(
         xproj[...], ordered, (((1,), (1,)), ((), ())), preferred_element_type=F32
     ).astype(BF16)
 
 
-def spread(pairs, target, first):
-    lane = lax.broadcasted_iota(jnp.int32, (STATE, LANES), 1)
-    entry = lax.broadcasted_iota(jnp.int32, (STATE, LANES), 0)
-    mask = jnp.where((lane == first + entry) | (lane == first + STATE + entry), 1.0, 0.0)
-    ones = jnp.ones((LANES, LANES), BF16)
-
-    def one(group, carry):
-        rows = pairs[pl.ds(pl.multiple_of(group * 16, 16), 16), :].astype(F32)
-        wide = jnp.broadcast_to(rows[:, None, :], (16, STATE, LANES)) * mask[None]
-        wide = wide.reshape(16 * STATE, LANES).astype(BF16)
-        place = pl.ds(pl.multiple_of(group * 16 * STATE, 16 * STATE), 16 * STATE)
-        target[place, :] = jnp.dot(wide, ones, preferred_element_type=F32)
-        return carry
-
-    lax.fori_loop(0, TOKENS // 16, one, 0)
-
-
-def four_times(block):
-    return jnp.concatenate([block] * 4, axis=1)
-
-
-def section_kernel(
-    p0, p1, p2, p3, dtproj, dt_bias, a_log, inner, step, pairs, packed, taken, entering
-):
+def columns_from(states, doc, group):
+    block = states[:, pl.ds(pl.multiple_of((doc >> 1) * LANES, LANES), LANES)]
+    offset = (doc & 1) * SECTION + group * 8
+    return pltpu.roll(block, (LANES - offset) & (LANES - 1), 1)
+
+
+def in_all_lanes(turned, index):
+    column = jnp.broadcast_to(turned[:, index : index + 1], (turned.shape[0], LANES))
+    return jnp.concatenate([column] * 4, axis=1)
+
+
+def section_kernel(p0, p1, p2, p3, inner, *refs):
+    sources, (step, states, packed, taken, *targets, arrived) = refs[:3], refs[3:]
+    copies = fetched(sources, targets, arrived)
+    dtproj, dt_bias, a_log = targets
     total = (p0[...].astype(F32) + p1[...].astype(F32)) + (
         p2[...].astype(F32) + p3[...].astype(F32)
     )
     low_rank = total[:RANK].astype(BF16)
-    states = total[RANK : RANK + 2 * STATE].T
-    high = states.astype(BF16)
-    low = (states - high.astype(F32)).astype(BF16)
-    pairs[...] = jnp.concatenate(
-        [
-            high[:, :STATE],
-            low[:, :STATE],
-            high[:, STATE:],
-            low[:, STATE:],
-            jnp.zeros((TOKENS, LANES - 4 * STATE), BF16),
-        ],
-        axis=1,
-    )
+    states[...] = total[RANK : RANK + 2 * STATE]
+    for copy in copies:
+        copy.wait()
     step[...] = jax.nn.softplus(
         lax.dot_general(
             low_rank, dtproj[...], (((0,), (0,)), ((), ())), preferred_element_type=F32
@@ -128,7 +125,6 @@
         + dt_bias[...]
     )
     taken[...] = step[...] * inner[...].astype(F32)
-    spread(pairs, entering, 0)
     rate = -jnp.exp(a_log[...])
 
     def document(doc, carry):
@@ -136,13 +132,13 @@
             first = pl.multiple_of(doc * SECTION + group * 8, 8)
             steps = step[pl.ds(first, 8), :]
             values = taken[pl.ds(first, 8), :]
+            entering = columns_from(states, doc, group)[:STATE]
             for i in range(8):
-                into = entering[pl.ds(pl.multiple_of((first + i) * STATE, STATE), STATE), :]
                 factor = jnp.exp(steps[i : i + 1] * rate)
-                state = factor * state + values[i : i + 1] * four_times(into)
+                state = factor * state + values[i : i + 1] * in_all_lanes(entering, i)
             return state
 
-        state = lax.fori_loop(0, SECTION // 8, eight, jnp.zeros(rate.shape, F32))
+        state = lax.fori_loop(0, SECTION // 8, eight, jnp.zeros(rate.shape, F32), unroll=8)
         packed[pl.ds(pl.multiple_of(doc * STATE, STATE), STATE), :] = state.astype(BF16)
         return carry
 
@@ -166,7 +162,7 @@
     earlier, refs = refs[:7], refs[7:]
     (
         step,
-        pairs,
+        states,
         inner,
         a_log,
         skip,
@@ -176,8 +172,6 @@
         totals,
         finals,
         taken,
-        entering,
-        leaving,
         scanned,
         weight,
         arrived,
@@ -195,8 +189,6 @@
         totals[8 * index : 8 * index + DOCS, :] = both[:DOCS] + both[DOCS:]
         finals[index] = packed[: DOCS * STATE]
     taken[...] = step[...] * inner[...].astype(F32)
-    spread(pairs, entering, 0)
-    spread(pairs, leaving, 2 * STATE)
     rate = -jnp.exp(a_log[...])
 
     def document(doc, carry):
@@ -210,17 +202,17 @@
             first = pl.multiple_of(doc * SECTION + group * 8, 8)
             steps = step[pl.ds(first, 8), :]
             values = taken[pl.ds(first, 8), :]
+            turned = columns_from(states, doc, group)
             sums = []
             for i in range(8):
-                where = pl.ds(pl.multiple_of((first + i) * STATE, STATE), STATE)
                 factor = jnp.exp(steps[i : i + 1] * rate)
-                state = factor * state + values[i : i + 1] * four_times(entering[where, :])
-                seen = state * four_times(leaving[where, :])
+                state = factor * state + values[i : i + 1] * in_all_lanes(turned[:STATE], i)
+                seen = state * in_all_lanes(turned[STATE:], i)
                 sums.append(jnp.sum(seen, axis=0, keepdims=True))
             scanned[pl.ds(first, 8), :] = jnp.concatenate(sums, axis=0)
             return state
 
-        lax.fori_loop(0, SECTION // 8, eight, state)
+        lax.fori_loop(0, SECTION // 8, eight, state, unroll=2)
         return carry
 
     lax.fori_loop(0, DOCS, document, 0)
@@ -236,6 +228,10 @@
         ).astype(BF16)
 
 
+def in_hbm(*values):
+    return [pltpu.with_memory_space_constraint(value, pltpu.HBM) for value in values]
+
+
 def whole(space=None):
     return pl.BlockSpec(memory_space=pltpu.VMEM if space is None else space)
 
@@ -248,12 +244,18 @@
             jax.ShapeDtypeStruct((TOKENS, channels), BF16),
             jax.ShapeDtypeStruct((xproj.shape[0], TOKENS), BF16),
         ),
-        in_specs=[whole()] * 5,
+        in_specs=[whole()] * 2 + [whole(pltpu.HBM)] * 3,
         out_specs=(whole(), whole()),
-        scratch_shapes=[pltpu.VMEM((16 + TOKENS, channels), F32)],
+        scratch_shapes=[
+            pltpu.VMEM((16 + TOKENS, channels), F32),
+            pltpu.VMEM(conv_weight.shape, F32),
+            pltpu.VMEM(conv_bias.shape, F32),
+            pltpu.VMEM(xproj.shape, BF16),
+            pltpu.SemaphoreType.DMA((3,)),
+        ],
         compiler_params=pltpu.CompilerParams(vmem_limit_bytes=16 << 20),
         name="mixer_in",
-    )(xin, edge, conv_weight, conv_bias, xproj)
+    )(xin, edge, *in_hbm(conv_weight, conv_bias, xproj))
 
 
 def section_scan(parts, dtproj, dt_bias, a_log, inner):
@@ -262,97 +264,82 @@
         section_kernel,
         out_shape=(
             jax.ShapeDtypeStruct((TOKENS, channels), F32),
-            jax.ShapeDtypeStruct((TOKENS, LANES), BF16),
+            jax.ShapeDtypeStruct((2 * STATE, TOKENS), F32),
             jax.ShapeDtypeStruct((DOCS * (STATE + 2), channels), BF16),
         ),
-        in_specs=[whole()] * 8,
+        in_specs=[whole()] * 5 + [whole(pltpu.HBM)] * 3,
         out_specs=(whole(),) * 3,
         scratch_shapes=[
             pltpu.VMEM((TOKENS, channels), F32),
-            pltpu.VMEM((TOKENS * STATE, LANES), F32),
+            pltpu.VMEM(dtproj.shape, BF16),
+            pltpu.VMEM(dt_bias.shape, F32),
+            pltpu.VMEM(a_log.shape, F32),
+            pltpu.SemaphoreType.DMA((3,)),
         ],
         compiler_params=pltpu.CompilerParams(vmem_limit_bytes=16 << 20),
         name="section_scan",
-    )(*parts, dtproj, dt_bias, a_log, inner)
-
-
-def mixer_out(core, earlier, step, pairs, inner, a_log, skip, zin, out_weight):
+    )(*parts, inner, *in_hbm(dtproj, dt_bias, a_log))
+
+
+def mixer_out(core, earlier, step, states, inner, a_log, skip, zin, out_weight):
     channels = inner.shape[1]
     return pl.pallas_call(
         mixer_out_kernel,
         out_shape=jax.ShapeDtypeStruct((TOKENS, D), BF16),
-        in_specs=[whole(pltpu.SMEM)] + [whole()] * 13 + [whole(pl.ANY)],
+        in_specs=[whole(pltpu.SMEM)] + [whole()] * 13 + [whole(pltpu.HBM)],
         out_specs=whole(),
         scratch_shapes=[
             pltpu.VMEM((64, channels), F32),
             pltpu.VMEM((7, DOCS * STATE, channels), F32),
             pltpu.VMEM((TOKENS, channels), F32),
-            pltpu.VMEM((TOKENS * STATE, LANES), F32),
-            pltpu.VMEM((TOKENS * STATE, LANES), F32),
             pltpu.VMEM((TOKENS, channels), F32),
             pltpu.VMEM(out_weight.shape, BF16),
             pltpu.SemaphoreType.DMA,
         ],
         compiler_params=pltpu.CompilerParams(vmem_limit_bytes=32 << 20),
         name="mixer_out",
-    )(core, *earlier, step, pairs, inner, a_log, skip, zin, out_weight)
+    )(core, *earlier, step, states, inner, a_log, skip, zin, *in_hbm(out_weight))
 
 
 def expert_kernel(count, *refs):
     inputs, (w_gate, w_up, w_down, mine, other, rows, total) = refs[:count], refs[count:]
-    block = pl.program_id(0)
-    last = pl.num_programs(0) - 1
     size = rows.shape[0]
-
-    @pl.when(block == 0)
-    def _():
-        low = 0
-        for part in inputs:
-            rows[low : low + part.shape[0], :] = part[...]
-            low += part.shape[0]
-
-    def tile(index, carry):
-        place = pl.ds(pl.multiple_of(index * 256, 256), 256)
-        these = rows[place, :]
-        gate_act = jnp.dot(these, w_gate[...], preferred_element_type=F32)
-        up_act = jnp.dot(these, w_up[...], preferred_element_type=F32)
+    low = 0
+    for part in inputs:
+        rows[low : low + part.shape[0], :] = part[...]
+        low += part.shape[0]
+
+    def units(block, carry):
+        place = pl.ds(pl.multiple_of(block * 256, 256), 256)
+        gate_act = jnp.dot(rows[...], w_gate[0, :, place], preferred_element_type=F32)
+        up_act = jnp.dot(rows[...], w_up[0, :, place], preferred_element_type=F32)
         hidden = (jax.nn.silu(gate_act) * up_act).astype(BF16)
         for low in range(0, D, 1024):
-            term = jnp.dot(hidden, w_down[:, low : low + 1024], preferred_element_type=F32)
-            before = jnp.where(block == 0, 0.0, total[place, low : low + 1024])
-            total[place, low : low + 1024] = before + term
+            term = jnp.dot(
+                hidden, w_down[0, place, low : low + 1024], preferred_element_type=F32
+            )
+            before = jnp.where(block == 0, 0.0, total[:, low : low + 1024])
+            total[:, low : low + 1024] = before + term
         return carry
 
-    lax.fori_loop(0, size // 256, tile, 0)
-
-    @pl.when(block == last)
-    def _():
-        mine[...] = total[: size // 2, :].astype(BF16)
-        other[...] = total[size // 2 :, :].astype(BF16)
+    lax.fori_loop(0, w_down.shape[1] // 256, units, 0)
+    mine[...] = total[: size // 2, :].astype(BF16)
+    other[...] = total[size // 2 :, :].astype(BF16)
 
 
 def expert_block(parts, w_gate, w_up, w_down):
     size = sum(part.shape[0] for part in parts)
-    units, width = w_down.shape[1], 256
-
-    def once(shape):
-        return pl.BlockSpec(shape, lambda i: (0, 0), pipeline_mode=pl.Buffered(1))
-
+    units = w_down.shape[1]
     return pl.pallas_call(
         lambda *refs: expert_kernel(len(parts), *refs),
         out_shape=(jax.ShapeDtypeStruct((size // 2, D), BF16),) * 2,
-        grid=(units // width,),
-        in_specs=[once(part.shape) for part in parts]
-        + [pl.BlockSpec((pl.Squeezed(), D, width), lambda i: (0, 0, i))] * 2
-        + [pl.BlockSpec((pl.Squeezed(), width, D), lambda i: (0, i, 0))],
-        out_specs=(once((size // 2, D)),) * 2,
+        in_specs=[whole()] * (len(parts) + 3),
+        out_specs=(whole(),) * 2,
         scratch_shapes=[pltpu.VMEM((size, D), BF16), pltpu.VMEM((size, D), F32)],
-        compiler_params=pltpu.CompilerParams(
-            dimension_semantics=("arbitrary",), vmem_limit_bytes=48 << 20
-        ),
+        compiler_params=pltpu.CompilerParams(vmem_limit_bytes=12 << 20),
         cost_estimate=pl.CostEstimate(
             flops=6 * size * D * units,
-            bytes_accessed=6 * D * units + 4 * size * D,
+            bytes_accessed=4 * size * D,
             transcendentals=size * units,
         ),
         name=f"experts_{size}",
@@ -380,6 +367,9 @@
     def paired(mine, other):
         return mine.astype(F32) + swapped(other).astype(F32)
 
+    w_gate, w_up, w_down = [
+        pltpu.with_memory_space_constraint(w, pltpu.VMEM) for w in (w_gate, w_up, w_down)
+    ]
     left = lax.ppermute(own, "seq", x_shift(1))
     right = lax.ppermute(own, "seq", x_shift(-1))
     own_out = expert_block([own, swapped(own)], w_gate, w_up, w_down)
@@ -431,13 +421,13 @@
     along_z = [projected] + from_others(projected, z_shift)
     projected = sum(part.astype(F32) for part in along_z).astype(BF16)
     parts = [projected] + from_others(projected, y_shift)
-    step, pairs, packed = section_scan(parts, dtproj_weight, dt_bias[None], a_log, inner)
+    step, states, packed = section_scan(parts, dtproj_weight, dt_bias[None], a_log, inner)
     columns = [lax.ppermute(packed, "seq", x_onward(by)) for by in (1, 2, 3)]
     partial_rows = mixer_out(
         (lax.axis_index("seq") % 2).reshape(1),
         columns + [swapped(packed)] + [swapped(column) for column in columns],
         step,
-        pairs,
+        states,
         inner,
         a_log,
         skip[None],

time: 254 us -> 239 us (0.941)
  Pallas kernels: 58 us -> 38.8 us
  waiting for transfers between devices: 118 us -> 121 us
    pallas_call x4, Pallas kernels: 40.3 us -> 25.1 us  [expert_block(): pl.pallas_call(lambda *refs: expert_kernel(len(parts), *refs), out_shape=...]
    ppermute x1, waiting for transfers between devices: 13.7 us -> 9.17 us  [experts(): left = lax.ppermute(own, 'seq', x_shift(1))]
    pallas_call x1, Pallas kernels: 12 us -> 8.17 us  [mixer_out(): pl.pallas_call(mixer_out_kernel, out_shape=jax.ShapeDtypeStruct((TOKENS,...]
    ppermute x1, waiting for transfers between devices: 2.12 us -> 5.9 us  [experts(): lax.ppermute(left[:half], 'seq', x_shift(1))]
    ppermute x1, waiting for transfers between devices: 1.39 us -> 5.17 us  [experts(): for_left = lax.ppermute(far_sum[half:], 'seq', x_shift(-1))]
    unnamed x29 -> x27, local copies, waits for them, and re-layouts: 7.05 us -> 8.51 us
  transfers between devices with their start and end apart: 33 -> 33, of which waited for: 23 -> 23; matrix products, arithmetic and copies ran while one was open for 1% -> 1% of each run, Pallas kernels for 12% -> 8%
where the time goes in v5:
time: 239 us; the launch traced here: 238 us
  waiting for transfers between devices  121 us (51%)
  starting transfers between devices  41.9 us (18%)
  Pallas kernels  38.8 us (16%)
  blocking collectives  19.6 us (8%)
  local copies, waits for them, and re-layouts  12 us (5%)
  other arithmetic  3.79 us (2%)
    all_to_all x1, waiting for transfers between devices, per_device(): lax.all_to_all(partial_rows, 'exp', split_axis=0, concat_axis=0, tiled=True)  30.2 us
    pallas_call x4, Pallas kernels, expert_block(): pl.pallas_call(lambda *refs: expert_kernel(len(parts), *refs), out_shape=...  25.1 us
    ppermute x1, waiting for transfers between devices, experts(): from_right = lax.ppermute(to_left.astype(BF16), 'seq', x_shift(-1))  21.8 us
    all_to_all x1, blocking collectives, per_device(): lax.all_to_all(jnp.tile(outgoing, (splits, 1)), 'exp', split_axis=0, conc...  19.6 us
    all_to_all x1, waiting for transfers between devices, per_device(): lax.all_to_all(own_rows.astype(BF16), 'exp', split_axis=0, concat_axis=0,...  17.1 us
    ppermute x6, waiting for transfers between devices, from_others(): return [lax.ppermute(value, 'exp', shift(by)) for by in (1, 2, 3)]  15.2 us
    ppermute x6, starting transfers between devices, from_others(): return [lax.ppermute(value, 'exp', shift(by)) for by in (1, 2, 3)]  11.8 us
    ppermute x1, waiting for transfers between devices, experts(): left = lax.ppermute(own, 'seq', x_shift(1))  9.17 us
  transfers between devices with their start and end apart: 33, of which 23 were waited for; matrix products, arithmetic and copies ran while one was open for 1% of the time, Pallas kernels for 8%

profile of v5, /device:TPU:0, one launch (start us, length us, event | category | flops | bytes accessed | tf_op | source)
XLA Modules:
  0.0 238.2 jit_solution(18235302633490671579)
XLA Ops:
  0.0 0.8 slice.18
  0.8 1.3 collective-permute-start
  2.1 1.0 reshape.82.xin
  3.1 1.5 mixer_in.1
  4.6 4.6 %collective-permute-start.3 = (bf16[288,256]{1,0:T(8,128)(2,1)S(1)}, bf16[288,256]{1,0:T(8,128)(2,1)S(1)}, u32[]{:S(2)}, u32[]{:S(2)}) collective-permute-start(bf16[288,256]{1,0:T(8,128)(2,1)S(1)} %get-tuple-element.26), channel_id=1, source_target_pairs={{0,3},{1,0},{2,1},{3,2},{4,7},{5,4},{6,5},{7,6},{8,11},{9,8},{10,9... | collective-permute-start | bytes 442376 | tf_op jit(solution)/shard_map/ppermute | solution.py:48
  9.3 1.3 collective-permute-start.1
  10.5 5.4 %collective-permute-done.3 = bf16[288,256]{1,0:T(8,128)(2,1)S(1)} collective-permute-done((bf16[288,256]{1,0:T(8,128)(2,1)S(1)}, bf16[288,256]{1,0:T(8,128)(2,1)S(1)}, u32[]{:S(2)}, u32[]{:S(2)}) %collective-permute-start.3) | collective-permute-done | bytes 147488 | tf_op jit(solution)/shard_map/ppermute | solution.py:48
  15.9 1.2 collective-permute-done.2
  17.1 2.9 %collective-permute-done.1 = bf16[288,256]{1,0:T(8,128)(2,1)S(1)} collective-permute-done((bf16[288,256]{1,0:T(8,128)(2,1)S(1)}, bf16[288,256]{1,0:T(8,128)(2,1)S(1)}, u32[]{:S(2)}, u32[]{:S(2)}) %collective-permute-start.1) | collective-permute-done | bytes 147488 | tf_op jit(solution)/shard_map/ppermute | solution.py:48
  20.1 1.6 collective-permute-start.4
  21.8 2.9 %collective-permute-start.5 = (bf16[288,256]{1,0:T(8,128)(2,1)S(1)}, bf16[288,256]{1,0:T(8,128)(2,1)S(1)}, u32[]{:S(2)}, u32[]{:S(2)}) collective-permute-start(bf16[288,256]{1,0:T(8,128)(2,1)S(1)} %add_convert_fusion.4.p0), channel_id=1, source_target_pairs={{0,8},{1,9},{2,10},{3,11},{4,12},{5,13},{6,14},{7,15},{8,0},{9,1},... | collective-permute-start | bytes 442376 | tf_op jit(solution)/shard_map/ppermute | solution.py:48
  24.7 1.3 collective-permute-start.6
  26.0 1.3 collective-permute-done.4.p1
  27.4 4.3 %collective-permute-done.5.p2 = bf16[288,256]{1,0:T(8,128)(2,1)S(1)} collective-permute-done((bf16[288,256]{1,0:T(8,128)(2,1)S(1)}, bf16[288,256]{1,0:T(8,128)(2,1)S(1)}, u32[]{:S(2)}, u32[]{:S(2)}) %collective-permute-start.5) | collective-permute-done | bytes 147488 | tf_op jit(solution)/shard_map/ppermute | solution.py:48
  31.7 4.0 %section_scan.1 = (f32[256,512]{1,0:T(8,128)S(1)}, f32[32,256]{1,0:T(8,128)S(1)}, bf16[72,512]{1,0:T(8,128)(2,1)S(1)}) custom-call(bf16[288,256]{1,0:T(8,128)(2,1)S(1)} %add_convert_fusion.4.p0, bf16[288,256]{1,0:T(8,128)(2,1)S(1)} %collective-permute-done.4.p1, bf16[288,256]{1,0:T(8,128)(2,1)S(1)} %collective-permute-done.5.p2, ...), custom_call_target="tpu_custom_call" | custom-call | tf_op jit(solution)/shard_map/section_scan/pallas_call | solution.py:263
  35.7 3.8 %collective-permute-start.7 = (bf16[72,512]{1,0:T(8,128)(2,1)S(1)}, bf16[72,512]{1,0:T(8,128)(2,1)S(1)}, u32[]{:S(2)}, u32[]{:S(2)}) collective-permute-start(bf16[72,512]{1,0:T(8,128)(2,1)S(1)} %get-tuple-element.28), channel_id=1, source_target_pairs={{0,32},{16,48},{32,64},{48,80},{64,96},{80,112},{1,33},{17,49},{33... | collective-permute-start | bytes 221192 | tf_op jit(solution)/shard_map/ppermute | solution.py:425
  39.5 3.1 %collective-permute-start.8 = (bf16[72,512]{1,0:T(8,128)(2,1)S(1)}, bf16[72,512]{1,0:T(8,128)(2,1)S(1)}, u32[]{:S(2)}, u32[]{:S(2)}) collective-permute-start(bf16[72,512]{1,0:T(8,128)(2,1)S(1)} %get-tuple-element.28), channel_id=1, source_target_pairs={{0,64},{16,80},{32,96},{48,112},{1,65},{17,81},{33,97},{49,113},{2... | collective-permute-start | bytes 221192 | tf_op jit(solution)/shard_map/ppermute | solution.py:425
  42.6 1.3 collective-permute-start.9
  44.0 0.5 collective-permute-start.11
  44.6 1.3 collective-permute-done.9.refs_2_
  46.0 1.2 collective-permute-done.13.refs_6_
  47.1 8.2 %mixer_out.1 = bf16[256,4096]{1,0:T(8,128)(2,1)} custom-call(s32[1]{0:T(128)} %bitcast.core, bf16[72,512]{1,0:T(8,128)(2,1)S(1)} %collective-permute-done.7.refs_0_, bf16[72,512]{1,0:T(8,128)(2,1)S(1)} %collective-permute-done.8.refs_1_, bf16[72,512]{1,0:T(8,128)(2,1)S(1)} %collective-permute-done.9.refs_2_, ...), custom_call_target="tpu_custom_call" | custom-call | tf_op jit(solution)/shard_map/mixer_out/pallas_call | solution.py:286
  55.3 4.1 %all-to-all-start = ((bf16[16,16,4096]{2,1,0:T(8,128)(2,1)}), bf16[16,16,4096]{2,1,0:T(8,128)(2,1)S(1)}, u32[]{:S(2)}, u32[]{:S(2)}) async-start(bf16[16,16,4096]{2,1,0:T(8,128)(2,1)} %bitcast.5), calls=%async_computation | async-start | bytes 4194304 | tf_op jit(solution)/shard_map/all_to_all | solution.py:437
  60.4 30.2 %all-to-all-done = bf16[16,16,4096]{2,1,0:T(8,128)(2,1)S(1)} async-done(((bf16[16,16,4096]{2,1,0:T(8,128)(2,1)}), bf16[16,16,4096]{2,1,0:T(8,128)(2,1)S(1)}, u32[]{:S(2)}, u32[]{:S(2)}) %all-to-all-start) | async-done | bytes 2097184 | tf_op jit(solution)/shard_map/all_to_all | solution.py:437
  90.6 0.3 convert_reduce_fusion
  91.3 0.3 convolution_convert_fusion
  91.8 19.6 %all_to_all.29 = bf16[16,8,4096]{2,1,0:T(8,128)(2,1)S(1)} all-to-all(bf16[16,8,4096]{2,1,0:T(8,128)(2,1)S(1)} %bitcast.28), channel_id=1, replica_groups=mesh['seq'=8,'exp'=16] {'exp'}, dimensions={0} | all-to-all | bytes 2097152 | tf_op jit(solution)/shard_map/all_to_all | solution.py:450
  111.4 3.5 %collective-permute-start.17 = (bf16[128,4096]{1,0:T(8,128)(2,1)S(1)}, bf16[128,4096]{1,0:T(8,128)(2,1)S(1)}, u32[]{:S(2)}, u32[]{:S(2)}) collective-permute-start(bf16[128,4096]{1,0:T(8,128)(2,1)S(1)} %bitcast.24), channel_id=1, source_target_pairs={{0,96},{16,112},{32,0},{48,16},{64,32},{80,48},{96,64},{112,80},{1... | collective-permute-start | bytes 3145736 | tf_op jit(solution)/shard_map/ppermute | solution.py:374
  114.9 2.8 %copy-done = bf16[1,4096,768]{2,1,0:T(8,128)(2,1)S(1)} copy-done((bf16[1,4096,768]{2,1,0:T(8,128)(2,1)S(1)}, bf16[1,4096,768]{2,1,0:T(8,128)(2,1)}, u32[]{:S(2)}) %copy-start) | copy-done | bytes 6291480
  117.7 2.8 %copy-done.2 = bf16[1,4096,768]{2,1,0:T(8,128)(2,1)S(1)} copy-done((bf16[1,4096,768]{2,1,0:T(8,128)(2,1)S(1)}, bf16[1,4096,768]{2,1,0:T(8,128)(2,1)}, u32[]{:S(2)}) %copy-start.2) | copy-done | bytes 6291480
  120.4 2.8 %copy-done.3 = bf16[1,768,4096]{2,1,0:T(8,128)(2,1)S(1)} copy-done((bf16[1,768,4096]{2,1,0:T(8,128)(2,1)S(1)}, bf16[1,768,4096]{2,1,0:T(8,128)(2,1)}, u32[]{:S(2)}) %copy-start.3) | copy-done | bytes 6291480
  123.2 6.3 %experts_256.4 = (bf16[128,4096]{1,0:T(8,128)(2,1)S(1)}, bf16[128,4096]{1,0:T(8,128)(2,1)S(1)}) custom-call(bf16[128,4096]{1,0:T(8,128)(2,1)S(1)} %bitcast.25, bf16[128,4096]{1,0:T(8,128)(2,1)S(1)} %collective-permute-done.14.refs_1_, bf16[1,4096,768]{2,1,0:T(8,128)(2,1)S(1)} %copy-done, bf16[1,4096,768]{2,1,0:T(8,128)(2,1)S(1)} %copy-done.2, ...), custom_call_target="tpu_custom_call" | custom-call | flops 4831838208 | bytes 4194304 | tf_op jit(solution)/shard_map/experts_256/pallas_call | solution.py:333
  129.5 9.2 %collective-permute-done.16.refs_0_ = bf16[128,4096]{1,0:T(8,128)(2,1)S(1)} collective-permute-done((bf16[128,4096]{1,0:T(8,128)(2,1)S(1)}, bf16[128,4096]{1,0:T(8,128)(2,1)S(1)}, u32[]{:S(2)}, u32[]{:S(2)}) %collective-permute-start.16) | collective-permute-done | bytes 1048608 | tf_op jit(solution)/shard_map/ppermute | solution.py:373
  138.8 1.8 collective-permute-start.19
  140.7 1.6 collective-permute-start.20
  142.3 6.3 %experts_256.6 = (bf16[128,4096]{1,0:T(8,128)(2,1)S(1)}, bf16[128,4096]{1,0:T(8,128)(2,1)S(1)}) custom-call(bf16[128,4096]{1,0:T(8,128)(2,1)S(1)} %collective-permute-done.16.refs_0_, bf16[128,4096]{1,0:T(8,128)(2,1)S(1)} %collective-permute-done.21.refs_1_, bf16[1,4096,768]{2,1,0:T(8,128)(2,1)S(1)} %copy-done.1, bf16[1,4096,768]{2,1,0:T(8,128)(2,1)S(1)} %copy-done.2, ...), custom_call_target="tpu_custom_call" | custom-call | flops 4831838208 | bytes 4194304 | tf_op jit(solution)/shard_map/experts_256/pallas_call | solution.py:333
  148.6 5.9 %collective-permute-done.19.refs_0_ = bf16[64,4096]{1,0:T(8,128)(2,1)S(1)} collective-permute-done((bf16[64,4096]{1,0:T(8,128)(2,1)S(1)}, bf16[64,4096]{1,0:T(8,128)(2,1)S(1)}, u32[]{:S(2)}, u32[]{:S(2)}) %collective-permute-start.19) | collective-permute-done | bytes 524320 | tf_op jit(solution)/shard_map/ppermute | solution.py:378
  154.5 0.4 collective-permute-done.20.refs_1_
  154.8 0.5 collective-permute-start.23
  155.3 1.4 collective-permute-done.22.refs_2_
  156.7 0.7 collective-permute-done.23.refs_3_
  157.5 6.3 %experts_256.7 = (bf16[128,4096]{1,0:T(8,128)(2,1)S(1)}, bf16[128,4096]{1,0:T(8,128)(2,1)S(1)}) custom-call(bf16[64,4096]{1,0:T(8,128)(2,1)S(1)} %collective-permute-done.19.refs_0_, bf16[64,4096]{1,0:T(8,128)(2,1)S(1)} %collective-permute-done.20.refs_1_, bf16[64,4096]{1,0:T(8,128)(2,1)S(1)} %collective-permute-done.22.refs_2_, ...), custom_call_target="tpu_custom_call" | custom-call | flops 4831838208 | bytes 4194304 | tf_op jit(solution)/shard_map/experts_256/pallas_call | solution.py:333
  163.8 0.2 collective-permute-start.24
  164.0 0.4 collective-permute-start.18
  164.5 2.0 collective-permute-done.24
  166.5 0.2 add_convert_fusion.3
  166.9 2.8 %collective-permute-start.26 = (bf16[64,4096]{1,0:T(8,128)(2,1)S(1)}, bf16[64,4096]{1,0:T(8,128)(2,1)S(1)}, u32[]{:S(2)}, u32[]{:S(2)}) collective-permute-start(bf16[64,4096]{1,0:T(8,128)(2,1)S(1)} %get-tuple-element.48), channel_id=1, source_target_pairs={{0,96},{16,112},{32,0},{48,16},{64,32},{80,48},{96,64},{112,80},{1... | collective-permute-start | bytes 1572872 | tf_op jit(solution)/shard_map/ppermute | solution.py:387
  169.7 6.3 %experts_256.5 = (bf16[128,4096]{1,0:T(8,128)(2,1)S(1)}, bf16[128,4096]{1,0:T(8,128)(2,1)S(1)}) custom-call(bf16[128,4096]{1,0:T(8,128)(2,1)S(1)} %collective-permute-done.17.refs_0_, bf16[128,4096]{1,0:T(8,128)(2,1)S(1)} %collective-permute-done.18.refs_1_, bf16[1,4096,768]{2,1,0:T(8,128)(2,1)S(1)} %copy-done.1, bf16[1,4096,768]{2,1,0:T(8,128)(2,1)S(1)} %bitcast.21, ...), custom_call_target="tpu_custom_call" | custom-call | flops 4831838208 | bytes 4194304 | tf_op jit(solution)/shard_map/experts_256/pallas_call | solution.py:333
  176.0 5.2 %collective-permute-done.26 = bf16[64,4096]{1,0:T(8,128)(2,1)S(1)} collective-permute-done((bf16[64,4096]{1,0:T(8,128)(2,1)S(1)}, bf16[64,4096]{1,0:T(8,128)(2,1)S(1)}, u32[]{:S(2)}, u32[]{:S(2)}) %collective-permute-start.26) | collective-permute-done | bytes 524320 | tf_op jit(solution)/shard_map/ppermute | solution.py:387
  181.1 3.4 %collective-permute-done.25 = bf16[64,4096]{1,0:T(8,128)(2,1)S(1)} collective-permute-done((bf16[64,4096]{1,0:T(8,128)(2,1)S(1)}, bf16[64,4096]{1,0:T(8,128)(2,1)S(1)}, u32[]{:S(2)}, u32[]{:S(2)}) %collective-permute-start.25) | collective-permute-done | bytes 524320 | tf_op jit(solution)/shard_map/ppermute | solution.py:386
  184.5 0.5 collective-permute-start.15
  185.1 0.3 add_convert_fusion.1
  185.4 0.4 collective-permute-start.30
  185.7 1.5 collective-permute-done.27
  187.2 0.3 add_convert_fusion.2
  187.5 0.4 collective-permute-start.28
  187.9 0.8 collective-permute-done.15
  188.7 21.8 %collective-permute-done.30 = bf16[128,4096]{1,0:T(8,128)(2,1)S(1)} collective-permute-done((bf16[128,4096]{1,0:T(8,128)(2,1)S(1)}, bf16[128,4096]{1,0:T(8,128)(2,1)S(1)}, u32[]{:S(2)}, u32[]{:S(2)}) %collective-permute-start.30) | collective-permute-done | bytes 1048608 | tf_op jit(solution)/shard_map/ppermute | solution.py:393
  210.5 3.5 %collective-permute-done.28 = bf16[128,4096]{1,0:T(8,128)(2,1)S(1)} collective-permute-done((bf16[128,4096]{1,0:T(8,128)(2,1)S(1)}, bf16[128,4096]{1,0:T(8,128)(2,1)S(1)}, u32[]{:S(2)}, u32[]{:S(2)}) %collective-permute-start.28) | collective-permute-done | bytes 1048608 | tf_op jit(solution)/shard_map/ppermute | solution.py:394
  214.0 1.6 fusion.1
  215.7 3.8 %all-to-all-start.2 = ((bf16[16,8,4096]{2,1,0:T(8,128)(2,1)}), bf16[16,8,4096]{2,1,0:T(8,128)(2,1)S(1)}, u32[]{:S(2)}, u32[]{:S(2)}) async-start(bf16[16,8,4096]{2,1,0:T(8,128)(2,1)} %fusion.1), calls=%async_computation.2 | async-start | bytes 2097152 | tf_op jit(solution)/shard_map/all_to_all | solution.py:454
  219.6 17.1 %all-to-all-done.2 = bf16[16,8,4096]{2,1,0:T(8,128)(2,1)S(1)} async-done(((bf16[16,8,4096]{2,1,0:T(8,128)(2,1)}), bf16[16,8,4096]{2,1,0:T(8,128)(2,1)S(1)}, u32[]{:S(2)}, u32[]{:S(2)}) %all-to-all-start.2) | async-done | bytes 1048608 | tf_op jit(solution)/shard_map/all_to_all | solution.py:454
  236.9 0.6 fusion
  237.5 0.7 reshape.84
  (76 shorter events, 2.5 us)
Async XLA Ops:
  0.0 47.1 %copy-start.4 = (f32[16,512]{1,0:T(8,128)S(1)}, f32[16,512]{1,0:T(8,128)}, u32[]{:S(2)}) copy-start(f32[16,512]{1,0:T(8,128)} %refs_10_.1) | copy-start | bytes 98308
  0.0 45.8 %copy-start.7 = (bf16[64,4,512]{2,1,0:T(4,128)(2,1)S(1)}, bf16[64,4,512]{2,1,0:T(4,128)(2,1)}, u32[]{:S(2)}) copy-start(bf16[64,4,512]{2,1,0:T(4,128)(2,1)} %param.18) | copy-start | bytes 786436
  0.0 47.1 %copy-start.5 = (f32[512]{0:T(512)S(1)}, f32[512]{0:T(512)}, u32[]{:S(2)}) copy-start(f32[512]{0:T(512)} %param.25) | copy-start | bytes 6148
  0.8 2.3 collective-permute-start
  4.6 11.3 %collective-permute-start.3 = (bf16[288,256]{1,0:T(8,128)(2,1)S(1)}, bf16[288,256]{1,0:T(8,128)(2,1)S(1)}, u32[]{:S(2)}, u32[]{:S(2)}) collective-permute-start(bf16[288,256]{1,0:T(8,128)(2,1)S(1)} %get-tuple-element.26), channel_id=1, source_target_pairs={{0,3},{1,0},{2,1},{3,2},{4,7},{5,4},{6,5},{7,6},{8,11},{9,8},{10,9... | collective-permute-start | bytes 442376 | tf_op jit(solution)/shard_map/ppermute | solution.py:48
  9.3 7.9 %collective-permute-start.2 = (bf16[288,256]{1,0:T(8,128)(2,1)S(1)}, bf16[288,256]{1,0:T(8,128)(2,1)S(1)}, u32[]{:S(2)}, u32[]{:S(2)}) collective-permute-start(bf16[288,256]{1,0:T(8,128)(2,1)S(1)} %get-tuple-element.26), channel_id=1, source_target_pairs={{0,2},{1,3},{2,0},{3,1},{4,6},{5,7},{6,4},{7,5},{8,10},{9,11},{10,... | collective-permute-start | bytes 442376 | tf_op jit(solution)/shard_map/ppermute | solution.py:48
  9.3 10.8 %collective-permute-start.1 = (bf16[288,256]{1,0:T(8,128)(2,1)S(1)}, bf16[288,256]{1,0:T(8,128)(2,1)S(1)}, u32[]{:S(2)}, u32[]{:S(2)}) collective-permute-start(bf16[288,256]{1,0:T(8,128)(2,1)S(1)} %get-tuple-element.26), channel_id=1, source_target_pairs={{0,1},{1,2},{2,3},{3,0},{4,5},{5,6},{6,7},{7,4},{8,9},{9,10},{10,1... | collective-permute-start | bytes 442376 | tf_op jit(solution)/shard_map/ppermute | solution.py:48
  20.1 7.2 %collective-permute-start.4 = (bf16[288,256]{1,0:T(8,128)(2,1)S(1)}, bf16[288,256]{1,0:T(8,128)(2,1)S(1)}, u32[]{:S(2)}, u32[]{:S(2)}) collective-permute-start(bf16[288,256]{1,0:T(8,128)(2,1)S(1)} %add_convert_fusion.4.p0), channel_id=1, source_target_pairs={{0,4},{1,5},{2,6},{3,7},{4,8},{5,9},{6,10},{7,11},{8,12},{9,13},{1... | collective-permute-start | bytes 442376 | tf_op jit(solution)/shard_map/ppermute | solution.py:48
  21.8 9.9 %collective-permute-start.5 = (bf16[288,256]{1,0:T(8,128)(2,1)S(1)}, bf16[288,256]{1,0:T(8,128)(2,1)S(1)}, u32[]{:S(2)}, u32[]{:S(2)}) collective-permute-start(bf16[288,256]{1,0:T(8,128)(2,1)S(1)} %add_convert_fusion.4.p0), channel_id=1, source_target_pairs={{0,8},{1,9},{2,10},{3,11},{4,12},{5,13},{6,14},{7,15},{8,0},{9,1},... | collective-permute-start | bytes 442376 | tf_op jit(solution)/shard_map/ppermute | solution.py:48
  24.7 7.0 %collective-permute-start.6 = (bf16[288,256]{1,0:T(8,128)(2,1)S(1)}, bf16[288,256]{1,0:T(8,128)(2,1)S(1)}, u32[]{:S(2)}, u32[]{:S(2)}) collective-permute-start(bf16[288,256]{1,0:T(8,128)(2,1)S(1)} %add_convert_fusion.4.p0), channel_id=1, source_target_pairs={{0,12},{1,13},{2,14},{3,15},{4,0},{5,1},{6,2},{7,3},{8,4},{9,5},{1... | collective-permute-start | bytes 442376 | tf_op jit(solution)/shard_map/ppermute | solution.py:48
  35.7 8.3 %collective-permute-start.7 = (bf16[72,512]{1,0:T(8,128)(2,1)S(1)}, bf16[72,512]{1,0:T(8,128)(2,1)S(1)}, u32[]{:S(2)}, u32[]{:S(2)}) collective-permute-start(bf16[72,512]{1,0:T(8,128)(2,1)S(1)} %get-tuple-element.28), channel_id=1, source_target_pairs={{0,32},{16,48},{32,64},{48,80},{64,96},{80,112},{1,33},{17,49},{33... | collective-permute-start | bytes 221192 | tf_op jit(solution)/shard_map/ppermute | solution.py:425
  39.5 5.1 %collective-permute-start.8 = (bf16[72,512]{1,0:T(8,128)(2,1)S(1)}, bf16[72,512]{1,0:T(8,128)(2,1)S(1)}, u32[]{:S(2)}, u32[]{:S(2)}) collective-permute-start(bf16[72,512]{1,0:T(8,128)(2,1)S(1)} %get-tuple-element.28), channel_id=1, source_target_pairs={{0,64},{16,80},{32,96},{48,112},{1,65},{17,81},{33,97},{49,113},{2... | collective-permute-start | bytes 221192 | tf_op jit(solution)/shard_map/ppermute | solution.py:425
  42.6 3.3 %collective-permute-start.9 = (bf16[72,512]{1,0:T(8,128)(2,1)S(1)}, bf16[72,512]{1,0:T(8,128)(2,1)S(1)}, u32[]{:S(2)}, u32[]{:S(2)}) collective-permute-start(bf16[72,512]{1,0:T(8,128)(2,1)S(1)} %get-tuple-element.28), channel_id=1, source_target_pairs={{0,96},{16,112},{1,97},{17,113},{2,98},{18,114},{3,99},{19,115},{4... | collective-permute-start | bytes 221192 | tf_op jit(solution)/shard_map/ppermute | solution.py:425
  43.9 2.0 collective-permute-start.10
  44.0 2.0 collective-permute-start.11
  44.5 1.4 collective-permute-start.12
  45.8 1.3 collective-permute-start.13
  55.3 4.1 %copy-start.6 = (bf16[4,4,4096]{2,1,0:T(4,128)(2,1)S(1)}, bf16[4,4,4096]{2,1,0:T(4,128)(2,1)}, u32[]{:S(2)}) copy-start(bf16[4,4,4096]{2,1,0:T(4,128)(2,1)} %param.27) | copy-start | bytes 393220
  55.3 4.2 %copy-start.9 = (s32[4,4,2]{1,2,0:T(2,128)S(1)}, s32[4,4,2]{1,2,0:T(2,128)}, u32[]{:S(2)}) copy-start(s32[4,4,2]{1,2,0:T(2,128)} %param.29) | copy-start | bytes 388
  55.3 35.3 %all-to-all-start = ((bf16[16,16,4096]{2,1,0:T(8,128)(2,1)}), bf16[16,16,4096]{2,1,0:T(8,128)(2,1)S(1)}, u32[]{:S(2)}, u32[]{:S(2)}) async-start(bf16[16,16,4096]{2,1,0:T(8,128)(2,1)} %bitcast.5), calls=%async_computation | async-start | bytes 4194304 | tf_op jit(solution)/shard_map/all_to_all | solution.py:437
  59.6 31.7 %copy-start.8 = (f32[4096]{0:T(1024)S(1)}, f32[4096]{0:T(1024)}, u32[]{:S(2)}) copy-start(f32[4096]{0:T(1024)} %param.28) | copy-start | bytes 49156
  111.4 3.5 %collective-permute-start.14 = (bf16[128,4096]{1,0:T(8,128)(2,1)S(1)}, bf16[128,4096]{1,0:T(8,128)(2,1)S(1)}, u32[]{:S(2)}, u32[]{:S(2)}) collective-permute-start(bf16[128,4096]{1,0:T(8,128)(2,1)S(1)} %bitcast.22), channel_id=1, source_target_pairs={{0,16},{16,0},{32,48},{48,32},{64,80},{80,64},{96,112},{112,96},{1... | collective-permute-start | bytes 3145736 | tf_op jit(solution)/shard_map/ppermute | solution.py:52
  111.4 27.3 %collective-permute-start.16 = (bf16[128,4096]{1,0:T(8,128)(2,1)S(1)}, bf16[128,4096]{1,0:T(8,128)(2,1)S(1)}, u32[]{:S(2)}, u32[]{:S(2)}) collective-permute-start(bf16[128,4096]{1,0:T(8,128)(2,1)S(1)} %bitcast.23), channel_id=1, source_target_pairs={{0,32},{16,48},{32,64},{48,80},{64,96},{80,112},{96,0},{112,16},{1... | collective-permute-start | bytes 3145736 | tf_op jit(solution)/shard_map/ppermute | solution.py:373
  111.4 27.4 %collective-permute-start.17 = (bf16[128,4096]{1,0:T(8,128)(2,1)S(1)}, bf16[128,4096]{1,0:T(8,128)(2,1)S(1)}, u32[]{:S(2)}, u32[]{:S(2)}) collective-permute-start(bf16[128,4096]{1,0:T(8,128)(2,1)S(1)} %bitcast.24), channel_id=1, source_target_pairs={{0,96},{16,112},{32,0},{48,16},{64,32},{80,48},{96,64},{112,80},{1... | collective-permute-start | bytes 3145736 | tf_op jit(solution)/shard_map/ppermute | solution.py:374
  114.9 2.8 %copy-start = (bf16[1,4096,768]{2,1,0:T(8,128)(2,1)S(1)}, bf16[1,4096,768]{2,1,0:T(8,128)(2,1)}, u32[]{:S(2)}) copy-start(bf16[1,4096,768]{2,1,0:T(8,128)(2,1)} %refs_4_.7) | copy-start | bytes 18874372
  117.7 2.8 %copy-start.2 = (bf16[1,4096,768]{2,1,0:T(8,128)(2,1)S(1)}, bf16[1,4096,768]{2,1,0:T(8,128)(2,1)}, u32[]{:S(2)}) copy-start(bf16[1,4096,768]{2,1,0:T(8,128)(2,1)} %refs_5_.1) | copy-start | bytes 18874372
  120.4 2.8 %copy-start.3 = (bf16[1,768,4096]{2,1,0:T(8,128)(2,1)S(1)}, bf16[1,768,4096]{2,1,0:T(8,128)(2,1)}, u32[]{:S(2)}) copy-start(bf16[1,768,4096]{2,1,0:T(8,128)(2,1)} %refs_6_.1) | copy-start | bytes 18874372
  123.2 19.0 %copy-start.1 = (bf16[1,4096,768]{2,1,0:T(8,128)(2,1)S(1)}, bf16[1,4096,768]{2,1,0:T(8,128)(2,1)}, u32[]{:S(2)}) copy-start(bf16[1,4096,768]{2,1,0:T(8,128)(2,1)} %refs_4_.7) | copy-start | bytes 18874372
  138.8 3.5 %collective-permute-start.21 = (bf16[128,4096]{1,0:T(8,128)(2,1)S(1)}, bf16[128,4096]{1,0:T(8,128)(2,1)S(1)}, u32[]{:S(2)}, u32[]{:S(2)}) collective-permute-start(bf16[128,4096]{1,0:T(8,128)(2,1)S(1)} %collective-permute-done.16.refs_0_), channel_id=1, source_target_pairs={{0,16},{16,0},{32,48},{48,32},{64,80},{80,64},{96,112},{112,96},{1... | collective-permute-start | bytes 3145736 | tf_op jit(solution)/shard_map/ppermute | solution.py:52
  138.8 15.6 %collective-permute-start.19 = (bf16[64,4096]{1,0:T(8,128)(2,1)S(1)}, bf16[64,4096]{1,0:T(8,128)(2,1)S(1)}, u32[]{:S(2)}, u32[]{:S(2)}) collective-permute-start(bf16[64,4096]{1,0:T(8,128)(2,1)S(1)} %slice.20), channel_id=1, source_target_pairs={{0,32},{16,48},{32,64},{48,80},{64,96},{80,112},{96,0},{112,16},{1... | collective-permute-start | bytes 1572872 | tf_op jit(solution)/shard_map/ppermute | solution.py:378
  140.7 14.1 %collective-permute-start.20 = (bf16[64,4096]{1,0:T(8,128)(2,1)S(1)}, bf16[64,4096]{1,0:T(8,128)(2,1)S(1)}, u32[]{:S(2)}, u32[]{:S(2)}) collective-permute-start(bf16[64,4096]{1,0:T(8,128)(2,1)S(1)} %slice.21), channel_id=1, source_target_pairs={{0,96},{16,112},{32,0},{48,16},{64,32},{80,48},{96,64},{112,80},{1... | collective-permute-start | bytes 1572872 | tf_op jit(solution)/shard_map/ppermute | solution.py:379
  142.3 27.4 %slice-start = ((s8[6291456]{0:T(1024)(128)(4,1)}), s8[4194304]{0:T(1024)(128)(4,1)S(1)}, s32[]{:S(2)}) async-start(s8[6291456]{0:T(1024)(128)(4,1)} %bitcast.20), calls=%async_computation.3 | async-start | bytes 8388608
  154.8 14.8 %slice-start.1 = ((s8[6291456]{0:T(1024)(128)(4,1)}), s8[2097152]{0:T(1024)(128)(4,1)S(1)}, s32[]{:S(2)}) async-start(s8[6291456]{0:T(1024)(128)(4,1)} %bitcast.20), calls=%async_computation.4 | async-start | bytes 4194304
  154.8 1.9 collective-permute-start.22
  154.8 2.7 %collective-permute-start.23 = (bf16[64,4096]{1,0:T(8,128)(2,1)S(1)}, bf16[64,4096]{1,0:T(8,128)(2,1)S(1)}, u32[]{:S(2)}, u32[]{:S(2)}) collective-permute-start(bf16[64,4096]{1,0:T(8,128)(2,1)S(1)} %collective-permute-done.20.refs_1_), channel_id=1, source_target_pairs={{0,16},{16,0},{32,48},{48,32},{64,80},{80,64},{96,112},{112,96},{1... | collective-permute-start | bytes 1572872 | tf_op jit(solution)/shard_map/ppermute | solution.py:52
  163.8 2.7 %collective-permute-start.24 = (bf16[128,4096]{1,0:T(8,128)(2,1)S(1)}, bf16[128,4096]{1,0:T(8,128)(2,1)S(1)}, u32[]{:S(2)}, u32[]{:S(2)}) collective-permute-start(bf16[128,4096]{1,0:T(8,128)(2,1)S(1)} %get-tuple-element.42), channel_id=1, source_target_pairs={{0,16},{16,0},{32,48},{48,32},{64,80},{80,64},{96,112},{112,96},{1... | collective-permute-start | bytes 3145736 | tf_op jit(solution)/shard_map/ppermute | solution.py:52
  164.0 5.7 %collective-permute-start.18 = (bf16[128,4096]{1,0:T(8,128)(2,1)S(1)}, bf16[128,4096]{1,0:T(8,128)(2,1)S(1)}, u32[]{:S(2)}, u32[]{:S(2)}) collective-permute-start(bf16[128,4096]{1,0:T(8,128)(2,1)S(1)} %collective-permute-done.17.refs_0_), channel_id=1, source_target_pairs={{0,16},{16,0},{32,48},{48,32},{64,80},{80,64},{96,112},{112,96},{1... | collective-permute-start | bytes 3145736 | tf_op jit(solution)/shard_map/ppermute | solution.py:52
  164.4 20.7 %collective-permute-start.29 = (bf16[128,4096]{1,0:T(8,128)(2,1)S(1)}, bf16[128,4096]{1,0:T(8,128)(2,1)S(1)}, u32[]{:S(2)}, u32[]{:S(2)}) collective-permute-start(bf16[128,4096]{1,0:T(8,128)(2,1)S(1)} %get-tuple-element.46), channel_id=1, source_target_pairs={{0,16},{16,0},{32,48},{48,32},{64,80},{80,64},{96,112},{112,96},{1... | collective-permute-start | bytes 3145736 | tf_op jit(solution)/shard_map/ppermute | solution.py:52
  166.9 14.3 %collective-permute-start.26 = (bf16[64,4096]{1,0:T(8,128)(2,1)S(1)}, bf16[64,4096]{1,0:T(8,128)(2,1)S(1)}, u32[]{:S(2)}, u32[]{:S(2)}) collective-permute-start(bf16[64,4096]{1,0:T(8,128)(2,1)S(1)} %get-tuple-element.48), channel_id=1, source_target_pairs={{0,96},{16,112},{32,0},{48,16},{64,32},{80,48},{96,64},{112,80},{1... | collective-permute-start | bytes 1572872 | tf_op jit(solution)/shard_map/ppermute | solution.py:387
  169.6 14.9 %collective-permute-start.25 = (bf16[64,4096]{1,0:T(8,128)(2,1)S(1)}, bf16[64,4096]{1,0:T(8,128)(2,1)S(1)}, u32[]{:S(2)}, u32[]{:S(2)}) collective-permute-start(bf16[64,4096]{1,0:T(8,128)(2,1)S(1)} %get-tuple-element.47), channel_id=1, source_target_pairs={{0,32},{16,48},{32,64},{48,80},{64,96},{80,112},{96,0},{112,16},{1... | collective-permute-start | bytes 1572872 | tf_op jit(solution)/shard_map/ppermute | solution.py:386
  184.5 2.7 %collective-permute-start.27 = (bf16[128,4096]{1,0:T(8,128)(2,1)S(1)}, bf16[128,4096]{1,0:T(8,128)(2,1)S(1)}, u32[]{:S(2)}, u32[]{:S(2)}) collective-permute-start(bf16[128,4096]{1,0:T(8,128)(2,1)S(1)} %get-tuple-element.44), channel_id=1, source_target_pairs={{0,16},{16,0},{32,48},{48,32},{64,80},{80,64},{96,112},{112,96},{1... | collective-permute-start | bytes 3145736 | tf_op jit(solution)/shard_map/ppermute | solution.py:52
  184.5 4.2 %collective-permute-start.15 = (bf16[128,4096]{1,0:T(8,128)(2,1)S(1)}, bf16[128,4096]{1,0:T(8,128)(2,1)S(1)}, u32[]{:S(2)}, u32[]{:S(2)}) collective-permute-start(bf16[128,4096]{1,0:T(8,128)(2,1)S(1)} %get-tuple-element.32), channel_id=1, source_target_pairs={{0,16},{16,0},{32,48},{48,32},{64,80},{80,64},{96,112},{112,96},{1... | collective-permute-start | bytes 3145736 | tf_op jit(solution)/shard_map/ppermute | solution.py:52
  185.4 25.1 %collective-permute-start.30 = (bf16[128,4096]{1,0:T(8,128)(2,1)S(1)}, bf16[128,4096]{1,0:T(8,128)(2,1)S(1)}, u32[]{:S(2)}, u32[]{:S(2)}) collective-permute-start(bf16[128,4096]{1,0:T(8,128)(2,1)S(1)} %add_convert_fusion.1), channel_id=1, source_target_pairs={{0,96},{16,112},{32,0},{48,16},{64,32},{80,48},{96,64},{112,80},{1... | collective-permute-start | bytes 3145736 | tf_op jit(solution)/shard_map/ppermute | solution.py:393
  187.5 26.5 %collective-permute-start.28 = (bf16[128,4096]{1,0:T(8,128)(2,1)S(1)}, bf16[128,4096]{1,0:T(8,128)(2,1)S(1)}, u32[]{:S(2)}, u32[]{:S(2)}) collective-permute-start(bf16[128,4096]{1,0:T(8,128)(2,1)S(1)} %add_convert_fusion.2), channel_id=1, source_target_pairs={{0,32},{16,48},{32,64},{48,80},{64,96},{80,112},{96,0},{112,16},{1... | collective-permute-start | bytes 3145736 | tf_op jit(solution)/shard_map/ppermute | solution.py:394
  215.7 3.8 %copy-start.10 = (bf16[4,4,2]{1,2,0:T(2,128)(2,1)S(1)}, bf16[4,4,2]{1,2,0:T(2,128)(2,1)}, u32[]{:S(2)}) copy-start(bf16[4,4,2]{1,2,0:T(2,128)(2,1)} %param.30) | copy-start | bytes 196
  215.7 21.1 %all-to-all-start.2 = ((bf16[16,8,4096]{2,1,0:T(8,128)(2,1)}), bf16[16,8,4096]{2,1,0:T(8,128)(2,1)S(1)}, u32[]{:S(2)}, u32[]{:S(2)}) async-start(bf16[16,8,4096]{2,1,0:T(8,128)(2,1)} %fusion.1), calls=%async_computation.2 | async-start | bytes 2097152 | tf_op jit(solution)/shard_map/all_to_all | solution.py:454

commit v6 on v5

--- a/solution.py
+++ b/solution.py
@@ -379,20 +379,25 @@
         lax.ppermute(right[half:], "seq", x_shift(-1)),
     ]
     left_out = expert_block([left, swapped(left)], w_gate, w_up, w_down)
-    far = list(after(far, left_out))
+    right_out = expert_block([right, swapped(right)], w_gate, w_up, w_down)
+    far, left_out, right_out = lax.optimization_barrier((far, left_out, right_out))
+    left_sum, right_sum = paired(*left_out), paired(*right_out)
+    from_right = lax.ppermute(left_sum[:half].astype(BF16), "seq", x_shift(-1))
+    from_left = lax.ppermute(right_sum[half:].astype(BF16), "seq", x_shift(1))
     far_out = expert_block(far + [swapped(part) for part in far], w_gate, w_up, w_down)
-    left_out = after(left_out, far_out)
+    far_out = after(far_out, from_right, from_left)
     far_sum = paired(*far_out).astype(BF16)
     for_right = lax.ppermute(far_sum[:half], "seq", x_shift(1))
     for_left = lax.ppermute(far_sum[half:], "seq", x_shift(-1))
-    right_out = expert_block([right, swapped(right)], w_gate, w_up, w_down)
-    right_out = after(right_out, for_right, for_left)
-    nothing = jnp.zeros((half, D), F32)
-    to_left = paired(*left_out) + jnp.concatenate([nothing, for_left.astype(F32)])
-    to_right = paired(*right_out) + jnp.concatenate([for_right.astype(F32), nothing])
-    from_right = lax.ppermute(to_left.astype(BF16), "seq", x_shift(-1))
-    from_left = lax.ppermute(to_right.astype(BF16), "seq", x_shift(1))
-    return paired(*own_out) + from_left.astype(F32) + from_right.astype(F32)
+    to_left = left_sum[half:] + for_left.astype(F32)
+    to_right = right_sum[:half] + for_right.astype(F32)
+    then_right = lax.ppermute(to_left.astype(BF16), "seq", x_shift(-1))
+    then_left = lax.ppermute(to_right.astype(BF16), "seq", x_shift(1))
+    return (
+        paired(*own_out)
+        + jnp.concatenate([from_right, then_right]).astype(F32)
+        + jnp.concatenate([then_left, from_left]).astype(F32)
+    )
 
 
 def per_device(

time: 239 us -> 231 us (0.967)
  waiting for transfers between devices: 121 us -> 104 us
  starting transfers between devices: 41.9 us -> 50.4 us
    ppermute x1, waiting for transfers between devices: 3.41 us -> 12 us  [experts(): for_right = lax.ppermute(far_sum[:half], 'seq', x_shift(1))]
    ppermute x2 -> x4, waiting for transfers between devices: 25.3 us -> 16.8 us  [the longest x1 11.2 us: experts(): then_left = lax.ppermute(to_right.astype(BF16), 'seq', x_shift(1))]
    ppermute x1, waiting for transfers between devices: 5.9 us -> 0.01 us  [experts(): lax.ppermute(left[:half], 'seq', x_shift(1))]
    ppermute x2 -> x4, starting transfers between devices: 0.71 us -> 6.11 us  [the longest x1 3.28 us: experts(): then_right = lax.ppermute(to_left.astype(BF16), 'seq', x_shift(-1))]
    ppermute x1, waiting for transfers between devices: 5.17 us -> 0.01 us  [experts(): for_left = lax.ppermute(far_sum[half:], 'seq', x_shift(-1))]
    ppermute x6, waiting for transfers between devices: 15.2 us -> 12.2 us  [from_others(): return [lax.ppermute(value, 'exp', shift(by)) for by in (1, 2, 3)]]
  transfers between devices with their start and end apart: 33 -> 35, of which waited for: 23 -> 17; matrix products, arithmetic and copies ran while one was open for 1% -> 1% of each run, Pallas kernels for 8% -> 11%
where the time goes in v6:
time: 231 us; the launch traced here: 230 us
  waiting for transfers between devices  104 us (45%)
  starting transfers between devices  50.4 us (22%)
  Pallas kernels  38.8 us (17%)
  blocking collectives  19.7 us (9%)
  local copies, waits for them, and re-layouts  12.1 us (5%)
  other arithmetic  3.87 us (2%)
    all_to_all x1, waiting for transfers between devices, per_device(): lax.all_to_all(partial_rows, 'exp', split_axis=0, concat_axis=0, tiled=True)  30.2 us
    pallas_call x4, Pallas kernels, expert_block(): pl.pallas_call(lambda *refs: expert_kernel(len(parts), *refs), out_shape=...  25.1 us
    all_to_all x1, blocking collectives, per_device(): lax.all_to_all(jnp.tile(outgoing, (splits, 1)), 'exp', split_axis=0, conc...  19.7 us
    all_to_all x1, waiting for transfers between devices, per_device(): lax.all_to_all(own_rows.astype(BF16), 'exp', split_axis=0, concat_axis=0,...  16.1 us
    ppermute x6, starting transfers between devices, from_others(): return [lax.ppermute(value, 'exp', shift(by)) for by in (1, 2, 3)]  13 us
    ppermute x6, waiting for transfers between devices, from_others(): return [lax.ppermute(value, 'exp', shift(by)) for by in (1, 2, 3)]  12.2 us
    ppermute x1, waiting for transfers between devices, experts(): for_right = lax.ppermute(far_sum[:half], 'seq', x_shift(1))  12 us
    ppermute x1, waiting for transfers between devices, experts(): then_left = lax.ppermute(to_right.astype(BF16), 'seq', x_shift(1))  11.2 us
  transfers between devices with their start and end apart: 35, of which 17 were waited for; matrix products, arithmetic and copies ran while one was open for 1% of the time, Pallas kernels for 11%

profile of v6, /device:TPU:0, one launch (start us, length us, event | category | flops | bytes accessed | tf_op | source)
XLA Modules:
  0.0 230.2 jit_solution(12168148646158710664)
XLA Ops:
  0.0 0.8 slice.32
  0.8 1.3 collective-permute-start
  2.1 1.0 reshape.82.xin
  3.1 1.5 mixer_in.1
  4.6 2.5 %collective-permute-start.1 = (bf16[288,256]{1,0:T(8,128)(2,1)S(1)}, bf16[288,256]{1,0:T(8,128)(2,1)S(1)}, u32[]{:S(2)}, u32[]{:S(2)}) collective-permute-start(bf16[288,256]{1,0:T(8,128)(2,1)S(1)} %get-tuple-element.28), channel_id=1, source_target_pairs={{0,1},{1,2},{2,3},{3,0},{4,5},{5,6},{6,7},{7,4},{8,9},{9,10},{10,1... | collective-permute-start | bytes 442376 | tf_op jit(solution)/shard_map/ppermute | solution.py:48
  7.2 3.6 %collective-permute-start.2 = (bf16[288,256]{1,0:T(8,128)(2,1)S(1)}, bf16[288,256]{1,0:T(8,128)(2,1)S(1)}, u32[]{:S(2)}, u32[]{:S(2)}) collective-permute-start(bf16[288,256]{1,0:T(8,128)(2,1)S(1)} %get-tuple-element.28), channel_id=1, source_target_pairs={{0,2},{1,3},{2,0},{3,1},{4,6},{5,7},{6,4},{7,5},{8,10},{9,11},{10,... | collective-permute-start | bytes 442376 | tf_op jit(solution)/shard_map/ppermute | solution.py:48
  10.7 1.0 collective-permute-start.3
  11.8 1.1 collective-permute-done.1
  12.9 4.9 %collective-permute-done.2 = bf16[288,256]{1,0:T(8,128)(2,1)S(1)} collective-permute-done((bf16[288,256]{1,0:T(8,128)(2,1)S(1)}, bf16[288,256]{1,0:T(8,128)(2,1)S(1)}, u32[]{:S(2)}, u32[]{:S(2)}) %collective-permute-start.2) | collective-permute-done | bytes 147488 | tf_op jit(solution)/shard_map/ppermute | solution.py:48
  17.9 1.6 collective-permute-start.4
  19.5 2.9 %collective-permute-start.5 = (bf16[288,256]{1,0:T(8,128)(2,1)S(1)}, bf16[288,256]{1,0:T(8,128)(2,1)S(1)}, u32[]{:S(2)}, u32[]{:S(2)}) collective-permute-start(bf16[288,256]{1,0:T(8,128)(2,1)S(1)} %add_convert_fusion.2.p0), channel_id=1, source_target_pairs={{0,8},{1,9},{2,10},{3,11},{4,12},{5,13},{6,14},{7,15},{8,0},{9,1},... | collective-permute-start | bytes 442376 | tf_op jit(solution)/shard_map/ppermute | solution.py:48
  22.5 1.3 collective-permute-start.6
  23.8 1.8 collective-permute-done.4.p1
  25.6 4.3 %collective-permute-done.5.p2 = bf16[288,256]{1,0:T(8,128)(2,1)S(1)} collective-permute-done((bf16[288,256]{1,0:T(8,128)(2,1)S(1)}, bf16[288,256]{1,0:T(8,128)(2,1)S(1)}, u32[]{:S(2)}, u32[]{:S(2)}) %collective-permute-start.5) | collective-permute-done | bytes 147488 | tf_op jit(solution)/shard_map/ppermute | solution.py:48
  29.9 4.0 %section_scan.1 = (f32[256,512]{1,0:T(8,128)S(1)}, f32[32,256]{1,0:T(8,128)S(1)}, bf16[72,512]{1,0:T(8,128)(2,1)S(1)}) custom-call(bf16[288,256]{1,0:T(8,128)(2,1)S(1)} %add_convert_fusion.2.p0, bf16[288,256]{1,0:T(8,128)(2,1)S(1)} %collective-permute-done.4.p1, bf16[288,256]{1,0:T(8,128)(2,1)S(1)} %collective-permute-done.5.p2, ...), custom_call_target="tpu_custom_call" | custom-call | tf_op jit(solution)/shard_map/section_scan/pallas_call | solution.py:263
  33.9 3.0 %collective-permute-start.7 = (bf16[72,512]{1,0:T(8,128)(2,1)S(1)}, bf16[72,512]{1,0:T(8,128)(2,1)S(1)}, u32[]{:S(2)}, u32[]{:S(2)}) collective-permute-start(bf16[72,512]{1,0:T(8,128)(2,1)S(1)} %get-tuple-element.30), channel_id=1, source_target_pairs={{0,32},{16,48},{32,64},{48,80},{64,96},{80,112},{1,33},{17,49},{33... | collective-permute-start | bytes 221192 | tf_op jit(solution)/shard_map/ppermute | solution.py:430
  36.9 3.1 %collective-permute-start.8 = (bf16[72,512]{1,0:T(8,128)(2,1)S(1)}, bf16[72,512]{1,0:T(8,128)(2,1)S(1)}, u32[]{:S(2)}, u32[]{:S(2)}) collective-permute-start(bf16[72,512]{1,0:T(8,128)(2,1)S(1)} %get-tuple-element.30), channel_id=1, source_target_pairs={{0,64},{16,80},{32,96},{48,112},{1,65},{17,81},{33,97},{49,113},{2... | collective-permute-start | bytes 221192 | tf_op jit(solution)/shard_map/ppermute | solution.py:430
  40.0 1.3 collective-permute-start.9
  41.4 0.5 collective-permute-start.11
  42.0 1.3 collective-permute-done.9.refs_2_
  43.4 1.2 collective-permute-done.13.refs_6_
  44.5 8.2 %mixer_out.1 = bf16[256,4096]{1,0:T(8,128)(2,1)} custom-call(s32[1]{0:T(128)} %bitcast.core, bf16[72,512]{1,0:T(8,128)(2,1)S(1)} %collective-permute-done.7.refs_0_, bf16[72,512]{1,0:T(8,128)(2,1)S(1)} %collective-permute-done.8.refs_1_, bf16[72,512]{1,0:T(8,128)(2,1)S(1)} %collective-permute-done.9.refs_2_, ...), custom_call_target="tpu_custom_call" | custom-call | tf_op jit(solution)/shard_map/mixer_out/pallas_call | solution.py:286
  52.7 6.1 %all-to-all-start = ((bf16[16,16,4096]{2,1,0:T(8,128)(2,1)}), bf16[16,16,4096]{2,1,0:T(8,128)(2,1)S(1)}, u32[]{:S(2)}, u32[]{:S(2)}) async-start(bf16[16,16,4096]{2,1,0:T(8,128)(2,1)} %bitcast.5), calls=%async_computation | async-start | bytes 4194304 | tf_op jit(solution)/shard_map/all_to_all | solution.py:442
  59.3 0.2 select_reduce_fusion.1
  59.8 30.2 %all-to-all-done = bf16[16,16,4096]{2,1,0:T(8,128)(2,1)S(1)} async-done(((bf16[16,16,4096]{2,1,0:T(8,128)(2,1)}), bf16[16,16,4096]{2,1,0:T(8,128)(2,1)S(1)}, u32[]{:S(2)}, u32[]{:S(2)}) %all-to-all-start) | async-done | bytes 2097184 | tf_op jit(solution)/shard_map/all_to_all | solution.py:442
  90.1 0.3 convert_reduce_fusion
  90.4 0.2 multiply_reduce_fusion
  90.8 0.3 convolution_convert_fusion
  91.2 19.7 %all_to_all.29 = bf16[16,8,4096]{2,1,0:T(8,128)(2,1)S(1)} all-to-all(bf16[16,8,4096]{2,1,0:T(8,128)(2,1)S(1)} %bitcast.26), channel_id=1, replica_groups=mesh['seq'=8,'exp'=16] {'exp'}, dimensions={0} | all-to-all | bytes 2097152 | tf_op jit(solution)/shard_map/all_to_all | solution.py:455
  110.9 3.6 %collective-permute-start.17 = (bf16[128,4096]{1,0:T(8,128)(2,1)S(1)}, bf16[128,4096]{1,0:T(8,128)(2,1)S(1)}, u32[]{:S(2)}, u32[]{:S(2)}) collective-permute-start(bf16[128,4096]{1,0:T(8,128)(2,1)S(1)} %bitcast.22), channel_id=1, source_target_pairs={{0,96},{16,112},{32,0},{48,16},{64,32},{80,48},{96,64},{112,80},{1... | collective-permute-start | bytes 3145736 | tf_op jit(solution)/shard_map/ppermute | solution.py:374
  114.5 2.8 %copy-done = bf16[1,4096,768]{2,1,0:T(8,128)(2,1)S(1)} copy-done((bf16[1,4096,768]{2,1,0:T(8,128)(2,1)S(1)}, bf16[1,4096,768]{2,1,0:T(8,128)(2,1)}, u32[]{:S(2)}) %copy-start) | copy-done | bytes 6291480
  117.3 2.8 %copy-done.2 = bf16[1,4096,768]{2,1,0:T(8,128)(2,1)S(1)} copy-done((bf16[1,4096,768]{2,1,0:T(8,128)(2,1)S(1)}, bf16[1,4096,768]{2,1,0:T(8,128)(2,1)}, u32[]{:S(2)}) %copy-start.2) | copy-done | bytes 6291480
  120.0 2.8 %copy-done.4 = bf16[1,768,4096]{2,1,0:T(8,128)(2,1)S(1)} copy-done((bf16[1,768,4096]{2,1,0:T(8,128)(2,1)S(1)}, bf16[1,768,4096]{2,1,0:T(8,128)(2,1)}, u32[]{:S(2)}) %copy-start.4) | copy-done | bytes 6291480
  122.8 6.3 %experts_256.4 = (bf16[128,4096]{1,0:T(8,128)(2,1)S(1)}, bf16[128,4096]{1,0:T(8,128)(2,1)S(1)}) custom-call(bf16[128,4096]{1,0:T(8,128)(2,1)S(1)} %bitcast.23, bf16[128,4096]{1,0:T(8,128)(2,1)S(1)} %collective-permute-done.14.refs_1_, bf16[1,4096,768]{2,1,0:T(8,128)(2,1)S(1)} %copy-done, bf16[1,4096,768]{2,1,0:T(8,128)(2,1)S(1)} %copy-done.2, ...), custom_call_target="tpu_custom_call" | custom-call | flops 4831838208 | bytes 4194304 | tf_op jit(solution)/shard_map/experts_256/pallas_call | solution.py:333
  129.1 9.2 %collective-permute-done.16.refs_0_ = bf16[128,4096]{1,0:T(8,128)(2,1)S(1)} collective-permute-done((bf16[128,4096]{1,0:T(8,128)(2,1)S(1)}, bf16[128,4096]{1,0:T(8,128)(2,1)S(1)}, u32[]{:S(2)}, u32[]{:S(2)}) %collective-permute-start.16) | collective-permute-done | bytes 1048608 | tf_op jit(solution)/shard_map/ppermute | solution.py:373
  138.3 0.5 collective-permute-start.20
  138.9 1.8 collective-permute-start.18
  140.6 1.6 collective-permute-start.19
  142.2 6.3 %experts_256.6 = (bf16[128,4096]{1,0:T(8,128)(2,1)S(1)}, bf16[128,4096]{1,0:T(8,128)(2,1)S(1)}) custom-call(bf16[128,4096]{1,0:T(8,128)(2,1)S(1)} %collective-permute-done.17.refs_0_, bf16[128,4096]{1,0:T(8,128)(2,1)S(1)} %collective-permute-done.21.refs_1_, bf16[1,4096,768]{2,1,0:T(8,128)(2,1)S(1)} %copy-done.1, bf16[1,4096,768]{2,1,0:T(8,128)(2,1)S(1)} %copy-done.3, ...), custom_call_target="tpu_custom_call" | custom-call | flops 4831838208 | bytes 4194304 | tf_op jit(solution)/shard_map/experts_256/pallas_call | solution.py:333
  148.5 6.3 %experts_256.5 = (bf16[128,4096]{1,0:T(8,128)(2,1)S(1)}, bf16[128,4096]{1,0:T(8,128)(2,1)S(1)}) custom-call(bf16[128,4096]{1,0:T(8,128)(2,1)S(1)} %collective-permute-done.16.refs_0_, bf16[128,4096]{1,0:T(8,128)(2,1)S(1)} %collective-permute-done.20.refs_1_, bf16[1,4096,768]{2,1,0:T(8,128)(2,1)S(1)} %copy-done.1, bf16[1,4096,768]{2,1,0:T(8,128)(2,1)S(1)} %copy-done.3, ...), custom_call_target="tpu_custom_call" | custom-call | flops 4831838208 | bytes 4194304 | tf_op jit(solution)/shard_map/experts_256/pallas_call | solution.py:333
  154.9 0.5 collective-permute-start.22
  155.5 0.4 collective-permute-start.25
  155.9 1.6 collective-permute-done.26
  157.6 0.3 convert_add_fusion
  157.9 0.5 collective-permute-start.27
  158.5 0.6 collective-permute-done.22
  159.1 0.3 convert_add_fusion.1
  159.4 2.2 collective-permute-start.23
  161.6 6.3 %experts_256.7 = (bf16[128,4096]{1,0:T(8,128)(2,1)S(1)}, bf16[128,4096]{1,0:T(8,128)(2,1)S(1)}) custom-call(bf16[64,4096]{1,0:T(8,128)(2,1)S(1)} %collective-permute-done.18.refs_0_, bf16[64,4096]{1,0:T(8,128)(2,1)S(1)} %collective-permute-done.19.refs_1_, bf16[64,4096]{1,0:T(8,128)(2,1)S(1)} %collective-permute-done.24.refs_2_, ...), custom_call_target="tpu_custom_call" | custom-call | flops 4831838208 | bytes 4194304 | tf_op jit(solution)/shard_map/experts_256/pallas_call | solution.py:333
  167.9 5.2 %collective-permute-done.27 = bf16[64,4096]{1,0:T(8,128)(2,1)S(1)} collective-permute-done((bf16[64,4096]{1,0:T(8,128)(2,1)S(1)}, bf16[64,4096]{1,0:T(8,128)(2,1)S(1)}, u32[]{:S(2)}, u32[]{:S(2)}) %collective-permute-start.27) | collective-permute-done | bytes 524320 | tf_op jit(solution)/shard_map/ppermute | solution.py:386
  173.2 0.3 collective-permute-done.23
  173.4 2.7 %collective-permute-done.28 = bf16[128,4096]{1,0:T(8,128)(2,1)S(1)} collective-permute-done((bf16[128,4096]{1,0:T(8,128)(2,1)S(1)}, bf16[128,4096]{1,0:T(8,128)(2,1)S(1)}, u32[]{:S(2)}, u32[]{:S(2)}) %collective-permute-start.28) | collective-permute-done | bytes 1048608 | tf_op jit(solution)/shard_map/ppermute | solution.py:52
  176.1 0.2 add_convert_fusion.1
  176.4 0.6 collective-permute-start.31
  177.1 3.0 %collective-permute-start.29 = (bf16[64,4096]{1,0:T(8,128)(2,1)S(1)}, bf16[64,4096]{1,0:T(8,128)(2,1)S(1)}, u32[]{:S(2)}, u32[]{:S(2)}) collective-permute-start(bf16[64,4096]{1,0:T(8,128)(2,1)S(1)} %get-tuple-element.52), channel_id=1, source_target_pairs={{0,96},{16,112},{32,0},{48,16},{64,32},{80,48},{96,64},{112,80},{1... | collective-permute-start | bytes 1572872 | tf_op jit(solution)/shard_map/ppermute | solution.py:391
  180.1 12.0 %collective-permute-done.31 = bf16[64,4096]{1,0:T(8,128)(2,1)S(1)} collective-permute-done((bf16[64,4096]{1,0:T(8,128)(2,1)S(1)}, bf16[64,4096]{1,0:T(8,128)(2,1)S(1)}, u32[]{:S(2)}, u32[]{:S(2)}) %collective-permute-start.31) | collective-permute-done | bytes 524320 | tf_op jit(solution)/shard_map/ppermute | solution.py:390
  192.4 3.3 %collective-permute-start.30 = (bf16[64,4096]{1,0:T(8,128)(2,1)S(1)}, bf16[64,4096]{1,0:T(8,128)(2,1)S(1)}, u32[]{:S(2)}, u32[]{:S(2)}) collective-permute-start(bf16[64,4096]{1,0:T(8,128)(2,1)S(1)} %fusion.3), channel_id=1, source_target_pairs={{0,96},{16,112},{32,0},{48,16},{64,32},{80,48},{96,64},{112,80},{1... | collective-permute-start | bytes 1572872 | tf_op jit(solution)/shard_map/ppermute | solution.py:394
  195.7 11.2 %collective-permute-done.32 = bf16[64,4096]{1,0:T(8,128)(2,1)S(1)} collective-permute-done((bf16[64,4096]{1,0:T(8,128)(2,1)S(1)}, bf16[64,4096]{1,0:T(8,128)(2,1)S(1)}, u32[]{:S(2)}, u32[]{:S(2)}) %collective-permute-start.32) | collective-permute-done | bytes 524320 | tf_op jit(solution)/shard_map/ppermute | solution.py:395
  206.9 1.6 fusion.1
  208.6 3.8 %all-to-all-start.2 = ((bf16[16,8,4096]{2,1,0:T(8,128)(2,1)}), bf16[16,8,4096]{2,1,0:T(8,128)(2,1)S(1)}, u32[]{:S(2)}, u32[]{:S(2)}) async-start(bf16[16,8,4096]{2,1,0:T(8,128)(2,1)} %fusion.1), calls=%async_computation.2 | async-start | bytes 2097152 | tf_op jit(solution)/shard_map/all_to_all | solution.py:459
  212.5 16.1 %all-to-all-done.2 = bf16[16,8,4096]{2,1,0:T(8,128)(2,1)S(1)} async-done(((bf16[16,8,4096]{2,1,0:T(8,128)(2,1)}), bf16[16,8,4096]{2,1,0:T(8,128)(2,1)S(1)}, u32[]{:S(2)}, u32[]{:S(2)}) %all-to-all-start.2) | async-done | bytes 1048608 | tf_op jit(solution)/shard_map/all_to_all | solution.py:459
  228.7 0.2 convert_reduce_fusion.1
  228.8 0.6 fusion
  229.5 0.7 reshape.84
  (83 shorter events, 2.4 us)
Async XLA Ops:
  0.0 44.5 %copy-start.6 = (f32[16,512]{1,0:T(8,128)S(1)}, f32[16,512]{1,0:T(8,128)}, u32[]{:S(2)}) copy-start(f32[16,512]{1,0:T(8,128)} %refs_10_.1) | copy-start | bytes 98308
  0.0 43.3 %copy-start.9 = (bf16[64,4,512]{2,1,0:T(4,128)(2,1)S(1)}, bf16[64,4,512]{2,1,0:T(4,128)(2,1)}, u32[]{:S(2)}) copy-start(bf16[64,4,512]{2,1,0:T(4,128)(2,1)} %param.18) | copy-start | bytes 786436
  0.0 44.5 %copy-start.7 = (f32[512]{0:T(512)S(1)}, f32[512]{0:T(512)}, u32[]{:S(2)}) copy-start(f32[512]{0:T(512)} %param.25) | copy-start | bytes 6148
  0.8 2.3 %collective-permute-start = (bf16[12,512]{1,0:T(8,128)(2,1)S(1)}, bf16[12,512]{1,0:T(8,128)(2,1)S(1)}, u32[]{:S(2)}, u32[]{:S(2)}) collective-permute-start(bf16[12,512]{1,0:T(8,128)(2,1)S(1)} %slice.33), channel_id=1, source_target_pairs={{0,16},{16,32},{32,48},{48,64},{64,80},{80,96},{96,112},{1,17},{17... | collective-permute-start | bytes 36872 | tf_op jit(solution)/shard_map/ppermute | solution.py:44
  4.6 8.2 %collective-permute-start.1 = (bf16[288,256]{1,0:T(8,128)(2,1)S(1)}, bf16[288,256]{1,0:T(8,128)(2,1)S(1)}, u32[]{:S(2)}, u32[]{:S(2)}) collective-permute-start(bf16[288,256]{1,0:T(8,128)(2,1)S(1)} %get-tuple-element.28), channel_id=1, source_target_pairs={{0,1},{1,2},{2,3},{3,0},{4,5},{5,6},{6,7},{7,4},{8,9},{9,10},{10,1... | collective-permute-start | bytes 442376 | tf_op jit(solution)/shard_map/ppermute | solution.py:48
  7.2 10.7 %collective-permute-start.2 = (bf16[288,256]{1,0:T(8,128)(2,1)S(1)}, bf16[288,256]{1,0:T(8,128)(2,1)S(1)}, u32[]{:S(2)}, u32[]{:S(2)}) collective-permute-start(bf16[288,256]{1,0:T(8,128)(2,1)S(1)} %get-tuple-element.28), channel_id=1, source_target_pairs={{0,2},{1,3},{2,0},{3,1},{4,6},{5,7},{6,4},{7,5},{8,10},{9,11},{10,... | collective-permute-start | bytes 442376 | tf_op jit(solution)/shard_map/ppermute | solution.py:48
  10.7 7.1 %collective-permute-start.3 = (bf16[288,256]{1,0:T(8,128)(2,1)S(1)}, bf16[288,256]{1,0:T(8,128)(2,1)S(1)}, u32[]{:S(2)}, u32[]{:S(2)}) collective-permute-start(bf16[288,256]{1,0:T(8,128)(2,1)S(1)} %get-tuple-element.28), channel_id=1, source_target_pairs={{0,3},{1,0},{2,1},{3,2},{4,7},{5,4},{6,5},{7,6},{8,11},{9,8},{10,9... | collective-permute-start | bytes 442376 | tf_op jit(solution)/shard_map/ppermute | solution.py:48
  17.9 7.7 %collective-permute-start.4 = (bf16[288,256]{1,0:T(8,128)(2,1)S(1)}, bf16[288,256]{1,0:T(8,128)(2,1)S(1)}, u32[]{:S(2)}, u32[]{:S(2)}) collective-permute-start(bf16[288,256]{1,0:T(8,128)(2,1)S(1)} %add_convert_fusion.2.p0), channel_id=1, source_target_pairs={{0,4},{1,5},{2,6},{3,7},{4,8},{5,9},{6,10},{7,11},{8,12},{9,13},{1... | collective-permute-start | bytes 442376 | tf_op jit(solution)/shard_map/ppermute | solution.py:48
  19.5 10.4 %collective-permute-start.5 = (bf16[288,256]{1,0:T(8,128)(2,1)S(1)}, bf16[288,256]{1,0:T(8,128)(2,1)S(1)}, u32[]{:S(2)}, u32[]{:S(2)}) collective-permute-start(bf16[288,256]{1,0:T(8,128)(2,1)S(1)} %add_convert_fusion.2.p0), channel_id=1, source_target_pairs={{0,8},{1,9},{2,10},{3,11},{4,12},{5,13},{6,14},{7,15},{8,0},{9,1},... | collective-permute-start | bytes 442376 | tf_op jit(solution)/shard_map/ppermute | solution.py:48
  22.5 7.5 %collective-permute-start.6 = (bf16[288,256]{1,0:T(8,128)(2,1)S(1)}, bf16[288,256]{1,0:T(8,128)(2,1)S(1)}, u32[]{:S(2)}, u32[]{:S(2)}) collective-permute-start(bf16[288,256]{1,0:T(8,128)(2,1)S(1)} %add_convert_fusion.2.p0), channel_id=1, source_target_pairs={{0,12},{1,13},{2,14},{3,15},{4,0},{5,1},{6,2},{7,3},{8,4},{9,5},{1... | collective-permute-start | bytes 442376 | tf_op jit(solution)/shard_map/ppermute | solution.py:48
  33.9 7.4 %collective-permute-start.7 = (bf16[72,512]{1,0:T(8,128)(2,1)S(1)}, bf16[72,512]{1,0:T(8,128)(2,1)S(1)}, u32[]{:S(2)}, u32[]{:S(2)}) collective-permute-start(bf16[72,512]{1,0:T(8,128)(2,1)S(1)} %get-tuple-element.30), channel_id=1, source_target_pairs={{0,32},{16,48},{32,64},{48,80},{64,96},{80,112},{1,33},{17,49},{33... | collective-permute-start | bytes 221192 | tf_op jit(solution)/shard_map/ppermute | solution.py:430
  36.9 5.0 %collective-permute-start.8 = (bf16[72,512]{1,0:T(8,128)(2,1)S(1)}, bf16[72,512]{1,0:T(8,128)(2,1)S(1)}, u32[]{:S(2)}, u32[]{:S(2)}) collective-permute-start(bf16[72,512]{1,0:T(8,128)(2,1)S(1)} %get-tuple-element.30), channel_id=1, source_target_pairs={{0,64},{16,80},{32,96},{48,112},{1,65},{17,81},{33,97},{49,113},{2... | collective-permute-start | bytes 221192 | tf_op jit(solution)/shard_map/ppermute | solution.py:430
  40.0 3.3 %collective-permute-start.9 = (bf16[72,512]{1,0:T(8,128)(2,1)S(1)}, bf16[72,512]{1,0:T(8,128)(2,1)S(1)}, u32[]{:S(2)}, u32[]{:S(2)}) collective-permute-start(bf16[72,512]{1,0:T(8,128)(2,1)S(1)} %get-tuple-element.30), channel_id=1, source_target_pairs={{0,96},{16,112},{1,97},{17,113},{2,98},{18,114},{3,99},{19,115},{4... | collective-permute-start | bytes 221192 | tf_op jit(solution)/shard_map/ppermute | solution.py:430
  41.3 2.0 collective-permute-start.10
  41.4 2.0 collective-permute-start.11
  42.0 1.4 collective-permute-start.12
  43.3 1.3 collective-permute-start.13
  52.7 6.2 %copy-start.8 = (bf16[4,4,4096]{2,1,0:T(4,128)(2,1)S(1)}, bf16[4,4,4096]{2,1,0:T(4,128)(2,1)}, u32[]{:S(2)}) copy-start(bf16[4,4,4096]{2,1,0:T(4,128)(2,1)} %param.27) | copy-start | bytes 393220
  52.7 6.2 %copy-start.11 = (s32[4,4,2]{1,2,0:T(2,128)S(1)}, s32[4,4,2]{1,2,0:T(2,128)}, u32[]{:S(2)}) copy-start(s32[4,4,2]{1,2,0:T(2,128)} %param.29) | copy-start | bytes 388
  52.7 37.3 %all-to-all-start = ((bf16[16,16,4096]{2,1,0:T(8,128)(2,1)}), bf16[16,16,4096]{2,1,0:T(8,128)(2,1)S(1)}, u32[]{:S(2)}, u32[]{:S(2)}) async-start(bf16[16,16,4096]{2,1,0:T(8,128)(2,1)} %bitcast.5), calls=%async_computation | async-start | bytes 4194304 | tf_op jit(solution)/shard_map/all_to_all | solution.py:442
  59.1 31.6 %copy-start.10 = (f32[4096]{0:T(1024)S(1)}, f32[4096]{0:T(1024)}, u32[]{:S(2)}) copy-start(f32[4096]{0:T(1024)} %param.28) | copy-start | bytes 49156
  110.9 3.6 %collective-permute-start.14 = (bf16[128,4096]{1,0:T(8,128)(2,1)S(1)}, bf16[128,4096]{1,0:T(8,128)(2,1)S(1)}, u32[]{:S(2)}, u32[]{:S(2)}) collective-permute-start(bf16[128,4096]{1,0:T(8,128)(2,1)S(1)} %bitcast.20), channel_id=1, source_target_pairs={{0,16},{16,0},{32,48},{48,32},{64,80},{80,64},{96,112},{112,96},{1... | collective-permute-start | bytes 3145736 | tf_op jit(solution)/shard_map/ppermute | solution.py:52
  110.9 27.4 %collective-permute-start.16 = (bf16[128,4096]{1,0:T(8,128)(2,1)S(1)}, bf16[128,4096]{1,0:T(8,128)(2,1)S(1)}, u32[]{:S(2)}, u32[]{:S(2)}) collective-permute-start(bf16[128,4096]{1,0:T(8,128)(2,1)S(1)} %bitcast.21), channel_id=1, source_target_pairs={{0,32},{16,48},{32,64},{48,80},{64,96},{80,112},{96,0},{112,16},{1... | collective-permute-start | bytes 3145736 | tf_op jit(solution)/shard_map/ppermute | solution.py:373
  110.9 27.4 %collective-permute-start.17 = (bf16[128,4096]{1,0:T(8,128)(2,1)S(1)}, bf16[128,4096]{1,0:T(8,128)(2,1)S(1)}, u32[]{:S(2)}, u32[]{:S(2)}) collective-permute-start(bf16[128,4096]{1,0:T(8,128)(2,1)S(1)} %bitcast.22), channel_id=1, source_target_pairs={{0,96},{16,112},{32,0},{48,16},{64,32},{80,48},{96,64},{112,80},{1... | collective-permute-start | bytes 3145736 | tf_op jit(solution)/shard_map/ppermute | solution.py:374
  114.5 2.8 %copy-start = (bf16[1,4096,768]{2,1,0:T(8,128)(2,1)S(1)}, bf16[1,4096,768]{2,1,0:T(8,128)(2,1)}, u32[]{:S(2)}) copy-start(bf16[1,4096,768]{2,1,0:T(8,128)(2,1)} %refs_4_.7) | copy-start | bytes 18874372
  117.3 2.8 %copy-start.2 = (bf16[1,4096,768]{2,1,0:T(8,128)(2,1)S(1)}, bf16[1,4096,768]{2,1,0:T(8,128)(2,1)}, u32[]{:S(2)}) copy-start(bf16[1,4096,768]{2,1,0:T(8,128)(2,1)} %refs_5_.1) | copy-start | bytes 18874372
  120.0 2.8 %copy-start.4 = (bf16[1,768,4096]{2,1,0:T(8,128)(2,1)S(1)}, bf16[1,768,4096]{2,1,0:T(8,128)(2,1)}, u32[]{:S(2)}) copy-start(bf16[1,768,4096]{2,1,0:T(8,128)(2,1)} %refs_6_.1) | copy-start | bytes 18874372
  122.8 19.4 %copy-start.1 = (bf16[1,4096,768]{2,1,0:T(8,128)(2,1)S(1)}, bf16[1,4096,768]{2,1,0:T(8,128)(2,1)}, u32[]{:S(2)}) copy-start(bf16[1,4096,768]{2,1,0:T(8,128)(2,1)} %refs_4_.7) | copy-start | bytes 18874372
  122.8 19.4 %copy-start.3 = (bf16[1,4096,768]{2,1,0:T(8,128)(2,1)S(1)}, bf16[1,4096,768]{2,1,0:T(8,128)(2,1)}, u32[]{:S(2)}) copy-start(bf16[1,4096,768]{2,1,0:T(8,128)(2,1)} %refs_5_.1) | copy-start | bytes 18874372
  122.8 19.4 %copy-start.5 = (bf16[1,768,4096]{2,1,0:T(8,128)(2,1)S(1)}, bf16[1,768,4096]{2,1,0:T(8,128)(2,1)}, u32[]{:S(2)}) copy-start(bf16[1,768,4096]{2,1,0:T(8,128)(2,1)} %refs_6_.1) | copy-start | bytes 18874372
  138.3 3.9 %collective-permute-start.21 = (bf16[128,4096]{1,0:T(8,128)(2,1)S(1)}, bf16[128,4096]{1,0:T(8,128)(2,1)S(1)}, u32[]{:S(2)}, u32[]{:S(2)}) collective-permute-start(bf16[128,4096]{1,0:T(8,128)(2,1)S(1)} %collective-permute-done.17.refs_0_), channel_id=1, source_target_pairs={{0,16},{16,0},{32,48},{48,32},{64,80},{80,64},{96,112},{112,96},{1... | collective-permute-start | bytes 3145736 | tf_op jit(solution)/shard_map/ppermute | solution.py:52
  138.3 10.2 %collective-permute-start.20 = (bf16[128,4096]{1,0:T(8,128)(2,1)S(1)}, bf16[128,4096]{1,0:T(8,128)(2,1)S(1)}, u32[]{:S(2)}, u32[]{:S(2)}) collective-permute-start(bf16[128,4096]{1,0:T(8,128)(2,1)S(1)} %collective-permute-done.16.refs_0_), channel_id=1, source_target_pairs={{0,16},{16,0},{32,48},{48,32},{64,80},{80,64},{96,112},{112,96},{1... | collective-permute-start | bytes 3145736 | tf_op jit(solution)/shard_map/ppermute | solution.py:52
  138.9 15.9 %collective-permute-start.18 = (bf16[64,4096]{1,0:T(8,128)(2,1)S(1)}, bf16[64,4096]{1,0:T(8,128)(2,1)S(1)}, u32[]{:S(2)}, u32[]{:S(2)}) collective-permute-start(bf16[64,4096]{1,0:T(8,128)(2,1)S(1)} %slice.34), channel_id=1, source_target_pairs={{0,32},{16,48},{32,64},{48,80},{64,96},{80,112},{96,0},{112,16},{1... | collective-permute-start | bytes 1572872 | tf_op jit(solution)/shard_map/ppermute | solution.py:378
  140.6 14.2 %collective-permute-start.19 = (bf16[64,4096]{1,0:T(8,128)(2,1)S(1)}, bf16[64,4096]{1,0:T(8,128)(2,1)S(1)}, u32[]{:S(2)}, u32[]{:S(2)}) collective-permute-start(bf16[64,4096]{1,0:T(8,128)(2,1)S(1)} %slice.35), channel_id=1, source_target_pairs={{0,96},{16,112},{32,0},{48,16},{64,32},{80,48},{96,64},{112,80},{1... | collective-permute-start | bytes 1572872 | tf_op jit(solution)/shard_map/ppermute | solution.py:379
  154.8 2.7 %collective-permute-start.26 = (bf16[128,4096]{1,0:T(8,128)(2,1)S(1)}, bf16[128,4096]{1,0:T(8,128)(2,1)S(1)}, u32[]{:S(2)}, u32[]{:S(2)}) collective-permute-start(bf16[128,4096]{1,0:T(8,128)(2,1)S(1)} %get-tuple-element.48), channel_id=1, source_target_pairs={{0,16},{16,0},{32,48},{48,32},{64,80},{80,64},{96,112},{112,96},{1... | collective-permute-start | bytes 3145736 | tf_op jit(solution)/shard_map/ppermute | solution.py:52
  154.9 4.1 %collective-permute-start.22 = (bf16[128,4096]{1,0:T(8,128)(2,1)S(1)}, bf16[128,4096]{1,0:T(8,128)(2,1)S(1)}, u32[]{:S(2)}, u32[]{:S(2)}) collective-permute-start(bf16[128,4096]{1,0:T(8,128)(2,1)S(1)} %get-tuple-element.42), channel_id=1, source_target_pairs={{0,16},{16,0},{32,48},{48,32},{64,80},{80,64},{96,112},{112,96},{1... | collective-permute-start | bytes 3145736 | tf_op jit(solution)/shard_map/ppermute | solution.py:52
  155.4 6.2 %collective-permute-start.24 = (bf16[64,4096]{1,0:T(8,128)(2,1)S(1)}, bf16[64,4096]{1,0:T(8,128)(2,1)S(1)}, u32[]{:S(2)}, u32[]{:S(2)}) collective-permute-start(bf16[64,4096]{1,0:T(8,128)(2,1)S(1)} %collective-permute-done.18.refs_0_), channel_id=1, source_target_pairs={{0,16},{16,0},{32,48},{48,32},{64,80},{80,64},{96,112},{112,96},{1... | collective-permute-start | bytes 1572872 | tf_op jit(solution)/shard_map/ppermute | solution.py:52
  155.5 6.1 %collective-permute-start.25 = (bf16[64,4096]{1,0:T(8,128)(2,1)S(1)}, bf16[64,4096]{1,0:T(8,128)(2,1)S(1)}, u32[]{:S(2)}, u32[]{:S(2)}) collective-permute-start(bf16[64,4096]{1,0:T(8,128)(2,1)S(1)} %collective-permute-done.19.refs_1_), channel_id=1, source_target_pairs={{0,16},{16,0},{32,48},{48,32},{64,80},{80,64},{96,112},{112,96},{1... | collective-permute-start | bytes 1572872 | tf_op jit(solution)/shard_map/ppermute | solution.py:52
  157.9 15.2 %collective-permute-start.27 = (bf16[64,4096]{1,0:T(8,128)(2,1)S(1)}, bf16[64,4096]{1,0:T(8,128)(2,1)S(1)}, u32[]{:S(2)}, u32[]{:S(2)}) collective-permute-start(bf16[64,4096]{1,0:T(8,128)(2,1)S(1)} %slice.56), channel_id=1, source_target_pairs={{0,32},{16,48},{32,64},{48,80},{64,96},{80,112},{96,0},{112,16},{1... | collective-permute-start | bytes 1572872 | tf_op jit(solution)/shard_map/ppermute | solution.py:386
  159.4 14.0 %collective-permute-start.23 = (bf16[64,4096]{1,0:T(8,128)(2,1)S(1)}, bf16[64,4096]{1,0:T(8,128)(2,1)S(1)}, u32[]{:S(2)}, u32[]{:S(2)}) collective-permute-start(bf16[64,4096]{1,0:T(8,128)(2,1)S(1)} %slice.57), channel_id=1, source_target_pairs={{0,96},{16,112},{32,0},{48,16},{64,32},{80,48},{96,64},{112,80},{1... | collective-permute-start | bytes 1572872 | tf_op jit(solution)/shard_map/ppermute | solution.py:385
  173.4 2.7 %collective-permute-start.28 = (bf16[128,4096]{1,0:T(8,128)(2,1)S(1)}, bf16[128,4096]{1,0:T(8,128)(2,1)S(1)}, u32[]{:S(2)}, u32[]{:S(2)}) collective-permute-start(bf16[128,4096]{1,0:T(8,128)(2,1)S(1)} %get-tuple-element.50), channel_id=1, source_target_pairs={{0,16},{16,0},{32,48},{48,32},{64,80},{80,64},{96,112},{112,96},{1... | collective-permute-start | bytes 3145736 | tf_op jit(solution)/shard_map/ppermute | solution.py:52
  176.4 15.6 %collective-permute-start.31 = (bf16[64,4096]{1,0:T(8,128)(2,1)S(1)}, bf16[64,4096]{1,0:T(8,128)(2,1)S(1)}, u32[]{:S(2)}, u32[]{:S(2)}) collective-permute-start(bf16[64,4096]{1,0:T(8,128)(2,1)S(1)} %get-tuple-element.51), channel_id=1, source_target_pairs={{0,32},{16,48},{32,64},{48,80},{64,96},{80,112},{96,0},{112,16},{1... | collective-permute-start | bytes 1572872 | tf_op jit(solution)/shard_map/ppermute | solution.py:390
  177.1 18.6 %collective-permute-start.15 = (bf16[128,4096]{1,0:T(8,128)(2,1)S(1)}, bf16[128,4096]{1,0:T(8,128)(2,1)S(1)}, u32[]{:S(2)}, u32[]{:S(2)}) collective-permute-start(bf16[128,4096]{1,0:T(8,128)(2,1)S(1)} %get-tuple-element.34), channel_id=1, source_target_pairs={{0,16},{16,0},{32,48},{48,32},{64,80},{80,64},{96,112},{112,96},{1... | collective-permute-start | bytes 3145736 | tf_op jit(solution)/shard_map/ppermute | solution.py:52
  177.1 15.2 %collective-permute-start.29 = (bf16[64,4096]{1,0:T(8,128)(2,1)S(1)}, bf16[64,4096]{1,0:T(8,128)(2,1)S(1)}, u32[]{:S(2)}, u32[]{:S(2)}) collective-permute-start(bf16[64,4096]{1,0:T(8,128)(2,1)S(1)} %get-tuple-element.52), channel_id=1, source_target_pairs={{0,96},{16,112},{32,0},{48,16},{64,32},{80,48},{96,64},{112,80},{1... | collective-permute-start | bytes 1572872 | tf_op jit(solution)/shard_map/ppermute | solution.py:391
  192.2 14.7 %collective-permute-start.32 = (bf16[64,4096]{1,0:T(8,128)(2,1)S(1)}, bf16[64,4096]{1,0:T(8,128)(2,1)S(1)}, u32[]{:S(2)}, u32[]{:S(2)}) collective-permute-start(bf16[64,4096]{1,0:T(8,128)(2,1)S(1)} %fusion.2), channel_id=1, source_target_pairs={{0,32},{16,48},{32,64},{48,80},{64,96},{80,112},{96,0},{112,16},{1... | collective-permute-start | bytes 1572872 | tf_op jit(solution)/shard_map/ppermute | solution.py:395
  192.4 14.5 %collective-permute-start.30 = (bf16[64,4096]{1,0:T(8,128)(2,1)S(1)}, bf16[64,4096]{1,0:T(8,128)(2,1)S(1)}, u32[]{:S(2)}, u32[]{:S(2)}) collective-permute-start(bf16[64,4096]{1,0:T(8,128)(2,1)S(1)} %fusion.3), channel_id=1, source_target_pairs={{0,96},{16,112},{32,0},{48,16},{64,32},{80,48},{96,64},{112,80},{1... | collective-permute-start | bytes 1572872 | tf_op jit(solution)/shard_map/ppermute | solution.py:394
  208.6 3.8 %copy-start.12 = (bf16[4,4,2]{1,2,0:T(2,128)(2,1)S(1)}, bf16[4,4,2]{1,2,0:T(2,128)(2,1)}, u32[]{:S(2)}) copy-start(bf16[4,4,2]{1,2,0:T(2,128)(2,1)} %param.30) | copy-start | bytes 196
  208.6 20.1 %all-to-all-start.2 = ((bf16[16,8,4096]{2,1,0:T(8,128)(2,1)}), bf16[16,8,4096]{2,1,0:T(8,128)(2,1)S(1)}, u32[]{:S(2)}, u32[]{:S(2)}) async-start(bf16[16,8,4096]{2,1,0:T(8,128)(2,1)} %fusion.1), calls=%async_computation.2 | async-start | bytes 2097152 | tf_op jit(solution)/shard_map/all_to_all | solution.py:459

commit v7 on v6

--- a/solution.py
+++ b/solution.py
@@ -29,10 +29,6 @@
 
 def x_shift(by):
     return [(x * 2 + c, (x + by) % 4 * 2 + c) for x in range(4) for c in range(2)]
-
-
-def x_onward(by):
-    return [(x * 2 + c, (x + by) * 2 + c) for x in range(4 - by) for c in range(2)]
 
 
 CORE = [(x * 2 + c, x * 2 + 1 - c) for x in range(4) for c in range(2)]
@@ -156,7 +152,7 @@
 
 
 def mixer_out_kernel(
-    core,
+    section,
     *refs,
 ):
     earlier, refs = refs[:7], refs[7:]
@@ -174,15 +170,19 @@
         taken,
         scanned,
         weight,
+        finished,
         arrived,
+        left,
     ) = refs
     copy = pltpu.make_async_copy(out_weight, weight, arrived)
     copy.start()
-    first = core[0] == 0
+    first = section[0] % 2 == 0
     partner = earlier[3][...].astype(F32)
     order = [jnp.where(first, 0.0, partner)]
     for by in (1, 2, 3):
-        mine, theirs = earlier[by - 1][...].astype(F32), earlier[3 + by][...].astype(F32)
+        before = section[0] >= 2 * by
+        mine = jnp.where(before, earlier[by - 1][...].astype(F32), 0.0)
+        theirs = jnp.where(before, earlier[3 + by][...].astype(F32), 0.0)
         order = [jnp.where(first, mine, theirs), jnp.where(first, theirs, mine)] + order
     for index, packed in enumerate(order):
         both = packed[DOCS * STATE :]
@@ -222,10 +222,19 @@
         document_major(True), mixed.astype(BF16), preferred_element_type=F32
     ).astype(BF16)
     copy.wait()
-    for low in range(0, D, 1024):
-        rows[:, low : low + 1024] = jnp.dot(
+    leaving = []
+    for index, low in enumerate(range(0, D, 1024)):
+        finished[index] = jnp.dot(
             ordered, weight[:, low : low + 1024], preferred_element_type=F32
         ).astype(BF16)
+        leaving.append(
+            pltpu.make_async_copy(
+                finished.at[index], rows.at[:, pl.ds(low, 1024)], left.at[index]
+            )
+        )
+        leaving[-1].start()
+    for copy in leaving:
+        copy.wait()
 
 
 def in_hbm(*values):
@@ -281,24 +290,26 @@
     )(*parts, inner, *in_hbm(dtproj, dt_bias, a_log))
 
 
-def mixer_out(core, earlier, step, states, inner, a_log, skip, zin, out_weight):
+def mixer_out(section, earlier, step, states, inner, a_log, skip, zin, out_weight):
     channels = inner.shape[1]
     return pl.pallas_call(
         mixer_out_kernel,
         out_shape=jax.ShapeDtypeStruct((TOKENS, D), BF16),
         in_specs=[whole(pltpu.SMEM)] + [whole()] * 13 + [whole(pltpu.HBM)],
-        out_specs=whole(),
+        out_specs=whole(pltpu.HBM),
         scratch_shapes=[
             pltpu.VMEM((64, channels), F32),
             pltpu.VMEM((7, DOCS * STATE, channels), F32),
             pltpu.VMEM((TOKENS, channels), F32),
             pltpu.VMEM((TOKENS, channels), F32),
             pltpu.VMEM(out_weight.shape, BF16),
+            pltpu.VMEM((D // 1024, TOKENS, 1024), BF16),
             pltpu.SemaphoreType.DMA,
+            pltpu.SemaphoreType.DMA((D // 1024,)),
         ],
         compiler_params=pltpu.CompilerParams(vmem_limit_bytes=32 << 20),
         name="mixer_out",
-    )(core, *earlier, step, states, inner, a_log, skip, zin, *in_hbm(out_weight))
+    )(section, *earlier, step, states, inner, a_log, skip, zin, *in_hbm(out_weight))
 
 
 def expert_kernel(count, *refs):
@@ -389,14 +400,16 @@
     far_sum = paired(*far_out).astype(BF16)
     for_right = lax.ppermute(far_sum[:half], "seq", x_shift(1))
     for_left = lax.ppermute(far_sum[half:], "seq", x_shift(-1))
+    own_sum = paired(*own_out)
     to_left = left_sum[half:] + for_left.astype(F32)
     to_right = right_sum[:half] + for_right.astype(F32)
+    first_half = own_sum[:half] + from_right.astype(F32)
+    second_half = own_sum[half:] + from_left.astype(F32)
+    first_half, second_half = lax.optimization_barrier((first_half, second_half))
     then_right = lax.ppermute(to_left.astype(BF16), "seq", x_shift(-1))
     then_left = lax.ppermute(to_right.astype(BF16), "seq", x_shift(1))
-    return (
-        paired(*own_out)
-        + jnp.concatenate([from_right, then_right]).astype(F32)
-        + jnp.concatenate([then_left, from_left]).astype(F32)
+    return jnp.concatenate(
+        [first_half + then_left.astype(F32), second_half + then_right.astype(F32)]
     )
 
 
@@ -427,9 +440,9 @@
     projected = sum(part.astype(F32) for part in along_z).astype(BF16)
     parts = [projected] + from_others(projected, y_shift)
     step, states, packed = section_scan(parts, dtproj_weight, dt_bias[None], a_log, inner)
-    columns = [lax.ppermute(packed, "seq", x_onward(by)) for by in (1, 2, 3)]
+    columns = [lax.ppermute(packed, "seq", x_shift(by)) for by in (1, 2, 3)]
     partial_rows = mixer_out(
-        (lax.axis_index("seq") % 2).reshape(1),
+        lax.axis_index("seq").reshape(1),
         columns + [swapped(packed)] + [swapped(column) for column in columns],
         step,
         states,

time: 231 us -> 229 us (level)
  starting transfers between devices: 50.4 us -> 46.4 us
    ppermute x1, waiting for transfers between devices: 0.29 us -> 3.57 us  [experts(): from_right = lax.ppermute(left_sum[:half].astype(BF16), 'seq', x_shift(-1))]
    ppermute x3, starting transfers between devices: 7.32 us -> 4.88 us  [per_device(): columns = [lax.ppermute(packed, 'seq', x_shift(by)) for by in (1, 2, 3)]]
  transfers between devices with their start and end apart: 35 -> 35, of which waited for: 17 -> 20; matrix products, arithmetic and copies ran while one was open for 1% -> 2% of each run, Pallas kernels for 11% -> 11%
where the time goes in v7:
time: 229 us
  waiting for transfers between devices  105 us (46%)
  starting transfers between devices  46.4 us (20%)
  Pallas kernels  38.4 us (17%)
  blocking collectives  21.2 us (9%)
  local copies, waits for them, and re-layouts  12.1 us (5%)
  other arithmetic  4.02 us (2%)
    all_to_all x1, waiting for transfers between devices, per_device(): lax.all_to_all(partial_rows, 'exp', split_axis=0, concat_axis=0, tiled=True)  29.8 us
    pallas_call x4, Pallas kernels, expert_block(): pl.pallas_call(lambda *refs: expert_kernel(len(parts), *refs), out_shape=...  25.1 us
    all_to_all x1, blocking collectives, per_device(): lax.all_to_all(jnp.tile(outgoing, (splits, 1)), 'exp', split_axis=0, conc...  21.2 us
    all_to_all x1, waiting for transfers between devices, per_device(): lax.all_to_all(own_rows.astype(BF16), 'exp', split_axis=0, concat_axis=0,...  15.7 us
    ppermute x6, starting transfers between devices, from_others(): return [lax.ppermute(value, 'exp', shift(by)) for by in (1, 2, 3)]  13 us
    ppermute x6, waiting for transfers between devices, from_others(): return [lax.ppermute(value, 'exp', shift(by)) for by in (1, 2, 3)]  12.2 us
    ppermute x1, waiting for transfers between devices, experts(): for_right = lax.ppermute(far_sum[:half], 'seq', x_shift(1))  11.6 us
    ppermute x1, waiting for transfers between devices, experts(): then_left = lax.ppermute(to_right.astype(BF16), 'seq', x_shift(1))  10.9 us
  transfers between devices with their start and end apart: 35, of which 20 were waited for; matrix products, arithmetic and copies ran while one was open for 2% of the time, Pallas kernels for 11%

profile of v7, /device:TPU:0, one launch (start us, length us, event | category | flops | bytes accessed | tf_op | source)
XLA Modules:
  0.0 228.8 jit_solution(654227073717550543)
XLA Ops:
  0.0 0.8 slice.38
  0.8 1.3 collective-permute-start
  2.1 1.0 reshape.84.xin
  3.1 1.5 mixer_in.1
  4.6 2.5 %collective-permute-start.1 = (bf16[288,256]{1,0:T(8,128)(2,1)S(1)}, bf16[288,256]{1,0:T(8,128)(2,1)S(1)}, u32[]{:S(2)}, u32[]{:S(2)}) collective-permute-start(bf16[288,256]{1,0:T(8,128)(2,1)S(1)} %get-tuple-element.30), channel_id=1, source_target_pairs={{0,1},{1,2},{2,3},{3,0},{4,5},{5,6},{6,7},{7,4},{8,9},{9,10},{10,1... | collective-permute-start | bytes 442376 | tf_op jit(solution)/shard_map/ppermute | solution.py:44
  7.2 3.6 %collective-permute-start.2 = (bf16[288,256]{1,0:T(8,128)(2,1)S(1)}, bf16[288,256]{1,0:T(8,128)(2,1)S(1)}, u32[]{:S(2)}, u32[]{:S(2)}) collective-permute-start(bf16[288,256]{1,0:T(8,128)(2,1)S(1)} %get-tuple-element.30), channel_id=1, source_target_pairs={{0,2},{1,3},{2,0},{3,1},{4,6},{5,7},{6,4},{7,5},{8,10},{9,11},{10,... | collective-permute-start | bytes 442376 | tf_op jit(solution)/shard_map/ppermute | solution.py:44
  10.7 1.0 collective-permute-start.3
  11.8 1.1 collective-permute-done.1
  12.9 4.9 %collective-permute-done.2 = bf16[288,256]{1,0:T(8,128)(2,1)S(1)} collective-permute-done((bf16[288,256]{1,0:T(8,128)(2,1)S(1)}, bf16[288,256]{1,0:T(8,128)(2,1)S(1)}, u32[]{:S(2)}, u32[]{:S(2)}) %collective-permute-start.2) | collective-permute-done | bytes 147488 | tf_op jit(solution)/shard_map/ppermute | solution.py:44
  17.9 1.6 collective-permute-start.4
  19.5 2.9 %collective-permute-start.5 = (bf16[288,256]{1,0:T(8,128)(2,1)S(1)}, bf16[288,256]{1,0:T(8,128)(2,1)S(1)}, u32[]{:S(2)}, u32[]{:S(2)}) collective-permute-start(bf16[288,256]{1,0:T(8,128)(2,1)S(1)} %add_convert_fusion.3.p0), channel_id=1, source_target_pairs={{0,8},{1,9},{2,10},{3,11},{4,12},{5,13},{6,14},{7,15},{8,0},{9,1},... | collective-permute-start | bytes 442376 | tf_op jit(solution)/shard_map/ppermute | solution.py:44
  22.5 1.3 collective-permute-start.6
  23.8 1.8 collective-permute-done.4.p1
  25.6 4.3 %collective-permute-done.5.p2 = bf16[288,256]{1,0:T(8,128)(2,1)S(1)} collective-permute-done((bf16[288,256]{1,0:T(8,128)(2,1)S(1)}, bf16[288,256]{1,0:T(8,128)(2,1)S(1)}, u32[]{:S(2)}, u32[]{:S(2)}) %collective-permute-start.5) | collective-permute-done | bytes 147488 | tf_op jit(solution)/shard_map/ppermute | solution.py:44
  29.9 4.0 %section_scan.1 = (f32[256,512]{1,0:T(8,128)S(1)}, f32[32,256]{1,0:T(8,128)S(1)}, bf16[72,512]{1,0:T(8,128)(2,1)S(1)}) custom-call(bf16[288,256]{1,0:T(8,128)(2,1)S(1)} %add_convert_fusion.3.p0, bf16[288,256]{1,0:T(8,128)(2,1)S(1)} %collective-permute-done.4.p1, bf16[288,256]{1,0:T(8,128)(2,1)S(1)} %collective-permute-done.5.p2, ...), custom_call_target="tpu_custom_call" | custom-call | tf_op jit(solution)/shard_map/section_scan/pallas_call | solution.py:272
  33.9 1.1 collective-permute-start.7
  35.1 1.2 collective-permute-start.8
  36.3 2.5 %collective-permute-start.9 = (bf16[72,512]{1,0:T(8,128)(2,1)S(1)}, bf16[72,512]{1,0:T(8,128)(2,1)S(1)}, u32[]{:S(2)}, u32[]{:S(2)}) collective-permute-start(bf16[72,512]{1,0:T(8,128)(2,1)S(1)} %get-tuple-element.32), channel_id=1, source_target_pairs={{0,96},{16,112},{32,0},{48,16},{64,32},{80,48},{96,64},{112,80},{1... | collective-permute-start | bytes 221192 | tf_op jit(solution)/shard_map/ppermute | solution.py:443
  38.8 1.2 collective-permute-done.7.refs_0_
  40.0 0.9 collective-permute-done.8.refs_1_
  40.9 0.4 collective-permute-done.9.refs_2_
  41.5 0.7 collective-permute-done.12.refs_5_
  42.2 0.4 collective-permute-done.13.refs_6_
  42.6 7.7 %mixer_out.1 = bf16[256,4096]{1,0:T(8,128)(2,1)} custom-call(s32[1]{0:T(128)} %bitcast.section, bf16[72,512]{1,0:T(8,128)(2,1)S(1)} %collective-permute-done.7.refs_0_, bf16[72,512]{1,0:T(8,128)(2,1)S(1)} %collective-permute-done.8.refs_1_, bf16[72,512]{1,0:T(8,128)(2,1)S(1)} %collective-permute-done.9.refs_2_, ...), custom_call_target="tpu_custom_call" | custom-call | tf_op jit(solution)/shard_map/mixer_out/pallas_call | solution.py:295
  50.4 6.0 %all-to-all-start = ((bf16[16,16,4096]{2,1,0:T(8,128)(2,1)}), bf16[16,16,4096]{2,1,0:T(8,128)(2,1)S(1)}, u32[]{:S(2)}, u32[]{:S(2)}) async-start(bf16[16,16,4096]{2,1,0:T(8,128)(2,1)} %bitcast.5), calls=%async_computation | async-start | bytes 4194304 | tf_op jit(solution)/shard_map/all_to_all | solution.py:455
  57.4 29.8 %all-to-all-done = bf16[16,16,4096]{2,1,0:T(8,128)(2,1)S(1)} async-done(((bf16[16,16,4096]{2,1,0:T(8,128)(2,1)}), bf16[16,16,4096]{2,1,0:T(8,128)(2,1)S(1)}, u32[]{:S(2)}, u32[]{:S(2)}) %all-to-all-start) | async-done | bytes 2097184 | tf_op jit(solution)/shard_map/all_to_all | solution.py:455
  87.2 0.3 convert_reduce_fusion
  87.9 0.3 convolution_convert_fusion
  88.3 21.2 %all_to_all.26 = bf16[16,8,4096]{2,1,0:T(8,128)(2,1)S(1)} all-to-all(bf16[16,8,4096]{2,1,0:T(8,128)(2,1)S(1)} %bitcast.26), channel_id=1, replica_groups=mesh['seq'=8,'exp'=16] {'exp'}, dimensions={0} | all-to-all | bytes 2097152 | tf_op jit(solution)/shard_map/all_to_all | solution.py:468
  109.6 0.4 collective-permute-start.16
  110.0 2.8 %collective-permute-start.17 = (bf16[128,4096]{1,0:T(8,128)(2,1)S(1)}, bf16[128,4096]{1,0:T(8,128)(2,1)S(1)}, u32[]{:S(2)}, u32[]{:S(2)}) collective-permute-start(bf16[128,4096]{1,0:T(8,128)(2,1)S(1)} %bitcast.22), channel_id=1, source_target_pairs={{0,96},{16,112},{32,0},{48,16},{64,32},{80,48},{96,64},{112,80},{1... | collective-permute-start | bytes 3145736 | tf_op jit(solution)/shard_map/ppermute | solution.py:385
  112.8 2.8 %copy-done = bf16[1,4096,768]{2,1,0:T(8,128)(2,1)S(1)} copy-done((bf16[1,4096,768]{2,1,0:T(8,128)(2,1)S(1)}, bf16[1,4096,768]{2,1,0:T(8,128)(2,1)}, u32[]{:S(2)}) %copy-start) | copy-done | bytes 6291480
  115.6 2.8 %copy-done.2 = bf16[1,4096,768]{2,1,0:T(8,128)(2,1)S(1)} copy-done((bf16[1,4096,768]{2,1,0:T(8,128)(2,1)S(1)}, bf16[1,4096,768]{2,1,0:T(8,128)(2,1)}, u32[]{:S(2)}) %copy-start.2) | copy-done | bytes 6291480
  118.4 2.8 %copy-done.4 = bf16[1,768,4096]{2,1,0:T(8,128)(2,1)S(1)} copy-done((bf16[1,768,4096]{2,1,0:T(8,128)(2,1)S(1)}, bf16[1,768,4096]{2,1,0:T(8,128)(2,1)}, u32[]{:S(2)}) %copy-start.4) | copy-done | bytes 6291480
  121.2 6.3 %experts_256.4 = (bf16[128,4096]{1,0:T(8,128)(2,1)S(1)}, bf16[128,4096]{1,0:T(8,128)(2,1)S(1)}) custom-call(bf16[128,4096]{1,0:T(8,128)(2,1)S(1)} %bitcast.23, bf16[128,4096]{1,0:T(8,128)(2,1)S(1)} %collective-permute-done.14.refs_1_, bf16[1,4096,768]{2,1,0:T(8,128)(2,1)S(1)} %copy-done, bf16[1,4096,768]{2,1,0:T(8,128)(2,1)S(1)} %copy-done.2, ...), custom_call_target="tpu_custom_call" | custom-call | flops 4831838208 | bytes 4194304 | tf_op jit(solution)/shard_map/experts_256/pallas_call | solution.py:344
  127.5 8.9 %collective-permute-done.16.refs_0_ = bf16[128,4096]{1,0:T(8,128)(2,1)S(1)} collective-permute-done((bf16[128,4096]{1,0:T(8,128)(2,1)S(1)}, bf16[128,4096]{1,0:T(8,128)(2,1)S(1)}, u32[]{:S(2)}, u32[]{:S(2)}) %collective-permute-start.16) | collective-permute-done | bytes 1048608 | tf_op jit(solution)/shard_map/ppermute | solution.py:384
  136.3 0.5 collective-permute-start.20
  136.9 0.3 collective-permute-start.18
  137.2 3.0 %collective-permute-start.19 = (bf16[64,4096]{1,0:T(8,128)(2,1)S(1)}, bf16[64,4096]{1,0:T(8,128)(2,1)S(1)}, u32[]{:S(2)}, u32[]{:S(2)}) collective-permute-start(bf16[64,4096]{1,0:T(8,128)(2,1)S(1)} %slice.42), channel_id=1, source_target_pairs={{0,96},{16,112},{32,0},{48,16},{64,32},{80,48},{96,64},{112,80},{1... | collective-permute-start | bytes 1572872 | tf_op jit(solution)/shard_map/ppermute | solution.py:390
  140.3 6.3 %experts_256.6 = (bf16[128,4096]{1,0:T(8,128)(2,1)S(1)}, bf16[128,4096]{1,0:T(8,128)(2,1)S(1)}) custom-call(bf16[128,4096]{1,0:T(8,128)(2,1)S(1)} %collective-permute-done.17.refs_0_, bf16[128,4096]{1,0:T(8,128)(2,1)S(1)} %collective-permute-done.21.refs_1_, bf16[1,4096,768]{2,1,0:T(8,128)(2,1)S(1)} %copy-done.1, bf16[1,4096,768]{2,1,0:T(8,128)(2,1)S(1)} %copy-done.3, ...), custom_call_target="tpu_custom_call" | custom-call | flops 4831838208 | bytes 4194304 | tf_op jit(solution)/shard_map/experts_256/pallas_call | solution.py:344
  146.6 6.3 %experts_256.5 = (bf16[128,4096]{1,0:T(8,128)(2,1)S(1)}, bf16[128,4096]{1,0:T(8,128)(2,1)S(1)}) custom-call(bf16[128,4096]{1,0:T(8,128)(2,1)S(1)} %collective-permute-done.16.refs_0_, bf16[128,4096]{1,0:T(8,128)(2,1)S(1)} %collective-permute-done.20.refs_1_, bf16[1,4096,768]{2,1,0:T(8,128)(2,1)S(1)} %copy-done.1, bf16[1,4096,768]{2,1,0:T(8,128)(2,1)S(1)} %copy-done.3, ...), custom_call_target="tpu_custom_call" | custom-call | flops 4831838208 | bytes 4194304 | tf_op jit(solution)/shard_map/experts_256/pallas_call | solution.py:344
  153.0 0.5 collective-permute-start.24
  153.6 0.4 collective-permute-start.26
  154.1 1.5 collective-permute-done.22
  155.6 0.3 convert_add_fusion.1
  156.0 2.2 collective-permute-start.23
  158.5 0.3 collective-permute-start.25
  158.8 0.6 collective-permute-done.26.refs_2_
  159.4 0.7 collective-permute-done.27.refs_3_
  160.1 6.3 %experts_256.7 = (bf16[128,4096]{1,0:T(8,128)(2,1)S(1)}, bf16[128,4096]{1,0:T(8,128)(2,1)S(1)}) custom-call(bf16[64,4096]{1,0:T(8,128)(2,1)S(1)} %collective-permute-done.18.refs_0_, bf16[64,4096]{1,0:T(8,128)(2,1)S(1)} %collective-permute-done.19.refs_1_, bf16[64,4096]{1,0:T(8,128)(2,1)S(1)} %collective-permute-done.26.refs_2_, ...), custom_call_target="tpu_custom_call" | custom-call | flops 4831838208 | bytes 4194304 | tf_op jit(solution)/shard_map/experts_256/pallas_call | solution.py:344
  166.4 3.6 %collective-permute-done.23 = bf16[64,4096]{1,0:T(8,128)(2,1)S(1)} collective-permute-done((bf16[64,4096]{1,0:T(8,128)(2,1)S(1)}, bf16[64,4096]{1,0:T(8,128)(2,1)S(1)}, u32[]{:S(2)}, u32[]{:S(2)}) %collective-permute-start.23) | collective-permute-done | bytes 524320 | tf_op jit(solution)/shard_map/ppermute | solution.py:396
  170.0 3.7 %collective-permute-done.25 = bf16[64,4096]{1,0:T(8,128)(2,1)S(1)} collective-permute-done((bf16[64,4096]{1,0:T(8,128)(2,1)S(1)}, bf16[64,4096]{1,0:T(8,128)(2,1)S(1)}, u32[]{:S(2)}, u32[]{:S(2)}) %collective-permute-start.25) | collective-permute-done | bytes 524320 | tf_op jit(solution)/shard_map/ppermute | solution.py:397
  173.7 0.3 convert_add_fusion.2
  173.9 2.4 %collective-permute-done.28 = bf16[128,4096]{1,0:T(8,128)(2,1)S(1)} collective-permute-done((bf16[128,4096]{1,0:T(8,128)(2,1)S(1)}, bf16[128,4096]{1,0:T(8,128)(2,1)S(1)}, u32[]{:S(2)}, u32[]{:S(2)}) %collective-permute-start.28) | collective-permute-done | bytes 1048608 | tf_op jit(solution)/shard_map/ppermute | solution.py:48
  176.7 0.3 slice_add_fusion.2
  177.0 3.3 %collective-permute-start.31 = (bf16[64,4096]{1,0:T(8,128)(2,1)S(1)}, bf16[64,4096]{1,0:T(8,128)(2,1)S(1)}, u32[]{:S(2)}, u32[]{:S(2)}) collective-permute-start(bf16[64,4096]{1,0:T(8,128)(2,1)S(1)} %get-tuple-element.58), channel_id=1, source_target_pairs={{0,96},{16,112},{32,0},{48,16},{64,32},{80,48},{96,64},{112,80},{1... | collective-permute-start | bytes 1572872 | tf_op jit(solution)/shard_map/ppermute | solution.py:402
  180.3 11.6 %collective-permute-done.29 = bf16[64,4096]{1,0:T(8,128)(2,1)S(1)} collective-permute-done((bf16[64,4096]{1,0:T(8,128)(2,1)S(1)}, bf16[64,4096]{1,0:T(8,128)(2,1)S(1)}, u32[]{:S(2)}, u32[]{:S(2)}) %collective-permute-start.29) | collective-permute-done | bytes 524320 | tf_op jit(solution)/shard_map/ppermute | solution.py:401
  192.2 3.3 %collective-permute-start.32 = (bf16[64,4096]{1,0:T(8,128)(2,1)S(1)}, bf16[64,4096]{1,0:T(8,128)(2,1)S(1)}, u32[]{:S(2)}, u32[]{:S(2)}) collective-permute-start(bf16[64,4096]{1,0:T(8,128)(2,1)S(1)} %fusion.1), channel_id=1, source_target_pairs={{0,96},{16,112},{32,0},{48,16},{64,32},{80,48},{96,64},{112,80},{1... | collective-permute-start | bytes 1572872 | tf_op jit(solution)/shard_map/ppermute | solution.py:409
  195.5 10.9 %collective-permute-done.30 = bf16[64,4096]{1,0:T(8,128)(2,1)S(1)} collective-permute-done((bf16[64,4096]{1,0:T(8,128)(2,1)S(1)}, bf16[64,4096]{1,0:T(8,128)(2,1)S(1)}, u32[]{:S(2)}, u32[]{:S(2)}) %collective-permute-start.30) | collective-permute-done | bytes 524320 | tf_op jit(solution)/shard_map/ppermute | solution.py:410
  206.7 1.1 maximum_bitcast_fusion
  207.7 3.7 %all-to-all-start.2 = ((bf16[16,8,4096]{2,1,0:T(8,128)(2,1)}), bf16[16,8,4096]{2,1,0:T(8,128)(2,1)S(1)}, u32[]{:S(2)}, u32[]{:S(2)}) async-start(bf16[16,8,4096]{2,1,0:T(8,128)(2,1)} %maximum_bitcast_fusion), calls=%async_computation.2 | async-start | bytes 2097152 | tf_op jit(solution)/shard_map/all_to_all | solution.py:472
  211.6 15.7 %all-to-all-done.2 = bf16[16,8,4096]{2,1,0:T(8,128)(2,1)S(1)} async-done(((bf16[16,8,4096]{2,1,0:T(8,128)(2,1)}), bf16[16,8,4096]{2,1,0:T(8,128)(2,1)S(1)}, u32[]{:S(2)}, u32[]{:S(2)}) %all-to-all-start.2) | async-done | bytes 1048608 | tf_op jit(solution)/shard_map/all_to_all | solution.py:472
  227.5 0.6 fusion
  228.1 0.7 reshape.86
  (87 shorter events, 3.6 us)
Async XLA Ops:
  0.0 42.6 %copy-start.6 = (f32[16,512]{1,0:T(8,128)S(1)}, f32[16,512]{1,0:T(8,128)}, u32[]{:S(2)}) copy-start(f32[16,512]{1,0:T(8,128)} %refs_10_.1) | copy-start | bytes 98308
  0.0 41.4 %copy-start.9 = (bf16[64,4,512]{2,1,0:T(4,128)(2,1)S(1)}, bf16[64,4,512]{2,1,0:T(4,128)(2,1)}, u32[]{:S(2)}) copy-start(bf16[64,4,512]{2,1,0:T(4,128)(2,1)} %param.18) | copy-start | bytes 786436
  0.0 42.6 %copy-start.7 = (f32[512]{0:T(512)S(1)}, f32[512]{0:T(512)}, u32[]{:S(2)}) copy-start(f32[512]{0:T(512)} %param.25) | copy-start | bytes 6148
  0.8 2.3 %collective-permute-start = (bf16[12,512]{1,0:T(8,128)(2,1)S(1)}, bf16[12,512]{1,0:T(8,128)(2,1)S(1)}, u32[]{:S(2)}, u32[]{:S(2)}) collective-permute-start(bf16[12,512]{1,0:T(8,128)(2,1)S(1)} %slice.39), channel_id=1, source_target_pairs={{0,16},{16,32},{32,48},{48,64},{64,80},{80,96},{96,112},{1,17},{17... | collective-permute-start | bytes 36872 | tf_op jit(solution)/shard_map/ppermute | solution.py:40
  4.6 8.2 %collective-permute-start.1 = (bf16[288,256]{1,0:T(8,128)(2,1)S(1)}, bf16[288,256]{1,0:T(8,128)(2,1)S(1)}, u32[]{:S(2)}, u32[]{:S(2)}) collective-permute-start(bf16[288,256]{1,0:T(8,128)(2,1)S(1)} %get-tuple-element.30), channel_id=1, source_target_pairs={{0,1},{1,2},{2,3},{3,0},{4,5},{5,6},{6,7},{7,4},{8,9},{9,10},{10,1... | collective-permute-start | bytes 442376 | tf_op jit(solution)/shard_map/ppermute | solution.py:44
  7.2 10.7 %collective-permute-start.2 = (bf16[288,256]{1,0:T(8,128)(2,1)S(1)}, bf16[288,256]{1,0:T(8,128)(2,1)S(1)}, u32[]{:S(2)}, u32[]{:S(2)}) collective-permute-start(bf16[288,256]{1,0:T(8,128)(2,1)S(1)} %get-tuple-element.30), channel_id=1, source_target_pairs={{0,2},{1,3},{2,0},{3,1},{4,6},{5,7},{6,4},{7,5},{8,10},{9,11},{10,... | collective-permute-start | bytes 442376 | tf_op jit(solution)/shard_map/ppermute | solution.py:44
  10.7 7.1 %collective-permute-start.3 = (bf16[288,256]{1,0:T(8,128)(2,1)S(1)}, bf16[288,256]{1,0:T(8,128)(2,1)S(1)}, u32[]{:S(2)}, u32[]{:S(2)}) collective-permute-start(bf16[288,256]{1,0:T(8,128)(2,1)S(1)} %get-tuple-element.30), channel_id=1, source_target_pairs={{0,3},{1,0},{2,1},{3,2},{4,7},{5,4},{6,5},{7,6},{8,11},{9,8},{10,9... | collective-permute-start | bytes 442376 | tf_op jit(solution)/shard_map/ppermute | solution.py:44
  17.9 7.7 %collective-permute-start.4 = (bf16[288,256]{1,0:T(8,128)(2,1)S(1)}, bf16[288,256]{1,0:T(8,128)(2,1)S(1)}, u32[]{:S(2)}, u32[]{:S(2)}) collective-permute-start(bf16[288,256]{1,0:T(8,128)(2,1)S(1)} %add_convert_fusion.3.p0), channel_id=1, source_target_pairs={{0,4},{1,5},{2,6},{3,7},{4,8},{5,9},{6,10},{7,11},{8,12},{9,13},{1... | collective-permute-start | bytes 442376 | tf_op jit(solution)/shard_map/ppermute | solution.py:44
  19.5 10.4 %collective-permute-start.5 = (bf16[288,256]{1,0:T(8,128)(2,1)S(1)}, bf16[288,256]{1,0:T(8,128)(2,1)S(1)}, u32[]{:S(2)}, u32[]{:S(2)}) collective-permute-start(bf16[288,256]{1,0:T(8,128)(2,1)S(1)} %add_convert_fusion.3.p0), channel_id=1, source_target_pairs={{0,8},{1,9},{2,10},{3,11},{4,12},{5,13},{6,14},{7,15},{8,0},{9,1},... | collective-permute-start | bytes 442376 | tf_op jit(solution)/shard_map/ppermute | solution.py:44
  22.5 7.5 %collective-permute-start.6 = (bf16[288,256]{1,0:T(8,128)(2,1)S(1)}, bf16[288,256]{1,0:T(8,128)(2,1)S(1)}, u32[]{:S(2)}, u32[]{:S(2)}) collective-permute-start(bf16[288,256]{1,0:T(8,128)(2,1)S(1)} %add_convert_fusion.3.p0), channel_id=1, source_target_pairs={{0,12},{1,13},{2,14},{3,15},{4,0},{5,1},{6,2},{7,3},{8,4},{9,5},{1... | collective-permute-start | bytes 442376 | tf_op jit(solution)/shard_map/ppermute | solution.py:44
  33.9 6.1 %collective-permute-start.7 = (bf16[72,512]{1,0:T(8,128)(2,1)S(1)}, bf16[72,512]{1,0:T(8,128)(2,1)S(1)}, u32[]{:S(2)}, u32[]{:S(2)}) collective-permute-start(bf16[72,512]{1,0:T(8,128)(2,1)S(1)} %get-tuple-element.32), channel_id=1, source_target_pairs={{0,32},{16,48},{32,64},{48,80},{64,96},{80,112},{96,0},{112,16},{1... | collective-permute-start | bytes 221192 | tf_op jit(solution)/shard_map/ppermute | solution.py:443
  35.1 5.9 %collective-permute-start.8 = (bf16[72,512]{1,0:T(8,128)(2,1)S(1)}, bf16[72,512]{1,0:T(8,128)(2,1)S(1)}, u32[]{:S(2)}, u32[]{:S(2)}) collective-permute-start(bf16[72,512]{1,0:T(8,128)(2,1)S(1)} %get-tuple-element.32), channel_id=1, source_target_pairs={{0,64},{16,80},{32,96},{48,112},{64,0},{80,16},{96,32},{112,48},{1... | collective-permute-start | bytes 221192 | tf_op jit(solution)/shard_map/ppermute | solution.py:443
  36.3 5.1 %collective-permute-start.9 = (bf16[72,512]{1,0:T(8,128)(2,1)S(1)}, bf16[72,512]{1,0:T(8,128)(2,1)S(1)}, u32[]{:S(2)}, u32[]{:S(2)}) collective-permute-start(bf16[72,512]{1,0:T(8,128)(2,1)S(1)} %get-tuple-element.32), channel_id=1, source_target_pairs={{0,96},{16,112},{32,0},{48,16},{64,32},{80,48},{96,64},{112,80},{1... | collective-permute-start | bytes 221192 | tf_op jit(solution)/shard_map/ppermute | solution.py:443
  38.8 2.7 %collective-permute-start.10 = (bf16[72,512]{1,0:T(8,128)(2,1)S(1)}, bf16[72,512]{1,0:T(8,128)(2,1)S(1)}, u32[]{:S(2)}, u32[]{:S(2)}) collective-permute-start(bf16[72,512]{1,0:T(8,128)(2,1)S(1)} %get-tuple-element.32), channel_id=1, source_target_pairs={{0,16},{16,0},{32,48},{48,32},{64,80},{80,64},{96,112},{112,96},{1... | collective-permute-start | bytes 221192 | tf_op jit(solution)/shard_map/ppermute | solution.py:48
  40.0 1.5 collective-permute-start.11
  40.9 1.3 collective-permute-start.12
  41.4 1.3 collective-permute-start.13
  50.4 6.1 %copy-start.8 = (bf16[4,4,4096]{2,1,0:T(4,128)(2,1)S(1)}, bf16[4,4,4096]{2,1,0:T(4,128)(2,1)}, u32[]{:S(2)}) copy-start(bf16[4,4,4096]{2,1,0:T(4,128)(2,1)} %param.27) | copy-start | bytes 393220
  50.4 6.1 %copy-start.11 = (s32[4,4,2]{1,2,0:T(2,128)S(1)}, s32[4,4,2]{1,2,0:T(2,128)}, u32[]{:S(2)}) copy-start(s32[4,4,2]{1,2,0:T(2,128)} %param.29) | copy-start | bytes 388
  50.4 36.8 %all-to-all-start = ((bf16[16,16,4096]{2,1,0:T(8,128)(2,1)}), bf16[16,16,4096]{2,1,0:T(8,128)(2,1)S(1)}, u32[]{:S(2)}, u32[]{:S(2)}) async-start(bf16[16,16,4096]{2,1,0:T(8,128)(2,1)} %bitcast.5), calls=%async_computation | async-start | bytes 4194304 | tf_op jit(solution)/shard_map/all_to_all | solution.py:455
  56.7 31.2 %copy-start.10 = (f32[4096]{0:T(1024)S(1)}, f32[4096]{0:T(1024)}, u32[]{:S(2)}) copy-start(f32[4096]{0:T(1024)} %param.28) | copy-start | bytes 49156
  109.6 3.2 %collective-permute-start.14 = (bf16[128,4096]{1,0:T(8,128)(2,1)S(1)}, bf16[128,4096]{1,0:T(8,128)(2,1)S(1)}, u32[]{:S(2)}, u32[]{:S(2)}) collective-permute-start(bf16[128,4096]{1,0:T(8,128)(2,1)S(1)} %bitcast.20), channel_id=1, source_target_pairs={{0,16},{16,0},{32,48},{48,32},{64,80},{80,64},{96,112},{112,96},{1... | collective-permute-start | bytes 3145736 | tf_op jit(solution)/shard_map/ppermute | solution.py:48
  109.6 26.8 %collective-permute-start.16 = (bf16[128,4096]{1,0:T(8,128)(2,1)S(1)}, bf16[128,4096]{1,0:T(8,128)(2,1)S(1)}, u32[]{:S(2)}, u32[]{:S(2)}) collective-permute-start(bf16[128,4096]{1,0:T(8,128)(2,1)S(1)} %bitcast.21), channel_id=1, source_target_pairs={{0,32},{16,48},{32,64},{48,80},{64,96},{80,112},{96,0},{112,16},{1... | collective-permute-start | bytes 3145736 | tf_op jit(solution)/shard_map/ppermute | solution.py:384
  110.0 26.4 %collective-permute-start.17 = (bf16[128,4096]{1,0:T(8,128)(2,1)S(1)}, bf16[128,4096]{1,0:T(8,128)(2,1)S(1)}, u32[]{:S(2)}, u32[]{:S(2)}) collective-permute-start(bf16[128,4096]{1,0:T(8,128)(2,1)S(1)} %bitcast.22), channel_id=1, source_target_pairs={{0,96},{16,112},{32,0},{48,16},{64,32},{80,48},{96,64},{112,80},{1... | collective-permute-start | bytes 3145736 | tf_op jit(solution)/shard_map/ppermute | solution.py:385
  112.8 2.8 %copy-start = (bf16[1,4096,768]{2,1,0:T(8,128)(2,1)S(1)}, bf16[1,4096,768]{2,1,0:T(8,128)(2,1)}, u32[]{:S(2)}) copy-start(bf16[1,4096,768]{2,1,0:T(8,128)(2,1)} %refs_4_.7) | copy-start | bytes 18874372
  115.6 2.8 %copy-start.2 = (bf16[1,4096,768]{2,1,0:T(8,128)(2,1)S(1)}, bf16[1,4096,768]{2,1,0:T(8,128)(2,1)}, u32[]{:S(2)}) copy-start(bf16[1,4096,768]{2,1,0:T(8,128)(2,1)} %refs_5_.1) | copy-start | bytes 18874372
  118.4 2.8 %copy-start.4 = (bf16[1,768,4096]{2,1,0:T(8,128)(2,1)S(1)}, bf16[1,768,4096]{2,1,0:T(8,128)(2,1)}, u32[]{:S(2)}) copy-start(bf16[1,768,4096]{2,1,0:T(8,128)(2,1)} %refs_6_.1) | copy-start | bytes 18874372
  121.2 19.1 %copy-start.1 = (bf16[1,4096,768]{2,1,0:T(8,128)(2,1)S(1)}, bf16[1,4096,768]{2,1,0:T(8,128)(2,1)}, u32[]{:S(2)}) copy-start(bf16[1,4096,768]{2,1,0:T(8,128)(2,1)} %refs_4_.7) | copy-start | bytes 18874372
  121.2 19.1 %copy-start.3 = (bf16[1,4096,768]{2,1,0:T(8,128)(2,1)S(1)}, bf16[1,4096,768]{2,1,0:T(8,128)(2,1)}, u32[]{:S(2)}) copy-start(bf16[1,4096,768]{2,1,0:T(8,128)(2,1)} %refs_5_.1) | copy-start | bytes 18874372
  121.2 19.1 %copy-start.5 = (bf16[1,768,4096]{2,1,0:T(8,128)(2,1)S(1)}, bf16[1,768,4096]{2,1,0:T(8,128)(2,1)}, u32[]{:S(2)}) copy-start(bf16[1,768,4096]{2,1,0:T(8,128)(2,1)} %refs_6_.1) | copy-start | bytes 18874372
  136.3 3.9 %collective-permute-start.21 = (bf16[128,4096]{1,0:T(8,128)(2,1)S(1)}, bf16[128,4096]{1,0:T(8,128)(2,1)S(1)}, u32[]{:S(2)}, u32[]{:S(2)}) collective-permute-start(bf16[128,4096]{1,0:T(8,128)(2,1)S(1)} %collective-permute-done.17.refs_0_), channel_id=1, source_target_pairs={{0,16},{16,0},{32,48},{48,32},{64,80},{80,64},{96,112},{112,96},{1... | collective-permute-start | bytes 3145736 | tf_op jit(solution)/shard_map/ppermute | solution.py:48
  136.3 10.2 %collective-permute-start.20 = (bf16[128,4096]{1,0:T(8,128)(2,1)S(1)}, bf16[128,4096]{1,0:T(8,128)(2,1)S(1)}, u32[]{:S(2)}, u32[]{:S(2)}) collective-permute-start(bf16[128,4096]{1,0:T(8,128)(2,1)S(1)} %collective-permute-done.16.refs_0_), channel_id=1, source_target_pairs={{0,16},{16,0},{32,48},{48,32},{64,80},{80,64},{96,112},{112,96},{1... | collective-permute-start | bytes 3145736 | tf_op jit(solution)/shard_map/ppermute | solution.py:48
  136.9 15.9 %collective-permute-start.18 = (bf16[64,4096]{1,0:T(8,128)(2,1)S(1)}, bf16[64,4096]{1,0:T(8,128)(2,1)S(1)}, u32[]{:S(2)}, u32[]{:S(2)}) collective-permute-start(bf16[64,4096]{1,0:T(8,128)(2,1)S(1)} %slice.41), channel_id=1, source_target_pairs={{0,32},{16,48},{32,64},{48,80},{64,96},{80,112},{96,0},{112,16},{1... | collective-permute-start | bytes 1572872 | tf_op jit(solution)/shard_map/ppermute | solution.py:389
  137.2 15.7 %collective-permute-start.19 = (bf16[64,4096]{1,0:T(8,128)(2,1)S(1)}, bf16[64,4096]{1,0:T(8,128)(2,1)S(1)}, u32[]{:S(2)}, u32[]{:S(2)}) collective-permute-start(bf16[64,4096]{1,0:T(8,128)(2,1)S(1)} %slice.42), channel_id=1, source_target_pairs={{0,96},{16,112},{32,0},{48,16},{64,32},{80,48},{96,64},{112,80},{1... | collective-permute-start | bytes 1572872 | tf_op jit(solution)/shard_map/ppermute | solution.py:390
  152.9 2.7 %collective-permute-start.22 = (bf16[128,4096]{1,0:T(8,128)(2,1)S(1)}, bf16[128,4096]{1,0:T(8,128)(2,1)S(1)}, u32[]{:S(2)}, u32[]{:S(2)}) collective-permute-start(bf16[128,4096]{1,0:T(8,128)(2,1)S(1)} %get-tuple-element.44), channel_id=1, source_target_pairs={{0,16},{16,0},{32,48},{48,32},{64,80},{80,64},{96,112},{112,96},{1... | collective-permute-start | bytes 3145736 | tf_op jit(solution)/shard_map/ppermute | solution.py:48
  153.0 5.2 %collective-permute-start.24 = (bf16[128,4096]{1,0:T(8,128)(2,1)S(1)}, bf16[128,4096]{1,0:T(8,128)(2,1)S(1)}, u32[]{:S(2)}, u32[]{:S(2)}) collective-permute-start(bf16[128,4096]{1,0:T(8,128)(2,1)S(1)} %get-tuple-element.46), channel_id=1, source_target_pairs={{0,16},{16,0},{32,48},{48,32},{64,80},{80,64},{96,112},{112,96},{1... | collective-permute-start | bytes 3145736 | tf_op jit(solution)/shard_map/ppermute | solution.py:48
  153.5 20.2 %collective-permute-start.15 = (bf16[128,4096]{1,0:T(8,128)(2,1)S(1)}, bf16[128,4096]{1,0:T(8,128)(2,1)S(1)}, u32[]{:S(2)}, u32[]{:S(2)}) collective-permute-start(bf16[128,4096]{1,0:T(8,128)(2,1)S(1)} %get-tuple-element.36), channel_id=1, source_target_pairs={{0,16},{16,0},{32,48},{48,32},{64,80},{80,64},{96,112},{112,96},{1... | collective-permute-start | bytes 3145736 | tf_op jit(solution)/shard_map/ppermute | solution.py:48
  153.6 5.8 %collective-permute-start.26 = (bf16[64,4096]{1,0:T(8,128)(2,1)S(1)}, bf16[64,4096]{1,0:T(8,128)(2,1)S(1)}, u32[]{:S(2)}, u32[]{:S(2)}) collective-permute-start(bf16[64,4096]{1,0:T(8,128)(2,1)S(1)} %collective-permute-done.18.refs_0_), channel_id=1, source_target_pairs={{0,16},{16,0},{32,48},{48,32},{64,80},{80,64},{96,112},{112,96},{1... | collective-permute-start | bytes 1572872 | tf_op jit(solution)/shard_map/ppermute | solution.py:48
  154.0 6.1 %collective-permute-start.27 = (bf16[64,4096]{1,0:T(8,128)(2,1)S(1)}, bf16[64,4096]{1,0:T(8,128)(2,1)S(1)}, u32[]{:S(2)}, u32[]{:S(2)}) collective-permute-start(bf16[64,4096]{1,0:T(8,128)(2,1)S(1)} %collective-permute-done.19.refs_1_), channel_id=1, source_target_pairs={{0,16},{16,0},{32,48},{48,32},{64,80},{80,64},{96,112},{112,96},{1... | collective-permute-start | bytes 1572872 | tf_op jit(solution)/shard_map/ppermute | solution.py:48
  156.0 14.0 %collective-permute-start.23 = (bf16[64,4096]{1,0:T(8,128)(2,1)S(1)}, bf16[64,4096]{1,0:T(8,128)(2,1)S(1)}, u32[]{:S(2)}, u32[]{:S(2)}) collective-permute-start(bf16[64,4096]{1,0:T(8,128)(2,1)S(1)} %slice.69), channel_id=1, source_target_pairs={{0,96},{16,112},{32,0},{48,16},{64,32},{80,48},{96,64},{112,80},{1... | collective-permute-start | bytes 1572872 | tf_op jit(solution)/shard_map/ppermute | solution.py:396
  158.5 15.2 %collective-permute-start.25 = (bf16[64,4096]{1,0:T(8,128)(2,1)S(1)}, bf16[64,4096]{1,0:T(8,128)(2,1)S(1)}, u32[]{:S(2)}, u32[]{:S(2)}) collective-permute-start(bf16[64,4096]{1,0:T(8,128)(2,1)S(1)} %slice.68), channel_id=1, source_target_pairs={{0,32},{16,48},{32,64},{48,80},{64,96},{80,112},{96,0},{112,16},{1... | collective-permute-start | bytes 1572872 | tf_op jit(solution)/shard_map/ppermute | solution.py:397
  173.7 2.7 %collective-permute-start.28 = (bf16[128,4096]{1,0:T(8,128)(2,1)S(1)}, bf16[128,4096]{1,0:T(8,128)(2,1)S(1)}, u32[]{:S(2)}, u32[]{:S(2)}) collective-permute-start(bf16[128,4096]{1,0:T(8,128)(2,1)S(1)} %get-tuple-element.53), channel_id=1, source_target_pairs={{0,16},{16,0},{32,48},{48,32},{64,80},{80,64},{96,112},{112,96},{1... | collective-permute-start | bytes 3145736 | tf_op jit(solution)/shard_map/ppermute | solution.py:48
  176.6 15.2 %collective-permute-start.29 = (bf16[64,4096]{1,0:T(8,128)(2,1)S(1)}, bf16[64,4096]{1,0:T(8,128)(2,1)S(1)}, u32[]{:S(2)}, u32[]{:S(2)}) collective-permute-start(bf16[64,4096]{1,0:T(8,128)(2,1)S(1)} %get-tuple-element.57), channel_id=1, source_target_pairs={{0,32},{16,48},{32,64},{48,80},{64,96},{80,112},{96,0},{112,16},{1... | collective-permute-start | bytes 1572872 | tf_op jit(solution)/shard_map/ppermute | solution.py:401
  177.0 15.1 %collective-permute-start.31 = (bf16[64,4096]{1,0:T(8,128)(2,1)S(1)}, bf16[64,4096]{1,0:T(8,128)(2,1)S(1)}, u32[]{:S(2)}, u32[]{:S(2)}) collective-permute-start(bf16[64,4096]{1,0:T(8,128)(2,1)S(1)} %get-tuple-element.58), channel_id=1, source_target_pairs={{0,96},{16,112},{32,0},{48,16},{64,32},{80,48},{96,64},{112,80},{1... | collective-permute-start | bytes 1572872 | tf_op jit(solution)/shard_map/ppermute | solution.py:402
  192.0 14.4 %collective-permute-start.30 = (bf16[64,4096]{1,0:T(8,128)(2,1)S(1)}, bf16[64,4096]{1,0:T(8,128)(2,1)S(1)}, u32[]{:S(2)}, u32[]{:S(2)}) collective-permute-start(bf16[64,4096]{1,0:T(8,128)(2,1)S(1)} %fusion.2), channel_id=1, source_target_pairs={{0,32},{16,48},{32,64},{48,80},{64,96},{80,112},{96,0},{112,16},{1... | collective-permute-start | bytes 1572872 | tf_op jit(solution)/shard_map/ppermute | solution.py:410
  192.2 14.3 %collective-permute-start.32 = (bf16[64,4096]{1,0:T(8,128)(2,1)S(1)}, bf16[64,4096]{1,0:T(8,128)(2,1)S(1)}, u32[]{:S(2)}, u32[]{:S(2)}) collective-permute-start(bf16[64,4096]{1,0:T(8,128)(2,1)S(1)} %fusion.1), channel_id=1, source_target_pairs={{0,96},{16,112},{32,0},{48,16},{64,32},{80,48},{96,64},{112,80},{1... | collective-permute-start | bytes 1572872 | tf_op jit(solution)/shard_map/ppermute | solution.py:409
  206.7 4.7 %copy-start.12 = (bf16[4,4,2]{1,2,0:T(2,128)(2,1)S(1)}, bf16[4,4,2]{1,2,0:T(2,128)(2,1)}, u32[]{:S(2)}) copy-start(bf16[4,4,2]{1,2,0:T(2,128)(2,1)} %param.30) | copy-start | bytes 196
  207.7 19.6 %all-to-all-start.2 = ((bf16[16,8,4096]{2,1,0:T(8,128)(2,1)}), bf16[16,8,4096]{2,1,0:T(8,128)(2,1)S(1)}, u32[]{:S(2)}, u32[]{:S(2)}) async-start(bf16[16,8,4096]{2,1,0:T(8,128)(2,1)} %maximum_bitcast_fusion), calls=%async_computation.2 | async-start | bytes 2097152 | tf_op jit(solution)/shard_map/all_to_all | solution.py:472

commit v8 on v7

--- a/solution.py
+++ b/solution.py
@@ -68,25 +68,23 @@
     return copies
 
 
-def mixer_in_kernel(xin, edge, *refs):
-    sources, (inner, projected, window, *targets, arrived) = refs[:3], refs[3:]
+def mixer_in_kernel(edge, *refs):
+    sources, (inner, projected, window, acted, *targets, arrived) = refs[:4], refs[4:]
     copies = fetched(sources, targets, arrived)
-    conv_weight, conv_bias, xproj = targets
-    window[16 - edge.shape[0] : 16, :] = edge[...].astype(F32)
-    window[16 : 16 + TOKENS, :] = xin[...].astype(F32)
-    copies[0].wait()
-    copies[1].wait()
-    blocks = []
-    for low in range(0, TOKENS, 64):
-        running = jnp.broadcast_to(conv_bias[...], (64, xin.shape[1]))
-        for offset in range(CONV):
-            tap = window[pl.ds(low + 16 - DOCS * (CONV - 1 - offset), 64), :]
-            running = running + conv_weight[offset : offset + 1, :] * tap
-        blocks.append(jax.nn.silu(running).astype(BF16))
-    by_position = jnp.concatenate(blocks, axis=0)
-    ordered = jnp.dot(document_major(False), by_position, preferred_element_type=F32).astype(BF16)
+    xin, conv_weight, conv_bias, xproj = targets
+    window[: CONV - 1] = edge[...].astype(F32)
+    for copy in copies[:3]:
+        copy.wait()
+    window[CONV - 1 :] = xin[...].astype(F32)
+    running = jnp.broadcast_to(conv_bias[...][None], acted.shape)
+    for offset in range(CONV):
+        running = running + conv_weight[offset : offset + 1, :][None] * window[
+            offset : offset + SECTION
+        ]
+    acted[...] = jax.nn.silu(running)
+    ordered = jnp.concatenate([acted[:, doc, :] for doc in range(DOCS)], axis=0).astype(BF16)
     inner[...] = ordered
-    copies[2].wait()
+    copies[3].wait()
     projected[...] = lax.dot_general(
         xproj[...], ordered, (((1,), (1,)), ((), ())), preferred_element_type=F32
     ).astype(BF16)
@@ -246,25 +244,27 @@
 
 
 def mixer_in(xin, edge, conv_weight, conv_bias, xproj):
-    channels = xin.shape[1]
+    channels = xin.shape[2]
     return pl.pallas_call(
         mixer_in_kernel,
         out_shape=(
             jax.ShapeDtypeStruct((TOKENS, channels), BF16),
             jax.ShapeDtypeStruct((xproj.shape[0], TOKENS), BF16),
         ),
-        in_specs=[whole()] * 2 + [whole(pltpu.HBM)] * 3,
+        in_specs=[whole()] + [whole(pltpu.HBM)] * 4,
         out_specs=(whole(), whole()),
         scratch_shapes=[
-            pltpu.VMEM((16 + TOKENS, channels), F32),
+            pltpu.VMEM((CONV - 1 + SECTION, DOCS, channels), F32),
+            pltpu.VMEM((SECTION, DOCS, channels), F32),
+            pltpu.VMEM(xin.shape, BF16),
             pltpu.VMEM(conv_weight.shape, F32),
             pltpu.VMEM(conv_bias.shape, F32),
             pltpu.VMEM(xproj.shape, BF16),
-            pltpu.SemaphoreType.DMA((3,)),
+            pltpu.SemaphoreType.DMA((4,)),
         ],
         compiler_params=pltpu.CompilerParams(vmem_limit_bytes=16 << 20),
         name="mixer_in",
-    )(xin, edge, *in_hbm(conv_weight, conv_bias, xproj))
+    )(edge, *in_hbm(xin, conv_weight, conv_bias, xproj))
 
 
 def section_scan(parts, dtproj, dt_bias, a_log, inner):
@@ -433,8 +433,7 @@
     w_down,
 ):
     channels = xin.shape[2]
-    xin = xin.reshape(TOKENS, channels)
-    edge = passed_along(xin[TOKENS - (CONV - 1) * DOCS :], "seq", 1)
+    edge = passed_along(xin[SECTION - (CONV - 1) :], "seq", 1)
     inner, projected = mixer_in(xin, edge, conv_weight, conv_bias[None], xproj_weight.T)
     along_z = [projected] + from_others(projected, z_shift)
     projected = sum(part.astype(F32) for part in along_z).astype(BF16)
@@ -474,8 +473,9 @@
     ).astype(F32)
     summed = jnp.sum(returned.reshape(splits, EXPERTS * capacity, D), axis=0)
     weights = jnp.sum(matches.astype(F32) * gate_vals.astype(F32)[None], axis=2)
-    expert_out = jnp.dot(weights.T, summed, precision=lax.Precision.HIGHEST)
-    return (hidden_state + expert_out).astype(BF16).reshape(resid.shape)
+    weights = weights.reshape((-1,) + resid.shape[:2])
+    expert_out = jnp.einsum("qab,qd->abd", weights, summed, precision=lax.Precision.HIGHEST)
+    return (hidden_state.reshape(resid.shape) + expert_out).astype(BF16)
 
 
 def solution(mesh):

time: 229 us -> 230 us (level)
  transfers between devices with their start and end apart: 35 -> 35, of which waited for: 20 -> 21; matrix products, arithmetic and copies ran while one was open for 2% -> 1% of each run, Pallas kernels for 11% -> 11%
where the time goes in v8:
time: 230 us; the launch traced here: 229 us
  waiting for transfers between devices  106 us (46%)
  starting transfers between devices  46.2 us (20%)
  Pallas kernels  39.2 us (17%)
  blocking collectives  21.2 us (9%)
  local copies, waits for them, and re-layouts  10.3 us (4%)
  other arithmetic  3.99 us (2%)
    all_to_all x1, waiting for transfers between devices, per_device(): lax.all_to_all(partial_rows, 'exp', split_axis=0, concat_axis=0, tiled=True)  29.8 us
    pallas_call x4, Pallas kernels, expert_block(): pl.pallas_call(lambda *refs: expert_kernel(len(parts), *refs), out_shape=...  25.1 us
    all_to_all x1, blocking collectives, per_device(): lax.all_to_all(jnp.tile(outgoing, (splits, 1)), 'exp', split_axis=0, conc...  21.2 us
    all_to_all x1, waiting for transfers between devices, per_device(): lax.all_to_all(own_rows.astype(BF16), 'exp', split_axis=0, concat_axis=0,...  15.7 us
    ppermute x6, starting transfers between devices, from_others(): return [lax.ppermute(value, 'exp', shift(by)) for by in (1, 2, 3)]  13 us
    ppermute x6, waiting for transfers between devices, from_others(): return [lax.ppermute(value, 'exp', shift(by)) for by in (1, 2, 3)]  12.2 us
    ppermute x1, waiting for transfers between devices, experts(): for_right = lax.ppermute(far_sum[:half], 'seq', x_shift(1))  11.6 us
    ppermute x1, waiting for transfers between devices, experts(): then_left = lax.ppermute(to_right.astype(BF16), 'seq', x_shift(1))  10.9 us
  transfers between devices with their start and end apart: 35, of which 21 were waited for; matrix products, arithmetic and copies ran while one was open for 1% of the time, Pallas kernels for 11%

profile of v8, /device:TPU:0, one launch (start us, length us, event | category | flops | bytes accessed | tf_op | source)
XLA Modules:
  0.0 229.2 jit_solution(16815688566048896072)
XLA Ops:
  0.0 0.8 slice.35
  0.8 1.3 collective-permute-start
  2.0 0.8 collective-permute-done.edge
  2.9 2.3 %mixer_in.1 = (bf16[256,512]{1,0:T(8,128)(2,1)S(1)}, bf16[288,256]{1,0:T(8,128)(2,1)S(1)}) custom-call(bf16[3,4,512]{2,1,0:T(4,128)(2,1)S(1)} %collective-permute-done.edge, bf16[64,4,512]{2,1,0:T(4,128)(2,1)} %refs_0_.2, f32[4,512]{1,0:T(4,128)} %refs_1_.1, f32[1,512]{1,0:T(1,128)} %bitcast.32, bf16[288,512]{1,0:T(8,128)(2,1)} %bitcast.30), custom_call_target="tpu_custom_call" | custom-call | tf_op jit(solution)/shard_map/mixer_in/pallas_call | solution.py:248
  5.2 2.5 %collective-permute-start.1 = (bf16[288,256]{1,0:T(8,128)(2,1)S(1)}, bf16[288,256]{1,0:T(8,128)(2,1)S(1)}, u32[]{:S(2)}, u32[]{:S(2)}) collective-permute-start(bf16[288,256]{1,0:T(8,128)(2,1)S(1)} %get-tuple-element.30), channel_id=1, source_target_pairs={{0,1},{1,2},{2,3},{3,0},{4,5},{5,6},{6,7},{7,4},{8,9},{9,10},{10,1... | collective-permute-start | bytes 442376 | tf_op jit(solution)/shard_map/ppermute | solution.py:44
  7.7 3.6 %collective-permute-start.2 = (bf16[288,256]{1,0:T(8,128)(2,1)S(1)}, bf16[288,256]{1,0:T(8,128)(2,1)S(1)}, u32[]{:S(2)}, u32[]{:S(2)}) collective-permute-start(bf16[288,256]{1,0:T(8,128)(2,1)S(1)} %get-tuple-element.30), channel_id=1, source_target_pairs={{0,2},{1,3},{2,0},{3,1},{4,6},{5,7},{6,4},{7,5},{8,10},{9,11},{10,... | collective-permute-start | bytes 442376 | tf_op jit(solution)/shard_map/ppermute | solution.py:44
  11.3 1.0 collective-permute-start.3
  12.3 1.1 collective-permute-done.1
  13.5 4.9 %collective-permute-done.2 = bf16[288,256]{1,0:T(8,128)(2,1)S(1)} collective-permute-done((bf16[288,256]{1,0:T(8,128)(2,1)S(1)}, bf16[288,256]{1,0:T(8,128)(2,1)S(1)}, u32[]{:S(2)}, u32[]{:S(2)}) %collective-permute-start.2) | collective-permute-done | bytes 147488 | tf_op jit(solution)/shard_map/ppermute | solution.py:44
  18.5 1.7 collective-permute-start.4
  20.1 2.9 %collective-permute-start.5 = (bf16[288,256]{1,0:T(8,128)(2,1)S(1)}, bf16[288,256]{1,0:T(8,128)(2,1)S(1)}, u32[]{:S(2)}, u32[]{:S(2)}) collective-permute-start(bf16[288,256]{1,0:T(8,128)(2,1)S(1)} %add_convert_fusion.3.p0), channel_id=1, source_target_pairs={{0,8},{1,9},{2,10},{3,11},{4,12},{5,13},{6,14},{7,15},{8,0},{9,1},... | collective-permute-start | bytes 442376 | tf_op jit(solution)/shard_map/ppermute | solution.py:44
  23.0 1.3 collective-permute-start.6
  24.4 1.8 collective-permute-done.4.p1
  26.2 4.3 %collective-permute-done.5.p2 = bf16[288,256]{1,0:T(8,128)(2,1)S(1)} collective-permute-done((bf16[288,256]{1,0:T(8,128)(2,1)S(1)}, bf16[288,256]{1,0:T(8,128)(2,1)S(1)}, u32[]{:S(2)}, u32[]{:S(2)}) %collective-permute-start.5) | collective-permute-done | bytes 147488 | tf_op jit(solution)/shard_map/ppermute | solution.py:44
  30.5 4.0 %section_scan.1 = (f32[256,512]{1,0:T(8,128)S(1)}, f32[32,256]{1,0:T(8,128)S(1)}, bf16[72,512]{1,0:T(8,128)(2,1)S(1)}) custom-call(bf16[288,256]{1,0:T(8,128)(2,1)S(1)} %add_convert_fusion.3.p0, bf16[288,256]{1,0:T(8,128)(2,1)S(1)} %collective-permute-done.4.p1, bf16[288,256]{1,0:T(8,128)(2,1)S(1)} %collective-permute-done.5.p2, ...), custom_call_target="tpu_custom_call" | custom-call | tf_op jit(solution)/shard_map/section_scan/pallas_call | solution.py:272
  34.5 1.0 collective-permute-start.7
  35.5 1.5 collective-permute-start.8
  37.0 2.4 %collective-permute-start.9 = (bf16[72,512]{1,0:T(8,128)(2,1)S(1)}, bf16[72,512]{1,0:T(8,128)(2,1)S(1)}, u32[]{:S(2)}, u32[]{:S(2)}) collective-permute-start(bf16[72,512]{1,0:T(8,128)(2,1)S(1)} %get-tuple-element.32), channel_id=1, source_target_pairs={{0,96},{16,112},{32,0},{48,16},{64,32},{80,48},{96,64},{112,80},{1... | collective-permute-start | bytes 221192 | tf_op jit(solution)/shard_map/ppermute | solution.py:442
  39.4 1.2 collective-permute-done.7.refs_0_
  40.6 0.8 collective-permute-done.8.refs_1_
  41.4 0.6 collective-permute-done.9.refs_2_
  42.0 0.6 collective-permute-done.12.refs_5_
  42.6 0.6 collective-permute-done.13.refs_6_
  43.2 7.7 %mixer_out.1 = bf16[256,4096]{1,0:T(8,128)(2,1)} custom-call(s32[1]{0:T(128)} %bitcast.section, bf16[72,512]{1,0:T(8,128)(2,1)S(1)} %collective-permute-done.7.refs_0_, bf16[72,512]{1,0:T(8,128)(2,1)S(1)} %collective-permute-done.8.refs_1_, bf16[72,512]{1,0:T(8,128)(2,1)S(1)} %collective-permute-done.9.refs_2_, ...), custom_call_target="tpu_custom_call" | custom-call | tf_op jit(solution)/shard_map/mixer_out/pallas_call | solution.py:295
  50.9 5.9 %all-to-all-start = ((bf16[16,16,4096]{2,1,0:T(8,128)(2,1)}), bf16[16,16,4096]{2,1,0:T(8,128)(2,1)S(1)}, u32[]{:S(2)}, u32[]{:S(2)}) async-start(bf16[16,16,4096]{2,1,0:T(8,128)(2,1)} %bitcast.5), calls=%async_computation | async-start | bytes 4194304 | tf_op jit(solution)/shard_map/all_to_all | solution.py:454
  57.2 0.2 select_reduce_fusion.1
  57.8 29.8 %all-to-all-done = bf16[16,16,4096]{2,1,0:T(8,128)(2,1)S(1)} async-done(((bf16[16,16,4096]{2,1,0:T(8,128)(2,1)}), bf16[16,16,4096]{2,1,0:T(8,128)(2,1)S(1)}, u32[]{:S(2)}, u32[]{:S(2)}) %all-to-all-start) | async-done | bytes 2097184 | tf_op jit(solution)/shard_map/all_to_all | solution.py:454
  87.6 0.3 convert_reduce_fusion
  88.3 0.3 convolution_convert_fusion
  88.7 21.2 %all_to_all.26 = bf16[16,8,4096]{2,1,0:T(8,128)(2,1)S(1)} all-to-all(bf16[16,8,4096]{2,1,0:T(8,128)(2,1)S(1)} %bitcast.29), channel_id=1, replica_groups=mesh['seq'=8,'exp'=16] {'exp'}, dimensions={0} | all-to-all | bytes 2097152 | tf_op jit(solution)/shard_map/all_to_all | solution.py:467
  110.1 3.1 %collective-permute-start.17 = (bf16[128,4096]{1,0:T(8,128)(2,1)S(1)}, bf16[128,4096]{1,0:T(8,128)(2,1)S(1)}, u32[]{:S(2)}, u32[]{:S(2)}) collective-permute-start(bf16[128,4096]{1,0:T(8,128)(2,1)S(1)} %bitcast.25), channel_id=1, source_target_pairs={{0,96},{16,112},{32,0},{48,16},{64,32},{80,48},{96,64},{112,80},{1... | collective-permute-start | bytes 3145736 | tf_op jit(solution)/shard_map/ppermute | solution.py:385
  113.2 2.8 %copy-done = bf16[1,4096,768]{2,1,0:T(8,128)(2,1)S(1)} copy-done((bf16[1,4096,768]{2,1,0:T(8,128)(2,1)S(1)}, bf16[1,4096,768]{2,1,0:T(8,128)(2,1)}, u32[]{:S(2)}) %copy-start) | copy-done | bytes 6291480
  116.0 2.8 %copy-done.2 = bf16[1,4096,768]{2,1,0:T(8,128)(2,1)S(1)} copy-done((bf16[1,4096,768]{2,1,0:T(8,128)(2,1)S(1)}, bf16[1,4096,768]{2,1,0:T(8,128)(2,1)}, u32[]{:S(2)}) %copy-start.2) | copy-done | bytes 6291480
  118.8 2.8 %copy-done.4 = bf16[1,768,4096]{2,1,0:T(8,128)(2,1)S(1)} copy-done((bf16[1,768,4096]{2,1,0:T(8,128)(2,1)S(1)}, bf16[1,768,4096]{2,1,0:T(8,128)(2,1)}, u32[]{:S(2)}) %copy-start.4) | copy-done | bytes 6291480
  121.6 6.3 %experts_256.4 = (bf16[128,4096]{1,0:T(8,128)(2,1)S(1)}, bf16[128,4096]{1,0:T(8,128)(2,1)S(1)}) custom-call(bf16[128,4096]{1,0:T(8,128)(2,1)S(1)} %bitcast.26, bf16[128,4096]{1,0:T(8,128)(2,1)S(1)} %collective-permute-done.14.refs_1_, bf16[1,4096,768]{2,1,0:T(8,128)(2,1)S(1)} %copy-done, bf16[1,4096,768]{2,1,0:T(8,128)(2,1)S(1)} %copy-done.2, ...), custom_call_target="tpu_custom_call" | custom-call | flops 4831838208 | bytes 4194304 | tf_op jit(solution)/shard_map/experts_256/pallas_call | solution.py:344
  127.9 8.9 %collective-permute-done.16.refs_0_ = bf16[128,4096]{1,0:T(8,128)(2,1)S(1)} collective-permute-done((bf16[128,4096]{1,0:T(8,128)(2,1)S(1)}, bf16[128,4096]{1,0:T(8,128)(2,1)S(1)}, u32[]{:S(2)}, u32[]{:S(2)}) %collective-permute-start.16) | collective-permute-done | bytes 1048608 | tf_op jit(solution)/shard_map/ppermute | solution.py:384
  136.8 0.5 collective-permute-start.20
  137.4 3.2 %collective-permute-start.19 = (bf16[64,4096]{1,0:T(8,128)(2,1)S(1)}, bf16[64,4096]{1,0:T(8,128)(2,1)S(1)}, u32[]{:S(2)}, u32[]{:S(2)}) collective-permute-start(bf16[64,4096]{1,0:T(8,128)(2,1)S(1)} %slice.38), channel_id=1, source_target_pairs={{0,96},{16,112},{32,0},{48,16},{64,32},{80,48},{96,64},{112,80},{1... | collective-permute-start | bytes 1572872 | tf_op jit(solution)/shard_map/ppermute | solution.py:390
  140.7 6.3 %experts_256.6 = (bf16[128,4096]{1,0:T(8,128)(2,1)S(1)}, bf16[128,4096]{1,0:T(8,128)(2,1)S(1)}) custom-call(bf16[128,4096]{1,0:T(8,128)(2,1)S(1)} %collective-permute-done.17.refs_0_, bf16[128,4096]{1,0:T(8,128)(2,1)S(1)} %collective-permute-done.21.refs_1_, bf16[1,4096,768]{2,1,0:T(8,128)(2,1)S(1)} %copy-done.1, bf16[1,4096,768]{2,1,0:T(8,128)(2,1)S(1)} %copy-done.3, ...), custom_call_target="tpu_custom_call" | custom-call | flops 4831838208 | bytes 4194304 | tf_op jit(solution)/shard_map/experts_256/pallas_call | solution.py:344
  147.0 6.3 %experts_256.5 = (bf16[128,4096]{1,0:T(8,128)(2,1)S(1)}, bf16[128,4096]{1,0:T(8,128)(2,1)S(1)}) custom-call(bf16[128,4096]{1,0:T(8,128)(2,1)S(1)} %collective-permute-done.16.refs_0_, bf16[128,4096]{1,0:T(8,128)(2,1)S(1)} %collective-permute-done.20.refs_1_, bf16[1,4096,768]{2,1,0:T(8,128)(2,1)S(1)} %copy-done.1, bf16[1,4096,768]{2,1,0:T(8,128)(2,1)S(1)} %copy-done.3, ...), custom_call_target="tpu_custom_call" | custom-call | flops 4831838208 | bytes 4194304 | tf_op jit(solution)/shard_map/experts_256/pallas_call | solution.py:344
  153.4 0.5 collective-permute-start.24
  154.0 0.4 collective-permute-start.26
  154.5 1.5 collective-permute-done.22
  156.0 0.3 convert_add_fusion.1
  156.4 2.2 collective-permute-start.23
  158.6 0.3 convert_add_fusion
  158.9 0.3 collective-permute-start.25
  159.2 0.6 collective-permute-done.26.refs_2_
  159.8 0.7 collective-permute-done.27.refs_3_
  160.5 6.3 %experts_256.7 = (bf16[128,4096]{1,0:T(8,128)(2,1)S(1)}, bf16[128,4096]{1,0:T(8,128)(2,1)S(1)}) custom-call(bf16[64,4096]{1,0:T(8,128)(2,1)S(1)} %collective-permute-done.18.refs_0_, bf16[64,4096]{1,0:T(8,128)(2,1)S(1)} %collective-permute-done.19.refs_1_, bf16[64,4096]{1,0:T(8,128)(2,1)S(1)} %collective-permute-done.26.refs_2_, ...), custom_call_target="tpu_custom_call" | custom-call | flops 4831838208 | bytes 4194304 | tf_op jit(solution)/shard_map/experts_256/pallas_call | solution.py:344
  166.8 3.6 %collective-permute-done.23 = bf16[64,4096]{1,0:T(8,128)(2,1)S(1)} collective-permute-done((bf16[64,4096]{1,0:T(8,128)(2,1)S(1)}, bf16[64,4096]{1,0:T(8,128)(2,1)S(1)}, u32[]{:S(2)}, u32[]{:S(2)}) %collective-permute-start.23) | collective-permute-done | bytes 524320 | tf_op jit(solution)/shard_map/ppermute | solution.py:396
  170.4 3.7 %collective-permute-done.25 = bf16[64,4096]{1,0:T(8,128)(2,1)S(1)} collective-permute-done((bf16[64,4096]{1,0:T(8,128)(2,1)S(1)}, bf16[64,4096]{1,0:T(8,128)(2,1)S(1)}, u32[]{:S(2)}, u32[]{:S(2)}) %collective-permute-start.25) | collective-permute-done | bytes 524320 | tf_op jit(solution)/shard_map/ppermute | solution.py:397
  174.1 0.3 convert_add_fusion.2
  174.3 2.4 %collective-permute-done.28 = bf16[128,4096]{1,0:T(8,128)(2,1)S(1)} collective-permute-done((bf16[128,4096]{1,0:T(8,128)(2,1)S(1)}, bf16[128,4096]{1,0:T(8,128)(2,1)S(1)}, u32[]{:S(2)}, u32[]{:S(2)}) %collective-permute-start.28) | collective-permute-done | bytes 1048608 | tf_op jit(solution)/shard_map/ppermute | solution.py:48
  176.7 0.2 add_convert_fusion
  177.2 0.3 slice_add_fusion.2
  177.4 3.3 %collective-permute-start.31 = (bf16[64,4096]{1,0:T(8,128)(2,1)S(1)}, bf16[64,4096]{1,0:T(8,128)(2,1)S(1)}, u32[]{:S(2)}, u32[]{:S(2)}) collective-permute-start(bf16[64,4096]{1,0:T(8,128)(2,1)S(1)} %get-tuple-element.58), channel_id=1, source_target_pairs={{0,96},{16,112},{32,0},{48,16},{64,32},{80,48},{96,64},{112,80},{1... | collective-permute-start | bytes 1572872 | tf_op jit(solution)/shard_map/ppermute | solution.py:402
  180.7 11.6 %collective-permute-done.29 = bf16[64,4096]{1,0:T(8,128)(2,1)S(1)} collective-permute-done((bf16[64,4096]{1,0:T(8,128)(2,1)S(1)}, bf16[64,4096]{1,0:T(8,128)(2,1)S(1)}, u32[]{:S(2)}, u32[]{:S(2)}) %collective-permute-start.29) | collective-permute-done | bytes 524320 | tf_op jit(solution)/shard_map/ppermute | solution.py:401
  192.6 3.3 %collective-permute-start.32 = (bf16[64,4096]{1,0:T(8,128)(2,1)S(1)}, bf16[64,4096]{1,0:T(8,128)(2,1)S(1)}, u32[]{:S(2)}, u32[]{:S(2)}) collective-permute-start(bf16[64,4096]{1,0:T(8,128)(2,1)S(1)} %fusion.1), channel_id=1, source_target_pairs={{0,96},{16,112},{32,0},{48,16},{64,32},{80,48},{96,64},{112,80},{1... | collective-permute-start | bytes 1572872 | tf_op jit(solution)/shard_map/ppermute | solution.py:409
  195.9 10.9 %collective-permute-done.30 = bf16[64,4096]{1,0:T(8,128)(2,1)S(1)} collective-permute-done((bf16[64,4096]{1,0:T(8,128)(2,1)S(1)}, bf16[64,4096]{1,0:T(8,128)(2,1)S(1)}, u32[]{:S(2)}, u32[]{:S(2)}) %collective-permute-start.30) | collective-permute-done | bytes 524320 | tf_op jit(solution)/shard_map/ppermute | solution.py:410
  207.1 1.1 maximum_bitcast_fusion
  208.2 3.7 %all-to-all-start.2 = ((bf16[16,8,4096]{2,1,0:T(8,128)(2,1)}), bf16[16,8,4096]{2,1,0:T(8,128)(2,1)S(1)}, u32[]{:S(2)}, u32[]{:S(2)}) async-start(bf16[16,8,4096]{2,1,0:T(8,128)(2,1)} %maximum_bitcast_fusion), calls=%async_computation.2 | async-start | bytes 2097152 | tf_op jit(solution)/shard_map/all_to_all | solution.py:471
  212.0 15.7 %all-to-all-done.2 = bf16[16,8,4096]{2,1,0:T(8,128)(2,1)S(1)} async-done(((bf16[16,8,4096]{2,1,0:T(8,128)(2,1)}), bf16[16,8,4096]{2,1,0:T(8,128)(2,1)S(1)}, u32[]{:S(2)}, u32[]{:S(2)}) %all-to-all-start.2) | async-done | bytes 1048608 | tf_op jit(solution)/shard_map/all_to_all | solution.py:471
  227.9 1.3 fusion
  (83 shorter events, 3.1 us)
Async XLA Ops:
  0.0 43.2 %copy-start.6 = (f32[16,512]{1,0:T(8,128)S(1)}, f32[16,512]{1,0:T(8,128)}, u32[]{:S(2)}) copy-start(f32[16,512]{1,0:T(8,128)} %refs_10_.1) | copy-start | bytes 98308
  0.0 41.9 %copy-start.9 = (bf16[64,4,512]{2,1,0:T(4,128)(2,1)S(1)}, bf16[64,4,512]{2,1,0:T(4,128)(2,1)}, u32[]{:S(2)}) copy-start(bf16[64,4,512]{2,1,0:T(4,128)(2,1)} %param.18) | copy-start | bytes 786436
  0.0 43.2 %copy-start.7 = (f32[512]{0:T(512)S(1)}, f32[512]{0:T(512)}, u32[]{:S(2)}) copy-start(f32[512]{0:T(512)} %param.25) | copy-start | bytes 6148
  0.8 2.1 collective-permute-start
  5.2 8.3 %collective-permute-start.1 = (bf16[288,256]{1,0:T(8,128)(2,1)S(1)}, bf16[288,256]{1,0:T(8,128)(2,1)S(1)}, u32[]{:S(2)}, u32[]{:S(2)}) collective-permute-start(bf16[288,256]{1,0:T(8,128)(2,1)S(1)} %get-tuple-element.30), channel_id=1, source_target_pairs={{0,1},{1,2},{2,3},{3,0},{4,5},{5,6},{6,7},{7,4},{8,9},{9,10},{10,1... | collective-permute-start | bytes 442376 | tf_op jit(solution)/shard_map/ppermute | solution.py:44
  7.7 10.7 %collective-permute-start.2 = (bf16[288,256]{1,0:T(8,128)(2,1)S(1)}, bf16[288,256]{1,0:T(8,128)(2,1)S(1)}, u32[]{:S(2)}, u32[]{:S(2)}) collective-permute-start(bf16[288,256]{1,0:T(8,128)(2,1)S(1)} %get-tuple-element.30), channel_id=1, source_target_pairs={{0,2},{1,3},{2,0},{3,1},{4,6},{5,7},{6,4},{7,5},{8,10},{9,11},{10,... | collective-permute-start | bytes 442376 | tf_op jit(solution)/shard_map/ppermute | solution.py:44
  11.3 7.1 %collective-permute-start.3 = (bf16[288,256]{1,0:T(8,128)(2,1)S(1)}, bf16[288,256]{1,0:T(8,128)(2,1)S(1)}, u32[]{:S(2)}, u32[]{:S(2)}) collective-permute-start(bf16[288,256]{1,0:T(8,128)(2,1)S(1)} %get-tuple-element.30), channel_id=1, source_target_pairs={{0,3},{1,0},{2,1},{3,2},{4,7},{5,4},{6,5},{7,6},{8,11},{9,8},{10,9... | collective-permute-start | bytes 442376 | tf_op jit(solution)/shard_map/ppermute | solution.py:44
  18.5 7.7 %collective-permute-start.4 = (bf16[288,256]{1,0:T(8,128)(2,1)S(1)}, bf16[288,256]{1,0:T(8,128)(2,1)S(1)}, u32[]{:S(2)}, u32[]{:S(2)}) collective-permute-start(bf16[288,256]{1,0:T(8,128)(2,1)S(1)} %add_convert_fusion.3.p0), channel_id=1, source_target_pairs={{0,4},{1,5},{2,6},{3,7},{4,8},{5,9},{6,10},{7,11},{8,12},{9,13},{1... | collective-permute-start | bytes 442376 | tf_op jit(solution)/shard_map/ppermute | solution.py:44
  20.1 10.4 %collective-permute-start.5 = (bf16[288,256]{1,0:T(8,128)(2,1)S(1)}, bf16[288,256]{1,0:T(8,128)(2,1)S(1)}, u32[]{:S(2)}, u32[]{:S(2)}) collective-permute-start(bf16[288,256]{1,0:T(8,128)(2,1)S(1)} %add_convert_fusion.3.p0), channel_id=1, source_target_pairs={{0,8},{1,9},{2,10},{3,11},{4,12},{5,13},{6,14},{7,15},{8,0},{9,1},... | collective-permute-start | bytes 442376 | tf_op jit(solution)/shard_map/ppermute | solution.py:44
  23.0 7.5 %collective-permute-start.6 = (bf16[288,256]{1,0:T(8,128)(2,1)S(1)}, bf16[288,256]{1,0:T(8,128)(2,1)S(1)}, u32[]{:S(2)}, u32[]{:S(2)}) collective-permute-start(bf16[288,256]{1,0:T(8,128)(2,1)S(1)} %add_convert_fusion.3.p0), channel_id=1, source_target_pairs={{0,12},{1,13},{2,14},{3,15},{4,0},{5,1},{6,2},{7,3},{8,4},{9,5},{1... | collective-permute-start | bytes 442376 | tf_op jit(solution)/shard_map/ppermute | solution.py:44
  34.5 6.1 %collective-permute-start.7 = (bf16[72,512]{1,0:T(8,128)(2,1)S(1)}, bf16[72,512]{1,0:T(8,128)(2,1)S(1)}, u32[]{:S(2)}, u32[]{:S(2)}) collective-permute-start(bf16[72,512]{1,0:T(8,128)(2,1)S(1)} %get-tuple-element.32), channel_id=1, source_target_pairs={{0,32},{16,48},{32,64},{48,80},{64,96},{80,112},{96,0},{112,16},{1... | collective-permute-start | bytes 221192 | tf_op jit(solution)/shard_map/ppermute | solution.py:442
  35.5 5.9 %collective-permute-start.8 = (bf16[72,512]{1,0:T(8,128)(2,1)S(1)}, bf16[72,512]{1,0:T(8,128)(2,1)S(1)}, u32[]{:S(2)}, u32[]{:S(2)}) collective-permute-start(bf16[72,512]{1,0:T(8,128)(2,1)S(1)} %get-tuple-element.32), channel_id=1, source_target_pairs={{0,64},{16,80},{32,96},{48,112},{64,0},{80,16},{96,32},{112,48},{1... | collective-permute-start | bytes 221192 | tf_op jit(solution)/shard_map/ppermute | solution.py:442
  37.0 5.0 %collective-permute-start.9 = (bf16[72,512]{1,0:T(8,128)(2,1)S(1)}, bf16[72,512]{1,0:T(8,128)(2,1)S(1)}, u32[]{:S(2)}, u32[]{:S(2)}) collective-permute-start(bf16[72,512]{1,0:T(8,128)(2,1)S(1)} %get-tuple-element.32), channel_id=1, source_target_pairs={{0,96},{16,112},{32,0},{48,16},{64,32},{80,48},{96,64},{112,80},{1... | collective-permute-start | bytes 221192 | tf_op jit(solution)/shard_map/ppermute | solution.py:442
  39.4 2.6 %collective-permute-start.10 = (bf16[72,512]{1,0:T(8,128)(2,1)S(1)}, bf16[72,512]{1,0:T(8,128)(2,1)S(1)}, u32[]{:S(2)}, u32[]{:S(2)}) collective-permute-start(bf16[72,512]{1,0:T(8,128)(2,1)S(1)} %get-tuple-element.32), channel_id=1, source_target_pairs={{0,16},{16,0},{32,48},{48,32},{64,80},{80,64},{96,112},{112,96},{1... | collective-permute-start | bytes 221192 | tf_op jit(solution)/shard_map/ppermute | solution.py:48
  40.6 1.5 collective-permute-start.11
  41.4 1.3 collective-permute-start.12
  41.9 1.3 collective-permute-start.13
  50.9 6.0 %copy-start.11 = (s32[4,4,2]{1,2,0:T(2,128)S(1)}, s32[4,4,2]{1,2,0:T(2,128)}, u32[]{:S(2)}) copy-start(s32[4,4,2]{1,2,0:T(2,128)} %param.29) | copy-start | bytes 388
  50.9 6.8 %copy-start.8 = (bf16[4,4,4096]{2,1,0:T(4,128)(2,1)S(1)}, bf16[4,4,4096]{2,1,0:T(4,128)(2,1)}, u32[]{:S(2)}) copy-start(bf16[4,4,4096]{2,1,0:T(4,128)(2,1)} %param.27) | copy-start | bytes 393220
  50.9 36.7 %all-to-all-start = ((bf16[16,16,4096]{2,1,0:T(8,128)(2,1)}), bf16[16,16,4096]{2,1,0:T(8,128)(2,1)S(1)}, u32[]{:S(2)}, u32[]{:S(2)}) async-start(bf16[16,16,4096]{2,1,0:T(8,128)(2,1)} %bitcast.5), calls=%async_computation | async-start | bytes 4194304 | tf_op jit(solution)/shard_map/all_to_all | solution.py:454
  56.9 31.4 %copy-start.10 = (f32[4096]{0:T(1024)S(1)}, f32[4096]{0:T(1024)}, u32[]{:S(2)}) copy-start(f32[4096]{0:T(1024)} %param.28) | copy-start | bytes 49156
  110.0 3.2 %collective-permute-start.14 = (bf16[128,4096]{1,0:T(8,128)(2,1)S(1)}, bf16[128,4096]{1,0:T(8,128)(2,1)S(1)}, u32[]{:S(2)}, u32[]{:S(2)}) collective-permute-start(bf16[128,4096]{1,0:T(8,128)(2,1)S(1)} %bitcast.23), channel_id=1, source_target_pairs={{0,16},{16,0},{32,48},{48,32},{64,80},{80,64},{96,112},{112,96},{1... | collective-permute-start | bytes 3145736 | tf_op jit(solution)/shard_map/ppermute | solution.py:48
  110.0 26.8 %collective-permute-start.16 = (bf16[128,4096]{1,0:T(8,128)(2,1)S(1)}, bf16[128,4096]{1,0:T(8,128)(2,1)S(1)}, u32[]{:S(2)}, u32[]{:S(2)}) collective-permute-start(bf16[128,4096]{1,0:T(8,128)(2,1)S(1)} %bitcast.24), channel_id=1, source_target_pairs={{0,32},{16,48},{32,64},{48,80},{64,96},{80,112},{96,0},{112,16},{1... | collective-permute-start | bytes 3145736 | tf_op jit(solution)/shard_map/ppermute | solution.py:384
  110.1 26.7 %collective-permute-start.17 = (bf16[128,4096]{1,0:T(8,128)(2,1)S(1)}, bf16[128,4096]{1,0:T(8,128)(2,1)S(1)}, u32[]{:S(2)}, u32[]{:S(2)}) collective-permute-start(bf16[128,4096]{1,0:T(8,128)(2,1)S(1)} %bitcast.25), channel_id=1, source_target_pairs={{0,96},{16,112},{32,0},{48,16},{64,32},{80,48},{96,64},{112,80},{1... | collective-permute-start | bytes 3145736 | tf_op jit(solution)/shard_map/ppermute | solution.py:385
  113.2 2.8 %copy-start = (bf16[1,4096,768]{2,1,0:T(8,128)(2,1)S(1)}, bf16[1,4096,768]{2,1,0:T(8,128)(2,1)}, u32[]{:S(2)}) copy-start(bf16[1,4096,768]{2,1,0:T(8,128)(2,1)} %refs_4_.7) | copy-start | bytes 18874372
  116.0 2.8 %copy-start.2 = (bf16[1,4096,768]{2,1,0:T(8,128)(2,1)S(1)}, bf16[1,4096,768]{2,1,0:T(8,128)(2,1)}, u32[]{:S(2)}) copy-start(bf16[1,4096,768]{2,1,0:T(8,128)(2,1)} %refs_5_.1) | copy-start | bytes 18874372
  118.8 2.8 %copy-start.4 = (bf16[1,768,4096]{2,1,0:T(8,128)(2,1)S(1)}, bf16[1,768,4096]{2,1,0:T(8,128)(2,1)}, u32[]{:S(2)}) copy-start(bf16[1,768,4096]{2,1,0:T(8,128)(2,1)} %refs_6_.1) | copy-start | bytes 18874372
  121.6 19.1 %copy-start.1 = (bf16[1,4096,768]{2,1,0:T(8,128)(2,1)S(1)}, bf16[1,4096,768]{2,1,0:T(8,128)(2,1)}, u32[]{:S(2)}) copy-start(bf16[1,4096,768]{2,1,0:T(8,128)(2,1)} %refs_4_.7) | copy-start | bytes 18874372
  121.6 19.1 %copy-start.3 = (bf16[1,4096,768]{2,1,0:T(8,128)(2,1)S(1)}, bf16[1,4096,768]{2,1,0:T(8,128)(2,1)}, u32[]{:S(2)}) copy-start(bf16[1,4096,768]{2,1,0:T(8,128)(2,1)} %refs_5_.1) | copy-start | bytes 18874372
  121.6 19.1 %copy-start.5 = (bf16[1,768,4096]{2,1,0:T(8,128)(2,1)S(1)}, bf16[1,768,4096]{2,1,0:T(8,128)(2,1)}, u32[]{:S(2)}) copy-start(bf16[1,768,4096]{2,1,0:T(8,128)(2,1)} %refs_6_.1) | copy-start | bytes 18874372
  136.7 3.9 %collective-permute-start.21 = (bf16[128,4096]{1,0:T(8,128)(2,1)S(1)}, bf16[128,4096]{1,0:T(8,128)(2,1)S(1)}, u32[]{:S(2)}, u32[]{:S(2)}) collective-permute-start(bf16[128,4096]{1,0:T(8,128)(2,1)S(1)} %collective-permute-done.17.refs_0_), channel_id=1, source_target_pairs={{0,16},{16,0},{32,48},{48,32},{64,80},{80,64},{96,112},{112,96},{1... | collective-permute-start | bytes 3145736 | tf_op jit(solution)/shard_map/ppermute | solution.py:48
  136.8 10.2 %collective-permute-start.20 = (bf16[128,4096]{1,0:T(8,128)(2,1)S(1)}, bf16[128,4096]{1,0:T(8,128)(2,1)S(1)}, u32[]{:S(2)}, u32[]{:S(2)}) collective-permute-start(bf16[128,4096]{1,0:T(8,128)(2,1)S(1)} %collective-permute-done.16.refs_0_), channel_id=1, source_target_pairs={{0,16},{16,0},{32,48},{48,32},{64,80},{80,64},{96,112},{112,96},{1... | collective-permute-start | bytes 3145736 | tf_op jit(solution)/shard_map/ppermute | solution.py:48
  137.3 15.9 %collective-permute-start.18 = (bf16[64,4096]{1,0:T(8,128)(2,1)S(1)}, bf16[64,4096]{1,0:T(8,128)(2,1)S(1)}, u32[]{:S(2)}, u32[]{:S(2)}) collective-permute-start(bf16[64,4096]{1,0:T(8,128)(2,1)S(1)} %slice.37), channel_id=1, source_target_pairs={{0,32},{16,48},{32,64},{48,80},{64,96},{80,112},{96,0},{112,16},{1... | collective-permute-start | bytes 1572872 | tf_op jit(solution)/shard_map/ppermute | solution.py:389
  137.4 15.9 %collective-permute-start.19 = (bf16[64,4096]{1,0:T(8,128)(2,1)S(1)}, bf16[64,4096]{1,0:T(8,128)(2,1)S(1)}, u32[]{:S(2)}, u32[]{:S(2)}) collective-permute-start(bf16[64,4096]{1,0:T(8,128)(2,1)S(1)} %slice.38), channel_id=1, source_target_pairs={{0,96},{16,112},{32,0},{48,16},{64,32},{80,48},{96,64},{112,80},{1... | collective-permute-start | bytes 1572872 | tf_op jit(solution)/shard_map/ppermute | solution.py:390
  153.3 2.7 %collective-permute-start.22 = (bf16[128,4096]{1,0:T(8,128)(2,1)S(1)}, bf16[128,4096]{1,0:T(8,128)(2,1)S(1)}, u32[]{:S(2)}, u32[]{:S(2)}) collective-permute-start(bf16[128,4096]{1,0:T(8,128)(2,1)S(1)} %get-tuple-element.44), channel_id=1, source_target_pairs={{0,16},{16,0},{32,48},{48,32},{64,80},{80,64},{96,112},{112,96},{1... | collective-permute-start | bytes 3145736 | tf_op jit(solution)/shard_map/ppermute | solution.py:48
  153.4 5.2 %collective-permute-start.24 = (bf16[128,4096]{1,0:T(8,128)(2,1)S(1)}, bf16[128,4096]{1,0:T(8,128)(2,1)S(1)}, u32[]{:S(2)}, u32[]{:S(2)}) collective-permute-start(bf16[128,4096]{1,0:T(8,128)(2,1)S(1)} %get-tuple-element.46), channel_id=1, source_target_pairs={{0,16},{16,0},{32,48},{48,32},{64,80},{80,64},{96,112},{112,96},{1... | collective-permute-start | bytes 3145736 | tf_op jit(solution)/shard_map/ppermute | solution.py:48
  153.9 20.2 %collective-permute-start.15 = (bf16[128,4096]{1,0:T(8,128)(2,1)S(1)}, bf16[128,4096]{1,0:T(8,128)(2,1)S(1)}, u32[]{:S(2)}, u32[]{:S(2)}) collective-permute-start(bf16[128,4096]{1,0:T(8,128)(2,1)S(1)} %get-tuple-element.36), channel_id=1, source_target_pairs={{0,16},{16,0},{32,48},{48,32},{64,80},{80,64},{96,112},{112,96},{1... | collective-permute-start | bytes 3145736 | tf_op jit(solution)/shard_map/ppermute | solution.py:48
  154.0 5.8 %collective-permute-start.26 = (bf16[64,4096]{1,0:T(8,128)(2,1)S(1)}, bf16[64,4096]{1,0:T(8,128)(2,1)S(1)}, u32[]{:S(2)}, u32[]{:S(2)}) collective-permute-start(bf16[64,4096]{1,0:T(8,128)(2,1)S(1)} %collective-permute-done.18.refs_0_), channel_id=1, source_target_pairs={{0,16},{16,0},{32,48},{48,32},{64,80},{80,64},{96,112},{112,96},{1... | collective-permute-start | bytes 1572872 | tf_op jit(solution)/shard_map/ppermute | solution.py:48
  154.4 6.1 %collective-permute-start.27 = (bf16[64,4096]{1,0:T(8,128)(2,1)S(1)}, bf16[64,4096]{1,0:T(8,128)(2,1)S(1)}, u32[]{:S(2)}, u32[]{:S(2)}) collective-permute-start(bf16[64,4096]{1,0:T(8,128)(2,1)S(1)} %collective-permute-done.19.refs_1_), channel_id=1, source_target_pairs={{0,16},{16,0},{32,48},{48,32},{64,80},{80,64},{96,112},{112,96},{1... | collective-permute-start | bytes 1572872 | tf_op jit(solution)/shard_map/ppermute | solution.py:48
  156.4 14.0 %collective-permute-start.23 = (bf16[64,4096]{1,0:T(8,128)(2,1)S(1)}, bf16[64,4096]{1,0:T(8,128)(2,1)S(1)}, u32[]{:S(2)}, u32[]{:S(2)}) collective-permute-start(bf16[64,4096]{1,0:T(8,128)(2,1)S(1)} %slice.65), channel_id=1, source_target_pairs={{0,96},{16,112},{32,0},{48,16},{64,32},{80,48},{96,64},{112,80},{1... | collective-permute-start | bytes 1572872 | tf_op jit(solution)/shard_map/ppermute | solution.py:396
  158.9 15.2 %collective-permute-start.25 = (bf16[64,4096]{1,0:T(8,128)(2,1)S(1)}, bf16[64,4096]{1,0:T(8,128)(2,1)S(1)}, u32[]{:S(2)}, u32[]{:S(2)}) collective-permute-start(bf16[64,4096]{1,0:T(8,128)(2,1)S(1)} %slice.64), channel_id=1, source_target_pairs={{0,32},{16,48},{32,64},{48,80},{64,96},{80,112},{96,0},{112,16},{1... | collective-permute-start | bytes 1572872 | tf_op jit(solution)/shard_map/ppermute | solution.py:397
  174.1 2.7 %collective-permute-start.28 = (bf16[128,4096]{1,0:T(8,128)(2,1)S(1)}, bf16[128,4096]{1,0:T(8,128)(2,1)S(1)}, u32[]{:S(2)}, u32[]{:S(2)}) collective-permute-start(bf16[128,4096]{1,0:T(8,128)(2,1)S(1)} %get-tuple-element.53), channel_id=1, source_target_pairs={{0,16},{16,0},{32,48},{48,32},{64,80},{80,64},{96,112},{112,96},{1... | collective-permute-start | bytes 3145736 | tf_op jit(solution)/shard_map/ppermute | solution.py:48
  177.1 15.2 %collective-permute-start.29 = (bf16[64,4096]{1,0:T(8,128)(2,1)S(1)}, bf16[64,4096]{1,0:T(8,128)(2,1)S(1)}, u32[]{:S(2)}, u32[]{:S(2)}) collective-permute-start(bf16[64,4096]{1,0:T(8,128)(2,1)S(1)} %get-tuple-element.57), channel_id=1, source_target_pairs={{0,32},{16,48},{32,64},{48,80},{64,96},{80,112},{96,0},{112,16},{1... | collective-permute-start | bytes 1572872 | tf_op jit(solution)/shard_map/ppermute | solution.py:401
  177.4 15.1 %collective-permute-start.31 = (bf16[64,4096]{1,0:T(8,128)(2,1)S(1)}, bf16[64,4096]{1,0:T(8,128)(2,1)S(1)}, u32[]{:S(2)}, u32[]{:S(2)}) collective-permute-start(bf16[64,4096]{1,0:T(8,128)(2,1)S(1)} %get-tuple-element.58), channel_id=1, source_target_pairs={{0,96},{16,112},{32,0},{48,16},{64,32},{80,48},{96,64},{112,80},{1... | collective-permute-start | bytes 1572872 | tf_op jit(solution)/shard_map/ppermute | solution.py:402
  192.4 14.4 %collective-permute-start.30 = (bf16[64,4096]{1,0:T(8,128)(2,1)S(1)}, bf16[64,4096]{1,0:T(8,128)(2,1)S(1)}, u32[]{:S(2)}, u32[]{:S(2)}) collective-permute-start(bf16[64,4096]{1,0:T(8,128)(2,1)S(1)} %fusion.2), channel_id=1, source_target_pairs={{0,32},{16,48},{32,64},{48,80},{64,96},{80,112},{96,0},{112,16},{1... | collective-permute-start | bytes 1572872 | tf_op jit(solution)/shard_map/ppermute | solution.py:410
  192.6 14.3 %collective-permute-start.32 = (bf16[64,4096]{1,0:T(8,128)(2,1)S(1)}, bf16[64,4096]{1,0:T(8,128)(2,1)S(1)}, u32[]{:S(2)}, u32[]{:S(2)}) collective-permute-start(bf16[64,4096]{1,0:T(8,128)(2,1)S(1)} %fusion.1), channel_id=1, source_target_pairs={{0,96},{16,112},{32,0},{48,16},{64,32},{80,48},{96,64},{112,80},{1... | collective-permute-start | bytes 1572872 | tf_op jit(solution)/shard_map/ppermute | solution.py:409
  207.1 4.7 %copy-start.12 = (bf16[4,4,2]{1,2,0:T(2,128)(2,1)S(1)}, bf16[4,4,2]{1,2,0:T(2,128)(2,1)}, u32[]{:S(2)}) copy-start(bf16[4,4,2]{1,2,0:T(2,128)(2,1)} %param.30) | copy-start | bytes 196
  208.2 19.6 %all-to-all-start.2 = ((bf16[16,8,4096]{2,1,0:T(8,128)(2,1)}), bf16[16,8,4096]{2,1,0:T(8,128)(2,1)S(1)}, u32[]{:S(2)}, u32[]{:S(2)}) async-start(bf16[16,8,4096]{2,1,0:T(8,128)(2,1)} %maximum_bitcast_fusion), calls=%async_computation.2 | async-start | bytes 2097152 | tf_op jit(solution)/shard_map/all_to_all | solution.py:471

commit v9 on v7

--- a/solution.py
+++ b/solution.py
@@ -403,6 +403,7 @@
     own_sum = paired(*own_out)
     to_left = left_sum[half:] + for_left.astype(F32)
     to_right = right_sum[:half] + for_right.astype(F32)
+    (own_sum,) = after((own_sum,), to_left, to_right)
     first_half = own_sum[:half] + from_right.astype(F32)
     second_half = own_sum[half:] + from_left.astype(F32)
     first_half, second_half = lax.optimization_barrier((first_half, second_half))
@@ -474,8 +475,9 @@
     ).astype(F32)
     summed = jnp.sum(returned.reshape(splits, EXPERTS * capacity, D), axis=0)
     weights = jnp.sum(matches.astype(F32) * gate_vals.astype(F32)[None], axis=2)
-    expert_out = jnp.dot(weights.T, summed, precision=lax.Precision.HIGHEST)
-    return (hidden_state + expert_out).astype(BF16).reshape(resid.shape)
+    weights = weights.reshape((-1,) + resid.shape[:2])
+    expert_out = jnp.einsum("qab,qd->abd", weights, summed, precision=lax.Precision.HIGHEST)
+    return (hidden_state.reshape(resid.shape) + expert_out).astype(BF16)
 
 
 def solution(mesh):

time: 229 us -> 229 us (level)
  no operation moved by 1% of the time
where the time goes in v9:
time: 229 us
  waiting for transfers between devices  106 us (46%)
  starting transfers between devices  45.5 us (20%)
  Pallas kernels  38.4 us (17%)
  blocking collectives  21.2 us (9%)
  local copies, waits for them, and re-layouts  11.4 us (5%)
  other arithmetic  3.94 us (2%)
    all_to_all x1, waiting for transfers between devices, per_device(): lax.all_to_all(partial_rows, 'exp', split_axis=0, concat_axis=0, tiled=True)  29.8 us
    pallas_call x4, Pallas kernels, expert_block(): pl.pallas_call(lambda *refs: expert_kernel(len(parts), *refs), out_shape=...  25.1 us
    all_to_all x1, blocking collectives, per_device(): lax.all_to_all(jnp.tile(outgoing, (splits, 1)), 'exp', split_axis=0, conc...  21.2 us
    all_to_all x1, waiting for transfers between devices, per_device(): lax.all_to_all(own_rows.astype(BF16), 'exp', split_axis=0, concat_axis=0,...  15.7 us
    ppermute x6, starting transfers between devices, from_others(): return [lax.ppermute(value, 'exp', shift(by)) for by in (1, 2, 3)]  13 us
    ppermute x6, waiting for transfers between devices, from_others(): return [lax.ppermute(value, 'exp', shift(by)) for by in (1, 2, 3)]  12.2 us
    ppermute x1, waiting for transfers between devices, experts(): for_right = lax.ppermute(far_sum[:half], 'seq', x_shift(1))  11.6 us
    ppermute x1, waiting for transfers between devices, experts(): then_left = lax.ppermute(to_right.astype(BF16), 'seq', x_shift(1))  10.7 us
  transfers between devices with their start and end apart: 35, of which 20 were waited for; matrix products, arithmetic and copies ran while one was open for 2% of the time, Pallas kernels for 11%

profile of v9, /device:TPU:0, one launch (start us, length us, event | category | flops | bytes accessed | tf_op | source)
XLA Modules:
  0.0 228.6 jit_solution(9840082006132410502)
XLA Ops:
  0.0 0.8 slice.38
  0.8 1.3 collective-permute-start
  2.1 1.0 reshape.86.xin
  3.1 1.5 mixer_in.1
  4.6 2.5 %collective-permute-start.1 = (bf16[288,256]{1,0:T(8,128)(2,1)S(1)}, bf16[288,256]{1,0:T(8,128)(2,1)S(1)}, u32[]{:S(2)}, u32[]{:S(2)}) collective-permute-start(bf16[288,256]{1,0:T(8,128)(2,1)S(1)} %get-tuple-element.31), channel_id=1, source_target_pairs={{0,1},{1,2},{2,3},{3,0},{4,5},{5,6},{6,7},{7,4},{8,9},{9,10},{10,1... | collective-permute-start | bytes 442376 | tf_op jit(solution)/shard_map/ppermute | solution.py:44
  7.2 3.6 %collective-permute-start.2 = (bf16[288,256]{1,0:T(8,128)(2,1)S(1)}, bf16[288,256]{1,0:T(8,128)(2,1)S(1)}, u32[]{:S(2)}, u32[]{:S(2)}) collective-permute-start(bf16[288,256]{1,0:T(8,128)(2,1)S(1)} %get-tuple-element.31), channel_id=1, source_target_pairs={{0,2},{1,3},{2,0},{3,1},{4,6},{5,7},{6,4},{7,5},{8,10},{9,11},{10,... | collective-permute-start | bytes 442376 | tf_op jit(solution)/shard_map/ppermute | solution.py:44
  10.7 1.0 collective-permute-start.3
  11.8 1.1 collective-permute-done.1
  12.9 4.9 %collective-permute-done.2 = bf16[288,256]{1,0:T(8,128)(2,1)S(1)} collective-permute-done((bf16[288,256]{1,0:T(8,128)(2,1)S(1)}, bf16[288,256]{1,0:T(8,128)(2,1)S(1)}, u32[]{:S(2)}, u32[]{:S(2)}) %collective-permute-start.2) | collective-permute-done | bytes 147488 | tf_op jit(solution)/shard_map/ppermute | solution.py:44
  17.9 1.6 collective-permute-start.4
  19.5 2.9 %collective-permute-start.5 = (bf16[288,256]{1,0:T(8,128)(2,1)S(1)}, bf16[288,256]{1,0:T(8,128)(2,1)S(1)}, u32[]{:S(2)}, u32[]{:S(2)}) collective-permute-start(bf16[288,256]{1,0:T(8,128)(2,1)S(1)} %add_convert_fusion.3.p0), channel_id=1, source_target_pairs={{0,8},{1,9},{2,10},{3,11},{4,12},{5,13},{6,14},{7,15},{8,0},{9,1},... | collective-permute-start | bytes 442376 | tf_op jit(solution)/shard_map/ppermute | solution.py:44
  22.5 1.3 collective-permute-start.6
  23.8 1.8 collective-permute-done.4.p1
  25.6 4.3 %collective-permute-done.5.p2 = bf16[288,256]{1,0:T(8,128)(2,1)S(1)} collective-permute-done((bf16[288,256]{1,0:T(8,128)(2,1)S(1)}, bf16[288,256]{1,0:T(8,128)(2,1)S(1)}, u32[]{:S(2)}, u32[]{:S(2)}) %collective-permute-start.5) | collective-permute-done | bytes 147488 | tf_op jit(solution)/shard_map/ppermute | solution.py:44
  29.9 4.0 %section_scan.1 = (f32[256,512]{1,0:T(8,128)S(1)}, f32[32,256]{1,0:T(8,128)S(1)}, bf16[72,512]{1,0:T(8,128)(2,1)S(1)}) custom-call(bf16[288,256]{1,0:T(8,128)(2,1)S(1)} %add_convert_fusion.3.p0, bf16[288,256]{1,0:T(8,128)(2,1)S(1)} %collective-permute-done.4.p1, bf16[288,256]{1,0:T(8,128)(2,1)S(1)} %collective-permute-done.5.p2, ...), custom_call_target="tpu_custom_call" | custom-call | tf_op jit(solution)/shard_map/section_scan/pallas_call | solution.py:272
  33.9 1.1 collective-permute-start.7
  35.1 1.2 collective-permute-start.8
  36.3 2.5 %collective-permute-start.9 = (bf16[72,512]{1,0:T(8,128)(2,1)S(1)}, bf16[72,512]{1,0:T(8,128)(2,1)S(1)}, u32[]{:S(2)}, u32[]{:S(2)}) collective-permute-start(bf16[72,512]{1,0:T(8,128)(2,1)S(1)} %get-tuple-element.33), channel_id=1, source_target_pairs={{0,96},{16,112},{32,0},{48,16},{64,32},{80,48},{96,64},{112,80},{1... | collective-permute-start | bytes 221192 | tf_op jit(solution)/shard_map/ppermute | solution.py:444
  38.8 1.2 collective-permute-done.7.refs_0_
  40.0 0.9 collective-permute-done.8.refs_1_
  40.9 0.4 collective-permute-done.9.refs_2_
  41.5 0.7 collective-permute-done.12.refs_5_
  42.2 0.4 collective-permute-done.13.refs_6_
  42.6 7.7 %mixer_out.1 = bf16[256,4096]{1,0:T(8,128)(2,1)} custom-call(s32[1]{0:T(128)} %bitcast.section, bf16[72,512]{1,0:T(8,128)(2,1)S(1)} %collective-permute-done.7.refs_0_, bf16[72,512]{1,0:T(8,128)(2,1)S(1)} %collective-permute-done.8.refs_1_, bf16[72,512]{1,0:T(8,128)(2,1)S(1)} %collective-permute-done.9.refs_2_, ...), custom_call_target="tpu_custom_call" | custom-call | tf_op jit(solution)/shard_map/mixer_out/pallas_call | solution.py:295
  50.4 6.0 %all-to-all-start = ((bf16[16,16,4096]{2,1,0:T(8,128)(2,1)}), bf16[16,16,4096]{2,1,0:T(8,128)(2,1)S(1)}, u32[]{:S(2)}, u32[]{:S(2)}) async-start(bf16[16,16,4096]{2,1,0:T(8,128)(2,1)} %bitcast.5), calls=%async_computation | async-start | bytes 4194304 | tf_op jit(solution)/shard_map/all_to_all | solution.py:456
  57.4 29.8 %all-to-all-done = bf16[16,16,4096]{2,1,0:T(8,128)(2,1)S(1)} async-done(((bf16[16,16,4096]{2,1,0:T(8,128)(2,1)}), bf16[16,16,4096]{2,1,0:T(8,128)(2,1)S(1)}, u32[]{:S(2)}, u32[]{:S(2)}) %all-to-all-start) | async-done | bytes 2097184 | tf_op jit(solution)/shard_map/all_to_all | solution.py:456
  87.2 0.3 convert_reduce_fusion
  87.8 0.3 convolution_convert_fusion
  88.3 21.2 %all_to_all.26 = bf16[16,8,4096]{2,1,0:T(8,128)(2,1)S(1)} all-to-all(bf16[16,8,4096]{2,1,0:T(8,128)(2,1)S(1)} %bitcast.31), channel_id=1, replica_groups=mesh['seq'=8,'exp'=16] {'exp'}, dimensions={0} | all-to-all | bytes 2097152 | tf_op jit(solution)/shard_map/all_to_all | solution.py:469
  109.5 0.4 collective-permute-start.16
  110.0 2.8 %collective-permute-start.17 = (bf16[128,4096]{1,0:T(8,128)(2,1)S(1)}, bf16[128,4096]{1,0:T(8,128)(2,1)S(1)}, u32[]{:S(2)}, u32[]{:S(2)}) collective-permute-start(bf16[128,4096]{1,0:T(8,128)(2,1)S(1)} %bitcast.27), channel_id=1, source_target_pairs={{0,96},{16,112},{32,0},{48,16},{64,32},{80,48},{96,64},{112,80},{1... | collective-permute-start | bytes 3145736 | tf_op jit(solution)/shard_map/ppermute | solution.py:385
  112.8 2.8 %copy-done = bf16[1,4096,768]{2,1,0:T(8,128)(2,1)S(1)} copy-done((bf16[1,4096,768]{2,1,0:T(8,128)(2,1)S(1)}, bf16[1,4096,768]{2,1,0:T(8,128)(2,1)}, u32[]{:S(2)}) %copy-start) | copy-done | bytes 6291480
  115.6 2.8 %copy-done.2 = bf16[1,4096,768]{2,1,0:T(8,128)(2,1)S(1)} copy-done((bf16[1,4096,768]{2,1,0:T(8,128)(2,1)S(1)}, bf16[1,4096,768]{2,1,0:T(8,128)(2,1)}, u32[]{:S(2)}) %copy-start.2) | copy-done | bytes 6291480
  118.3 2.8 %copy-done.3 = bf16[1,768,4096]{2,1,0:T(8,128)(2,1)S(1)} copy-done((bf16[1,768,4096]{2,1,0:T(8,128)(2,1)S(1)}, bf16[1,768,4096]{2,1,0:T(8,128)(2,1)}, u32[]{:S(2)}) %copy-start.3) | copy-done | bytes 6291480
  121.1 6.3 %experts_256.4 = (bf16[128,4096]{1,0:T(8,128)(2,1)S(1)}, bf16[128,4096]{1,0:T(8,128)(2,1)S(1)}) custom-call(bf16[128,4096]{1,0:T(8,128)(2,1)S(1)} %bitcast.28, bf16[128,4096]{1,0:T(8,128)(2,1)S(1)} %collective-permute-done.14.refs_1_, bf16[1,4096,768]{2,1,0:T(8,128)(2,1)S(1)} %copy-done, bf16[1,4096,768]{2,1,0:T(8,128)(2,1)S(1)} %copy-done.2, ...), custom_call_target="tpu_custom_call" | custom-call | flops 4831838208 | bytes 4194304 | tf_op jit(solution)/shard_map/experts_256/pallas_call | solution.py:344
  127.4 8.9 %collective-permute-done.16.refs_0_ = bf16[128,4096]{1,0:T(8,128)(2,1)S(1)} collective-permute-done((bf16[128,4096]{1,0:T(8,128)(2,1)S(1)}, bf16[128,4096]{1,0:T(8,128)(2,1)S(1)}, u32[]{:S(2)}, u32[]{:S(2)}) %collective-permute-start.16) | collective-permute-done | bytes 1048608 | tf_op jit(solution)/shard_map/ppermute | solution.py:384
  136.3 0.5 collective-permute-start.20
  136.9 0.3 collective-permute-start.18
  137.2 3.0 %collective-permute-start.19 = (bf16[64,4096]{1,0:T(8,128)(2,1)S(1)}, bf16[64,4096]{1,0:T(8,128)(2,1)S(1)}, u32[]{:S(2)}, u32[]{:S(2)}) collective-permute-start(bf16[64,4096]{1,0:T(8,128)(2,1)S(1)} %slice.41), channel_id=1, source_target_pairs={{0,96},{16,112},{32,0},{48,16},{64,32},{80,48},{96,64},{112,80},{1... | collective-permute-start | bytes 1572872 | tf_op jit(solution)/shard_map/ppermute | solution.py:390
  140.2 6.3 %experts_256.6 = (bf16[128,4096]{1,0:T(8,128)(2,1)S(1)}, bf16[128,4096]{1,0:T(8,128)(2,1)S(1)}) custom-call(bf16[128,4096]{1,0:T(8,128)(2,1)S(1)} %collective-permute-done.17.refs_0_, bf16[128,4096]{1,0:T(8,128)(2,1)S(1)} %collective-permute-done.21.refs_1_, bf16[1,4096,768]{2,1,0:T(8,128)(2,1)S(1)} %copy-done.1, bf16[1,4096,768]{2,1,0:T(8,128)(2,1)S(1)} %copy-done.2, ...), custom_call_target="tpu_custom_call" | custom-call | flops 4831838208 | bytes 4194304 | tf_op jit(solution)/shard_map/experts_256/pallas_call | solution.py:344
  146.5 6.3 %experts_256.5 = (bf16[128,4096]{1,0:T(8,128)(2,1)S(1)}, bf16[128,4096]{1,0:T(8,128)(2,1)S(1)}) custom-call(bf16[128,4096]{1,0:T(8,128)(2,1)S(1)} %collective-permute-done.16.refs_0_, bf16[128,4096]{1,0:T(8,128)(2,1)S(1)} %collective-permute-done.20.refs_1_, bf16[1,4096,768]{2,1,0:T(8,128)(2,1)S(1)} %copy-done.1, bf16[1,4096,768]{2,1,0:T(8,128)(2,1)S(1)} %copy-done.2, ...), custom_call_target="tpu_custom_call" | custom-call | flops 4831838208 | bytes 4194304 | tf_op jit(solution)/shard_map/experts_256/pallas_call | solution.py:344
  152.9 0.5 collective-permute-start.26
  153.5 0.4 collective-permute-start.24
  154.0 1.6 collective-permute-done.22
  155.6 0.2 convert_add_fusion.1
  155.9 2.2 collective-permute-start.25
  158.1 0.2 convert_add_fusion
  158.6 6.3 %experts_256.7 = (bf16[128,4096]{1,0:T(8,128)(2,1)S(1)}, bf16[128,4096]{1,0:T(8,128)(2,1)S(1)}) custom-call(bf16[64,4096]{1,0:T(8,128)(2,1)S(1)} %collective-permute-done.18.refs_0_, bf16[64,4096]{1,0:T(8,128)(2,1)S(1)} %collective-permute-done.19.refs_1_, bf16[64,4096]{1,0:T(8,128)(2,1)S(1)} %collective-permute-done.23.refs_2_, ...), custom_call_target="tpu_custom_call" | custom-call | flops 4831838208 | bytes 4194304 | tf_op jit(solution)/shard_map/experts_256/pallas_call | solution.py:344
  164.9 5.1 %collective-permute-done.25 = bf16[64,4096]{1,0:T(8,128)(2,1)S(1)} collective-permute-done((bf16[64,4096]{1,0:T(8,128)(2,1)S(1)}, bf16[64,4096]{1,0:T(8,128)(2,1)S(1)}, u32[]{:S(2)}, u32[]{:S(2)}) %collective-permute-start.25) | collective-permute-done | bytes 524320 | tf_op jit(solution)/shard_map/ppermute | solution.py:396
  169.9 3.4 %collective-permute-done.27 = bf16[64,4096]{1,0:T(8,128)(2,1)S(1)} collective-permute-done((bf16[64,4096]{1,0:T(8,128)(2,1)S(1)}, bf16[64,4096]{1,0:T(8,128)(2,1)S(1)}, u32[]{:S(2)}, u32[]{:S(2)}) %collective-permute-start.27) | collective-permute-done | bytes 524320 | tf_op jit(solution)/shard_map/ppermute | solution.py:397
  173.4 0.5 collective-permute-start.15
  173.9 2.1 collective-permute-done.28
  176.1 0.2 add_convert_fusion
  176.5 1.1 collective-permute-done.15
  177.6 0.3 convert_add_fusion.2
  177.8 2.2 collective-permute-start.29
  180.0 11.6 %collective-permute-done.30 = bf16[64,4096]{1,0:T(8,128)(2,1)S(1)} collective-permute-done((bf16[64,4096]{1,0:T(8,128)(2,1)S(1)}, bf16[64,4096]{1,0:T(8,128)(2,1)S(1)}, u32[]{:S(2)}, u32[]{:S(2)}) %collective-permute-start.30) | collective-permute-done | bytes 524320 | tf_op jit(solution)/shard_map/ppermute | solution.py:401
  191.9 3.3 %collective-permute-start.32 = (bf16[64,4096]{1,0:T(8,128)(2,1)S(1)}, bf16[64,4096]{1,0:T(8,128)(2,1)S(1)}, u32[]{:S(2)}, u32[]{:S(2)}) collective-permute-start(bf16[64,4096]{1,0:T(8,128)(2,1)S(1)} %slice_add_fusion.1), channel_id=1, source_target_pairs={{0,96},{16,112},{32,0},{48,16},{64,32},{80,48},{96,64},{112,80},{1... | collective-permute-start | bytes 1572872 | tf_op jit(solution)/shard_map/ppermute | solution.py:410
  195.2 0.3 convert_add_fusion.3
  195.5 10.7 %collective-permute-done.31 = bf16[64,4096]{1,0:T(8,128)(2,1)S(1)} collective-permute-done((bf16[64,4096]{1,0:T(8,128)(2,1)S(1)}, bf16[64,4096]{1,0:T(8,128)(2,1)S(1)}, u32[]{:S(2)}, u32[]{:S(2)}) %collective-permute-start.31) | collective-permute-done | bytes 524320 | tf_op jit(solution)/shard_map/ppermute | solution.py:411
  206.4 1.1 maximum_bitcast_fusion
  207.5 3.7 %all-to-all-start.2 = ((bf16[16,8,4096]{2,1,0:T(8,128)(2,1)}), bf16[16,8,4096]{2,1,0:T(8,128)(2,1)S(1)}, u32[]{:S(2)}, u32[]{:S(2)}) async-start(bf16[16,8,4096]{2,1,0:T(8,128)(2,1)} %maximum_bitcast_fusion), calls=%async_computation.2 | async-start | bytes 2097152 | tf_op jit(solution)/shard_map/all_to_all | solution.py:473
  211.3 15.7 %all-to-all-done.2 = bf16[16,8,4096]{2,1,0:T(8,128)(2,1)S(1)} async-done(((bf16[16,8,4096]{2,1,0:T(8,128)(2,1)}), bf16[16,8,4096]{2,1,0:T(8,128)(2,1)S(1)}, u32[]{:S(2)}, u32[]{:S(2)}) %all-to-all-start.2) | async-done | bytes 1048608 | tf_op jit(solution)/shard_map/all_to_all | solution.py:473
  227.2 1.3 fusion
  (86 shorter events, 3.2 us)
Async XLA Ops:
  0.0 42.6 %copy-start.4 = (f32[16,512]{1,0:T(8,128)S(1)}, f32[16,512]{1,0:T(8,128)}, u32[]{:S(2)}) copy-start(f32[16,512]{1,0:T(8,128)} %refs_10_.1) | copy-start | bytes 98308
  0.0 41.4 %copy-start.7 = (bf16[64,4,512]{2,1,0:T(4,128)(2,1)S(1)}, bf16[64,4,512]{2,1,0:T(4,128)(2,1)}, u32[]{:S(2)}) copy-start(bf16[64,4,512]{2,1,0:T(4,128)(2,1)} %param.18) | copy-start | bytes 786436
  0.0 42.6 %copy-start.5 = (f32[512]{0:T(512)S(1)}, f32[512]{0:T(512)}, u32[]{:S(2)}) copy-start(f32[512]{0:T(512)} %param.25) | copy-start | bytes 6148
  0.8 2.3 %collective-permute-start = (bf16[12,512]{1,0:T(8,128)(2,1)S(1)}, bf16[12,512]{1,0:T(8,128)(2,1)S(1)}, u32[]{:S(2)}, u32[]{:S(2)}) collective-permute-start(bf16[12,512]{1,0:T(8,128)(2,1)S(1)} %slice.39), channel_id=1, source_target_pairs={{0,16},{16,32},{32,48},{48,64},{64,80},{80,96},{96,112},{1,17},{17... | collective-permute-start | bytes 36872 | tf_op jit(solution)/shard_map/ppermute | solution.py:40
  4.6 8.2 %collective-permute-start.1 = (bf16[288,256]{1,0:T(8,128)(2,1)S(1)}, bf16[288,256]{1,0:T(8,128)(2,1)S(1)}, u32[]{:S(2)}, u32[]{:S(2)}) collective-permute-start(bf16[288,256]{1,0:T(8,128)(2,1)S(1)} %get-tuple-element.31), channel_id=1, source_target_pairs={{0,1},{1,2},{2,3},{3,0},{4,5},{5,6},{6,7},{7,4},{8,9},{9,10},{10,1... | collective-permute-start | bytes 442376 | tf_op jit(solution)/shard_map/ppermute | solution.py:44
  7.2 10.7 %collective-permute-start.2 = (bf16[288,256]{1,0:T(8,128)(2,1)S(1)}, bf16[288,256]{1,0:T(8,128)(2,1)S(1)}, u32[]{:S(2)}, u32[]{:S(2)}) collective-permute-start(bf16[288,256]{1,0:T(8,128)(2,1)S(1)} %get-tuple-element.31), channel_id=1, source_target_pairs={{0,2},{1,3},{2,0},{3,1},{4,6},{5,7},{6,4},{7,5},{8,10},{9,11},{10,... | collective-permute-start | bytes 442376 | tf_op jit(solution)/shard_map/ppermute | solution.py:44
  10.7 7.1 %collective-permute-start.3 = (bf16[288,256]{1,0:T(8,128)(2,1)S(1)}, bf16[288,256]{1,0:T(8,128)(2,1)S(1)}, u32[]{:S(2)}, u32[]{:S(2)}) collective-permute-start(bf16[288,256]{1,0:T(8,128)(2,1)S(1)} %get-tuple-element.31), channel_id=1, source_target_pairs={{0,3},{1,0},{2,1},{3,2},{4,7},{5,4},{6,5},{7,6},{8,11},{9,8},{10,9... | collective-permute-start | bytes 442376 | tf_op jit(solution)/shard_map/ppermute | solution.py:44
  17.9 7.7 %collective-permute-start.4 = (bf16[288,256]{1,0:T(8,128)(2,1)S(1)}, bf16[288,256]{1,0:T(8,128)(2,1)S(1)}, u32[]{:S(2)}, u32[]{:S(2)}) collective-permute-start(bf16[288,256]{1,0:T(8,128)(2,1)S(1)} %add_convert_fusion.3.p0), channel_id=1, source_target_pairs={{0,4},{1,5},{2,6},{3,7},{4,8},{5,9},{6,10},{7,11},{8,12},{9,13},{1... | collective-permute-start | bytes 442376 | tf_op jit(solution)/shard_map/ppermute | solution.py:44
  19.5 10.4 %collective-permute-start.5 = (bf16[288,256]{1,0:T(8,128)(2,1)S(1)}, bf16[288,256]{1,0:T(8,128)(2,1)S(1)}, u32[]{:S(2)}, u32[]{:S(2)}) collective-permute-start(bf16[288,256]{1,0:T(8,128)(2,1)S(1)} %add_convert_fusion.3.p0), channel_id=1, source_target_pairs={{0,8},{1,9},{2,10},{3,11},{4,12},{5,13},{6,14},{7,15},{8,0},{9,1},... | collective-permute-start | bytes 442376 | tf_op jit(solution)/shard_map/ppermute | solution.py:44
  22.5 7.5 %collective-permute-start.6 = (bf16[288,256]{1,0:T(8,128)(2,1)S(1)}, bf16[288,256]{1,0:T(8,128)(2,1)S(1)}, u32[]{:S(2)}, u32[]{:S(2)}) collective-permute-start(bf16[288,256]{1,0:T(8,128)(2,1)S(1)} %add_convert_fusion.3.p0), channel_id=1, source_target_pairs={{0,12},{1,13},{2,14},{3,15},{4,0},{5,1},{6,2},{7,3},{8,4},{9,5},{1... | collective-permute-start | bytes 442376 | tf_op jit(solution)/shard_map/ppermute | solution.py:44
  33.9 6.1 %collective-permute-start.7 = (bf16[72,512]{1,0:T(8,128)(2,1)S(1)}, bf16[72,512]{1,0:T(8,128)(2,1)S(1)}, u32[]{:S(2)}, u32[]{:S(2)}) collective-permute-start(bf16[72,512]{1,0:T(8,128)(2,1)S(1)} %get-tuple-element.33), channel_id=1, source_target_pairs={{0,32},{16,48},{32,64},{48,80},{64,96},{80,112},{96,0},{112,16},{1... | collective-permute-start | bytes 221192 | tf_op jit(solution)/shard_map/ppermute | solution.py:444
  35.1 5.9 %collective-permute-start.8 = (bf16[72,512]{1,0:T(8,128)(2,1)S(1)}, bf16[72,512]{1,0:T(8,128)(2,1)S(1)}, u32[]{:S(2)}, u32[]{:S(2)}) collective-permute-start(bf16[72,512]{1,0:T(8,128)(2,1)S(1)} %get-tuple-element.33), channel_id=1, source_target_pairs={{0,64},{16,80},{32,96},{48,112},{64,0},{80,16},{96,32},{112,48},{1... | collective-permute-start | bytes 221192 | tf_op jit(solution)/shard_map/ppermute | solution.py:444
  36.3 5.1 %collective-permute-start.9 = (bf16[72,512]{1,0:T(8,128)(2,1)S(1)}, bf16[72,512]{1,0:T(8,128)(2,1)S(1)}, u32[]{:S(2)}, u32[]{:S(2)}) collective-permute-start(bf16[72,512]{1,0:T(8,128)(2,1)S(1)} %get-tuple-element.33), channel_id=1, source_target_pairs={{0,96},{16,112},{32,0},{48,16},{64,32},{80,48},{96,64},{112,80},{1... | collective-permute-start | bytes 221192 | tf_op jit(solution)/shard_map/ppermute | solution.py:444
  38.8 2.7 %collective-permute-start.10 = (bf16[72,512]{1,0:T(8,128)(2,1)S(1)}, bf16[72,512]{1,0:T(8,128)(2,1)S(1)}, u32[]{:S(2)}, u32[]{:S(2)}) collective-permute-start(bf16[72,512]{1,0:T(8,128)(2,1)S(1)} %get-tuple-element.33), channel_id=1, source_target_pairs={{0,16},{16,0},{32,48},{48,32},{64,80},{80,64},{96,112},{112,96},{1... | collective-permute-start | bytes 221192 | tf_op jit(solution)/shard_map/ppermute | solution.py:48
  40.0 1.5 collective-permute-start.11
  40.9 1.3 collective-permute-start.12
  41.4 1.3 collective-permute-start.13
  50.4 6.1 %copy-start.9 = (s32[4,4,2]{1,2,0:T(2,128)S(1)}, s32[4,4,2]{1,2,0:T(2,128)}, u32[]{:S(2)}) copy-start(s32[4,4,2]{1,2,0:T(2,128)} %param.29) | copy-start | bytes 388
  50.4 6.9 %copy-start.6 = (bf16[4,4,4096]{2,1,0:T(4,128)(2,1)S(1)}, bf16[4,4,4096]{2,1,0:T(4,128)(2,1)}, u32[]{:S(2)}) copy-start(bf16[4,4,4096]{2,1,0:T(4,128)(2,1)} %param.27) | copy-start | bytes 393220
  50.4 36.8 %all-to-all-start = ((bf16[16,16,4096]{2,1,0:T(8,128)(2,1)}), bf16[16,16,4096]{2,1,0:T(8,128)(2,1)S(1)}, u32[]{:S(2)}, u32[]{:S(2)}) async-start(bf16[16,16,4096]{2,1,0:T(8,128)(2,1)} %bitcast.5), calls=%async_computation | async-start | bytes 4194304 | tf_op jit(solution)/shard_map/all_to_all | solution.py:456
  56.5 31.4 %copy-start.8 = (f32[4096]{0:T(1024)S(1)}, f32[4096]{0:T(1024)}, u32[]{:S(2)}) copy-start(f32[4096]{0:T(1024)} %param.28) | copy-start | bytes 49156
  109.5 3.2 %collective-permute-start.14 = (bf16[128,4096]{1,0:T(8,128)(2,1)S(1)}, bf16[128,4096]{1,0:T(8,128)(2,1)S(1)}, u32[]{:S(2)}, u32[]{:S(2)}) collective-permute-start(bf16[128,4096]{1,0:T(8,128)(2,1)S(1)} %bitcast.25), channel_id=1, source_target_pairs={{0,16},{16,0},{32,48},{48,32},{64,80},{80,64},{96,112},{112,96},{1... | collective-permute-start | bytes 3145736 | tf_op jit(solution)/shard_map/ppermute | solution.py:48
  109.5 26.8 %collective-permute-start.16 = (bf16[128,4096]{1,0:T(8,128)(2,1)S(1)}, bf16[128,4096]{1,0:T(8,128)(2,1)S(1)}, u32[]{:S(2)}, u32[]{:S(2)}) collective-permute-start(bf16[128,4096]{1,0:T(8,128)(2,1)S(1)} %bitcast.26), channel_id=1, source_target_pairs={{0,32},{16,48},{32,64},{48,80},{64,96},{80,112},{96,0},{112,16},{1... | collective-permute-start | bytes 3145736 | tf_op jit(solution)/shard_map/ppermute | solution.py:384
  110.0 26.4 %collective-permute-start.17 = (bf16[128,4096]{1,0:T(8,128)(2,1)S(1)}, bf16[128,4096]{1,0:T(8,128)(2,1)S(1)}, u32[]{:S(2)}, u32[]{:S(2)}) collective-permute-start(bf16[128,4096]{1,0:T(8,128)(2,1)S(1)} %bitcast.27), channel_id=1, source_target_pairs={{0,96},{16,112},{32,0},{48,16},{64,32},{80,48},{96,64},{112,80},{1... | collective-permute-start | bytes 3145736 | tf_op jit(solution)/shard_map/ppermute | solution.py:385
  112.8 2.8 %copy-start = (bf16[1,4096,768]{2,1,0:T(8,128)(2,1)S(1)}, bf16[1,4096,768]{2,1,0:T(8,128)(2,1)}, u32[]{:S(2)}) copy-start(bf16[1,4096,768]{2,1,0:T(8,128)(2,1)} %refs_4_.7) | copy-start | bytes 18874372
  115.6 2.8 %copy-start.2 = (bf16[1,4096,768]{2,1,0:T(8,128)(2,1)S(1)}, bf16[1,4096,768]{2,1,0:T(8,128)(2,1)}, u32[]{:S(2)}) copy-start(bf16[1,4096,768]{2,1,0:T(8,128)(2,1)} %refs_5_.1) | copy-start | bytes 18874372
  118.3 2.8 %copy-start.3 = (bf16[1,768,4096]{2,1,0:T(8,128)(2,1)S(1)}, bf16[1,768,4096]{2,1,0:T(8,128)(2,1)}, u32[]{:S(2)}) copy-start(bf16[1,768,4096]{2,1,0:T(8,128)(2,1)} %refs_6_.1) | copy-start | bytes 18874372
  121.1 19.1 %copy-start.1 = (bf16[1,4096,768]{2,1,0:T(8,128)(2,1)S(1)}, bf16[1,4096,768]{2,1,0:T(8,128)(2,1)}, u32[]{:S(2)}) copy-start(bf16[1,4096,768]{2,1,0:T(8,128)(2,1)} %refs_4_.7) | copy-start | bytes 18874372
  136.3 3.9 %collective-permute-start.21 = (bf16[128,4096]{1,0:T(8,128)(2,1)S(1)}, bf16[128,4096]{1,0:T(8,128)(2,1)S(1)}, u32[]{:S(2)}, u32[]{:S(2)}) collective-permute-start(bf16[128,4096]{1,0:T(8,128)(2,1)S(1)} %collective-permute-done.17.refs_0_), channel_id=1, source_target_pairs={{0,16},{16,0},{32,48},{48,32},{64,80},{80,64},{96,112},{112,96},{1... | collective-permute-start | bytes 3145736 | tf_op jit(solution)/shard_map/ppermute | solution.py:48
  136.3 10.2 %collective-permute-start.20 = (bf16[128,4096]{1,0:T(8,128)(2,1)S(1)}, bf16[128,4096]{1,0:T(8,128)(2,1)S(1)}, u32[]{:S(2)}, u32[]{:S(2)}) collective-permute-start(bf16[128,4096]{1,0:T(8,128)(2,1)S(1)} %collective-permute-done.16.refs_0_), channel_id=1, source_target_pairs={{0,16},{16,0},{32,48},{48,32},{64,80},{80,64},{96,112},{112,96},{1... | collective-permute-start | bytes 3145736 | tf_op jit(solution)/shard_map/ppermute | solution.py:48
  136.9 15.9 %collective-permute-start.18 = (bf16[64,4096]{1,0:T(8,128)(2,1)S(1)}, bf16[64,4096]{1,0:T(8,128)(2,1)S(1)}, u32[]{:S(2)}, u32[]{:S(2)}) collective-permute-start(bf16[64,4096]{1,0:T(8,128)(2,1)S(1)} %slice.40), channel_id=1, source_target_pairs={{0,32},{16,48},{32,64},{48,80},{64,96},{80,112},{96,0},{112,16},{1... | collective-permute-start | bytes 1572872 | tf_op jit(solution)/shard_map/ppermute | solution.py:389
  137.2 15.7 %collective-permute-start.19 = (bf16[64,4096]{1,0:T(8,128)(2,1)S(1)}, bf16[64,4096]{1,0:T(8,128)(2,1)S(1)}, u32[]{:S(2)}, u32[]{:S(2)}) collective-permute-start(bf16[64,4096]{1,0:T(8,128)(2,1)S(1)} %slice.41), channel_id=1, source_target_pairs={{0,96},{16,112},{32,0},{48,16},{64,32},{80,48},{96,64},{112,80},{1... | collective-permute-start | bytes 1572872 | tf_op jit(solution)/shard_map/ppermute | solution.py:390
  140.2 18.4 %slice-start = ((s8[6291456]{0:T(1024)(128)(4,1)}), s8[4194304]{0:T(1024)(128)(4,1)S(1)}, s32[]{:S(2)}) async-start(s8[6291456]{0:T(1024)(128)(4,1)} %bitcast.23), calls=%async_computation.3 | async-start | bytes 8388608
  146.5 12.1 %slice-start.1 = ((s8[6291456]{0:T(1024)(128)(4,1)}), s8[2097152]{0:T(1024)(128)(4,1)S(1)}, s32[]{:S(2)}) async-start(s8[6291456]{0:T(1024)(128)(4,1)} %bitcast.23), calls=%async_computation.4 | async-start | bytes 4194304
  152.9 2.7 %collective-permute-start.22 = (bf16[128,4096]{1,0:T(8,128)(2,1)S(1)}, bf16[128,4096]{1,0:T(8,128)(2,1)S(1)}, u32[]{:S(2)}, u32[]{:S(2)}) collective-permute-start(bf16[128,4096]{1,0:T(8,128)(2,1)S(1)} %get-tuple-element.45), channel_id=1, source_target_pairs={{0,16},{16,0},{32,48},{48,32},{64,80},{80,64},{96,112},{112,96},{1... | collective-permute-start | bytes 3145736 | tf_op jit(solution)/shard_map/ppermute | solution.py:48
  152.9 5.2 %collective-permute-start.26 = (bf16[128,4096]{1,0:T(8,128)(2,1)S(1)}, bf16[128,4096]{1,0:T(8,128)(2,1)S(1)}, u32[]{:S(2)}, u32[]{:S(2)}) collective-permute-start(bf16[128,4096]{1,0:T(8,128)(2,1)S(1)} %get-tuple-element.51), channel_id=1, source_target_pairs={{0,16},{16,0},{32,48},{48,32},{64,80},{80,64},{96,112},{112,96},{1... | collective-permute-start | bytes 3145736 | tf_op jit(solution)/shard_map/ppermute | solution.py:48
  153.4 5.1 %collective-permute-start.23 = (bf16[64,4096]{1,0:T(8,128)(2,1)S(1)}, bf16[64,4096]{1,0:T(8,128)(2,1)S(1)}, u32[]{:S(2)}, u32[]{:S(2)}) collective-permute-start(bf16[64,4096]{1,0:T(8,128)(2,1)S(1)} %collective-permute-done.18.refs_0_), channel_id=1, source_target_pairs={{0,16},{16,0},{32,48},{48,32},{64,80},{80,64},{96,112},{112,96},{1... | collective-permute-start | bytes 1572872 | tf_op jit(solution)/shard_map/ppermute | solution.py:48
  153.5 5.1 %collective-permute-start.24 = (bf16[64,4096]{1,0:T(8,128)(2,1)S(1)}, bf16[64,4096]{1,0:T(8,128)(2,1)S(1)}, u32[]{:S(2)}, u32[]{:S(2)}) collective-permute-start(bf16[64,4096]{1,0:T(8,128)(2,1)S(1)} %collective-permute-done.19.refs_1_), channel_id=1, source_target_pairs={{0,16},{16,0},{32,48},{48,32},{64,80},{80,64},{96,112},{112,96},{1... | collective-permute-start | bytes 1572872 | tf_op jit(solution)/shard_map/ppermute | solution.py:48
  155.9 14.0 %collective-permute-start.25 = (bf16[64,4096]{1,0:T(8,128)(2,1)S(1)}, bf16[64,4096]{1,0:T(8,128)(2,1)S(1)}, u32[]{:S(2)}, u32[]{:S(2)}) collective-permute-start(bf16[64,4096]{1,0:T(8,128)(2,1)S(1)} %slice.63), channel_id=1, source_target_pairs={{0,96},{16,112},{32,0},{48,16},{64,32},{80,48},{96,64},{112,80},{1... | collective-permute-start | bytes 1572872 | tf_op jit(solution)/shard_map/ppermute | solution.py:396
  158.4 15.0 %collective-permute-start.27 = (bf16[64,4096]{1,0:T(8,128)(2,1)S(1)}, bf16[64,4096]{1,0:T(8,128)(2,1)S(1)}, u32[]{:S(2)}, u32[]{:S(2)}) collective-permute-start(bf16[64,4096]{1,0:T(8,128)(2,1)S(1)} %slice.62), channel_id=1, source_target_pairs={{0,32},{16,48},{32,64},{48,80},{64,96},{80,112},{96,0},{112,16},{1... | collective-permute-start | bytes 1572872 | tf_op jit(solution)/shard_map/ppermute | solution.py:397
  173.4 2.7 %collective-permute-start.28 = (bf16[128,4096]{1,0:T(8,128)(2,1)S(1)}, bf16[128,4096]{1,0:T(8,128)(2,1)S(1)}, u32[]{:S(2)}, u32[]{:S(2)}) collective-permute-start(bf16[128,4096]{1,0:T(8,128)(2,1)S(1)} %get-tuple-element.53), channel_id=1, source_target_pairs={{0,16},{16,0},{32,48},{48,32},{64,80},{80,64},{96,112},{112,96},{1... | collective-permute-start | bytes 3145736 | tf_op jit(solution)/shard_map/ppermute | solution.py:48
  173.4 4.2 %collective-permute-start.15 = (bf16[128,4096]{1,0:T(8,128)(2,1)S(1)}, bf16[128,4096]{1,0:T(8,128)(2,1)S(1)}, u32[]{:S(2)}, u32[]{:S(2)}) collective-permute-start(bf16[128,4096]{1,0:T(8,128)(2,1)S(1)} %get-tuple-element.37), channel_id=1, source_target_pairs={{0,16},{16,0},{32,48},{48,32},{64,80},{80,64},{96,112},{112,96},{1... | collective-permute-start | bytes 3145736 | tf_op jit(solution)/shard_map/ppermute | solution.py:48
  176.4 15.2 %collective-permute-start.30 = (bf16[64,4096]{1,0:T(8,128)(2,1)S(1)}, bf16[64,4096]{1,0:T(8,128)(2,1)S(1)}, u32[]{:S(2)}, u32[]{:S(2)}) collective-permute-start(bf16[64,4096]{1,0:T(8,128)(2,1)S(1)} %get-tuple-element.59), channel_id=1, source_target_pairs={{0,32},{16,48},{32,64},{48,80},{64,96},{80,112},{96,0},{112,16},{1... | collective-permute-start | bytes 1572872 | tf_op jit(solution)/shard_map/ppermute | solution.py:401
  177.8 14.0 %collective-permute-start.29 = (bf16[64,4096]{1,0:T(8,128)(2,1)S(1)}, bf16[64,4096]{1,0:T(8,128)(2,1)S(1)}, u32[]{:S(2)}, u32[]{:S(2)}) collective-permute-start(bf16[64,4096]{1,0:T(8,128)(2,1)S(1)} %get-tuple-element.60), channel_id=1, source_target_pairs={{0,96},{16,112},{32,0},{48,16},{64,32},{80,48},{96,64},{112,80},{1... | collective-permute-start | bytes 1572872 | tf_op jit(solution)/shard_map/ppermute | solution.py:402
  191.7 14.4 %collective-permute-start.31 = (bf16[64,4096]{1,0:T(8,128)(2,1)S(1)}, bf16[64,4096]{1,0:T(8,128)(2,1)S(1)}, u32[]{:S(2)}, u32[]{:S(2)}) collective-permute-start(bf16[64,4096]{1,0:T(8,128)(2,1)S(1)} %slice_add_fusion), channel_id=1, source_target_pairs={{0,32},{16,48},{32,64},{48,80},{64,96},{80,112},{96,0},{112,16},{1... | collective-permute-start | bytes 1572872 | tf_op jit(solution)/shard_map/ppermute | solution.py:411
  191.9 14.3 %collective-permute-start.32 = (bf16[64,4096]{1,0:T(8,128)(2,1)S(1)}, bf16[64,4096]{1,0:T(8,128)(2,1)S(1)}, u32[]{:S(2)}, u32[]{:S(2)}) collective-permute-start(bf16[64,4096]{1,0:T(8,128)(2,1)S(1)} %slice_add_fusion.1), channel_id=1, source_target_pairs={{0,96},{16,112},{32,0},{48,16},{64,32},{80,48},{96,64},{112,80},{1... | collective-permute-start | bytes 1572872 | tf_op jit(solution)/shard_map/ppermute | solution.py:410
  206.4 4.8 %copy-start.10 = (bf16[4,4,2]{1,2,0:T(2,128)(2,1)S(1)}, bf16[4,4,2]{1,2,0:T(2,128)(2,1)}, u32[]{:S(2)}) copy-start(bf16[4,4,2]{1,2,0:T(2,128)(2,1)} %param.30) | copy-start | bytes 196
  207.5 19.6 %all-to-all-start.2 = ((bf16[16,8,4096]{2,1,0:T(8,128)(2,1)}), bf16[16,8,4096]{2,1,0:T(8,128)(2,1)S(1)}, u32[]{:S(2)}, u32[]{:S(2)}) async-start(bf16[16,8,4096]{2,1,0:T(8,128)(2,1)} %maximum_bitcast_fusion), calls=%async_computation.2 | async-start | bytes 2097152 | tf_op jit(solution)/shard_map/all_to_all | solution.py:473

commit v10 on v9

--- a/solution.py
+++ b/solution.py
@@ -384,7 +384,8 @@
     left = lax.ppermute(own, "seq", x_shift(1))
     right = lax.ppermute(own, "seq", x_shift(-1))
     own_out = expert_block([own, swapped(own)], w_gate, w_up, w_down)
-    left, right = after((left, right), own_out)
+    own_sum = paired(*own_out)
+    left, right = after((left, right), own_sum)
     far = [
         lax.ppermute(left[:half], "seq", x_shift(1)),
         lax.ppermute(right[half:], "seq", x_shift(-1)),
@@ -400,7 +401,6 @@
     far_sum = paired(*far_out).astype(BF16)
     for_right = lax.ppermute(far_sum[:half], "seq", x_shift(1))
     for_left = lax.ppermute(far_sum[half:], "seq", x_shift(-1))
-    own_sum = paired(*own_out)
     to_left = left_sum[half:] + for_left.astype(F32)
     to_right = right_sum[:half] + for_right.astype(F32)
     (own_sum,) = after((own_sum,), to_left, to_right)

time: 229 us -> 247 us (1.079)
  waiting for transfers between devices: 106 us -> 123 us
    ppermute x1, waiting for transfers between devices: 8.88 us -> 23.1 us  [experts(): left = lax.ppermute(own, 'seq', x_shift(1))]
    unnamed x27 -> x25, local copies, waits for them, and re-layouts: 8.52 us -> 8.51 us
  transfers between devices with their start and end apart: 35 -> 35, of which waited for: 20 -> 20; matrix products, arithmetic and copies ran while one was open for 2% -> 1% of each run, Pallas kernels for 11% -> 8%
where the time goes in v10:
time: 247 us; the launch traced here: 246 us
  waiting for transfers between devices  123 us (50%)
  starting transfers between devices  46.5 us (19%)
  Pallas kernels  38.4 us (16%)
  blocking collectives  21.2 us (9%)
  local copies, waits for them, and re-layouts  11.4 us (5%)
  other arithmetic  4 us (2%)
    all_to_all x1, waiting for transfers between devices, per_device(): lax.all_to_all(partial_rows, 'exp', split_axis=0, concat_axis=0, tiled=True)  29.8 us
    pallas_call x4, Pallas kernels, expert_block(): pl.pallas_call(lambda *refs: expert_kernel(len(parts), *refs), out_shape=...  25.1 us
    ppermute x1, waiting for transfers between devices, experts(): left = lax.ppermute(own, 'seq', x_shift(1))  23.1 us
    all_to_all x1, blocking collectives, per_device(): lax.all_to_all(jnp.tile(outgoing, (splits, 1)), 'exp', split_axis=0, conc...  21.2 us
    all_to_all x1, waiting for transfers between devices, per_device(): lax.all_to_all(own_rows.astype(BF16), 'exp', split_axis=0, concat_axis=0,...  15.7 us
    ppermute x6, starting transfers between devices, from_others(): return [lax.ppermute(value, 'exp', shift(by)) for by in (1, 2, 3)]  13 us
    ppermute x6, waiting for transfers between devices, from_others(): return [lax.ppermute(value, 'exp', shift(by)) for by in (1, 2, 3)]  12.2 us
    ppermute x1, waiting for transfers between devices, experts(): for_right = lax.ppermute(far_sum[:half], 'seq', x_shift(1))  11.9 us
  transfers between devices with their start and end apart: 35, of which 20 were waited for; matrix products, arithmetic and copies ran while one was open for 1% of the time, Pallas kernels for 8%

profile of v10, /device:TPU:0, one launch (start us, length us, event | category | flops | bytes accessed | tf_op | source)
XLA Modules:
  0.0 246.2 jit_solution(15437642088872443816)
XLA Ops:
  0.0 0.8 slice.38
  0.8 1.3 collective-permute-start
  2.1 1.0 reshape.86.xin
  3.1 1.5 mixer_in.1
  4.6 2.5 %collective-permute-start.1 = (bf16[288,256]{1,0:T(8,128)(2,1)S(1)}, bf16[288,256]{1,0:T(8,128)(2,1)S(1)}, u32[]{:S(2)}, u32[]{:S(2)}) collective-permute-start(bf16[288,256]{1,0:T(8,128)(2,1)S(1)} %get-tuple-element.31), channel_id=1, source_target_pairs={{0,1},{1,2},{2,3},{3,0},{4,5},{5,6},{6,7},{7,4},{8,9},{9,10},{10,1... | collective-permute-start | bytes 442376 | tf_op jit(solution)/shard_map/ppermute | solution.py:44
  7.2 3.6 %collective-permute-start.2 = (bf16[288,256]{1,0:T(8,128)(2,1)S(1)}, bf16[288,256]{1,0:T(8,128)(2,1)S(1)}, u32[]{:S(2)}, u32[]{:S(2)}) collective-permute-start(bf16[288,256]{1,0:T(8,128)(2,1)S(1)} %get-tuple-element.31), channel_id=1, source_target_pairs={{0,2},{1,3},{2,0},{3,1},{4,6},{5,7},{6,4},{7,5},{8,10},{9,11},{10,... | collective-permute-start | bytes 442376 | tf_op jit(solution)/shard_map/ppermute | solution.py:44
  10.7 1.0 collective-permute-start.3
  11.8 1.1 collective-permute-done.1
  12.9 4.9 %collective-permute-done.2 = bf16[288,256]{1,0:T(8,128)(2,1)S(1)} collective-permute-done((bf16[288,256]{1,0:T(8,128)(2,1)S(1)}, bf16[288,256]{1,0:T(8,128)(2,1)S(1)}, u32[]{:S(2)}, u32[]{:S(2)}) %collective-permute-start.2) | collective-permute-done | bytes 147488 | tf_op jit(solution)/shard_map/ppermute | solution.py:44
  17.9 1.6 collective-permute-start.4
  19.5 2.9 %collective-permute-start.5 = (bf16[288,256]{1,0:T(8,128)(2,1)S(1)}, bf16[288,256]{1,0:T(8,128)(2,1)S(1)}, u32[]{:S(2)}, u32[]{:S(2)}) collective-permute-start(bf16[288,256]{1,0:T(8,128)(2,1)S(1)} %add_convert_fusion.3.p0), channel_id=1, source_target_pairs={{0,8},{1,9},{2,10},{3,11},{4,12},{5,13},{6,14},{7,15},{8,0},{9,1},... | collective-permute-start | bytes 442376 | tf_op jit(solution)/shard_map/ppermute | solution.py:44
  22.5 1.3 collective-permute-start.6
  23.8 1.8 collective-permute-done.4.p1
  25.6 4.3 %collective-permute-done.5.p2 = bf16[288,256]{1,0:T(8,128)(2,1)S(1)} collective-permute-done((bf16[288,256]{1,0:T(8,128)(2,1)S(1)}, bf16[288,256]{1,0:T(8,128)(2,1)S(1)}, u32[]{:S(2)}, u32[]{:S(2)}) %collective-permute-start.5) | collective-permute-done | bytes 147488 | tf_op jit(solution)/shard_map/ppermute | solution.py:44
  29.9 4.0 %section_scan.1 = (f32[256,512]{1,0:T(8,128)S(1)}, f32[32,256]{1,0:T(8,128)S(1)}, bf16[72,512]{1,0:T(8,128)(2,1)S(1)}) custom-call(bf16[288,256]{1,0:T(8,128)(2,1)S(1)} %add_convert_fusion.3.p0, bf16[288,256]{1,0:T(8,128)(2,1)S(1)} %collective-permute-done.4.p1, bf16[288,256]{1,0:T(8,128)(2,1)S(1)} %collective-permute-done.5.p2, ...), custom_call_target="tpu_custom_call" | custom-call | tf_op jit(solution)/shard_map/section_scan/pallas_call | solution.py:272
  33.9 1.1 collective-permute-start.7
  35.1 1.2 collective-permute-start.8
  36.3 2.5 %collective-permute-start.9 = (bf16[72,512]{1,0:T(8,128)(2,1)S(1)}, bf16[72,512]{1,0:T(8,128)(2,1)S(1)}, u32[]{:S(2)}, u32[]{:S(2)}) collective-permute-start(bf16[72,512]{1,0:T(8,128)(2,1)S(1)} %get-tuple-element.33), channel_id=1, source_target_pairs={{0,96},{16,112},{32,0},{48,16},{64,32},{80,48},{96,64},{112,80},{1... | collective-permute-start | bytes 221192 | tf_op jit(solution)/shard_map/ppermute | solution.py:444
  38.8 1.2 collective-permute-done.7.refs_0_
  40.0 0.9 collective-permute-done.8.refs_1_
  40.9 0.4 collective-permute-done.9.refs_2_
  41.5 0.7 collective-permute-done.12.refs_5_
  42.2 0.4 collective-permute-done.13.refs_6_
  42.6 7.7 %mixer_out.1 = bf16[256,4096]{1,0:T(8,128)(2,1)} custom-call(s32[1]{0:T(128)} %bitcast.section, bf16[72,512]{1,0:T(8,128)(2,1)S(1)} %collective-permute-done.7.refs_0_, bf16[72,512]{1,0:T(8,128)(2,1)S(1)} %collective-permute-done.8.refs_1_, bf16[72,512]{1,0:T(8,128)(2,1)S(1)} %collective-permute-done.9.refs_2_, ...), custom_call_target="tpu_custom_call" | custom-call | tf_op jit(solution)/shard_map/mixer_out/pallas_call | solution.py:295
  50.4 6.0 %all-to-all-start = ((bf16[16,16,4096]{2,1,0:T(8,128)(2,1)}), bf16[16,16,4096]{2,1,0:T(8,128)(2,1)S(1)}, u32[]{:S(2)}, u32[]{:S(2)}) async-start(bf16[16,16,4096]{2,1,0:T(8,128)(2,1)} %bitcast.5), calls=%async_computation | async-start | bytes 4194304 | tf_op jit(solution)/shard_map/all_to_all | solution.py:456
  57.4 29.8 %all-to-all-done = bf16[16,16,4096]{2,1,0:T(8,128)(2,1)S(1)} async-done(((bf16[16,16,4096]{2,1,0:T(8,128)(2,1)}), bf16[16,16,4096]{2,1,0:T(8,128)(2,1)S(1)}, u32[]{:S(2)}, u32[]{:S(2)}) %all-to-all-start) | async-done | bytes 2097184 | tf_op jit(solution)/shard_map/all_to_all | solution.py:456
  87.2 0.3 convert_reduce_fusion
  87.8 0.3 convolution_convert_fusion
  88.3 21.2 %all_to_all.26 = bf16[16,8,4096]{2,1,0:T(8,128)(2,1)S(1)} all-to-all(bf16[16,8,4096]{2,1,0:T(8,128)(2,1)S(1)} %bitcast.29), channel_id=1, replica_groups=mesh['seq'=8,'exp'=16] {'exp'}, dimensions={0} | all-to-all | bytes 2097152 | tf_op jit(solution)/shard_map/all_to_all | solution.py:469
  109.5 2.7 %collective-permute-done.14.refs_1_ = bf16[128,4096]{1,0:T(8,128)(2,1)S(1)} collective-permute-done((bf16[128,4096]{1,0:T(8,128)(2,1)S(1)}, bf16[128,4096]{1,0:T(8,128)(2,1)S(1)}, u32[]{:S(2)}, u32[]{:S(2)}) %collective-permute-start.14) | collective-permute-done | bytes 1048608 | tf_op jit(solution)/shard_map/ppermute | solution.py:48
  112.2 2.8 %copy-done = bf16[1,4096,768]{2,1,0:T(8,128)(2,1)S(1)} copy-done((bf16[1,4096,768]{2,1,0:T(8,128)(2,1)S(1)}, bf16[1,4096,768]{2,1,0:T(8,128)(2,1)}, u32[]{:S(2)}) %copy-start) | copy-done | bytes 6291480
  115.0 2.8 %copy-done.2 = bf16[1,4096,768]{2,1,0:T(8,128)(2,1)S(1)} copy-done((bf16[1,4096,768]{2,1,0:T(8,128)(2,1)S(1)}, bf16[1,4096,768]{2,1,0:T(8,128)(2,1)}, u32[]{:S(2)}) %copy-start.2) | copy-done | bytes 6291480
  117.7 2.8 %copy-done.4 = bf16[1,768,4096]{2,1,0:T(8,128)(2,1)S(1)} copy-done((bf16[1,768,4096]{2,1,0:T(8,128)(2,1)S(1)}, bf16[1,768,4096]{2,1,0:T(8,128)(2,1)}, u32[]{:S(2)}) %copy-start.4) | copy-done | bytes 6291480
  120.5 6.3 %experts_256.4 = (bf16[128,4096]{1,0:T(8,128)(2,1)S(1)}, bf16[128,4096]{1,0:T(8,128)(2,1)S(1)}) custom-call(bf16[128,4096]{1,0:T(8,128)(2,1)S(1)} %bitcast.24, bf16[128,4096]{1,0:T(8,128)(2,1)S(1)} %collective-permute-done.14.refs_1_, bf16[1,4096,768]{2,1,0:T(8,128)(2,1)S(1)} %copy-done, bf16[1,4096,768]{2,1,0:T(8,128)(2,1)S(1)} %copy-done.2, ...), custom_call_target="tpu_custom_call" | custom-call | flops 4831838208 | bytes 4194304 | tf_op jit(solution)/shard_map/experts_256/pallas_call | solution.py:344
  126.8 0.4 collective-permute-start.15
  127.2 0.4 collective-permute-start.16
  127.7 2.8 %collective-permute-start.17 = (bf16[128,4096]{1,0:T(8,128)(2,1)S(1)}, bf16[128,4096]{1,0:T(8,128)(2,1)S(1)}, u32[]{:S(2)}, u32[]{:S(2)}) collective-permute-start(bf16[128,4096]{1,0:T(8,128)(2,1)S(1)} %bitcast.26), channel_id=1, source_target_pairs={{0,96},{16,112},{32,0},{48,16},{64,32},{80,48},{96,64},{112,80},{1... | collective-permute-start | bytes 3145736 | tf_op jit(solution)/shard_map/ppermute | solution.py:385
  130.5 0.3 convert_add_fusion.2
  130.7 23.1 %collective-permute-done.16.refs_0_ = bf16[128,4096]{1,0:T(8,128)(2,1)S(1)} collective-permute-done((bf16[128,4096]{1,0:T(8,128)(2,1)S(1)}, bf16[128,4096]{1,0:T(8,128)(2,1)S(1)}, u32[]{:S(2)}, u32[]{:S(2)}) %collective-permute-start.16) | collective-permute-done | bytes 1048608 | tf_op jit(solution)/shard_map/ppermute | solution.py:384
  153.9 0.5 collective-permute-start.20
  154.5 0.3 collective-permute-start.18
  154.7 3.0 %collective-permute-start.19 = (bf16[64,4096]{1,0:T(8,128)(2,1)S(1)}, bf16[64,4096]{1,0:T(8,128)(2,1)S(1)}, u32[]{:S(2)}, u32[]{:S(2)}) collective-permute-start(bf16[64,4096]{1,0:T(8,128)(2,1)S(1)} %slice.41), channel_id=1, source_target_pairs={{0,96},{16,112},{32,0},{48,16},{64,32},{80,48},{96,64},{112,80},{1... | collective-permute-start | bytes 1572872 | tf_op jit(solution)/shard_map/ppermute | solution.py:391
  157.8 6.3 %experts_256.6 = (bf16[128,4096]{1,0:T(8,128)(2,1)S(1)}, bf16[128,4096]{1,0:T(8,128)(2,1)S(1)}) custom-call(bf16[128,4096]{1,0:T(8,128)(2,1)S(1)} %collective-permute-done.17.refs_0_, bf16[128,4096]{1,0:T(8,128)(2,1)S(1)} %collective-permute-done.21.refs_1_, bf16[1,4096,768]{2,1,0:T(8,128)(2,1)S(1)} %copy-done.1, bf16[1,4096,768]{2,1,0:T(8,128)(2,1)S(1)} %copy-done.3, ...), custom_call_target="tpu_custom_call" | custom-call | flops 4831838208 | bytes 4194304 | tf_op jit(solution)/shard_map/experts_256/pallas_call | solution.py:344
  164.1 6.3 %experts_256.5 = (bf16[128,4096]{1,0:T(8,128)(2,1)S(1)}, bf16[128,4096]{1,0:T(8,128)(2,1)S(1)}) custom-call(bf16[128,4096]{1,0:T(8,128)(2,1)S(1)} %collective-permute-done.16.refs_0_, bf16[128,4096]{1,0:T(8,128)(2,1)S(1)} %collective-permute-done.20.refs_1_, bf16[1,4096,768]{2,1,0:T(8,128)(2,1)S(1)} %copy-done.1, bf16[1,4096,768]{2,1,0:T(8,128)(2,1)S(1)} %copy-done.3, ...), custom_call_target="tpu_custom_call" | custom-call | flops 4831838208 | bytes 4194304 | tf_op jit(solution)/shard_map/experts_256/pallas_call | solution.py:344
  170.5 0.5 collective-permute-start.26
  171.1 0.4 collective-permute-start.24
  171.5 1.6 collective-permute-done.22
  173.2 0.2 convert_add_fusion.1
  173.5 2.2 collective-permute-start.25
  175.7 0.3 convert_add_fusion
  176.2 6.3 %experts_256.7 = (bf16[128,4096]{1,0:T(8,128)(2,1)S(1)}, bf16[128,4096]{1,0:T(8,128)(2,1)S(1)}) custom-call(bf16[64,4096]{1,0:T(8,128)(2,1)S(1)} %collective-permute-done.18.refs_0_, bf16[64,4096]{1,0:T(8,128)(2,1)S(1)} %collective-permute-done.19.refs_1_, bf16[64,4096]{1,0:T(8,128)(2,1)S(1)} %collective-permute-done.23.refs_2_, ...), custom_call_target="tpu_custom_call" | custom-call | flops 4831838208 | bytes 4194304 | tf_op jit(solution)/shard_map/experts_256/pallas_call | solution.py:344
  182.4 5.1 %collective-permute-done.25 = bf16[64,4096]{1,0:T(8,128)(2,1)S(1)} collective-permute-done((bf16[64,4096]{1,0:T(8,128)(2,1)S(1)}, bf16[64,4096]{1,0:T(8,128)(2,1)S(1)}, u32[]{:S(2)}, u32[]{:S(2)}) %collective-permute-start.25) | collective-permute-done | bytes 524320 | tf_op jit(solution)/shard_map/ppermute | solution.py:397
  187.5 3.4 %collective-permute-done.27 = bf16[64,4096]{1,0:T(8,128)(2,1)S(1)} collective-permute-done((bf16[64,4096]{1,0:T(8,128)(2,1)S(1)}, bf16[64,4096]{1,0:T(8,128)(2,1)S(1)}, u32[]{:S(2)}, u32[]{:S(2)}) %collective-permute-start.27) | collective-permute-done | bytes 524320 | tf_op jit(solution)/shard_map/ppermute | solution.py:398
  190.9 2.7 %collective-permute-done.28 = bf16[128,4096]{1,0:T(8,128)(2,1)S(1)} collective-permute-done((bf16[128,4096]{1,0:T(8,128)(2,1)S(1)}, bf16[128,4096]{1,0:T(8,128)(2,1)S(1)}, u32[]{:S(2)}, u32[]{:S(2)}) %collective-permute-start.28) | collective-permute-done | bytes 1048608 | tf_op jit(solution)/shard_map/ppermute | solution.py:48
  193.6 0.2 add_convert_fusion
  194.0 3.2 %collective-permute-start.29 = (bf16[64,4096]{1,0:T(8,128)(2,1)S(1)}, bf16[64,4096]{1,0:T(8,128)(2,1)S(1)}, u32[]{:S(2)}, u32[]{:S(2)}) collective-permute-start(bf16[64,4096]{1,0:T(8,128)(2,1)S(1)} %get-tuple-element.60), channel_id=1, source_target_pairs={{0,96},{16,112},{32,0},{48,16},{64,32},{80,48},{96,64},{112,80},{1... | collective-permute-start | bytes 1572872 | tf_op jit(solution)/shard_map/ppermute | solution.py:403
  197.3 11.9 %collective-permute-done.30 = bf16[64,4096]{1,0:T(8,128)(2,1)S(1)} collective-permute-done((bf16[64,4096]{1,0:T(8,128)(2,1)S(1)}, bf16[64,4096]{1,0:T(8,128)(2,1)S(1)}, u32[]{:S(2)}, u32[]{:S(2)}) %collective-permute-start.30) | collective-permute-done | bytes 524320 | tf_op jit(solution)/shard_map/ppermute | solution.py:402
  209.6 3.3 %collective-permute-start.32 = (bf16[64,4096]{1,0:T(8,128)(2,1)S(1)}, bf16[64,4096]{1,0:T(8,128)(2,1)S(1)}, u32[]{:S(2)}, u32[]{:S(2)}) collective-permute-start(bf16[64,4096]{1,0:T(8,128)(2,1)S(1)} %slice_add_fusion.1), channel_id=1, source_target_pairs={{0,96},{16,112},{32,0},{48,16},{64,32},{80,48},{96,64},{112,80},{1... | collective-permute-start | bytes 1572872 | tf_op jit(solution)/shard_map/ppermute | solution.py:410
  212.8 0.2 convert_add_fusion.3
  213.1 10.7 %collective-permute-done.31 = bf16[64,4096]{1,0:T(8,128)(2,1)S(1)} collective-permute-done((bf16[64,4096]{1,0:T(8,128)(2,1)S(1)}, bf16[64,4096]{1,0:T(8,128)(2,1)S(1)}, u32[]{:S(2)}, u32[]{:S(2)}) %collective-permute-start.31) | collective-permute-done | bytes 524320 | tf_op jit(solution)/shard_map/ppermute | solution.py:411
  224.0 1.1 maximum_bitcast_fusion
  225.1 3.7 %all-to-all-start.2 = ((bf16[16,8,4096]{2,1,0:T(8,128)(2,1)}), bf16[16,8,4096]{2,1,0:T(8,128)(2,1)S(1)}, u32[]{:S(2)}, u32[]{:S(2)}) async-start(bf16[16,8,4096]{2,1,0:T(8,128)(2,1)} %maximum_bitcast_fusion), calls=%async_computation.2 | async-start | bytes 2097152 | tf_op jit(solution)/shard_map/all_to_all | solution.py:473
  228.9 15.7 %all-to-all-done.2 = bf16[16,8,4096]{2,1,0:T(8,128)(2,1)S(1)} async-done(((bf16[16,8,4096]{2,1,0:T(8,128)(2,1)}), bf16[16,8,4096]{2,1,0:T(8,128)(2,1)S(1)}, u32[]{:S(2)}, u32[]{:S(2)}) %all-to-all-start.2) | async-done | bytes 1048608 | tf_op jit(solution)/shard_map/all_to_all | solution.py:473
  244.8 1.3 fusion
  (83 shorter events, 3.2 us)
Async XLA Ops:
  0.0 42.6 %copy-start.5 = (f32[16,512]{1,0:T(8,128)S(1)}, f32[16,512]{1,0:T(8,128)}, u32[]{:S(2)}) copy-start(f32[16,512]{1,0:T(8,128)} %refs_10_.1) | copy-start | bytes 98308
  0.0 41.4 %copy-start.8 = (bf16[64,4,512]{2,1,0:T(4,128)(2,1)S(1)}, bf16[64,4,512]{2,1,0:T(4,128)(2,1)}, u32[]{:S(2)}) copy-start(bf16[64,4,512]{2,1,0:T(4,128)(2,1)} %param.18) | copy-start | bytes 786436
  0.0 42.6 %copy-start.6 = (f32[512]{0:T(512)S(1)}, f32[512]{0:T(512)}, u32[]{:S(2)}) copy-start(f32[512]{0:T(512)} %param.25) | copy-start | bytes 6148
  0.8 2.3 collective-permute-start
  4.6 8.2 %collective-permute-start.1 = (bf16[288,256]{1,0:T(8,128)(2,1)S(1)}, bf16[288,256]{1,0:T(8,128)(2,1)S(1)}, u32[]{:S(2)}, u32[]{:S(2)}) collective-permute-start(bf16[288,256]{1,0:T(8,128)(2,1)S(1)} %get-tuple-element.31), channel_id=1, source_target_pairs={{0,1},{1,2},{2,3},{3,0},{4,5},{5,6},{6,7},{7,4},{8,9},{9,10},{10,1... | collective-permute-start | bytes 442376 | tf_op jit(solution)/shard_map/ppermute | solution.py:44
  7.2 10.7 %collective-permute-start.2 = (bf16[288,256]{1,0:T(8,128)(2,1)S(1)}, bf16[288,256]{1,0:T(8,128)(2,1)S(1)}, u32[]{:S(2)}, u32[]{:S(2)}) collective-permute-start(bf16[288,256]{1,0:T(8,128)(2,1)S(1)} %get-tuple-element.31), channel_id=1, source_target_pairs={{0,2},{1,3},{2,0},{3,1},{4,6},{5,7},{6,4},{7,5},{8,10},{9,11},{10,... | collective-permute-start | bytes 442376 | tf_op jit(solution)/shard_map/ppermute | solution.py:44
  10.7 7.1 %collective-permute-start.3 = (bf16[288,256]{1,0:T(8,128)(2,1)S(1)}, bf16[288,256]{1,0:T(8,128)(2,1)S(1)}, u32[]{:S(2)}, u32[]{:S(2)}) collective-permute-start(bf16[288,256]{1,0:T(8,128)(2,1)S(1)} %get-tuple-element.31), channel_id=1, source_target_pairs={{0,3},{1,0},{2,1},{3,2},{4,7},{5,4},{6,5},{7,6},{8,11},{9,8},{10,9... | collective-permute-start | bytes 442376 | tf_op jit(solution)/shard_map/ppermute | solution.py:44
  17.9 7.7 %collective-permute-start.4 = (bf16[288,256]{1,0:T(8,128)(2,1)S(1)}, bf16[288,256]{1,0:T(8,128)(2,1)S(1)}, u32[]{:S(2)}, u32[]{:S(2)}) collective-permute-start(bf16[288,256]{1,0:T(8,128)(2,1)S(1)} %add_convert_fusion.3.p0), channel_id=1, source_target_pairs={{0,4},{1,5},{2,6},{3,7},{4,8},{5,9},{6,10},{7,11},{8,12},{9,13},{1... | collective-permute-start | bytes 442376 | tf_op jit(solution)/shard_map/ppermute | solution.py:44
  19.5 10.4 %collective-permute-start.5 = (bf16[288,256]{1,0:T(8,128)(2,1)S(1)}, bf16[288,256]{1,0:T(8,128)(2,1)S(1)}, u32[]{:S(2)}, u32[]{:S(2)}) collective-permute-start(bf16[288,256]{1,0:T(8,128)(2,1)S(1)} %add_convert_fusion.3.p0), channel_id=1, source_target_pairs={{0,8},{1,9},{2,10},{3,11},{4,12},{5,13},{6,14},{7,15},{8,0},{9,1},... | collective-permute-start | bytes 442376 | tf_op jit(solution)/shard_map/ppermute | solution.py:44
  22.5 7.5 %collective-permute-start.6 = (bf16[288,256]{1,0:T(8,128)(2,1)S(1)}, bf16[288,256]{1,0:T(8,128)(2,1)S(1)}, u32[]{:S(2)}, u32[]{:S(2)}) collective-permute-start(bf16[288,256]{1,0:T(8,128)(2,1)S(1)} %add_convert_fusion.3.p0), channel_id=1, source_target_pairs={{0,12},{1,13},{2,14},{3,15},{4,0},{5,1},{6,2},{7,3},{8,4},{9,5},{1... | collective-permute-start | bytes 442376 | tf_op jit(solution)/shard_map/ppermute | solution.py:44
  33.9 6.1 %collective-permute-start.7 = (bf16[72,512]{1,0:T(8,128)(2,1)S(1)}, bf16[72,512]{1,0:T(8,128)(2,1)S(1)}, u32[]{:S(2)}, u32[]{:S(2)}) collective-permute-start(bf16[72,512]{1,0:T(8,128)(2,1)S(1)} %get-tuple-element.33), channel_id=1, source_target_pairs={{0,32},{16,48},{32,64},{48,80},{64,96},{80,112},{96,0},{112,16},{1... | collective-permute-start | bytes 221192 | tf_op jit(solution)/shard_map/ppermute | solution.py:444
  35.1 5.9 %collective-permute-start.8 = (bf16[72,512]{1,0:T(8,128)(2,1)S(1)}, bf16[72,512]{1,0:T(8,128)(2,1)S(1)}, u32[]{:S(2)}, u32[]{:S(2)}) collective-permute-start(bf16[72,512]{1,0:T(8,128)(2,1)S(1)} %get-tuple-element.33), channel_id=1, source_target_pairs={{0,64},{16,80},{32,96},{48,112},{64,0},{80,16},{96,32},{112,48},{1... | collective-permute-start | bytes 221192 | tf_op jit(solution)/shard_map/ppermute | solution.py:444
  36.3 5.1 %collective-permute-start.9 = (bf16[72,512]{1,0:T(8,128)(2,1)S(1)}, bf16[72,512]{1,0:T(8,128)(2,1)S(1)}, u32[]{:S(2)}, u32[]{:S(2)}) collective-permute-start(bf16[72,512]{1,0:T(8,128)(2,1)S(1)} %get-tuple-element.33), channel_id=1, source_target_pairs={{0,96},{16,112},{32,0},{48,16},{64,32},{80,48},{96,64},{112,80},{1... | collective-permute-start | bytes 221192 | tf_op jit(solution)/shard_map/ppermute | solution.py:444
  38.8 2.7 %collective-permute-start.10 = (bf16[72,512]{1,0:T(8,128)(2,1)S(1)}, bf16[72,512]{1,0:T(8,128)(2,1)S(1)}, u32[]{:S(2)}, u32[]{:S(2)}) collective-permute-start(bf16[72,512]{1,0:T(8,128)(2,1)S(1)} %get-tuple-element.33), channel_id=1, source_target_pairs={{0,16},{16,0},{32,48},{48,32},{64,80},{80,64},{96,112},{112,96},{1... | collective-permute-start | bytes 221192 | tf_op jit(solution)/shard_map/ppermute | solution.py:48
  40.0 1.5 collective-permute-start.11
  40.9 1.3 collective-permute-start.12
  41.4 1.3 collective-permute-start.13
  50.4 6.1 %copy-start.10 = (s32[4,4,2]{1,2,0:T(2,128)S(1)}, s32[4,4,2]{1,2,0:T(2,128)}, u32[]{:S(2)}) copy-start(s32[4,4,2]{1,2,0:T(2,128)} %param.29) | copy-start | bytes 388
  50.4 6.9 %copy-start.7 = (bf16[4,4,4096]{2,1,0:T(4,128)(2,1)S(1)}, bf16[4,4,4096]{2,1,0:T(4,128)(2,1)}, u32[]{:S(2)}) copy-start(bf16[4,4,4096]{2,1,0:T(4,128)(2,1)} %param.27) | copy-start | bytes 393220
  50.4 36.8 %all-to-all-start = ((bf16[16,16,4096]{2,1,0:T(8,128)(2,1)}), bf16[16,16,4096]{2,1,0:T(8,128)(2,1)S(1)}, u32[]{:S(2)}, u32[]{:S(2)}) async-start(bf16[16,16,4096]{2,1,0:T(8,128)(2,1)} %bitcast.5), calls=%async_computation | async-start | bytes 4194304 | tf_op jit(solution)/shard_map/all_to_all | solution.py:456
  56.4 31.4 %copy-start.9 = (f32[4096]{0:T(1024)S(1)}, f32[4096]{0:T(1024)}, u32[]{:S(2)}) copy-start(f32[4096]{0:T(1024)} %param.28) | copy-start | bytes 49156
  109.5 2.7 %collective-permute-start.14 = (bf16[128,4096]{1,0:T(8,128)(2,1)S(1)}, bf16[128,4096]{1,0:T(8,128)(2,1)S(1)}, u32[]{:S(2)}, u32[]{:S(2)}) collective-permute-start(bf16[128,4096]{1,0:T(8,128)(2,1)S(1)} %bitcast.23), channel_id=1, source_target_pairs={{0,16},{16,0},{32,48},{48,32},{64,80},{80,64},{96,112},{112,96},{1... | collective-permute-start | bytes 3145736 | tf_op jit(solution)/shard_map/ppermute | solution.py:48
  112.2 2.8 %copy-start = (bf16[1,4096,768]{2,1,0:T(8,128)(2,1)S(1)}, bf16[1,4096,768]{2,1,0:T(8,128)(2,1)}, u32[]{:S(2)}) copy-start(bf16[1,4096,768]{2,1,0:T(8,128)(2,1)} %refs_4_.7) | copy-start | bytes 18874372
  115.0 2.8 %copy-start.2 = (bf16[1,4096,768]{2,1,0:T(8,128)(2,1)S(1)}, bf16[1,4096,768]{2,1,0:T(8,128)(2,1)}, u32[]{:S(2)}) copy-start(bf16[1,4096,768]{2,1,0:T(8,128)(2,1)} %refs_5_.1) | copy-start | bytes 18874372
  117.7 2.8 %copy-start.4 = (bf16[1,768,4096]{2,1,0:T(8,128)(2,1)S(1)}, bf16[1,768,4096]{2,1,0:T(8,128)(2,1)}, u32[]{:S(2)}) copy-start(bf16[1,768,4096]{2,1,0:T(8,128)(2,1)} %refs_6_.1) | copy-start | bytes 18874372
  120.5 37.2 %copy-start.3 = (bf16[1,4096,768]{2,1,0:T(8,128)(2,1)S(1)}, bf16[1,4096,768]{2,1,0:T(8,128)(2,1)}, u32[]{:S(2)}) copy-start(bf16[1,4096,768]{2,1,0:T(8,128)(2,1)} %refs_5_.1) | copy-start | bytes 18874372
  126.8 3.7 %collective-permute-start.15 = (bf16[128,4096]{1,0:T(8,128)(2,1)S(1)}, bf16[128,4096]{1,0:T(8,128)(2,1)S(1)}, u32[]{:S(2)}, u32[]{:S(2)}) collective-permute-start(bf16[128,4096]{1,0:T(8,128)(2,1)S(1)} %get-tuple-element.37), channel_id=1, source_target_pairs={{0,16},{16,0},{32,48},{48,32},{64,80},{80,64},{96,112},{112,96},{1... | collective-permute-start | bytes 3145736 | tf_op jit(solution)/shard_map/ppermute | solution.py:48
  127.2 26.6 %collective-permute-start.16 = (bf16[128,4096]{1,0:T(8,128)(2,1)S(1)}, bf16[128,4096]{1,0:T(8,128)(2,1)S(1)}, u32[]{:S(2)}, u32[]{:S(2)}) collective-permute-start(bf16[128,4096]{1,0:T(8,128)(2,1)S(1)} %bitcast.25), channel_id=1, source_target_pairs={{0,32},{16,48},{32,64},{48,80},{64,96},{80,112},{96,0},{112,16},{1... | collective-permute-start | bytes 3145736 | tf_op jit(solution)/shard_map/ppermute | solution.py:384
  127.7 26.2 %collective-permute-start.17 = (bf16[128,4096]{1,0:T(8,128)(2,1)S(1)}, bf16[128,4096]{1,0:T(8,128)(2,1)S(1)}, u32[]{:S(2)}, u32[]{:S(2)}) collective-permute-start(bf16[128,4096]{1,0:T(8,128)(2,1)S(1)} %bitcast.26), channel_id=1, source_target_pairs={{0,96},{16,112},{32,0},{48,16},{64,32},{80,48},{96,64},{112,80},{1... | collective-permute-start | bytes 3145736 | tf_op jit(solution)/shard_map/ppermute | solution.py:385
  130.5 27.3 %copy-start.1 = (bf16[1,4096,768]{2,1,0:T(8,128)(2,1)S(1)}, bf16[1,4096,768]{2,1,0:T(8,128)(2,1)}, u32[]{:S(2)}) copy-start(bf16[1,4096,768]{2,1,0:T(8,128)(2,1)} %refs_4_.7) | copy-start | bytes 18874372
  153.9 3.9 %collective-permute-start.21 = (bf16[128,4096]{1,0:T(8,128)(2,1)S(1)}, bf16[128,4096]{1,0:T(8,128)(2,1)S(1)}, u32[]{:S(2)}, u32[]{:S(2)}) collective-permute-start(bf16[128,4096]{1,0:T(8,128)(2,1)S(1)} %collective-permute-done.17.refs_0_), channel_id=1, source_target_pairs={{0,16},{16,0},{32,48},{48,32},{64,80},{80,64},{96,112},{112,96},{1... | collective-permute-start | bytes 3145736 | tf_op jit(solution)/shard_map/ppermute | solution.py:48
  153.9 10.2 %collective-permute-start.20 = (bf16[128,4096]{1,0:T(8,128)(2,1)S(1)}, bf16[128,4096]{1,0:T(8,128)(2,1)S(1)}, u32[]{:S(2)}, u32[]{:S(2)}) collective-permute-start(bf16[128,4096]{1,0:T(8,128)(2,1)S(1)} %collective-permute-done.16.refs_0_), channel_id=1, source_target_pairs={{0,16},{16,0},{32,48},{48,32},{64,80},{80,64},{96,112},{112,96},{1... | collective-permute-start | bytes 3145736 | tf_op jit(solution)/shard_map/ppermute | solution.py:48
  154.5 15.9 %collective-permute-start.18 = (bf16[64,4096]{1,0:T(8,128)(2,1)S(1)}, bf16[64,4096]{1,0:T(8,128)(2,1)S(1)}, u32[]{:S(2)}, u32[]{:S(2)}) collective-permute-start(bf16[64,4096]{1,0:T(8,128)(2,1)S(1)} %slice.40), channel_id=1, source_target_pairs={{0,32},{16,48},{32,64},{48,80},{64,96},{80,112},{96,0},{112,16},{1... | collective-permute-start | bytes 1572872 | tf_op jit(solution)/shard_map/ppermute | solution.py:390
  154.7 15.7 %collective-permute-start.19 = (bf16[64,4096]{1,0:T(8,128)(2,1)S(1)}, bf16[64,4096]{1,0:T(8,128)(2,1)S(1)}, u32[]{:S(2)}, u32[]{:S(2)}) collective-permute-start(bf16[64,4096]{1,0:T(8,128)(2,1)S(1)} %slice.41), channel_id=1, source_target_pairs={{0,96},{16,112},{32,0},{48,16},{64,32},{80,48},{96,64},{112,80},{1... | collective-permute-start | bytes 1572872 | tf_op jit(solution)/shard_map/ppermute | solution.py:391
  170.4 2.7 %collective-permute-start.22 = (bf16[128,4096]{1,0:T(8,128)(2,1)S(1)}, bf16[128,4096]{1,0:T(8,128)(2,1)S(1)}, u32[]{:S(2)}, u32[]{:S(2)}) collective-permute-start(bf16[128,4096]{1,0:T(8,128)(2,1)S(1)} %get-tuple-element.45), channel_id=1, source_target_pairs={{0,16},{16,0},{32,48},{48,32},{64,80},{80,64},{96,112},{112,96},{1... | collective-permute-start | bytes 3145736 | tf_op jit(solution)/shard_map/ppermute | solution.py:48
  170.5 5.2 %collective-permute-start.26 = (bf16[128,4096]{1,0:T(8,128)(2,1)S(1)}, bf16[128,4096]{1,0:T(8,128)(2,1)S(1)}, u32[]{:S(2)}, u32[]{:S(2)}) collective-permute-start(bf16[128,4096]{1,0:T(8,128)(2,1)S(1)} %get-tuple-element.51), channel_id=1, source_target_pairs={{0,16},{16,0},{32,48},{48,32},{64,80},{80,64},{96,112},{112,96},{1... | collective-permute-start | bytes 3145736 | tf_op jit(solution)/shard_map/ppermute | solution.py:48
  171.0 5.1 %collective-permute-start.23 = (bf16[64,4096]{1,0:T(8,128)(2,1)S(1)}, bf16[64,4096]{1,0:T(8,128)(2,1)S(1)}, u32[]{:S(2)}, u32[]{:S(2)}) collective-permute-start(bf16[64,4096]{1,0:T(8,128)(2,1)S(1)} %collective-permute-done.18.refs_0_), channel_id=1, source_target_pairs={{0,16},{16,0},{32,48},{48,32},{64,80},{80,64},{96,112},{112,96},{1... | collective-permute-start | bytes 1572872 | tf_op jit(solution)/shard_map/ppermute | solution.py:48
  171.1 5.1 %collective-permute-start.24 = (bf16[64,4096]{1,0:T(8,128)(2,1)S(1)}, bf16[64,4096]{1,0:T(8,128)(2,1)S(1)}, u32[]{:S(2)}, u32[]{:S(2)}) collective-permute-start(bf16[64,4096]{1,0:T(8,128)(2,1)S(1)} %collective-permute-done.19.refs_1_), channel_id=1, source_target_pairs={{0,16},{16,0},{32,48},{48,32},{64,80},{80,64},{96,112},{112,96},{1... | collective-permute-start | bytes 1572872 | tf_op jit(solution)/shard_map/ppermute | solution.py:48
  173.5 14.0 %collective-permute-start.25 = (bf16[64,4096]{1,0:T(8,128)(2,1)S(1)}, bf16[64,4096]{1,0:T(8,128)(2,1)S(1)}, u32[]{:S(2)}, u32[]{:S(2)}) collective-permute-start(bf16[64,4096]{1,0:T(8,128)(2,1)S(1)} %slice.63), channel_id=1, source_target_pairs={{0,96},{16,112},{32,0},{48,16},{64,32},{80,48},{96,64},{112,80},{1... | collective-permute-start | bytes 1572872 | tf_op jit(solution)/shard_map/ppermute | solution.py:397
  176.0 15.0 %collective-permute-start.27 = (bf16[64,4096]{1,0:T(8,128)(2,1)S(1)}, bf16[64,4096]{1,0:T(8,128)(2,1)S(1)}, u32[]{:S(2)}, u32[]{:S(2)}) collective-permute-start(bf16[64,4096]{1,0:T(8,128)(2,1)S(1)} %slice.62), channel_id=1, source_target_pairs={{0,32},{16,48},{32,64},{48,80},{64,96},{80,112},{96,0},{112,16},{1... | collective-permute-start | bytes 1572872 | tf_op jit(solution)/shard_map/ppermute | solution.py:398
  190.9 2.7 %collective-permute-start.28 = (bf16[128,4096]{1,0:T(8,128)(2,1)S(1)}, bf16[128,4096]{1,0:T(8,128)(2,1)S(1)}, u32[]{:S(2)}, u32[]{:S(2)}) collective-permute-start(bf16[128,4096]{1,0:T(8,128)(2,1)S(1)} %get-tuple-element.53), channel_id=1, source_target_pairs={{0,16},{16,0},{32,48},{48,32},{64,80},{80,64},{96,112},{112,96},{1... | collective-permute-start | bytes 3145736 | tf_op jit(solution)/shard_map/ppermute | solution.py:48
  194.0 15.2 %collective-permute-start.30 = (bf16[64,4096]{1,0:T(8,128)(2,1)S(1)}, bf16[64,4096]{1,0:T(8,128)(2,1)S(1)}, u32[]{:S(2)}, u32[]{:S(2)}) collective-permute-start(bf16[64,4096]{1,0:T(8,128)(2,1)S(1)} %get-tuple-element.59), channel_id=1, source_target_pairs={{0,32},{16,48},{32,64},{48,80},{64,96},{80,112},{96,0},{112,16},{1... | collective-permute-start | bytes 1572872 | tf_op jit(solution)/shard_map/ppermute | solution.py:402
  194.0 15.4 %collective-permute-start.29 = (bf16[64,4096]{1,0:T(8,128)(2,1)S(1)}, bf16[64,4096]{1,0:T(8,128)(2,1)S(1)}, u32[]{:S(2)}, u32[]{:S(2)}) collective-permute-start(bf16[64,4096]{1,0:T(8,128)(2,1)S(1)} %get-tuple-element.60), channel_id=1, source_target_pairs={{0,96},{16,112},{32,0},{48,16},{64,32},{80,48},{96,64},{112,80},{1... | collective-permute-start | bytes 1572872 | tf_op jit(solution)/shard_map/ppermute | solution.py:403
  209.3 14.4 %collective-permute-start.31 = (bf16[64,4096]{1,0:T(8,128)(2,1)S(1)}, bf16[64,4096]{1,0:T(8,128)(2,1)S(1)}, u32[]{:S(2)}, u32[]{:S(2)}) collective-permute-start(bf16[64,4096]{1,0:T(8,128)(2,1)S(1)} %slice_add_fusion), channel_id=1, source_target_pairs={{0,32},{16,48},{32,64},{48,80},{64,96},{80,112},{96,0},{112,16},{1... | collective-permute-start | bytes 1572872 | tf_op jit(solution)/shard_map/ppermute | solution.py:411
  209.6 14.3 %collective-permute-start.32 = (bf16[64,4096]{1,0:T(8,128)(2,1)S(1)}, bf16[64,4096]{1,0:T(8,128)(2,1)S(1)}, u32[]{:S(2)}, u32[]{:S(2)}) collective-permute-start(bf16[64,4096]{1,0:T(8,128)(2,1)S(1)} %slice_add_fusion.1), channel_id=1, source_target_pairs={{0,96},{16,112},{32,0},{48,16},{64,32},{80,48},{96,64},{112,80},{1... | collective-permute-start | bytes 1572872 | tf_op jit(solution)/shard_map/ppermute | solution.py:410
  224.0 4.8 %copy-start.11 = (bf16[4,4,2]{1,2,0:T(2,128)(2,1)S(1)}, bf16[4,4,2]{1,2,0:T(2,128)(2,1)}, u32[]{:S(2)}) copy-start(bf16[4,4,2]{1,2,0:T(2,128)(2,1)} %param.30) | copy-start | bytes 196
  225.1 19.6 %all-to-all-start.2 = ((bf16[16,8,4096]{2,1,0:T(8,128)(2,1)}), bf16[16,8,4096]{2,1,0:T(8,128)(2,1)S(1)}, u32[]{:S(2)}, u32[]{:S(2)}) async-start(bf16[16,8,4096]{2,1,0:T(8,128)(2,1)} %maximum_bitcast_fusion), calls=%async_computation.2 | async-start | bytes 2097152 | tf_op jit(solution)/shard_map/all_to_all | solution.py:473

commit v11 on v9

--- a/solution.py
+++ b/solution.py
@@ -391,7 +391,10 @@
     ]
     left_out = expert_block([left, swapped(left)], w_gate, w_up, w_down)
     right_out = expert_block([right, swapped(right)], w_gate, w_up, w_down)
-    far, left_out, right_out = lax.optimization_barrier((far, left_out, right_out))
+    own_sum = paired(*own_out)
+    far, left_out, right_out, own_sum = lax.optimization_barrier(
+        (far, left_out, right_out, own_sum)
+    )
     left_sum, right_sum = paired(*left_out), paired(*right_out)
     from_right = lax.ppermute(left_sum[:half].astype(BF16), "seq", x_shift(-1))
     from_left = lax.ppermute(right_sum[half:].astype(BF16), "seq", x_shift(1))
@@ -400,7 +403,6 @@
     far_sum = paired(*far_out).astype(BF16)
     for_right = lax.ppermute(far_sum[:half], "seq", x_shift(1))
     for_left = lax.ppermute(far_sum[half:], "seq", x_shift(-1))
-    own_sum = paired(*own_out)
     to_left = left_sum[half:] + for_left.astype(F32)
     to_right = right_sum[:half] + for_right.astype(F32)
     (own_sum,) = after((own_sum,), to_left, to_right)

time: 229 us -> 229 us (level)
    unnamed x27 -> x25, local copies, waits for them, and re-layouts: 8.52 us -> 8.51 us
  transfers between devices with their start and end apart: 35 -> 35, of which waited for: 20 -> 18; matrix products, arithmetic and copies ran while one was open for 2% -> 2% of each run, Pallas kernels for 11% -> 11%
where the time goes in v11:
time: 229 us
  waiting for transfers between devices  105 us (46%)
  starting transfers between devices  46.2 us (20%)
  Pallas kernels  38.4 us (17%)
  blocking collectives  21.2 us (9%)
  local copies, waits for them, and re-layouts  11.4 us (5%)
  other arithmetic  4 us (2%)
    all_to_all x1, waiting for transfers between devices, per_device(): lax.all_to_all(partial_rows, 'exp', split_axis=0, concat_axis=0, tiled=True)  29.8 us
    pallas_call x4, Pallas kernels, expert_block(): pl.pallas_call(lambda *refs: expert_kernel(len(parts), *refs), out_shape=...  25.2 us
    all_to_all x1, blocking collectives, per_device(): lax.all_to_all(jnp.tile(outgoing, (splits, 1)), 'exp', split_axis=0, conc...  21.2 us
    all_to_all x1, waiting for transfers between devices, per_device(): lax.all_to_all(own_rows.astype(BF16), 'exp', split_axis=0, concat_axis=0,...  15.7 us
    ppermute x6, starting transfers between devices, from_others(): return [lax.ppermute(value, 'exp', shift(by)) for by in (1, 2, 3)]  13 us
    ppermute x6, waiting for transfers between devices, from_others(): return [lax.ppermute(value, 'exp', shift(by)) for by in (1, 2, 3)]  12.2 us
    ppermute x1, waiting for transfers between devices, experts(): for_right = lax.ppermute(far_sum[:half], 'seq', x_shift(1))  11.9 us
    ppermute x1, waiting for transfers between devices, experts(): then_left = lax.ppermute(to_right.astype(BF16), 'seq', x_shift(1))  10.7 us
  transfers between devices with their start and end apart: 35, of which 18 were waited for; matrix products, arithmetic and copies ran while one was open for 2% of the time, Pallas kernels for 11%

profile of v11, /device:TPU:0, one launch (start us, length us, event | category | flops | bytes accessed | tf_op | source)
XLA Modules:
  0.0 228.8 jit_solution(18182439529858294866)
XLA Ops:
  0.0 0.8 slice.38
  0.8 1.3 collective-permute-start
  2.1 1.0 reshape.86.xin
  3.1 1.5 mixer_in.1
  4.6 2.5 %collective-permute-start.1 = (bf16[288,256]{1,0:T(8,128)(2,1)S(1)}, bf16[288,256]{1,0:T(8,128)(2,1)S(1)}, u32[]{:S(2)}, u32[]{:S(2)}) collective-permute-start(bf16[288,256]{1,0:T(8,128)(2,1)S(1)} %get-tuple-element.32), channel_id=1, source_target_pairs={{0,1},{1,2},{2,3},{3,0},{4,5},{5,6},{6,7},{7,4},{8,9},{9,10},{10,1... | collective-permute-start | bytes 442376 | tf_op jit(solution)/shard_map/ppermute | solution.py:44
  7.2 3.6 %collective-permute-start.2 = (bf16[288,256]{1,0:T(8,128)(2,1)S(1)}, bf16[288,256]{1,0:T(8,128)(2,1)S(1)}, u32[]{:S(2)}, u32[]{:S(2)}) collective-permute-start(bf16[288,256]{1,0:T(8,128)(2,1)S(1)} %get-tuple-element.32), channel_id=1, source_target_pairs={{0,2},{1,3},{2,0},{3,1},{4,6},{5,7},{6,4},{7,5},{8,10},{9,11},{10,... | collective-permute-start | bytes 442376 | tf_op jit(solution)/shard_map/ppermute | solution.py:44
  10.7 1.0 collective-permute-start.3
  11.8 1.1 collective-permute-done.1
  12.9 4.9 %collective-permute-done.2 = bf16[288,256]{1,0:T(8,128)(2,1)S(1)} collective-permute-done((bf16[288,256]{1,0:T(8,128)(2,1)S(1)}, bf16[288,256]{1,0:T(8,128)(2,1)S(1)}, u32[]{:S(2)}, u32[]{:S(2)}) %collective-permute-start.2) | collective-permute-done | bytes 147488 | tf_op jit(solution)/shard_map/ppermute | solution.py:44
  17.9 1.6 collective-permute-start.4
  19.5 2.9 %collective-permute-start.5 = (bf16[288,256]{1,0:T(8,128)(2,1)S(1)}, bf16[288,256]{1,0:T(8,128)(2,1)S(1)}, u32[]{:S(2)}, u32[]{:S(2)}) collective-permute-start(bf16[288,256]{1,0:T(8,128)(2,1)S(1)} %add_convert_fusion.3.p0), channel_id=1, source_target_pairs={{0,8},{1,9},{2,10},{3,11},{4,12},{5,13},{6,14},{7,15},{8,0},{9,1},... | collective-permute-start | bytes 442376 | tf_op jit(solution)/shard_map/ppermute | solution.py:44
  22.5 1.3 collective-permute-start.6
  23.8 1.8 collective-permute-done.4.p1
  25.6 4.3 %collective-permute-done.5.p2 = bf16[288,256]{1,0:T(8,128)(2,1)S(1)} collective-permute-done((bf16[288,256]{1,0:T(8,128)(2,1)S(1)}, bf16[288,256]{1,0:T(8,128)(2,1)S(1)}, u32[]{:S(2)}, u32[]{:S(2)}) %collective-permute-start.5) | collective-permute-done | bytes 147488 | tf_op jit(solution)/shard_map/ppermute | solution.py:44
  29.9 4.0 %section_scan.1 = (f32[256,512]{1,0:T(8,128)S(1)}, f32[32,256]{1,0:T(8,128)S(1)}, bf16[72,512]{1,0:T(8,128)(2,1)S(1)}) custom-call(bf16[288,256]{1,0:T(8,128)(2,1)S(1)} %add_convert_fusion.3.p0, bf16[288,256]{1,0:T(8,128)(2,1)S(1)} %collective-permute-done.4.p1, bf16[288,256]{1,0:T(8,128)(2,1)S(1)} %collective-permute-done.5.p2, ...), custom_call_target="tpu_custom_call" | custom-call | tf_op jit(solution)/shard_map/section_scan/pallas_call | solution.py:272
  33.9 1.1 collective-permute-start.7
  35.1 1.2 collective-permute-start.8
  36.3 2.5 %collective-permute-start.9 = (bf16[72,512]{1,0:T(8,128)(2,1)S(1)}, bf16[72,512]{1,0:T(8,128)(2,1)S(1)}, u32[]{:S(2)}, u32[]{:S(2)}) collective-permute-start(bf16[72,512]{1,0:T(8,128)(2,1)S(1)} %get-tuple-element.34), channel_id=1, source_target_pairs={{0,96},{16,112},{32,0},{48,16},{64,32},{80,48},{96,64},{112,80},{1... | collective-permute-start | bytes 221192 | tf_op jit(solution)/shard_map/ppermute | solution.py:446
  38.8 1.2 collective-permute-done.7.refs_0_
  40.0 0.9 collective-permute-done.8.refs_1_
  40.9 0.4 collective-permute-done.9.refs_2_
  41.5 0.7 collective-permute-done.12.refs_5_
  42.2 0.4 collective-permute-done.13.refs_6_
  42.6 7.7 %mixer_out.1 = bf16[256,4096]{1,0:T(8,128)(2,1)} custom-call(s32[1]{0:T(128)} %bitcast.section, bf16[72,512]{1,0:T(8,128)(2,1)S(1)} %collective-permute-done.7.refs_0_, bf16[72,512]{1,0:T(8,128)(2,1)S(1)} %collective-permute-done.8.refs_1_, bf16[72,512]{1,0:T(8,128)(2,1)S(1)} %collective-permute-done.9.refs_2_, ...), custom_call_target="tpu_custom_call" | custom-call | tf_op jit(solution)/shard_map/mixer_out/pallas_call | solution.py:295
  50.4 6.0 %all-to-all-start = ((bf16[16,16,4096]{2,1,0:T(8,128)(2,1)}), bf16[16,16,4096]{2,1,0:T(8,128)(2,1)S(1)}, u32[]{:S(2)}, u32[]{:S(2)}) async-start(bf16[16,16,4096]{2,1,0:T(8,128)(2,1)} %bitcast.5), calls=%async_computation | async-start | bytes 4194304 | tf_op jit(solution)/shard_map/all_to_all | solution.py:458
  56.8 0.2 select_reduce_fusion.1
  57.4 29.8 %all-to-all-done = bf16[16,16,4096]{2,1,0:T(8,128)(2,1)S(1)} async-done(((bf16[16,16,4096]{2,1,0:T(8,128)(2,1)}), bf16[16,16,4096]{2,1,0:T(8,128)(2,1)S(1)}, u32[]{:S(2)}, u32[]{:S(2)}) %all-to-all-start) | async-done | bytes 2097184 | tf_op jit(solution)/shard_map/all_to_all | solution.py:458
  87.2 0.3 convert_reduce_fusion
  87.8 0.3 convolution_convert_fusion
  88.3 21.2 %all_to_all.26 = bf16[16,8,4096]{2,1,0:T(8,128)(2,1)S(1)} all-to-all(bf16[16,8,4096]{2,1,0:T(8,128)(2,1)S(1)} %bitcast.29), channel_id=1, replica_groups=mesh['seq'=8,'exp'=16] {'exp'}, dimensions={0} | all-to-all | bytes 2097152 | tf_op jit(solution)/shard_map/all_to_all | solution.py:471
  109.5 0.4 collective-permute-start.14
  109.9 2.8 %collective-permute-start.15 = (bf16[128,4096]{1,0:T(8,128)(2,1)S(1)}, bf16[128,4096]{1,0:T(8,128)(2,1)S(1)}, u32[]{:S(2)}, u32[]{:S(2)}) collective-permute-start(bf16[128,4096]{1,0:T(8,128)(2,1)S(1)} %bitcast.25), channel_id=1, source_target_pairs={{0,96},{16,112},{32,0},{48,16},{64,32},{80,48},{96,64},{112,80},{1... | collective-permute-start | bytes 3145736 | tf_op jit(solution)/shard_map/ppermute | solution.py:385
  112.8 2.8 %copy-done = bf16[1,4096,768]{2,1,0:T(8,128)(2,1)S(1)} copy-done((bf16[1,4096,768]{2,1,0:T(8,128)(2,1)S(1)}, bf16[1,4096,768]{2,1,0:T(8,128)(2,1)}, u32[]{:S(2)}) %copy-start) | copy-done | bytes 6291480
  115.5 2.8 %copy-done.2 = bf16[1,4096,768]{2,1,0:T(8,128)(2,1)S(1)} copy-done((bf16[1,4096,768]{2,1,0:T(8,128)(2,1)S(1)}, bf16[1,4096,768]{2,1,0:T(8,128)(2,1)}, u32[]{:S(2)}) %copy-start.2) | copy-done | bytes 6291480
  118.3 2.8 %copy-done.4 = bf16[1,768,4096]{2,1,0:T(8,128)(2,1)S(1)} copy-done((bf16[1,768,4096]{2,1,0:T(8,128)(2,1)S(1)}, bf16[1,768,4096]{2,1,0:T(8,128)(2,1)}, u32[]{:S(2)}) %copy-start.4) | copy-done | bytes 6291480
  121.1 6.3 %experts_256.4 = (bf16[128,4096]{1,0:T(8,128)(2,1)S(1)}, bf16[128,4096]{1,0:T(8,128)(2,1)S(1)}) custom-call(bf16[128,4096]{1,0:T(8,128)(2,1)S(1)} %bitcast.26, bf16[128,4096]{1,0:T(8,128)(2,1)S(1)} %collective-permute-done.16.refs_1_, bf16[1,4096,768]{2,1,0:T(8,128)(2,1)S(1)} %copy-done, bf16[1,4096,768]{2,1,0:T(8,128)(2,1)S(1)} %copy-done.2, ...), custom_call_target="tpu_custom_call" | custom-call | flops 4831838208 | bytes 4194304 | tf_op jit(solution)/shard_map/experts_256/pallas_call | solution.py:344
  127.5 8.8 %collective-permute-done.14.refs_0_ = bf16[128,4096]{1,0:T(8,128)(2,1)S(1)} collective-permute-done((bf16[128,4096]{1,0:T(8,128)(2,1)S(1)}, bf16[128,4096]{1,0:T(8,128)(2,1)S(1)}, u32[]{:S(2)}, u32[]{:S(2)}) %collective-permute-start.14) | collective-permute-done | bytes 1048608 | tf_op jit(solution)/shard_map/ppermute | solution.py:384
  136.3 0.5 collective-permute-start.19
  136.9 0.3 collective-permute-start.17
  137.2 3.0 %collective-permute-start.18 = (bf16[64,4096]{1,0:T(8,128)(2,1)S(1)}, bf16[64,4096]{1,0:T(8,128)(2,1)S(1)}, u32[]{:S(2)}, u32[]{:S(2)}) collective-permute-start(bf16[64,4096]{1,0:T(8,128)(2,1)S(1)} %slice.41), channel_id=1, source_target_pairs={{0,96},{16,112},{32,0},{48,16},{64,32},{80,48},{96,64},{112,80},{1... | collective-permute-start | bytes 1572872 | tf_op jit(solution)/shard_map/ppermute | solution.py:390
  140.2 0.2 convert_add_fusion.2
  140.5 6.3 %experts_256.6 = (bf16[128,4096]{1,0:T(8,128)(2,1)S(1)}, bf16[128,4096]{1,0:T(8,128)(2,1)S(1)}) custom-call(bf16[128,4096]{1,0:T(8,128)(2,1)S(1)} %collective-permute-done.15.refs_0_, bf16[128,4096]{1,0:T(8,128)(2,1)S(1)} %collective-permute-done.20.refs_1_, bf16[1,4096,768]{2,1,0:T(8,128)(2,1)S(1)} %copy-done.1, bf16[1,4096,768]{2,1,0:T(8,128)(2,1)S(1)} %copy-done.3, ...), custom_call_target="tpu_custom_call" | custom-call | flops 4831838208 | bytes 4194304 | tf_op jit(solution)/shard_map/experts_256/pallas_call | solution.py:344
  146.8 6.3 %experts_256.5 = (bf16[128,4096]{1,0:T(8,128)(2,1)S(1)}, bf16[128,4096]{1,0:T(8,128)(2,1)S(1)}) custom-call(bf16[128,4096]{1,0:T(8,128)(2,1)S(1)} %collective-permute-done.14.refs_0_, bf16[128,4096]{1,0:T(8,128)(2,1)S(1)} %collective-permute-done.19.refs_1_, bf16[1,4096,768]{2,1,0:T(8,128)(2,1)S(1)} %copy-done.1, bf16[1,4096,768]{2,1,0:T(8,128)(2,1)S(1)} %copy-done.3, ...), custom_call_target="tpu_custom_call" | custom-call | flops 4831838208 | bytes 4194304 | tf_op jit(solution)/shard_map/experts_256/pallas_call | solution.py:344
  153.2 0.5 collective-permute-start.26
  153.8 0.4 collective-permute-start.24
  154.2 1.6 collective-permute-done.22
  155.9 0.2 convert_add_fusion.1
  156.2 1.9 collective-permute-start.25
  158.1 0.3 convert_add_fusion
  158.4 0.5 collective-permute-start.27
  158.9 6.3 %experts_256.7 = (bf16[128,4096]{1,0:T(8,128)(2,1)S(1)}, bf16[128,4096]{1,0:T(8,128)(2,1)S(1)}) custom-call(bf16[64,4096]{1,0:T(8,128)(2,1)S(1)} %collective-permute-done.17.refs_0_, bf16[64,4096]{1,0:T(8,128)(2,1)S(1)} %collective-permute-done.18.refs_1_, bf16[64,4096]{1,0:T(8,128)(2,1)S(1)} %collective-permute-done.23.refs_2_, ...), custom_call_target="tpu_custom_call" | custom-call | flops 4831838208 | bytes 4194304 | tf_op jit(solution)/shard_map/experts_256/pallas_call | solution.py:344
  165.2 5.0 %collective-permute-done.25 = bf16[64,4096]{1,0:T(8,128)(2,1)S(1)} collective-permute-done((bf16[64,4096]{1,0:T(8,128)(2,1)S(1)}, bf16[64,4096]{1,0:T(8,128)(2,1)S(1)}, u32[]{:S(2)}, u32[]{:S(2)}) %collective-permute-start.25) | collective-permute-done | bytes 524320 | tf_op jit(solution)/shard_map/ppermute | solution.py:399
  170.2 3.4 %collective-permute-done.27 = bf16[64,4096]{1,0:T(8,128)(2,1)S(1)} collective-permute-done((bf16[64,4096]{1,0:T(8,128)(2,1)S(1)}, bf16[64,4096]{1,0:T(8,128)(2,1)S(1)}, u32[]{:S(2)}, u32[]{:S(2)}) %collective-permute-start.27) | collective-permute-done | bytes 524320 | tf_op jit(solution)/shard_map/ppermute | solution.py:400
  173.6 2.7 %collective-permute-done.28 = bf16[128,4096]{1,0:T(8,128)(2,1)S(1)} collective-permute-done((bf16[128,4096]{1,0:T(8,128)(2,1)S(1)}, bf16[128,4096]{1,0:T(8,128)(2,1)S(1)}, u32[]{:S(2)}, u32[]{:S(2)}) %collective-permute-start.28) | collective-permute-done | bytes 1048608 | tf_op jit(solution)/shard_map/ppermute | solution.py:48
  176.3 0.2 add_convert_fusion
  176.7 3.2 %collective-permute-start.29 = (bf16[64,4096]{1,0:T(8,128)(2,1)S(1)}, bf16[64,4096]{1,0:T(8,128)(2,1)S(1)}, u32[]{:S(2)}, u32[]{:S(2)}) collective-permute-start(bf16[64,4096]{1,0:T(8,128)(2,1)S(1)} %get-tuple-element.62), channel_id=1, source_target_pairs={{0,96},{16,112},{32,0},{48,16},{64,32},{80,48},{96,64},{112,80},{1... | collective-permute-start | bytes 1572872 | tf_op jit(solution)/shard_map/ppermute | solution.py:405
  179.9 11.9 %collective-permute-done.30 = bf16[64,4096]{1,0:T(8,128)(2,1)S(1)} collective-permute-done((bf16[64,4096]{1,0:T(8,128)(2,1)S(1)}, bf16[64,4096]{1,0:T(8,128)(2,1)S(1)}, u32[]{:S(2)}, u32[]{:S(2)}) %collective-permute-start.30) | collective-permute-done | bytes 524320 | tf_op jit(solution)/shard_map/ppermute | solution.py:404
  192.2 3.3 %collective-permute-start.32 = (bf16[64,4096]{1,0:T(8,128)(2,1)S(1)}, bf16[64,4096]{1,0:T(8,128)(2,1)S(1)}, u32[]{:S(2)}, u32[]{:S(2)}) collective-permute-start(bf16[64,4096]{1,0:T(8,128)(2,1)S(1)} %slice_add_fusion.1), channel_id=1, source_target_pairs={{0,96},{16,112},{32,0},{48,16},{64,32},{80,48},{96,64},{112,80},{1... | collective-permute-start | bytes 1572872 | tf_op jit(solution)/shard_map/ppermute | solution.py:412
  195.5 0.2 convert_add_fusion.3
  195.8 10.7 %collective-permute-done.31 = bf16[64,4096]{1,0:T(8,128)(2,1)S(1)} collective-permute-done((bf16[64,4096]{1,0:T(8,128)(2,1)S(1)}, bf16[64,4096]{1,0:T(8,128)(2,1)S(1)}, u32[]{:S(2)}, u32[]{:S(2)}) %collective-permute-start.31) | collective-permute-done | bytes 524320 | tf_op jit(solution)/shard_map/ppermute | solution.py:413
  206.7 1.1 maximum_bitcast_fusion
  207.8 3.7 %all-to-all-start.2 = ((bf16[16,8,4096]{2,1,0:T(8,128)(2,1)}), bf16[16,8,4096]{2,1,0:T(8,128)(2,1)S(1)}, u32[]{:S(2)}, u32[]{:S(2)}) async-start(bf16[16,8,4096]{2,1,0:T(8,128)(2,1)} %maximum_bitcast_fusion), calls=%async_computation.2 | async-start | bytes 2097152 | tf_op jit(solution)/shard_map/all_to_all | solution.py:475
  211.6 15.7 %all-to-all-done.2 = bf16[16,8,4096]{2,1,0:T(8,128)(2,1)S(1)} async-done(((bf16[16,8,4096]{2,1,0:T(8,128)(2,1)}), bf16[16,8,4096]{2,1,0:T(8,128)(2,1)S(1)}, u32[]{:S(2)}, u32[]{:S(2)}) %all-to-all-start.2) | async-done | bytes 1048608 | tf_op jit(solution)/shard_map/all_to_all | solution.py:475
  227.5 1.3 fusion
  (83 shorter events, 3.0 us)
Async XLA Ops:
  0.0 42.6 %copy-start.5 = (f32[16,512]{1,0:T(8,128)S(1)}, f32[16,512]{1,0:T(8,128)}, u32[]{:S(2)}) copy-start(f32[16,512]{1,0:T(8,128)} %refs_10_.1) | copy-start | bytes 98308
  0.0 41.4 %copy-start.8 = (bf16[64,4,512]{2,1,0:T(4,128)(2,1)S(1)}, bf16[64,4,512]{2,1,0:T(4,128)(2,1)}, u32[]{:S(2)}) copy-start(bf16[64,4,512]{2,1,0:T(4,128)(2,1)} %param.18) | copy-start | bytes 786436
  0.0 42.6 %copy-start.6 = (f32[512]{0:T(512)S(1)}, f32[512]{0:T(512)}, u32[]{:S(2)}) copy-start(f32[512]{0:T(512)} %param.25) | copy-start | bytes 6148
  0.8 2.3 %collective-permute-start = (bf16[12,512]{1,0:T(8,128)(2,1)S(1)}, bf16[12,512]{1,0:T(8,128)(2,1)S(1)}, u32[]{:S(2)}, u32[]{:S(2)}) collective-permute-start(bf16[12,512]{1,0:T(8,128)(2,1)S(1)} %slice.39), channel_id=1, source_target_pairs={{0,16},{16,32},{32,48},{48,64},{64,80},{80,96},{96,112},{1,17},{17... | collective-permute-start | bytes 36872 | tf_op jit(solution)/shard_map/ppermute | solution.py:40
  4.6 8.2 %collective-permute-start.1 = (bf16[288,256]{1,0:T(8,128)(2,1)S(1)}, bf16[288,256]{1,0:T(8,128)(2,1)S(1)}, u32[]{:S(2)}, u32[]{:S(2)}) collective-permute-start(bf16[288,256]{1,0:T(8,128)(2,1)S(1)} %get-tuple-element.32), channel_id=1, source_target_pairs={{0,1},{1,2},{2,3},{3,0},{4,5},{5,6},{6,7},{7,4},{8,9},{9,10},{10,1... | collective-permute-start | bytes 442376 | tf_op jit(solution)/shard_map/ppermute | solution.py:44
  7.2 10.7 %collective-permute-start.2 = (bf16[288,256]{1,0:T(8,128)(2,1)S(1)}, bf16[288,256]{1,0:T(8,128)(2,1)S(1)}, u32[]{:S(2)}, u32[]{:S(2)}) collective-permute-start(bf16[288,256]{1,0:T(8,128)(2,1)S(1)} %get-tuple-element.32), channel_id=1, source_target_pairs={{0,2},{1,3},{2,0},{3,1},{4,6},{5,7},{6,4},{7,5},{8,10},{9,11},{10,... | collective-permute-start | bytes 442376 | tf_op jit(solution)/shard_map/ppermute | solution.py:44
  10.7 7.1 %collective-permute-start.3 = (bf16[288,256]{1,0:T(8,128)(2,1)S(1)}, bf16[288,256]{1,0:T(8,128)(2,1)S(1)}, u32[]{:S(2)}, u32[]{:S(2)}) collective-permute-start(bf16[288,256]{1,0:T(8,128)(2,1)S(1)} %get-tuple-element.32), channel_id=1, source_target_pairs={{0,3},{1,0},{2,1},{3,2},{4,7},{5,4},{6,5},{7,6},{8,11},{9,8},{10,9... | collective-permute-start | bytes 442376 | tf_op jit(solution)/shard_map/ppermute | solution.py:44
  17.9 7.7 %collective-permute-start.4 = (bf16[288,256]{1,0:T(8,128)(2,1)S(1)}, bf16[288,256]{1,0:T(8,128)(2,1)S(1)}, u32[]{:S(2)}, u32[]{:S(2)}) collective-permute-start(bf16[288,256]{1,0:T(8,128)(2,1)S(1)} %add_convert_fusion.3.p0), channel_id=1, source_target_pairs={{0,4},{1,5},{2,6},{3,7},{4,8},{5,9},{6,10},{7,11},{8,12},{9,13},{1... | collective-permute-start | bytes 442376 | tf_op jit(solution)/shard_map/ppermute | solution.py:44
  19.5 10.4 %collective-permute-start.5 = (bf16[288,256]{1,0:T(8,128)(2,1)S(1)}, bf16[288,256]{1,0:T(8,128)(2,1)S(1)}, u32[]{:S(2)}, u32[]{:S(2)}) collective-permute-start(bf16[288,256]{1,0:T(8,128)(2,1)S(1)} %add_convert_fusion.3.p0), channel_id=1, source_target_pairs={{0,8},{1,9},{2,10},{3,11},{4,12},{5,13},{6,14},{7,15},{8,0},{9,1},... | collective-permute-start | bytes 442376 | tf_op jit(solution)/shard_map/ppermute | solution.py:44
  22.5 7.5 %collective-permute-start.6 = (bf16[288,256]{1,0:T(8,128)(2,1)S(1)}, bf16[288,256]{1,0:T(8,128)(2,1)S(1)}, u32[]{:S(2)}, u32[]{:S(2)}) collective-permute-start(bf16[288,256]{1,0:T(8,128)(2,1)S(1)} %add_convert_fusion.3.p0), channel_id=1, source_target_pairs={{0,12},{1,13},{2,14},{3,15},{4,0},{5,1},{6,2},{7,3},{8,4},{9,5},{1... | collective-permute-start | bytes 442376 | tf_op jit(solution)/shard_map/ppermute | solution.py:44
  33.9 6.1 %collective-permute-start.7 = (bf16[72,512]{1,0:T(8,128)(2,1)S(1)}, bf16[72,512]{1,0:T(8,128)(2,1)S(1)}, u32[]{:S(2)}, u32[]{:S(2)}) collective-permute-start(bf16[72,512]{1,0:T(8,128)(2,1)S(1)} %get-tuple-element.34), channel_id=1, source_target_pairs={{0,32},{16,48},{32,64},{48,80},{64,96},{80,112},{96,0},{112,16},{1... | collective-permute-start | bytes 221192 | tf_op jit(solution)/shard_map/ppermute | solution.py:446
  35.1 5.9 %collective-permute-start.8 = (bf16[72,512]{1,0:T(8,128)(2,1)S(1)}, bf16[72,512]{1,0:T(8,128)(2,1)S(1)}, u32[]{:S(2)}, u32[]{:S(2)}) collective-permute-start(bf16[72,512]{1,0:T(8,128)(2,1)S(1)} %get-tuple-element.34), channel_id=1, source_target_pairs={{0,64},{16,80},{32,96},{48,112},{64,0},{80,16},{96,32},{112,48},{1... | collective-permute-start | bytes 221192 | tf_op jit(solution)/shard_map/ppermute | solution.py:446
  36.3 5.1 %collective-permute-start.9 = (bf16[72,512]{1,0:T(8,128)(2,1)S(1)}, bf16[72,512]{1,0:T(8,128)(2,1)S(1)}, u32[]{:S(2)}, u32[]{:S(2)}) collective-permute-start(bf16[72,512]{1,0:T(8,128)(2,1)S(1)} %get-tuple-element.34), channel_id=1, source_target_pairs={{0,96},{16,112},{32,0},{48,16},{64,32},{80,48},{96,64},{112,80},{1... | collective-permute-start | bytes 221192 | tf_op jit(solution)/shard_map/ppermute | solution.py:446
  38.8 2.7 %collective-permute-start.10 = (bf16[72,512]{1,0:T(8,128)(2,1)S(1)}, bf16[72,512]{1,0:T(8,128)(2,1)S(1)}, u32[]{:S(2)}, u32[]{:S(2)}) collective-permute-start(bf16[72,512]{1,0:T(8,128)(2,1)S(1)} %get-tuple-element.34), channel_id=1, source_target_pairs={{0,16},{16,0},{32,48},{48,32},{64,80},{80,64},{96,112},{112,96},{1... | collective-permute-start | bytes 221192 | tf_op jit(solution)/shard_map/ppermute | solution.py:48
  40.0 1.5 collective-permute-start.11
  40.9 1.3 collective-permute-start.12
  41.4 1.3 collective-permute-start.13
  50.4 6.1 %copy-start.10 = (s32[4,4,2]{1,2,0:T(2,128)S(1)}, s32[4,4,2]{1,2,0:T(2,128)}, u32[]{:S(2)}) copy-start(s32[4,4,2]{1,2,0:T(2,128)} %param.29) | copy-start | bytes 388
  50.4 6.9 %copy-start.7 = (bf16[4,4,4096]{2,1,0:T(4,128)(2,1)S(1)}, bf16[4,4,4096]{2,1,0:T(4,128)(2,1)}, u32[]{:S(2)}) copy-start(bf16[4,4,4096]{2,1,0:T(4,128)(2,1)} %param.27) | copy-start | bytes 393220
  50.4 36.8 %all-to-all-start = ((bf16[16,16,4096]{2,1,0:T(8,128)(2,1)}), bf16[16,16,4096]{2,1,0:T(8,128)(2,1)S(1)}, u32[]{:S(2)}, u32[]{:S(2)}) async-start(bf16[16,16,4096]{2,1,0:T(8,128)(2,1)} %bitcast.5), calls=%async_computation | async-start | bytes 4194304 | tf_op jit(solution)/shard_map/all_to_all | solution.py:458
  56.4 31.4 %copy-start.9 = (f32[4096]{0:T(1024)S(1)}, f32[4096]{0:T(1024)}, u32[]{:S(2)}) copy-start(f32[4096]{0:T(1024)} %param.28) | copy-start | bytes 49156
  109.5 3.2 %collective-permute-start.16 = (bf16[128,4096]{1,0:T(8,128)(2,1)S(1)}, bf16[128,4096]{1,0:T(8,128)(2,1)S(1)}, u32[]{:S(2)}, u32[]{:S(2)}) collective-permute-start(bf16[128,4096]{1,0:T(8,128)(2,1)S(1)} %bitcast.23), channel_id=1, source_target_pairs={{0,16},{16,0},{32,48},{48,32},{64,80},{80,64},{96,112},{112,96},{1... | collective-permute-start | bytes 3145736 | tf_op jit(solution)/shard_map/ppermute | solution.py:48
  109.5 26.8 %collective-permute-start.14 = (bf16[128,4096]{1,0:T(8,128)(2,1)S(1)}, bf16[128,4096]{1,0:T(8,128)(2,1)S(1)}, u32[]{:S(2)}, u32[]{:S(2)}) collective-permute-start(bf16[128,4096]{1,0:T(8,128)(2,1)S(1)} %bitcast.24), channel_id=1, source_target_pairs={{0,32},{16,48},{32,64},{48,80},{64,96},{80,112},{96,0},{112,16},{1... | collective-permute-start | bytes 3145736 | tf_op jit(solution)/shard_map/ppermute | solution.py:384
  109.9 26.4 %collective-permute-start.15 = (bf16[128,4096]{1,0:T(8,128)(2,1)S(1)}, bf16[128,4096]{1,0:T(8,128)(2,1)S(1)}, u32[]{:S(2)}, u32[]{:S(2)}) collective-permute-start(bf16[128,4096]{1,0:T(8,128)(2,1)S(1)} %bitcast.25), channel_id=1, source_target_pairs={{0,96},{16,112},{32,0},{48,16},{64,32},{80,48},{96,64},{112,80},{1... | collective-permute-start | bytes 3145736 | tf_op jit(solution)/shard_map/ppermute | solution.py:385
  112.8 2.8 %copy-start = (bf16[1,4096,768]{2,1,0:T(8,128)(2,1)S(1)}, bf16[1,4096,768]{2,1,0:T(8,128)(2,1)}, u32[]{:S(2)}) copy-start(bf16[1,4096,768]{2,1,0:T(8,128)(2,1)} %refs_4_.7) | copy-start | bytes 18874372
  115.5 2.8 %copy-start.2 = (bf16[1,4096,768]{2,1,0:T(8,128)(2,1)S(1)}, bf16[1,4096,768]{2,1,0:T(8,128)(2,1)}, u32[]{:S(2)}) copy-start(bf16[1,4096,768]{2,1,0:T(8,128)(2,1)} %refs_5_.1) | copy-start | bytes 18874372
  118.3 2.8 %copy-start.4 = (bf16[1,768,4096]{2,1,0:T(8,128)(2,1)S(1)}, bf16[1,768,4096]{2,1,0:T(8,128)(2,1)}, u32[]{:S(2)}) copy-start(bf16[1,768,4096]{2,1,0:T(8,128)(2,1)} %refs_6_.1) | copy-start | bytes 18874372
  121.1 19.4 %copy-start.3 = (bf16[1,4096,768]{2,1,0:T(8,128)(2,1)S(1)}, bf16[1,4096,768]{2,1,0:T(8,128)(2,1)}, u32[]{:S(2)}) copy-start(bf16[1,4096,768]{2,1,0:T(8,128)(2,1)} %refs_5_.1) | copy-start | bytes 18874372
  127.4 12.8 %collective-permute-start.21 = (bf16[128,4096]{1,0:T(8,128)(2,1)S(1)}, bf16[128,4096]{1,0:T(8,128)(2,1)S(1)}, u32[]{:S(2)}, u32[]{:S(2)}) collective-permute-start(bf16[128,4096]{1,0:T(8,128)(2,1)S(1)} %get-tuple-element.38), channel_id=1, source_target_pairs={{0,16},{16,0},{32,48},{48,32},{64,80},{80,64},{96,112},{112,96},{1... | collective-permute-start | bytes 3145736 | tf_op jit(solution)/shard_map/ppermute | solution.py:48
  136.3 4.2 %copy-start.1 = (bf16[1,4096,768]{2,1,0:T(8,128)(2,1)S(1)}, bf16[1,4096,768]{2,1,0:T(8,128)(2,1)}, u32[]{:S(2)}) copy-start(bf16[1,4096,768]{2,1,0:T(8,128)(2,1)} %refs_4_.7) | copy-start | bytes 18874372
  136.3 4.2 %collective-permute-start.20 = (bf16[128,4096]{1,0:T(8,128)(2,1)S(1)}, bf16[128,4096]{1,0:T(8,128)(2,1)S(1)}, u32[]{:S(2)}, u32[]{:S(2)}) collective-permute-start(bf16[128,4096]{1,0:T(8,128)(2,1)S(1)} %collective-permute-done.15.refs_0_), channel_id=1, source_target_pairs={{0,16},{16,0},{32,48},{48,32},{64,80},{80,64},{96,112},{112,96},{1... | collective-permute-start | bytes 3145736 | tf_op jit(solution)/shard_map/ppermute | solution.py:48
  136.3 10.5 %collective-permute-start.19 = (bf16[128,4096]{1,0:T(8,128)(2,1)S(1)}, bf16[128,4096]{1,0:T(8,128)(2,1)S(1)}, u32[]{:S(2)}, u32[]{:S(2)}) collective-permute-start(bf16[128,4096]{1,0:T(8,128)(2,1)S(1)} %collective-permute-done.14.refs_0_), channel_id=1, source_target_pairs={{0,16},{16,0},{32,48},{48,32},{64,80},{80,64},{96,112},{112,96},{1... | collective-permute-start | bytes 3145736 | tf_op jit(solution)/shard_map/ppermute | solution.py:48
  136.9 16.2 %collective-permute-start.17 = (bf16[64,4096]{1,0:T(8,128)(2,1)S(1)}, bf16[64,4096]{1,0:T(8,128)(2,1)S(1)}, u32[]{:S(2)}, u32[]{:S(2)}) collective-permute-start(bf16[64,4096]{1,0:T(8,128)(2,1)S(1)} %slice.40), channel_id=1, source_target_pairs={{0,32},{16,48},{32,64},{48,80},{64,96},{80,112},{96,0},{112,16},{1... | collective-permute-start | bytes 1572872 | tf_op jit(solution)/shard_map/ppermute | solution.py:389
  137.2 15.9 %collective-permute-start.18 = (bf16[64,4096]{1,0:T(8,128)(2,1)S(1)}, bf16[64,4096]{1,0:T(8,128)(2,1)S(1)}, u32[]{:S(2)}, u32[]{:S(2)}) collective-permute-start(bf16[64,4096]{1,0:T(8,128)(2,1)S(1)} %slice.41), channel_id=1, source_target_pairs={{0,96},{16,112},{32,0},{48,16},{64,32},{80,48},{96,64},{112,80},{1... | collective-permute-start | bytes 1572872 | tf_op jit(solution)/shard_map/ppermute | solution.py:390
  153.1 2.7 %collective-permute-start.22 = (bf16[128,4096]{1,0:T(8,128)(2,1)S(1)}, bf16[128,4096]{1,0:T(8,128)(2,1)S(1)}, u32[]{:S(2)}, u32[]{:S(2)}) collective-permute-start(bf16[128,4096]{1,0:T(8,128)(2,1)S(1)} %get-tuple-element.47), channel_id=1, source_target_pairs={{0,16},{16,0},{32,48},{48,32},{64,80},{80,64},{96,112},{112,96},{1... | collective-permute-start | bytes 3145736 | tf_op jit(solution)/shard_map/ppermute | solution.py:48
  153.2 4.9 %collective-permute-start.26 = (bf16[128,4096]{1,0:T(8,128)(2,1)S(1)}, bf16[128,4096]{1,0:T(8,128)(2,1)S(1)}, u32[]{:S(2)}, u32[]{:S(2)}) collective-permute-start(bf16[128,4096]{1,0:T(8,128)(2,1)S(1)} %get-tuple-element.53), channel_id=1, source_target_pairs={{0,16},{16,0},{32,48},{48,32},{64,80},{80,64},{96,112},{112,96},{1... | collective-permute-start | bytes 3145736 | tf_op jit(solution)/shard_map/ppermute | solution.py:48
  153.7 5.2 %collective-permute-start.23 = (bf16[64,4096]{1,0:T(8,128)(2,1)S(1)}, bf16[64,4096]{1,0:T(8,128)(2,1)S(1)}, u32[]{:S(2)}, u32[]{:S(2)}) collective-permute-start(bf16[64,4096]{1,0:T(8,128)(2,1)S(1)} %collective-permute-done.17.refs_0_), channel_id=1, source_target_pairs={{0,16},{16,0},{32,48},{48,32},{64,80},{80,64},{96,112},{112,96},{1... | collective-permute-start | bytes 1572872 | tf_op jit(solution)/shard_map/ppermute | solution.py:48
  153.8 5.1 %collective-permute-start.24 = (bf16[64,4096]{1,0:T(8,128)(2,1)S(1)}, bf16[64,4096]{1,0:T(8,128)(2,1)S(1)}, u32[]{:S(2)}, u32[]{:S(2)}) collective-permute-start(bf16[64,4096]{1,0:T(8,128)(2,1)S(1)} %collective-permute-done.18.refs_1_), channel_id=1, source_target_pairs={{0,16},{16,0},{32,48},{48,32},{64,80},{80,64},{96,112},{112,96},{1... | collective-permute-start | bytes 1572872 | tf_op jit(solution)/shard_map/ppermute | solution.py:48
  156.2 14.0 %collective-permute-start.25 = (bf16[64,4096]{1,0:T(8,128)(2,1)S(1)}, bf16[64,4096]{1,0:T(8,128)(2,1)S(1)}, u32[]{:S(2)}, u32[]{:S(2)}) collective-permute-start(bf16[64,4096]{1,0:T(8,128)(2,1)S(1)} %slice.63), channel_id=1, source_target_pairs={{0,96},{16,112},{32,0},{48,16},{64,32},{80,48},{96,64},{112,80},{1... | collective-permute-start | bytes 1572872 | tf_op jit(solution)/shard_map/ppermute | solution.py:399
  158.4 15.2 %collective-permute-start.27 = (bf16[64,4096]{1,0:T(8,128)(2,1)S(1)}, bf16[64,4096]{1,0:T(8,128)(2,1)S(1)}, u32[]{:S(2)}, u32[]{:S(2)}) collective-permute-start(bf16[64,4096]{1,0:T(8,128)(2,1)S(1)} %slice.62), channel_id=1, source_target_pairs={{0,32},{16,48},{32,64},{48,80},{64,96},{80,112},{96,0},{112,16},{1... | collective-permute-start | bytes 1572872 | tf_op jit(solution)/shard_map/ppermute | solution.py:400
  173.6 2.7 %collective-permute-start.28 = (bf16[128,4096]{1,0:T(8,128)(2,1)S(1)}, bf16[128,4096]{1,0:T(8,128)(2,1)S(1)}, u32[]{:S(2)}, u32[]{:S(2)}) collective-permute-start(bf16[128,4096]{1,0:T(8,128)(2,1)S(1)} %get-tuple-element.55), channel_id=1, source_target_pairs={{0,16},{16,0},{32,48},{48,32},{64,80},{80,64},{96,112},{112,96},{1... | collective-permute-start | bytes 3145736 | tf_op jit(solution)/shard_map/ppermute | solution.py:48
  176.6 15.2 %collective-permute-start.30 = (bf16[64,4096]{1,0:T(8,128)(2,1)S(1)}, bf16[64,4096]{1,0:T(8,128)(2,1)S(1)}, u32[]{:S(2)}, u32[]{:S(2)}) collective-permute-start(bf16[64,4096]{1,0:T(8,128)(2,1)S(1)} %get-tuple-element.61), channel_id=1, source_target_pairs={{0,32},{16,48},{32,64},{48,80},{64,96},{80,112},{96,0},{112,16},{1... | collective-permute-start | bytes 1572872 | tf_op jit(solution)/shard_map/ppermute | solution.py:404
  176.7 15.4 %collective-permute-start.29 = (bf16[64,4096]{1,0:T(8,128)(2,1)S(1)}, bf16[64,4096]{1,0:T(8,128)(2,1)S(1)}, u32[]{:S(2)}, u32[]{:S(2)}) collective-permute-start(bf16[64,4096]{1,0:T(8,128)(2,1)S(1)} %get-tuple-element.62), channel_id=1, source_target_pairs={{0,96},{16,112},{32,0},{48,16},{64,32},{80,48},{96,64},{112,80},{1... | collective-permute-start | bytes 1572872 | tf_op jit(solution)/shard_map/ppermute | solution.py:405
  192.0 14.4 %collective-permute-start.31 = (bf16[64,4096]{1,0:T(8,128)(2,1)S(1)}, bf16[64,4096]{1,0:T(8,128)(2,1)S(1)}, u32[]{:S(2)}, u32[]{:S(2)}) collective-permute-start(bf16[64,4096]{1,0:T(8,128)(2,1)S(1)} %slice_add_fusion), channel_id=1, source_target_pairs={{0,32},{16,48},{32,64},{48,80},{64,96},{80,112},{96,0},{112,16},{1... | collective-permute-start | bytes 1572872 | tf_op jit(solution)/shard_map/ppermute | solution.py:413
  192.2 14.3 %collective-permute-start.32 = (bf16[64,4096]{1,0:T(8,128)(2,1)S(1)}, bf16[64,4096]{1,0:T(8,128)(2,1)S(1)}, u32[]{:S(2)}, u32[]{:S(2)}) collective-permute-start(bf16[64,4096]{1,0:T(8,128)(2,1)S(1)} %slice_add_fusion.1), channel_id=1, source_target_pairs={{0,96},{16,112},{32,0},{48,16},{64,32},{80,48},{96,64},{112,80},{1... | collective-permute-start | bytes 1572872 | tf_op jit(solution)/shard_map/ppermute | solution.py:412
  206.7 4.8 %copy-start.11 = (bf16[4,4,2]{1,2,0:T(2,128)(2,1)S(1)}, bf16[4,4,2]{1,2,0:T(2,128)(2,1)}, u32[]{:S(2)}) copy-start(bf16[4,4,2]{1,2,0:T(2,128)(2,1)} %param.30) | copy-start | bytes 196
  207.8 19.6 %all-to-all-start.2 = ((bf16[16,8,4096]{2,1,0:T(8,128)(2,1)}), bf16[16,8,4096]{2,1,0:T(8,128)(2,1)S(1)}, u32[]{:S(2)}, u32[]{:S(2)}) async-start(bf16[16,8,4096]{2,1,0:T(8,128)(2,1)} %maximum_bitcast_fusion), calls=%async_computation.2 | async-start | bytes 2097152 | tf_op jit(solution)/shard_map/all_to_all | solution.py:475
